TPU v7x, 256 devices: a whole 4x4x8 slice. The times are simulated.
256 devices in a mesh: filt: 2 (over core), row: 4 (over x), col: 32 (over z, y).
Axes of the slice: x: 4, y: 4, z: 8, core: 2. Of those that a mesh axis runs over, the one named last changes fastest.
Arguments:
- particles: bfloat16 [24576, 256], P(('filt', 'row', 'col')), parts along dimension 0, may hold values from -6 to 6
- cotangent: bfloat16 [24576, 256], P(('filt', 'row', 'col')), parts along dimension 0, may hold values from -3 to 3
- row_potential: bfloat16 [24576], P(('filt', 'row', 'col')), parts along dimension 0, may hold values from -0.099609375 to 0.099609375
- col_potential: bfloat16 [24576], P(('filt', 'row', 'col')), parts along dimension 0, may hold values from -0.099609375 to 0.099609375
- weights: bfloat16 [24576], P(('filt', 'row', 'col')), parts along dimension 0, may hold values from 0.5 to 18
Outputs:
- grad_particles: bfloat16 [24576, 256], P(('filt', 'row', 'col')), parts along dimension 0
- grad_weights: float32 [24576], P(('filt', 'row', 'col')), parts along dimension 0
There are 2 independent parts, one for each index of `filt`. A program takes and returns all parts, laid end to end along the dimension named above; each array names one. Nothing has to cross between parts.
All inputs are finite; a program needn't handle non-finite values.
Results may differ from a plain program's by a relative error of at most 0.02.
Values may be sent and summed in bfloat16 or wider, within the bound.
No kernel may reach another device: no remote copies, remote signals or barrier semaphores. Data moves between devices by JAX's collectives and lax.ppermute only.
A program may use at most 64 MiB of HBM per device.

v0:
```python
import jax
import jax.numpy as jnp
from jax import lax
from jax.sharding import PartitionSpec as P

ITERS = 4


EPS = 0.09


def local(particles, cotangent, row_potential, col_potential, weights):
    row_parts, row_fpot, row_wts = (
        lax.all_gather(particles, "col", axis=0, tiled=True),
        lax.all_gather(row_potential, "col", axis=0, tiled=True),
        lax.all_gather(weights, "col", axis=0, tiled=True),
    )
    col_parts, col_grads, col_gpot = (
        lax.all_gather(particles, "row", axis=0, tiled=True),
        lax.all_gather(cotangent, "row", axis=0, tiled=True),
        lax.all_gather(col_potential, "row", axis=0, tiled=True),
    )
    own = particles.shape[0]
    width = particles.shape[1]
    rows = row_parts.shape[0]
    cols = col_parts.shape[0]
    blk = 512
    count = rows // blk
    row_float = row_parts.astype(jnp.float32)
    row_sq = jnp.sum(row_float * row_float, axis=1)
    col_float = col_parts.astype(jnp.float32)
    col_sq = jnp.sum(col_float * col_float, axis=1)
    fpot = row_fpot.astype(jnp.float32)
    gpot = col_gpot.astype(jnp.float32)
    stacked = jnp.concatenate([col_parts, col_grads], axis=0)
    items = (
        row_parts.reshape(count, blk, width),
        fpot.reshape(count, blk),
        row_sq.reshape(count, blk),
    )

    def plan_from(cross, pot_blk, sq_blk):
        cost = (sq_blk[:, None] + col_sq[None, :] - 2.0 * cross) / (2.0 * width)
        return jnp.exp((pot_blk[:, None] + gpot[None, :] - cost) / EPS)

    def plan_only(part_blk, pot_blk, sq_blk):
        cross = jnp.einsum("rd,cd->rc", part_blk, col_parts, preferred_element_type=jnp.float32)
        return plan_from(cross, pot_blk, sq_blk)

    def first(carry, item):
        part_blk, pot_blk, sq_blk = item
        both = jnp.einsum("rd,cd->rc", part_blk, stacked, preferred_element_type=jnp.float32)
        plan = plan_from(both[:, :cols], pot_blk, sq_blk)
        weighted = plan * both[:, cols:]
        return (
            (carry[0] + jnp.sum(plan, axis=0), carry[1] + jnp.sum(weighted, axis=0)),
            (jnp.sum(plan, axis=1), jnp.sum(weighted, axis=1)),
        )

    zeros_c = jnp.zeros((cols,), jnp.float32)
    (colmass_part, colph_part), (rowmass_part, rowph_part) = lax.scan(
        first, (zeros_c, zeros_c), items
    )
    rowmass, rowph = lax.psum((rowmass_part.reshape(rows), rowph_part.reshape(rows)), "col")
    colmass, colph = lax.psum((colmass_part, colph_part), "row")
    psi = zeros_c
    phi = jnp.zeros((rows,), jnp.float32)
    for step in range(ITERS):

        def apply_rows(carry, item):
            plan = plan_only(item[0], item[1], item[2])
            return (carry, jnp.dot(plan, psi, precision=lax.Precision.HIGHEST))

        unused, row_apply = lax.scan(apply_rows, jnp.zeros((), jnp.float32), items)
        row_total = lax.psum(row_apply.reshape(rows), "col")
        phi = -(rowph + row_total) / rowmass

        def apply_cols(acc, item):
            plan = plan_only(item[0], item[1], item[2])
            return (acc + jnp.dot(item[3], plan, precision=lax.Precision.HIGHEST), None)

        col_apply, unused_out = lax.scan(apply_cols, zeros_c, items + (phi.reshape(count, blk),))
        col_total = lax.psum(col_apply, "row")
        psi = -(colph + col_total) / colmass

    def last(acc, item):
        part_blk, pot_blk, sq_blk, phi_blk = item
        both = jnp.einsum("rd,cd->rc", part_blk, stacked, preferred_element_type=jnp.float32)
        plan = plan_from(both[:, :cols], pot_blk, sq_blk)
        mixed = plan * (both[:, cols:] + phi_blk[:, None] + psi[None, :])
        qrow = jnp.sum(mixed, axis=1)
        plan_bf = plan.astype(jnp.bfloat16)
        mixed_bf = mixed.astype(jnp.bfloat16)
        rowterm = jnp.dot(plan_bf, col_grads, preferred_element_type=jnp.float32)
        rowterm = rowterm + (
            jnp.dot(mixed_bf, col_parts, preferred_element_type=jnp.float32)
            - qrow[:, None] * part_blk.astype(jnp.float32)
        ) / (width * EPS)
        return (
            acc + jnp.einsum("rc,rd->cd", mixed_bf, part_blk, preferred_element_type=jnp.float32),
            rowterm,
        )

    col_acc, row_terms = lax.scan(
        last, jnp.zeros((cols, width), jnp.float32), items + (phi.reshape(count, blk),)
    )
    row_terms = row_terms.reshape(rows, width)
    start = lax.axis_index("col") * own
    summed = lax.psum(row_terms.astype(jnp.bfloat16), "col").astype(jnp.float32)
    row_own = lax.dynamic_slice_in_dim(summed, start, own, 0)
    col_own = lax.psum_scatter(
        col_acc.astype(jnp.bfloat16), "row", scatter_dimension=0, tiled=True
    ).astype(jnp.float32)
    grad_particles = (row_own + col_own / (width * EPS)).astype(jnp.bfloat16)
    phi_own = lax.dynamic_slice_in_dim(phi, start, own, 0)
    own_wts = weights.astype(jnp.float32)
    total, wphi = lax.psum((jnp.sum(own_wts), jnp.sum(own_wts * phi_own)), ("row", "col"))
    count_all = rows * lax.axis_size("row")
    grad_weights = -(count_all / total) * (phi_own - wphi / total)
    return (grad_particles, grad_weights)


def solution(mesh):
    return jax.shard_map(
        local,
        mesh=mesh,
        in_specs=(
            P(("filt", "row", "col"), None),
            P(("filt", "row", "col"), None),
            P(("filt", "row", "col")),
            P(("filt", "row", "col")),
            P(("filt", "row", "col")),
        ),
        out_specs=(P(("filt", "row", "col"), None), P(("filt", "row", "col"))),
        check_vma=False,
    )
```

profile of v0, /device:TPU:8, one launch (start us, length us, event | category | flops | bytes accessed | tf_op | source)
XLA Modules:
  0.0 1151.9 jit_solution(2241112115767740689)
XLA Ops:
  8.0 1.3 dynamic-slice
  9.9 0.9 dynamic-update-slice
  10.7 75.0 %all-reduce = bf16[3072]{0:T(1024)(128)(2,1)S(1)} all-reduce(bf16[3072]{0:T(1024)(128)(2,1)S(1)} %dynamic-update-slice), channel_id=1, replica_groups=mesh['filt'=2,'row'=4,'col'=32] {'col'}, use_global_device_ids=true, to_apply=%add | all-reduce | flops 3072 | bytes 12288
  85.8 1.3 dynamic-slice.1
  87.6 0.9 dynamic-update-slice.1
  88.5 10.5 all-reduce.1
  99.0 12.3 %all_gather.18 = bf16[384,256]{1,0:T(8,128)(2,1)S(1)} all-gather(bf16[96,256]{1,0:T(8,128)(2,1)} %param.25), channel_id=1, replica_groups=mesh['filt'=2,'row'=4,'col'=32] {'row'}, dimensions={0}, use_global_device_ids=true | all-gather | bytes 245760 | tf_op jit(solution)/shard_map/all_gather | solution.py:19
  111.3 12.3 %all_gather.19 = bf16[384,256]{1,0:T(8,128)(2,1)S(1)} all-gather(bf16[96,256]{1,0:T(8,128)(2,1)} %param.26), channel_id=1, replica_groups=mesh['filt'=2,'row'=4,'col'=32] {'row'}, dimensions={0}, use_global_device_ids=true | all-gather | bytes 245760 | tf_op jit(solution)/shard_map/all_gather | solution.py:20
  123.9 2.0 multiply_reduce_fusion
  125.9 7.0 while.118
  132.9 7.5 while.117
  133.4 0.8 fusion.226
  134.6 0.8 fusion.226
  135.9 0.8 fusion.226
  137.1 0.8 fusion.226
  138.4 0.8 fusion.226
  139.6 0.8 fusion.226
  140.5 139.2 %all-reduce.3 = (f32[3072]{0:T(1024)S(1)}, f32[3072]{0:T(1024)S(1)}, f32[3072]{0:T(1024)S(1)}) all-reduce(f32[3072]{0:T(1024)S(1)} %reshape.119, f32[3072]{0:T(1024)S(1)} %reshape.117, f32[3072]{0:T(1024)S(1)} %reshape.118), channel_id=1, replica_groups=mesh['filt'=2,'row'=4,'col'=32] {'col'}, use_global_device_ids=true, to_apply=%region_13.14 | all-reduce | flops 9216 | bytes 73728 | tf_op jit(solution)/shard_map/psum | solution.py:64
  279.7 5.8 while.119
  285.5 7.9 all-reduce.4
  294.0 7.5 while.124
  300.6 0.8 fusion.268
  301.5 137.7 %psum.111 = f32[3072]{0:T(1024)S(1)} all-reduce(f32[3072]{0:T(1024)S(1)} %reshape.121), channel_id=1, replica_groups=mesh['filt'=2,'row'=4,'col'=32] {'col'}, use_global_device_ids=true, to_apply=%region_20.21 | all-reduce | flops 3072 | bytes 24576 | tf_op jit(solution)/shard_map/psum | solution.py:75
  439.2 5.8 while.120
  445.0 9.7 psum.112
  455.3 7.5 while.125
  462.8 137.7 %psum.113 = f32[3072]{0:T(1024)S(1)} all-reduce(f32[3072]{0:T(1024)S(1)} %reshape.123), channel_id=1, replica_groups=mesh['filt'=2,'row'=4,'col'=32] {'col'}, use_global_device_ids=true, to_apply=%region_26.27 | all-reduce | flops 3072 | bytes 24576 | tf_op jit(solution)/shard_map/psum | solution.py:75
  600.5 5.8 while.121
  606.3 7.7 psum.114
  614.7 7.5 while.126
  615.1 0.8 fusion.280
  616.3 0.8 fusion.280
  617.6 0.8 fusion.280
  618.8 0.8 fusion.280
  620.1 0.8 fusion.280
  621.3 0.8 fusion.280
  622.2 138.0 %psum.115 = f32[3072]{0:T(1024)S(1)} all-reduce(f32[3072]{0:T(1024)S(1)} %reshape.125), channel_id=1, replica_groups=mesh['filt'=2,'row'=4,'col'=32] {'col'}, use_global_device_ids=true, to_apply=%region_32.33 | all-reduce | flops 3072 | bytes 24576 | tf_op jit(solution)/shard_map/psum | solution.py:75
  760.2 5.8 while.122
  765.9 9.7 psum.116
  775.7 16.9 %while.123 = (s32[]{:T(128)}, f32[384,256]{1,0:T(8,128)S(1)}, bf16[6,512,256]{2,1,0:T(8,128)(2,1)}, f32[6,512]{1,0:T(8,128)S(1)}, f32[384]{0:T(512)S(1)}, /*inde...) while((s32[]{:T(128)}, f32[384,256]{1,0:T(8,128)S(1)}, ...), condition=%wide.region_38.39_spmd.clone, body=%wide.region_36.38_spmd.clone.sunk | while | flops 508100096 | bytes 9079975 | solution.py:104
  777.1 1.0 fusion.262
  779.9 1.0 fusion.262
  782.7 1.0 fusion.262
  785.5 1.0 fusion.262
  788.4 1.0 fusion.262
  791.2 1.0 fusion.262
  794.8 346.5 %all-reduce.2 = (f32[]{:T(128)}, f32[]{:T(128)}) all-reduce(f32[]{:T(128)} %get-tuple-element.718, f32[]{:T(128)} %get-tuple-element.717), channel_id=1, replica_groups=mesh['filt'=2,'row'=4,'col'=32] {'row','col'}, use_global_device_ids=true, to_apply=%region_44.45 | all-reduce | flops 2 | bytes 16 | tf_op jit(solution)/shard_map/psum | solution.py:117
  1143.9 1.5 add_convert_fusion
  (322 shorter events, 64.2 us)
Async XLA Ops:
  7.2 116.7 %all-gather.2.cloned.1.call-start = ((), (), s32[]{:S(2)}) async-start(), calls=%async_computation.1 | async-start | bytes 1622016 | tf_op jit(solution)/shard_map/all_gather | solution.py:14
  7.9 1136.0 %reduce-scatter.2.cloned.1.call-start = ((), (), s32[]{:S(2)}) async-start(), calls=%async_computation.3 | async-start | bytes 245760 | tf_op jit(solution)/shard_map/reduce_scatter | solution.py:111
  123.8 2.1 copy-start
  293.4 0.6 copy-start.2
  454.7 0.6 copy-start.3
  614.1 0.6 copy-start.1
  792.6 1.5 copy-start.4
  793.4 350.6 %all-reduce.7.cloned.1.call-start = ((), (), s32[]{:S(2)}) async-start(), calls=%async_computation.2 | async-start | bytes 3145728 | tf_op jit(solution)/shard_map/psum | solution.py:109
Sparse Core Ops, SparseCore 0:
  10.6 78.8 all-gather.1
  793.5 18.2 reduce-scatter.1
  815.6 149.9 all-reduce.6
where the time goes:
time: 1150 us
  blocking collectives  1040 us (90%)
  matrix products  65.2 us (6%)
  between operations  17.3 us (2%)
  other arithmetic  12.4 us (1%)
    psum x3, blocking collectives, local(): row_total = lax.psum(row_apply.reshape(rows), 'col')  413 us
    psum x1, blocking collectives, local(): lax.psum((jnp.sum(own_wts), jnp.sum(own_wts * phi_own)), ('row', 'col'))  347 us
    psum x1, blocking collectives, local(): lax.psum((rowmass_part.reshape(rows), rowph_part.reshape(rows)), 'col')  139 us
    unnamed x2, blocking collectives  85.5 us
    psum x3, blocking collectives, local(): col_total = lax.psum(col_apply, 'row')  27.2 us
  transfers between devices with their start and end apart: 3, of which 0 were waited for; matrix products, arithmetic and copies ran while one was open for 0% of the time, Pallas kernels for 0%

commit v1 on v0

v1 whole, which is shorter than its diff:
```python
import functools

import jax
import jax.numpy as jnp
from jax import lax
from jax.experimental import pallas as pl
from jax.experimental.pallas import tpu as pltpu
from jax.sharding import Mesh
from jax.sharding import PartitionSpec as P

ITERS = 4


EPS = 0.09

LANES = 128
AUX = 16
F32 = jnp.float32
BF16 = jnp.bfloat16


def params():
    return pltpu.CompilerParams(vmem_limit_bytes=40 << 20)


def whole(n):
    return [pl.BlockSpec(memory_space=pltpu.VMEM)] * n


def eye(own):
    rows = lax.broadcasted_iota(jnp.int32, (own, LANES), 0)
    lanes = lax.broadcasted_iota(jnp.int32, (own, LANES), 1)
    return rows == lanes


def to_row(col, own):
    return jnp.sum(jnp.where(eye(own), col, 0.0), axis=0, keepdims=True)


def to_col(row, own):
    return jnp.sum(jnp.where(eye(own), row, 0.0), axis=1, keepdims=True)


def lanes_of(col):
    out = []
    for k in range(col.shape[0] // LANES):
        out.append(to_row(col[k * LANES : (k + 1) * LANES], LANES))
    return jnp.concatenate(out, axis=1)


def fold(block):
    return jnp.sum(block.reshape(block.shape[0] // 8, 8, block.shape[1]), axis=0)


def put_lanes(ref, slots, base, row):
    for k in range(row.shape[1] // LANES):
        piece = row[:, k * LANES : (k + 1) * LANES]
        for s in range(slots):
            ref[s, base + k : base + k + 1, :] = piece


def build(own, width, isrc, jsrc, pi_ref, pj_ref, plan_ref, xi_ref, xj_ref, gj_ref, w_ref, mass_ref, col_ref):
    cols = jsrc * own
    scale = 1.0 / (2.0 * width * EPS)
    bias = []
    for s in range(jsrc):
        part = pj_ref[s, 0:own, :]
        xj_ref[s * own : (s + 1) * own, :] = part
        gj_ref[s * own : (s + 1) * own, :] = pj_ref[s, own : 2 * own, :]
        pf = part.astype(F32)
        sq = jnp.sum(pf * pf, axis=1, keepdims=True)
        pot = to_col(pj_ref[s, 2 * own : 2 * own + AUX, :].astype(F32)[0:1, 0:LANES], own)
        bias.append(pot / EPS - sq * scale)
    jbias = lanes_of(jnp.concatenate(bias, axis=0))
    xj = xj_ref[...]
    gj = gj_ref[...]

    def step(s, acc):
        part = pi_ref[s, 0:own, :]
        xi_ref[pl.ds(pl.multiple_of(s * own, own), own), :] = part
        aux = pi_ref[s, own : own + AUX, :].astype(F32)
        w_ref[pl.ds(s, 1), :] = aux[1:2, 0:LANES]
        pf = part.astype(F32)
        sq = jnp.sum(pf * pf, axis=1, keepdims=True)
        ibias = to_col(aux[0:1, 0:LANES], own) / EPS - sq * scale
        dims = (((1,), (1,)), ((), ()))
        cross = lax.dot_general(part, xj, dims, preferred_element_type=F32)
        inner = lax.dot_general(part, gj, dims, preferred_element_type=F32)
        plan = jnp.exp(cross * (2.0 * scale) + jbias + ibias)
        plan_ref[pl.ds(pl.multiple_of(s * own, own), own), :] = plan
        weighted = plan * inner
        mass = to_row(jnp.sum(plan, axis=1, keepdims=True), own)
        ph = to_row(jnp.sum(weighted, axis=1, keepdims=True), own)
        mass_ref[0, pl.ds(s, 1), :] = mass
        mass_ref[0, pl.ds(isrc + s, 1), :] = ph
        return acc[0] + fold(plan), acc[1] + fold(weighted)

    zero = jnp.zeros((8, cols), F32)
    cmass, cph = lax.fori_loop(0, isrc, step, (zero, zero))
    for s in range(1, isrc):
        mass_ref[s] = mass_ref[0]
    col_ref[...] = jnp.zeros_like(col_ref)
    cmass = jnp.sum(cmass, axis=0, keepdims=True)
    cph = jnp.sum(cph, axis=0, keepdims=True)
    for k in range(cols // LANES):
        col_ref[k : k + 1, :] = cmass[:, k * LANES : (k + 1) * LANES]
        col_ref[8 + k : 9 + k, :] = cph[:, k * LANES : (k + 1) * LANES]


def apply_cols(own, isrc, phi_ref, plan_ref):
    cols = plan_ref.shape[1]

    def step(s, acc):
        col = to_col(phi_ref[pl.ds(s, 1), :], own)
        block = plan_ref[pl.ds(pl.multiple_of(s * own, own), own), :]
        return acc + fold(block * col)

    acc = lax.fori_loop(0, isrc, step, jnp.zeros((8, cols), F32))
    return jnp.sum(acc, axis=0, keepdims=True)


def valid(own, value):
    lanes = lax.broadcasted_iota(jnp.int32, value.shape, 1)
    return jnp.where(lanes < own, value, 0.0)


def phi_first(own, isrc, jsrc, got_ref, col_ref, plan_ref, mass_ref, phi_ref, send_ref):
    total = jnp.sum(got_ref[...], axis=0)
    mass_ref[...] = total
    phi_ref[...] = valid(own, -total[isrc:] / total[:isrc])
    applied = apply_cols(own, isrc, phi_ref, plan_ref)
    for s in range(jsrc):
        send_ref[s, 0:16, :] = col_ref[...]
        send_ref[s, 16:24, :] = jnp.zeros((8, LANES), F32)
    put_lanes(send_ref, jsrc, 16, applied)


def phi_next(own, isrc, jsrc, got_ref, mass_ref, w_ref, plan_ref, phi_ref, send_ref):
    total = jnp.sum(got_ref[...], axis=0)
    mass = mass_ref[...]
    phi = valid(own, -(mass[isrc:] + total) / mass[:isrc])
    phi_ref[...] = phi
    applied = apply_cols(own, isrc, phi_ref, plan_ref)
    wts = valid(own, w_ref[...])
    wsum = jnp.sum(wts, axis=0, keepdims=True)
    wphi = jnp.sum(wts * phi, axis=0, keepdims=True)
    for s in range(jsrc):
        send_ref[s, 6:7, :] = wsum
        send_ref[s, 7:8, :] = wphi
    put_lanes(send_ref, jsrc, 0, applied)


def row_of(value, count):
    return jnp.concatenate([value[k : k + 1, :] for k in range(count)], axis=1)


def apply_rows(own, isrc, psi, plan_ref, send_ref):
    def step(s, carry):
        block = plan_ref[pl.ds(pl.multiple_of(s * own, own), own), :]
        col = jnp.sum(block * psi, axis=1, keepdims=True)
        send_ref[0, pl.ds(s, 1), :] = to_row(col, own)
        return carry

    lax.fori_loop(0, isrc, step, 0)
    for s in range(1, isrc):
        send_ref[s] = send_ref[0]


def psi_first(own, isrc, got_ref, plan_ref, col_ref, send_ref):
    total = jnp.sum(got_ref[...], axis=0)
    col_ref[...] = total[:16]
    count = plan_ref.shape[1] // LANES
    psi = row_of(-(total[8:16] + total[16:24]) / total[0:8], count)
    apply_rows(own, isrc, psi, plan_ref, send_ref)


def psi_next(own, isrc, got_ref, col_ref, plan_ref, send_ref):
    total = jnp.sum(got_ref[...], axis=0)
    count = plan_ref.shape[1] // LANES
    psi = row_of(-(col_ref[8:16] + total) / col_ref[0:8], count)
    apply_rows(own, isrc, psi, plan_ref, send_ref)


def finish(own, width, isrc, jsrc, every, got_ref, col_ref, phi_ref, plan_ref, xi_ref, xj_ref, gj_ref, row_ref, out_ref, gw_ref, acc_ref):
    total = jnp.sum(got_ref[...], axis=0)
    count = plan_ref.shape[1] // LANES
    psi = row_of(-(col_ref[8:16] + total) / col_ref[0:8], count)
    wsum = jnp.sum(total[6:7], axis=1, keepdims=True)
    wphi = jnp.sum(total[7:8], axis=1, keepdims=True)
    gw_ref[...] = -(every / wsum) * (phi_ref[...] - wphi / wsum)
    xj = xj_ref[...]
    gj = gj_ref[...]
    scale = 1.0 / (width * EPS)
    acc_ref[...] = jnp.zeros_like(acc_ref)

    def step(s, carry):
        part = xi_ref[pl.ds(pl.multiple_of(s * own, own), own), :]
        plan = plan_ref[pl.ds(pl.multiple_of(s * own, own), own), :]
        col = to_col(phi_ref[pl.ds(s, 1), :], own)
        inner = lax.dot_general(part, gj, (((1,), (1,)), ((), ())), preferred_element_type=F32)
        mixed = plan * (inner + (col + psi))
        qrow = jnp.sum(mixed, axis=1, keepdims=True)
        mixed_bf = mixed.astype(BF16)
        term = jnp.dot(plan.astype(BF16), gj, preferred_element_type=F32)
        term += (jnp.dot(mixed_bf, xj, preferred_element_type=F32) - qrow * part.astype(F32)) * scale
        row_ref[s] = term.astype(BF16)
        acc_ref[...] += lax.dot_general(mixed_bf, part, (((0,), (0,)), ((), ())), preferred_element_type=F32)
        return carry

    lax.fori_loop(0, isrc, step, 0)
    for s in range(jsrc):
        out_ref[s] = (acc_ref[s * own : (s + 1) * own, :] * scale).astype(BF16)


def local(particles, cotangent, row_potential, col_potential, weights):
    own, width = particles.shape
    iaxes, jaxes = ("row", "y"), ("z",)
    isrc = lax.axis_size("row") * lax.axis_size("y")
    jsrc = lax.axis_size("z")
    rows, cols = isrc * own, jsrc * own

    def swap(value, axes):
        return lax.all_to_all(value, axes, 0, 0, tiled=True)

    def aux(*vectors):
        block = jnp.stack([jnp.pad(v, (0, width - own)) for v in vectors])
        return jnp.pad(block, ((0, AUX - len(vectors)), (0, 0)))

    ipack = jnp.concatenate([particles, aux(row_potential, weights)], axis=0)
    jpack = jnp.concatenate([particles, cotangent, aux(col_potential)], axis=0)
    igot = swap(jnp.broadcast_to(ipack, (isrc,) + ipack.shape), iaxes)
    jgot = swap(jnp.broadcast_to(jpack, (jsrc,) + jpack.shape), jaxes)

    def call(body, outs, *args, scratch=()):
        return pl.pallas_call(
            body,
            out_shape=[jax.ShapeDtypeStruct(s, d) for s, d in outs],
            in_specs=whole(len(args)),
            out_specs=whole(len(outs)),
            scratch_shapes=list(scratch),
            compiler_params=params(),
        )(*args)

    plan, xi, xj, gj, wts, mass_send, col_part = call(
        functools.partial(build, own, width, isrc, jsrc),
        [
            ((rows, cols), F32),
            ((rows, width), BF16),
            ((cols, width), BF16),
            ((cols, width), BF16),
            ((isrc, LANES), F32),
            ((isrc, 2 * isrc, LANES), F32),
            ((16, LANES), F32),
        ],
        igot,
        jgot,
    )
    got = swap(mass_send, iaxes)
    mass, phi, send = call(
        functools.partial(phi_first, own, isrc, jsrc),
        [((2 * isrc, LANES), F32), ((isrc, LANES), F32), ((jsrc, 24, LANES), F32)],
        got,
        col_part,
        plan,
    )
    got = swap(send, jaxes)
    col, send = call(
        functools.partial(psi_first, own, isrc),
        [((16, LANES), F32), ((isrc, isrc, LANES), F32)],
        got,
        plan,
    )
    for step in range(1, ITERS):
        got = swap(send, iaxes)
        phi, send = call(
            functools.partial(phi_next, own, isrc, jsrc),
            [((isrc, LANES), F32), ((jsrc, 8, LANES), F32)],
            got,
            mass,
            wts,
            plan,
        )
        got = swap(send, jaxes)
        if step < ITERS - 1:
            (send,) = call(
                functools.partial(psi_next, own, isrc),
                [((isrc, isrc, LANES), F32)],
                got,
                col,
                plan,
            )
    row_send, col_send, gw = call(
        functools.partial(finish, own, width, isrc, jsrc, float(isrc * jsrc * own)),
        [
            ((isrc, own, width), BF16),
            ((jsrc, own, width), BF16),
            ((isrc, LANES), F32),
        ],
        got,
        col,
        phi,
        plan,
        xi,
        xj,
        gj,
        scratch=[pltpu.VMEM((cols, width), F32)],
    )
    row_got = swap(row_send, iaxes)
    col_got = swap(col_send, jaxes)
    grad = jnp.sum(row_got.astype(F32), axis=0) + jnp.sum(col_got.astype(F32), axis=0)
    mine = lax.axis_index("row") * lax.axis_size("y") + lax.axis_index("y")
    grad_weights = lax.dynamic_slice(gw, (mine, 0), (1, own)).reshape(own)
    return (grad.astype(BF16), grad_weights)


def solution(mesh):
    filt, row, col = mesh.devices.shape
    split = Mesh(mesh.devices.reshape(filt, row, 8, col // 8), ("filt", "row", "z", "y"))
    spec = ("filt", "row", "z", "y")
    return jax.shard_map(
        local,
        mesh=split,
        in_specs=(P(spec, None), P(spec, None), P(spec), P(spec), P(spec)),
        out_specs=(P(spec, None), P(spec)),
        check_vma=False,
    )
```

time: 1150 us -> 209 us (0.18)
  blocking collectives: 1040 us -> 133 us
  matrix products: 65.2 us -> 0 us
  Pallas kernels: 0 us -> 33.3 us
  waiting for transfers between devices: 1.4 us -> 22.7 us
  between operations: 17.3 us -> 0.67 us
  starting transfers between devices: 0.12 us -> 12.4 us
    psum x9 -> x0, blocking collectives: 934 us -> none  [the longest x3 413 us: local(): row_total = lax.psum(row_apply.reshape(rows), 'col')]
    all_to_all x0 -> x10, blocking collectives: none -> 133 us  [swap(): return lax.all_to_all(value, axes, 0, 0, tiled=True)]
    unnamed x2 -> x0, blocking collectives: 85.5 us -> none
    dot_general x126 -> x0, matrix products: 65.2 us -> none  [the longest x48 19.1 us: plan_only(): jnp.einsum('rd,cd->rc', part_blk, col_parts, preferred_element_type=jnp.f...]
    pallas_call x0 -> x9, Pallas kernels: none -> 33.3 us  [call(): pl.pallas_call(body, out_shape=[jax.ShapeDtypeStruct(s, d) for s, d in ou...]
    all_gather x2 -> x0, blocking collectives: 24.7 us -> none  [the longest x1 12.3 us: local(): lax.all_gather(particles, 'row', axis=0, tiled=True)]
    all_to_all x0 -> x2, waiting for transfers between devices: none -> 22.7 us  [swap(): return lax.all_to_all(value, axes, 0, 0, tiled=True)]
    all_to_all x0 -> x2, starting transfers between devices: none -> 12.4 us  [swap(): return lax.all_to_all(value, axes, 0, 0, tiled=True)]
  transfers between devices with their start and end apart: 3 -> 2, of which waited for: 0 -> 2; matrix products, arithmetic and copies ran while one was open for 0% -> 1% of each run, Pallas kernels for 0% -> 0%
where the time goes in v1:
time: 209 us; the launch traced here: 208 us
  blocking collectives  133 us (64%)
  Pallas kernels  33.3 us (16%)
  waiting for transfers between devices  22.7 us (11%)
  starting transfers between devices  12.4 us (6%)
  local copies, waits for them, and re-layouts  3.57 us (2%)
  other arithmetic  2.44 us (1%)
    all_to_all x10, blocking collectives, swap(): return lax.all_to_all(value, axes, 0, 0, tiled=True)  133 us
    pallas_call x9, Pallas kernels, call(): pl.pallas_call(body, out_shape=[jax.ShapeDtypeStruct(s, d) for s, d in ou...  33.3 us
    all_to_all x2, waiting for transfers between devices, swap(): return lax.all_to_all(value, axes, 0, 0, tiled=True)  22.7 us
    all_to_all x2, starting transfers between devices, swap(): return lax.all_to_all(value, axes, 0, 0, tiled=True)  12.4 us
  transfers between devices with their start and end apart: 2, of which 2 were waited for; matrix products, arithmetic and copies ran while one was open for 1% of the time, Pallas kernels for 0%

profile of v1, /device:TPU:8, one launch (start us, length us, event | category | flops | bytes accessed | tf_op | source)
XLA Modules:
  0.0 208.5 jit_solution(2710725987934587935)
XLA Ops:
  0.6 0.7 pad.18
  1.3 0.7 pad.19
  2.0 0.8 pad_maximum_fusion
  2.8 1.0 broadcast_in_dim.6
  3.8 7.4 %all-to-all-start = ((bf16[16,112,256]{2,1,0:T(8,128)(2,1)}), bf16[16,112,256]{2,1,0:T(8,128)(2,1)S(1)}, u32[]{:S(2)}, u32[]{:S(2)}) async-start(bf16[16,112,256]{2,1,0:T(8,128)(2,1)} %broadcast_in_dim.6), calls=%async_computation | async-start | bytes 1835008 | tf_op jit(solution)/shard_map/all_to_all | solution.py:223
  11.2 0.7 pad.21
  11.8 0.8 fusion.1
  12.7 13.2 %all-to-all-done.pi_ref = bf16[16,112,256]{2,1,0:T(8,128)(2,1)S(1)} async-done(((bf16[16,112,256]{2,1,0:T(8,128)(2,1)}), bf16[16,112,256]{2,1,0:T(8,128)(2,1)S(1)}, u32[]{:S(2)}, u32[]{:S(2)}) %all-to-all-start) | async-done | bytes 917536 | tf_op jit(solution)/shard_map/all_to_all | solution.py:223
  25.8 0.1 broadcast_in_dim.7
  25.9 30.5 %all_to_all.60.pj_ref = bf16[8,208,256]{2,1,0:T(8,128)(2,1)S(1)} all-to-all(bf16[8,208,256]{2,1,0:T(8,128)(2,1)S(1)} %broadcast_in_dim.7), channel_id=1, replica_groups=mesh['filt'=2,'row'=4,'z'=8,'y'=4] {'z'}, dimensions={0} | all-to-all | bytes 1703936 | tf_op jit(solution)/shard_map/all_to_all | solution.py:223
  56.4 8.0 %shard_map.68 = (f32[1536,768]{1,0:T(8,128)S(1)}, bf16[1536,256]{1,0:T(8,128)(2,1)S(1)}, bf16[768,256]{1,0:T(8,128)(2,1)S(1)}, bf16[768,256]{1,0:T(8,128)(2,1)S(...) custom-call(bf16[16,112,256]{2,1,0:T(8,128)(2,1)S(1)} %all-to-all-done.pi_ref, ...), custom_call_target="tpu_custom_call" | custom-call | tf_op jit(solution)/shard_map/pallas_call | solution.py:235
  64.4 12.5 %all_to_all.61.got_ref = f32[16,32,128]{2,1,0:T(8,128)S(1)} all-to-all(f32[16,32,128]{2,1,0:T(8,128)S(1)} %get-tuple-element.20), channel_id=1, replica_groups=mesh['filt'=2,'row'=4,'z'=8,'y'=4] {'row','y'}, dimensions={0} | all-to-all | bytes 524288 | tf_op jit(solution)/shard_map/all_to_all | solution.py:223
  76.9 2.1 %shard_map.69 = (f32[32,128]{1,0:T(8,128)S(1)}, f32[16,128]{1,0:T(8,128)}, f32[8,24,128]{2,1,0:T(8,128)S(1)}) custom-call(f32[16,32,128]{2,1,0:T(8,128)S(1)} %all_to_all.61.got_ref, f32[16,128]{1,0:T(8,128)S(1)} %get-tuple-element.21.col_ref, f32[1536,768]{1,0:T(8,128)S(1)} %get-tuple-element.22.plan_ref), custom_call_target="tpu_custom_call" | custom-call | tf_op jit(solution)/shard_map/pallas_call | solution.py:235
  79.0 11.1 %all_to_all.62.got_ref = f32[8,24,128]{2,1,0:T(8,128)S(1)} all-to-all(f32[8,24,128]{2,1,0:T(8,128)S(1)} %get-tuple-element.23), channel_id=1, replica_groups=mesh['filt'=2,'row'=4,'z'=8,'y'=4] {'z'}, dimensions={0} | all-to-all | bytes 196608 | tf_op jit(solution)/shard_map/all_to_all | solution.py:223
  90.1 1.7 shard_map.70
  91.8 11.4 %all_to_all.63.got_ref = f32[16,16,128]{2,1,0:T(8,128)S(1)} all-to-all(f32[16,16,128]{2,1,0:T(8,128)S(1)} %get-tuple-element.24), channel_id=1, replica_groups=mesh['filt'=2,'row'=4,'z'=8,'y'=4] {'row','y'}, dimensions={0} | all-to-all | bytes 262144 | tf_op jit(solution)/shard_map/all_to_all | solution.py:223
  103.2 2.2 %shard_map.71 = (f32[16,128]{1,0:T(8,128)}, f32[8,8,128]{2,1,0:T(8,128)S(1)}) custom-call(f32[16,16,128]{2,1,0:T(8,128)S(1)} %all_to_all.63.got_ref, f32[32,128]{1,0:T(8,128)S(1)} %get-tuple-element.25.mass_ref, f32[16,128]{1,0:T(8,128)S(1)} %get-tuple-element.26.w_ref, f32[1536,768]{1,0:T(8,128)S(1)} %get-tuple-element.22.plan_ref), custom_call_target="tpu_custom_call" | custom-call | tf_op jit(solution)/shard_map/pallas_call | solution.py:235
  105.4 10.4 %all_to_all.64.got_ref = f32[8,8,128]{2,1,0:T(8,128)S(1)} all-to-all(f32[8,8,128]{2,1,0:T(8,128)S(1)} %get-tuple-element.27), channel_id=1, replica_groups=mesh['filt'=2,'row'=4,'z'=8,'y'=4] {'z'}, dimensions={0} | all-to-all | bytes 65536 | tf_op jit(solution)/shard_map/all_to_all | solution.py:223
  115.8 1.7 shard_map.72
  117.5 11.2 %all_to_all.65.got_ref = f32[16,16,128]{2,1,0:T(8,128)S(1)} all-to-all(f32[16,16,128]{2,1,0:T(8,128)S(1)} %shard_map.72), channel_id=1, replica_groups=mesh['filt'=2,'row'=4,'z'=8,'y'=4] {'row','y'}, dimensions={0} | all-to-all | bytes 262144 | tf_op jit(solution)/shard_map/all_to_all | solution.py:223
  128.8 2.2 %shard_map.73 = (f32[16,128]{1,0:T(8,128)}, f32[8,8,128]{2,1,0:T(8,128)S(1)}) custom-call(f32[16,16,128]{2,1,0:T(8,128)S(1)} %all_to_all.65.got_ref, f32[32,128]{1,0:T(8,128)S(1)} %get-tuple-element.25.mass_ref, f32[16,128]{1,0:T(8,128)S(1)} %get-tuple-element.26.w_ref, f32[1536,768]{1,0:T(8,128)S(1)} %get-tuple-element.22.plan_ref), custom_call_target="tpu_custom_call" | custom-call | tf_op jit(solution)/shard_map/pallas_call | solution.py:235
  131.0 10.4 %all_to_all.66.got_ref = f32[8,8,128]{2,1,0:T(8,128)S(1)} all-to-all(f32[8,8,128]{2,1,0:T(8,128)S(1)} %get-tuple-element.29), channel_id=1, replica_groups=mesh['filt'=2,'row'=4,'z'=8,'y'=4] {'z'}, dimensions={0} | all-to-all | bytes 65536 | tf_op jit(solution)/shard_map/all_to_all | solution.py:223
  141.4 1.7 shard_map.74
  143.1 11.2 %all_to_all.67.got_ref = f32[16,16,128]{2,1,0:T(8,128)S(1)} all-to-all(f32[16,16,128]{2,1,0:T(8,128)S(1)} %shard_map.74), channel_id=1, replica_groups=mesh['filt'=2,'row'=4,'z'=8,'y'=4] {'row','y'}, dimensions={0} | all-to-all | bytes 262144 | tf_op jit(solution)/shard_map/all_to_all | solution.py:223
  154.3 1.6 shard_map.75
  156.0 10.4 %all_to_all.68.got_ref = f32[8,8,128]{2,1,0:T(8,128)S(1)} all-to-all(f32[8,8,128]{2,1,0:T(8,128)S(1)} %get-tuple-element.30), channel_id=1, replica_groups=mesh['filt'=2,'row'=4,'z'=8,'y'=4] {'z'}, dimensions={0} | all-to-all | bytes 65536 | tf_op jit(solution)/shard_map/all_to_all | solution.py:223
  166.4 11.9 %shard_map.76 = (bf16[16,96,256]{2,1,0:T(8,128)(2,1)}, bf16[8,96,256]{2,1,0:T(8,128)(2,1)S(1)}, f32[16,128]{1,0:T(8,128)S(1)}) custom-call(f32[8,8,128]{2,1,0:T(8,128)S(1)} %all_to_all.68.got_ref, f32[16,128]{1,0:T(8,128)S(1)} %get-tuple-element.28.col_ref, f32[16,128]{1,0:T(8,128)S(1)} %get-tuple-element.31.phi_ref, ...), custom_call_target="tpu_custom_call" | custom-call | tf_op jit(solution)/shard_map/pallas_call | solution.py:235
  178.3 14.3 %all_to_all.69 = bf16[8,96,256]{2,1,0:T(8,128)(2,1)S(1)} all-to-all(bf16[8,96,256]{2,1,0:T(8,128)(2,1)S(1)} %get-tuple-element.36), channel_id=1, replica_groups=mesh['filt'=2,'row'=4,'z'=8,'y'=4] {'z'}, dimensions={0} | all-to-all | bytes 786432 | tf_op jit(solution)/shard_map/all_to_all | solution.py:223
  192.5 5.1 %all-to-all-start.10 = ((bf16[16,96,256]{2,1,0:T(8,128)(2,1)}), bf16[16,96,256]{2,1,0:T(8,128)(2,1)S(1)}, u32[]{:S(2)}, u32[]{:S(2)}) async-start(bf16[16,96,256]{2,1,0:T(8,128)(2,1)} %get-tuple-element.35), calls=%async_computation.10 | async-start | bytes 1572864 | tf_op jit(solution)/shard_map/all_to_all | solution.py:223
  197.6 0.5 dynamic-slice_bitcast_fusion
  198.1 0.1 convert_reduce_fusion.1
  198.2 9.6 %all-to-all-done.10 = bf16[16,96,256]{2,1,0:T(8,128)(2,1)S(1)} async-done(((bf16[16,96,256]{2,1,0:T(8,128)(2,1)}), bf16[16,96,256]{2,1,0:T(8,128)(2,1)S(1)}, u32[]{:S(2)}, u32[]{:S(2)}) %all-to-all-start.10) | async-done | bytes 786464 | tf_op jit(solution)/shard_map/all_to_all | solution.py:223
  207.7 0.1 convert_reduce_fusion
  207.8 0.6 add_convert_fusion
  (4 shorter events, 0.0 us)
Async XLA Ops:
  3.8 22.1 %all-to-all-start = ((bf16[16,112,256]{2,1,0:T(8,128)(2,1)}), bf16[16,112,256]{2,1,0:T(8,128)(2,1)S(1)}, u32[]{:S(2)}, u32[]{:S(2)}) async-start(bf16[16,112,256]{2,1,0:T(8,128)(2,1)} %broadcast_in_dim.6), calls=%async_computation | async-start | bytes 1835008 | tf_op jit(solution)/shard_map/all_to_all | solution.py:223
  192.5 15.2 %all-to-all-start.10 = ((bf16[16,96,256]{2,1,0:T(8,128)(2,1)}), bf16[16,96,256]{2,1,0:T(8,128)(2,1)S(1)}, u32[]{:S(2)}, u32[]{:S(2)}) async-start(bf16[16,96,256]{2,1,0:T(8,128)(2,1)} %get-tuple-element.35), calls=%async_computation.10 | async-start | bytes 1572864 | tf_op jit(solution)/shard_map/all_to_all | solution.py:223

commit v2 on v1

v2 whole, which is shorter than its diff:
```python
import functools

import jax
import jax.numpy as jnp
from jax import lax
from jax.experimental import pallas as pl
from jax.experimental.pallas import tpu as pltpu
from jax.sharding import Mesh
from jax.sharding import PartitionSpec as P

ITERS = 4


EPS = 0.09

LANES = 128
AUX = 16
F32 = jnp.float32
BF16 = jnp.bfloat16


def params():
    return pltpu.CompilerParams(vmem_limit_bytes=4 << 20)


def whole(n):
    return [pl.BlockSpec(memory_space=pltpu.VMEM)] * n


def eye(own):
    rows = lax.broadcasted_iota(jnp.int32, (own, LANES), 0)
    lanes = lax.broadcasted_iota(jnp.int32, (own, LANES), 1)
    return rows == lanes


def to_row(col, own):
    return jnp.sum(jnp.where(eye(own), col, 0.0), axis=0, keepdims=True)


def to_col(row, own):
    return jnp.sum(jnp.where(eye(own), row, 0.0), axis=1, keepdims=True)


def lanes_of(col):
    out = []
    for k in range(col.shape[0] // LANES):
        out.append(to_row(col[k * LANES : (k + 1) * LANES], LANES))
    return jnp.concatenate(out, axis=1)


def slots_of(value, own, count):
    return jnp.concatenate([to_row(value[k * own : (k + 1) * own], own) for k in range(count)], axis=0)


def column_of(value, own, count):
    return jnp.concatenate([to_col(value[k : k + 1], own) for k in range(count)], axis=0)


def fold(block):
    return jnp.sum(block.reshape(block.shape[0] // 8, 8, block.shape[1]), axis=0)


def put_lanes(ref, slots, base, row):
    for k in range(row.shape[1] // LANES):
        piece = row[:, k * LANES : (k + 1) * LANES]
        for s in range(slots):
            ref[s, base + k : base + k + 1, :] = piece


def pack(own, width, isrc, x_ref, gy_ref, f_ref, g_ref, w_ref, ipack_ref, jpack_ref, line_ref):
    line_ref[...] = jnp.zeros_like(line_ref)
    line_ref[0:1, 0:own] = f_ref[...].astype(F32)
    line_ref[1:2, 0:own] = w_ref[...].astype(F32)
    x = x_ref[...]
    lines = line_ref[...].astype(BF16)
    for s in range(isrc):
        ipack_ref[s, 0:own, :] = x
        ipack_ref[s, own : own + AUX, :] = lines
    jpack_ref[0:own, :] = x
    jpack_ref[own : 2 * own, :] = gy_ref[...]
    line_ref[0:1, 0:own] = g_ref[...].astype(F32)
    jpack_ref[2 * own : 2 * own + AUX, :] = line_ref[...].astype(BF16)


GROUP = 4
NT = (((1,), (1,)), ((), ()))
TN = (((0,), (0,)), ((), ()))


def behind(k, count):
    me = lax.axis_index("z")
    return lax.rem(me + count - k, count)


def ahead(k, count):
    return lax.rem(lax.axis_index("z") + k, count)


def build(own, width, isrc, jsrc, *refs):
    pi_ref, pj_refs = refs[0], refs[1 : 1 + jsrc]
    plan_ref, xi_ref, xj_ref, gj_ref, w_ref, mass_ref, col_ref, bias_ref = refs[1 + jsrc :]
    cols = jsrc * own
    scale = 1.0 / (2.0 * width * EPS)
    for k in range(jsrc):
        src = pj_refs[k]
        place = pl.ds(pl.multiple_of(behind(k, jsrc) * own, own), own)
        part = src[0:own, :]
        xj_ref[place, :] = part
        gj_ref[place, :] = src[own : 2 * own, :]
        pf = part.astype(F32)
        sq = jnp.sum(pf * pf, axis=1, keepdims=True)
        pot = to_col(src[2 * own : 2 * own + AUX, :].astype(F32)[0:1, 0:LANES], own)
        bias_ref[place, :] = pot / EPS - sq * scale
    jbias = lanes_of(bias_ref[...])
    xj = xj_ref[...]
    gj = gj_ref[...]
    span = GROUP * own

    def step(t, acc):
        base = pl.multiple_of(t * span, span)
        ibias = []
        for k in range(GROUP):
            s = t * GROUP + k
            part = pi_ref[s, 0:own, :]
            xi_ref[pl.ds(pl.multiple_of(base + k * own, own), own), :] = part
            aux = pi_ref[s, own : own + AUX, :].astype(F32)
            w_ref[pl.ds(s, 1), :] = aux[1:2, 0:LANES]
            pf = part.astype(F32)
            sq = jnp.sum(pf * pf, axis=1, keepdims=True)
            ibias.append(to_col(aux[0:1, 0:LANES], own) / EPS - sq * scale)
        ibias = jnp.concatenate(ibias, axis=0)
        part = xi_ref[pl.ds(base, span), :]
        cross = lax.dot_general(part, xj, NT, preferred_element_type=F32)
        plan = jnp.exp(cross * (2.0 * scale) + jbias + ibias)
        plan_ref[pl.ds(base, span), :] = plan
        weighted = plan * lax.dot_general(part, gj, NT, preferred_element_type=F32)
        mass = slots_of(jnp.sum(plan, axis=1, keepdims=True), own, GROUP)
        ph = slots_of(jnp.sum(weighted, axis=1, keepdims=True), own, GROUP)
        for k in range(GROUP):
            mass_ref[0, pl.ds(t * GROUP + k, 1), :] = mass[k : k + 1]
            mass_ref[0, pl.ds(isrc + t * GROUP + k, 1), :] = ph[k : k + 1]
        return acc[0] + fold(plan), acc[1] + fold(weighted)

    zero = jnp.zeros((8, cols), F32)
    cmass, cph = lax.fori_loop(0, isrc // GROUP, step, (zero, zero))
    for s in range(1, isrc):
        mass_ref[s] = mass_ref[0]
    col_ref[...] = jnp.zeros_like(col_ref)
    cmass = jnp.sum(cmass, axis=0, keepdims=True)
    cph = jnp.sum(cph, axis=0, keepdims=True)
    for k in range(cols // LANES):
        col_ref[k : k + 1, :] = cmass[:, k * LANES : (k + 1) * LANES]
        col_ref[8 + k : 9 + k, :] = cph[:, k * LANES : (k + 1) * LANES]


def prepare(own, isrc, plan_ref, xi_ref, gj_ref, base_ref, inner_ref):
    gj = gj_ref[...]
    span = GROUP * own

    def step(t, carry):
        at = pl.ds(pl.multiple_of(t * span, span), span)
        inner_ref[at, :] = lax.dot_general(xi_ref[at, :], gj, NT, preferred_element_type=F32)
        base_ref[at, :] = jnp.dot(plan_ref[at, :].astype(BF16), gj, preferred_element_type=F32)
        return carry

    lax.fori_loop(0, isrc // GROUP, step, 0)


def apply_cols(own, isrc, phi, plan_ref):
    span = GROUP * own
    acc = None
    for t in range(isrc // GROUP):
        col = column_of(phi[t * GROUP : (t + 1) * GROUP], own, GROUP)
        part = fold(plan_ref[t * span : (t + 1) * span, :] * col)
        acc = part if acc is None else acc + part
    return jnp.sum(acc, axis=0, keepdims=True)


def valid(own, value):
    lanes = lax.broadcasted_iota(jnp.int32, value.shape, 1)
    return jnp.where(lanes < own, value, 0.0)


def phi_first(own, isrc, jsrc, got_ref, col_ref, plan_ref, mass_ref, send_ref):
    total = jnp.sum(got_ref[...], axis=0)
    mass_ref[...] = total
    phi = valid(own, -total[isrc:] / total[:isrc])
    applied = apply_cols(own, isrc, phi, plan_ref)
    for s in range(jsrc):
        send_ref[s, 0:16, :] = col_ref[...]
        send_ref[s, 16:24, :] = jnp.zeros((8, LANES), F32)
    put_lanes(send_ref, jsrc, 16, applied)


def phi_next(own, isrc, jsrc, got_ref, mass_ref, w_ref, plan_ref, phi_ref, send_ref):
    total = jnp.sum(got_ref[...], axis=0)
    mass = mass_ref[...]
    phi = valid(own, -(mass[isrc:] + total) / mass[:isrc])
    phi_ref[...] = phi
    applied = apply_cols(own, isrc, phi, plan_ref)
    wts = valid(own, w_ref[...])
    wsum = jnp.sum(wts, axis=0, keepdims=True)
    wphi = jnp.sum(wts * phi, axis=0, keepdims=True)
    for s in range(jsrc):
        send_ref[s, 6:7, :] = wsum
        send_ref[s, 7:8, :] = wphi
    put_lanes(send_ref, jsrc, 0, applied)


def row_of(value, count):
    return jnp.concatenate([value[k : k + 1, :] for k in range(count)], axis=1)


def apply_rows(own, isrc, psi, plan_ref, send_ref):
    span = GROUP * own
    for t in range(isrc // GROUP):
        col = jnp.sum(plan_ref[t * span : (t + 1) * span, :] * psi, axis=1, keepdims=True)
        part = slots_of(col, own, GROUP)
        for s in range(isrc):
            send_ref[s, t * GROUP : (t + 1) * GROUP, :] = part


def psi_first(own, isrc, got_ref, plan_ref, col_ref, send_ref):
    total = jnp.sum(got_ref[...], axis=0)
    col_ref[...] = total[:16]
    count = plan_ref.shape[1] // LANES
    psi = row_of(-(total[8:16] + total[16:24]) / total[0:8], count)
    apply_rows(own, isrc, psi, plan_ref, send_ref)


def psi_next(own, isrc, got_ref, col_ref, plan_ref, send_ref):
    total = jnp.sum(got_ref[...], axis=0)
    count = plan_ref.shape[1] // LANES
    psi = row_of(-(col_ref[8:16] + total) / col_ref[0:8], count)
    apply_rows(own, isrc, psi, plan_ref, send_ref)


def finish_cols(own, width, isrc, jsrc, every, *refs):
    got_ref, col_ref, phi_ref, plan_ref, inner_ref, xi_ref = refs[:6]
    mixed_ref, q_ref, gw_ref = refs[6:9]
    out_refs, acc_ref = refs[9 : 9 + jsrc], refs[9 + jsrc]
    total = jnp.sum(got_ref[...], axis=0)
    count = plan_ref.shape[1] // LANES
    psi = row_of(-(col_ref[8:16] + total) / col_ref[0:8], count)
    wsum = jnp.sum(total[6:7], axis=1, keepdims=True)
    wphi = jnp.sum(total[7:8], axis=1, keepdims=True)
    gw_ref[...] = -(every / wsum) * (phi_ref[...] - wphi / wsum)
    span = GROUP * own
    for t in range(isrc // GROUP):
        at = slice(t * span, (t + 1) * span)
        col = column_of(phi_ref[t * GROUP : (t + 1) * GROUP, :], own, GROUP)
        mixed = plan_ref[at, :] * (inner_ref[at, :] + (col + psi))
        q_ref[at, :] = jnp.sum(mixed, axis=1, keepdims=True)
        mixed = mixed.astype(BF16)
        mixed_ref[at, :] = mixed
        term = lax.dot_general(mixed, xi_ref[at, :], TN, preferred_element_type=F32)
        if t:
            term = acc_ref[...] + term
        acc_ref[...] = term
    scale = 1.0 / (width * EPS)
    for k in range(jsrc):
        place = pl.ds(pl.multiple_of(ahead(k, jsrc) * own, own), own)
        out_refs[k][...] = (acc_ref[place, :] * scale).astype(BF16)


def finish_rows(own, width, isrc, base_ref, mixed_ref, q_ref, xi_ref, xj_ref, row_ref):
    scale = 1.0 / (width * EPS)
    span = GROUP * own
    xj = xj_ref[...]
    for t in range(isrc // GROUP):
        at = slice(t * span, (t + 1) * span)
        term = jnp.dot(mixed_ref[at, :], xj, preferred_element_type=F32)
        term = base_ref[at, :] + (term - q_ref[at, :] * xi_ref[at, :].astype(F32)) * scale
        term = term.astype(BF16)
        for k in range(GROUP):
            row_ref[t * GROUP + k] = term[k * own : (k + 1) * own]


def total_up(jsrc, *refs):
    rows_ref, parts, out_ref = refs[0], refs[1 : 1 + jsrc], refs[1 + jsrc]
    acc = jnp.sum(rows_ref[...].astype(F32), axis=0)
    for part in parts:
        acc += part[...].astype(F32)
    out_ref[...] = acc.astype(BF16)


def local(particles, cotangent, row_potential, col_potential, weights):
    own, width = particles.shape
    iaxes, jaxes = ("row", "y"), ("z",)
    isrc = lax.axis_size("row") * lax.axis_size("y")
    jsrc = lax.axis_size("z")
    rows, cols = isrc * own, jsrc * own
    far = sorted(range(1, jsrc), key=lambda k: -min(k, jsrc - k))

    def swap(value, axes):
        return lax.all_to_all(value, axes, 0, 0, tiled=True)

    def shift(value, k):
        return lax.ppermute(value, "z", [(i, (i + k) % jsrc) for i in range(jsrc)])

    def call(body, micros, outs, *args, scratch=()):
        return pl.pallas_call(
            body,
            out_shape=[jax.ShapeDtypeStruct(s, d) for s, d in outs],
            in_specs=whole(len(args)),
            out_specs=whole(len(outs)),
            scratch_shapes=list(scratch),
            compiler_params=params(),
            cost_estimate=pl.CostEstimate(flops=int(micros * 1e9), bytes_accessed=1024, transcendentals=0),
        )(*args)

    ipack, jpack = call(
        functools.partial(pack, own, width, isrc),
        2,
        [((isrc, own + AUX, width), BF16), ((2 * own + AUX, width), BF16)],
        particles,
        cotangent,
        row_potential.reshape(1, own),
        col_potential.reshape(1, own),
        weights.reshape(1, own),
        scratch=[pltpu.VMEM((AUX, width), F32)],
    )
    jgot = {k: shift(jpack, k) for k in far}
    igot = swap(ipack, iaxes)
    plan, xi, xj, gj, wts, send, col_part = call(
        functools.partial(build, own, width, isrc, jsrc),
        8,
        [
            ((rows, cols), F32),
            ((rows, width), BF16),
            ((cols, width), BF16),
            ((cols, width), BF16),
            ((isrc, LANES), F32),
            ((isrc, 2 * isrc, LANES), F32),
            ((16, LANES), F32),
        ],
        igot,
        jpack,
        *[jgot[k] for k in range(1, jsrc)],
        scratch=[pltpu.VMEM((cols, 1), F32)],
    )
    got = swap(send, iaxes)
    base, inner = call(
        functools.partial(prepare, own, isrc),
        4,
        [((rows, width), F32), ((rows, cols), F32)],
        plan,
        xi,
        gj,
    )
    mass, send = call(
        functools.partial(phi_first, own, isrc, jsrc),
        2,
        [((2 * isrc, LANES), F32), ((jsrc, 24, LANES), F32)],
        got,
        col_part,
        plan,
    )
    got = swap(send, jaxes)
    col, send = call(
        functools.partial(psi_first, own, isrc),
        2,
        [((16, LANES), F32), ((isrc, isrc, LANES), F32)],
        got,
        plan,
    )
    for step in range(1, ITERS):
        got = swap(send, iaxes)
        phi, send = call(
            functools.partial(phi_next, own, isrc, jsrc),
            2,
            [((isrc, LANES), F32), ((jsrc, 8, LANES), F32)],
            got,
            mass,
            wts,
            plan,
        )
        got = swap(send, jaxes)
        if step < ITERS - 1:
            (send,) = call(
                functools.partial(psi_next, own, isrc),
                2,
                [((isrc, isrc, LANES), F32)],
                got,
                col,
                plan,
            )
    mixed, q, gw, *col_sends = call(
        functools.partial(finish_cols, own, width, isrc, jsrc, float(isrc * jsrc * own)),
        5,
        [((rows, cols), BF16), ((rows, 1), F32), ((isrc, LANES), F32)] + [((own, width), BF16)] * jsrc,
        got,
        col,
        phi,
        plan,
        inner,
        xi,
        scratch=[pltpu.VMEM((cols, width), F32)],
    )
    col_got = [col_sends[0]] + [shift(col_sends[k], k) for k in far]
    (row_send,) = call(
        functools.partial(finish_rows, own, width, isrc),
        3,
        [((isrc, own, width), BF16)],
        base,
        mixed,
        q,
        xi,
        xj,
    )
    row_got = swap(row_send, iaxes)
    (grad,) = call(functools.partial(total_up, jsrc), 1, [((own, width), BF16)], row_got, *col_got)
    mine = lax.axis_index("row") * lax.axis_size("y") + lax.axis_index("y")
    grad_weights = lax.dynamic_slice(gw, (mine, 0), (1, own)).reshape(own)
    return (grad, grad_weights)


def solution(mesh):
    filt, row, col = mesh.devices.shape
    split = Mesh(mesh.devices.reshape(filt, row, 8, col // 8), ("filt", "row", "z", "y"))
    spec = ("filt", "row", "z", "y")
    return jax.shard_map(
        local,
        mesh=split,
        in_specs=(P(spec, None), P(spec, None), P(spec), P(spec), P(spec)),
        out_specs=(P(spec, None), P(spec)),
        check_vma=False,
    )
```

time: 209 us -> 180 us (0.86)
  blocking collectives: 133 us -> 81.4 us
  starting transfers between devices: 12.4 us -> 52.2 us
  Pallas kernels: 33.3 us -> 16.1 us
  local copies, waits for them, and re-layouts: 3.57 us -> 14.4 us
  waiting for transfers between devices: 22.7 us -> 13.8 us
  other arithmetic: 2.44 us -> 0 us
    all_to_all x10 -> x7, blocking collectives: 133 us -> 81.4 us  [swap(): return lax.all_to_all(value, axes, 0, 0, tiled=True)]
    ppermute x0 -> x14, starting transfers between devices: none -> 36.2 us  [shift(): return lax.ppermute(value, 'z', [(i, (i + k) % jsrc) for i in range(jsrc)])]
    all_to_all x2 -> x3, waiting for transfers between devices: 22.7 us -> 1.21 us  [swap(): return lax.all_to_all(value, axes, 0, 0, tiled=True)]
    pallas_call x9 -> x13, Pallas kernels: 33.3 us -> 16.1 us  [call(): pl.pallas_call(body, out_shape=[jax.ShapeDtypeStruct(s, d) for s, d in ou...]
    unnamed x0 -> x32, local copies, waits for them, and re-layouts: none -> 13.9 us
    ppermute x0 -> x14, waiting for transfers between devices: none -> 12.5 us  [shift(): return lax.ppermute(value, 'z', [(i, (i + k) % jsrc) for i in range(jsrc)])]
    all_to_all x2 -> x3, starting transfers between devices: 12.4 us -> 16 us  [swap(): return lax.all_to_all(value, axes, 0, 0, tiled=True)]
  transfers between devices with their start and end apart: 2 -> 17, of which waited for: 2 -> 7; matrix products, arithmetic and copies ran while one was open for 1% -> 0% of each run, Pallas kernels for 0% -> 1%
where the time goes in v2:
time: 180 us; the launch traced here: 179 us
  blocking collectives  81.4 us (45%)
  starting transfers between devices  52.2 us (29%)
  Pallas kernels  16.1 us (9%)
  local copies, waits for them, and re-layouts  14.4 us (8%)
  waiting for transfers between devices  13.8 us (8%)
    all_to_all x7, blocking collectives, swap(): return lax.all_to_all(value, axes, 0, 0, tiled=True)  81.4 us
    ppermute x14, starting transfers between devices, shift(): return lax.ppermute(value, 'z', [(i, (i + k) % jsrc) for i in range(jsrc)])  36.2 us
    pallas_call x13, Pallas kernels, call(): pl.pallas_call(body, out_shape=[jax.ShapeDtypeStruct(s, d) for s, d in ou...  16.1 us
    all_to_all x3, starting transfers between devices, swap(): return lax.all_to_all(value, axes, 0, 0, tiled=True)  16 us
    unnamed x32, local copies, waits for them, and re-layouts  13.9 us
    ppermute x14, waiting for transfers between devices, shift(): return lax.ppermute(value, 'z', [(i, (i + k) % jsrc) for i in range(jsrc)])  12.5 us
  transfers between devices with their start and end apart: 17, of which 7 were waited for; matrix products, arithmetic and copies ran while one was open for 0% of the time, Pallas kernels for 1%

profile of v2, /device:TPU:8, one launch (start us, length us, event | category | flops | bytes accessed | tf_op | source)
XLA Modules:
  0.0 178.7 jit_solution(1580124771510059463)
XLA Ops:
  0.6 0.8 copy-done
  1.4 0.8 copy-done.1
  2.2 0.7 copy-done.2
  2.9 0.7 copy-done.3
  3.5 0.7 copy-done.4
  4.2 1.0 shard_map.68
  5.2 7.4 %all-to-all-start = ((bf16[16,112,256]{2,1,0:T(8,128)(2,1)}), bf16[16,112,256]{2,1,0:T(8,128)(2,1)S(1)}, u32[]{:S(2)}, u32[]{:S(2)}) async-start(bf16[16,112,256]{2,1,0:T(8,128)(2,1)} %get-tuple-element.32), calls=%async_computation | async-start | bytes 1835008 | tf_op jit(solution)/shard_map/all_to_all | solution.py:296
  12.6 1.9 %collective-permute-start = (bf16[208,256]{1,0:T(8,128)(2,1)S(1)}, bf16[208,256]{1,0:T(8,128)(2,1)S(1)}, u32[]{:S(2)}, u32[]{:S(2)}) collective-permute-start(bf16[208,256]{1,0:T(8,128)(2,1)S(1)} %get-tuple-element.33.refs_1_), channel_id=1, source_target_pairs={{0,4},{4,8},{8,12},{12,16},{16,20},{20,24},{24,28},{28,0},{1,5},{5... | collective-permute-start | bytes 319496 | tf_op jit(solution)/shard_map/ppermute | solution.py:299
  14.5 3.3 %collective-permute-start.1 = (bf16[208,256]{1,0:T(8,128)(2,1)S(1)}, bf16[208,256]{1,0:T(8,128)(2,1)S(1)}, u32[]{:S(2)}, u32[]{:S(2)}) collective-permute-start(bf16[208,256]{1,0:T(8,128)(2,1)S(1)} %get-tuple-element.33.refs_1_), channel_id=1, source_target_pairs={{0,8},{4,12},{8,16},{12,20},{16,24},{20,28},{24,0},{28,4},{1,9},{5... | collective-permute-start | bytes 319496 | tf_op jit(solution)/shard_map/ppermute | solution.py:299
  17.8 4.0 %collective-permute-start.2 = (bf16[208,256]{1,0:T(8,128)(2,1)S(1)}, bf16[208,256]{1,0:T(8,128)(2,1)S(1)}, u32[]{:S(2)}, u32[]{:S(2)}) collective-permute-start(bf16[208,256]{1,0:T(8,128)(2,1)S(1)} %get-tuple-element.33.refs_1_), channel_id=1, source_target_pairs={{0,12},{4,16},{8,20},{12,24},{16,28},{20,0},{24,4},{28,8},{1,13},{... | collective-permute-start | bytes 319496 | tf_op jit(solution)/shard_map/ppermute | solution.py:299
  22.4 4.9 %collective-permute-start.4 = (bf16[208,256]{1,0:T(8,128)(2,1)S(1)}, bf16[208,256]{1,0:T(8,128)(2,1)S(1)}, u32[]{:S(2)}, u32[]{:S(2)}) collective-permute-start(bf16[208,256]{1,0:T(8,128)(2,1)S(1)} %get-tuple-element.33.refs_1_), channel_id=1, source_target_pairs={{0,20},{4,24},{8,28},{12,0},{16,4},{20,8},{24,12},{28,16},{1,21},{... | collective-permute-start | bytes 319496 | tf_op jit(solution)/shard_map/ppermute | solution.py:299
  27.3 2.7 %collective-permute-start.5 = (bf16[208,256]{1,0:T(8,128)(2,1)S(1)}, bf16[208,256]{1,0:T(8,128)(2,1)S(1)}, u32[]{:S(2)}, u32[]{:S(2)}) collective-permute-start(bf16[208,256]{1,0:T(8,128)(2,1)S(1)} %get-tuple-element.33.refs_1_), channel_id=1, source_target_pairs={{0,24},{4,28},{8,0},{12,4},{16,8},{20,12},{24,16},{28,20},{1,25},{... | collective-permute-start | bytes 319496 | tf_op jit(solution)/shard_map/ppermute | solution.py:299
  30.0 1.0 collective-permute-done.1.refs_3_
  31.0 2.0 %collective-permute-start.6 = (bf16[208,256]{1,0:T(8,128)(2,1)S(1)}, bf16[208,256]{1,0:T(8,128)(2,1)S(1)}, u32[]{:S(2)}, u32[]{:S(2)}) collective-permute-start(bf16[208,256]{1,0:T(8,128)(2,1)S(1)} %get-tuple-element.33.refs_1_), channel_id=1, source_target_pairs={{0,28},{4,0},{8,4},{12,8},{16,12},{20,16},{24,20},{28,24},{1,29},{... | collective-permute-start | bytes 319496 | tf_op jit(solution)/shard_map/ppermute | solution.py:299
  33.0 2.8 %collective-permute-done.2.refs_4_ = bf16[208,256]{1,0:T(8,128)(2,1)S(1)} collective-permute-done((bf16[208,256]{1,0:T(8,128)(2,1)S(1)}, bf16[208,256]{1,0:T(8,128)(2,1)S(1)}, u32[]{:S(2)}, u32[]{:S(2)}) %collective-permute-start.2) | collective-permute-done | bytes 106528 | tf_op jit(solution)/shard_map/ppermute | solution.py:299
  35.7 5.1 %collective-permute-done.4.refs_6_ = bf16[208,256]{1,0:T(8,128)(2,1)S(1)} collective-permute-done((bf16[208,256]{1,0:T(8,128)(2,1)S(1)}, bf16[208,256]{1,0:T(8,128)(2,1)S(1)}, u32[]{:S(2)}, u32[]{:S(2)}) %collective-permute-start.4) | collective-permute-done | bytes 106528 | tf_op jit(solution)/shard_map/ppermute | solution.py:299
  41.4 1.6 collective-permute-done.6.refs_8_
  42.9 3.7 %shard_map.69 = (f32[1536,768]{1,0:T(8,128)S(1)}, bf16[1536,256]{1,0:T(8,128)(2,1)S(1)}, bf16[768,256]{1,0:T(8,128)(2,1)S(1)}, bf16[768,256]{1,0:T(8,128)(2,1)S(...) custom-call(bf16[16,112,256]{2,1,0:T(8,128)(2,1)S(1)} %all-to-all-done.refs_0_, ...), custom_call_target="tpu_custom_call" | custom-call | flops 8000000000 | bytes 1024 | tf_op jit(solution)/shard_map/pallas_call | solution.py:302
  46.7 14.0 %all_to_all.50.got_ref = f32[16,32,128]{2,1,0:T(8,128)S(1)} all-to-all(f32[16,32,128]{2,1,0:T(8,128)S(1)} %get-tuple-element.38), channel_id=1, replica_groups=mesh['filt'=2,'row'=4,'z'=8,'y'=4] {'row','y'}, dimensions={0} | all-to-all | bytes 524288 | tf_op jit(solution)/shard_map/all_to_all | solution.py:296
  60.7 0.7 shard_map.71
  61.3 12.7 %all_to_all.51.got_ref = f32[8,24,128]{2,1,0:T(8,128)S(1)} all-to-all(f32[8,24,128]{2,1,0:T(8,128)S(1)} %get-tuple-element.40), channel_id=1, replica_groups=mesh['filt'=2,'row'=4,'z'=8,'y'=4] {'z'}, dimensions={0} | all-to-all | bytes 196608 | tf_op jit(solution)/shard_map/all_to_all | solution.py:296
  74.5 11.3 %all_to_all.52.got_ref = f32[16,16,128]{2,1,0:T(8,128)S(1)} all-to-all(f32[16,16,128]{2,1,0:T(8,128)S(1)} %get-tuple-element.41), channel_id=1, replica_groups=mesh['filt'=2,'row'=4,'z'=8,'y'=4] {'row','y'}, dimensions={0} | all-to-all | bytes 262144 | tf_op jit(solution)/shard_map/all_to_all | solution.py:296
  85.8 0.7 shard_map.73
  86.5 10.4 %all_to_all.53.got_ref = f32[8,8,128]{2,1,0:T(8,128)S(1)} all-to-all(f32[8,8,128]{2,1,0:T(8,128)S(1)} %get-tuple-element.44), channel_id=1, replica_groups=mesh['filt'=2,'row'=4,'z'=8,'y'=4] {'z'}, dimensions={0} | all-to-all | bytes 65536 | tf_op jit(solution)/shard_map/all_to_all | solution.py:296
  97.3 11.2 %all_to_all.54.got_ref = f32[16,16,128]{2,1,0:T(8,128)S(1)} all-to-all(f32[16,16,128]{2,1,0:T(8,128)S(1)} %shard_map.74), channel_id=1, replica_groups=mesh['filt'=2,'row'=4,'z'=8,'y'=4] {'row','y'}, dimensions={0} | all-to-all | bytes 262144 | tf_op jit(solution)/shard_map/all_to_all | solution.py:296
  108.5 0.7 shard_map.75
  109.2 10.4 %all_to_all.55.got_ref = f32[8,8,128]{2,1,0:T(8,128)S(1)} all-to-all(f32[8,8,128]{2,1,0:T(8,128)S(1)} %get-tuple-element.46), channel_id=1, replica_groups=mesh['filt'=2,'row'=4,'z'=8,'y'=4] {'z'}, dimensions={0} | all-to-all | bytes 65536 | tf_op jit(solution)/shard_map/all_to_all | solution.py:296
  120.0 11.4 %all_to_all.56.got_ref = f32[16,16,128]{2,1,0:T(8,128)S(1)} all-to-all(f32[16,16,128]{2,1,0:T(8,128)S(1)} %shard_map.76), channel_id=1, replica_groups=mesh['filt'=2,'row'=4,'z'=8,'y'=4] {'row','y'}, dimensions={0} | all-to-all | bytes 262144 | tf_op jit(solution)/shard_map/all_to_all | solution.py:296
  131.4 1.3 shard_map.77
  132.7 3.5 %all-to-all-start.8 = ((f32[8,8,128]{2,1,0:T(8,128)}), f32[8,8,128]{2,1,0:T(8,128)S(1)}, u32[]{:S(2)}, u32[]{:S(2)}) async-start(f32[8,8,128]{2,1,0:T(8,128)} %get-tuple-element.47), calls=%async_computation.8 | async-start | bytes 65536 | tf_op jit(solution)/shard_map/all_to_all | solution.py:296
  136.2 2.3 %copy-done.6 = f32[1536,768]{1,0:T(8,128)S(1)} copy-done((f32[1536,768]{1,0:T(8,128)S(1)}, f32[1536,768]{1,0:T(8,128)}, u32[]{:S(2)}) %copy-start.6) | copy-done | bytes 4718616
  138.6 2.0 %shard_map.70 = (f32[1536,256]{1,0:T(8,128)S(1)}, f32[1536,768]{1,0:T(8,128)S(1)}) custom-call(f32[1536,768]{1,0:T(8,128)S(1)} %copy-done.6, bf16[1536,256]{1,0:T(8,128)(2,1)S(1)} %copy-done.11, bf16[768,256]{1,0:T(8,128)(2,1)S(1)} %copy-done.15), custom_call_target="tpu_custom_call" | custom-call | flops 4000000000 | bytes 1024 | tf_op jit(solution)/shard_map/pallas_call | solution.py:302
  140.6 2.1 %copy-done.8 = f32[1536,768]{1,0:T(8,128)} copy-done((f32[1536,768]{1,0:T(8,128)}, f32[1536,768]{1,0:T(8,128)S(1)}, u32[]{:S(2)}) %copy-start.8) | copy-done | bytes 4718616
  142.7 1.2 all-to-all-done.8.refs_0_
  144.0 2.3 %copy-done.7 = f32[1536,768]{1,0:T(8,128)S(1)} copy-done((f32[1536,768]{1,0:T(8,128)S(1)}, f32[1536,768]{1,0:T(8,128)}, u32[]{:S(2)}) %copy-start.7) | copy-done | bytes 4718616
  146.3 2.3 %copy-done.9 = f32[1536,768]{1,0:T(8,128)S(1)} copy-done((f32[1536,768]{1,0:T(8,128)S(1)}, f32[1536,768]{1,0:T(8,128)}, u32[]{:S(2)}) %copy-start.9) | copy-done | bytes 4718616
  148.6 1.1 copy-done.12
  149.8 2.3 %shard_map.78 = (bf16[1536,768]{1,0:T(8,128)(2,1)S(1)}, f32[1536,1]{1,0:T(8,128)S(1)}, f32[16,128]{1,0:T(8,128)S(1)}, bf16[96,256]{1,0:T(8,128)(2,1)S(1)}, bf16[...) custom-call(f32[8,8,128]{2,1,0:T(8,128)S(1)} %all-to-all-done.8.refs, ...), custom_call_target="tpu_custom_call" | custom-call | flops 5000000000 | bytes 1024 | tf_op jit(solution)/shard_map/pallas_call | solution.py:302
  152.1 1.8 shard_map.79
  153.9 5.0 %all-to-all-start.9 = ((bf16[16,96,256]{2,1,0:T(8,128)(2,1)}), bf16[16,96,256]{2,1,0:T(8,128)(2,1)S(1)}, u32[]{:S(2)}, u32[]{:S(2)}) async-start(bf16[16,96,256]{2,1,0:T(8,128)(2,1)} %shard_map.79), calls=%async_computation.9 | async-start | bytes 1572864 | tf_op jit(solution)/shard_map/all_to_all | solution.py:296
  158.9 4.4 %collective-permute-start.7 = (bf16[96,256]{1,0:T(8,128)(2,1)S(1)}, bf16[96,256]{1,0:T(8,128)(2,1)S(1)}, u32[]{:S(2)}, u32[]{:S(2)}) collective-permute-start(bf16[96,256]{1,0:T(8,128)(2,1)S(1)} %get-tuple-element.54), channel_id=1, source_target_pairs={{0,16},{4,20},{8,24},{12,28},{16,0},{20,4},{24,8},{28,12},{1,17},{... | collective-permute-start | bytes 147464 | tf_op jit(solution)/shard_map/ppermute | solution.py:299
  163.4 0.6 collective-permute-start.8
  164.0 4.4 %collective-permute-start.9 = (bf16[96,256]{1,0:T(8,128)(2,1)S(1)}, bf16[96,256]{1,0:T(8,128)(2,1)S(1)}, u32[]{:S(2)}, u32[]{:S(2)}) collective-permute-start(bf16[96,256]{1,0:T(8,128)(2,1)S(1)} %get-tuple-element.56), channel_id=1, source_target_pairs={{0,20},{4,24},{8,28},{12,0},{16,4},{20,8},{24,12},{28,16},{1,21},{... | collective-permute-start | bytes 147464 | tf_op jit(solution)/shard_map/ppermute | solution.py:299
  169.0 3.5 %collective-permute-start.11 = (bf16[96,256]{1,0:T(8,128)(2,1)S(1)}, bf16[96,256]{1,0:T(8,128)(2,1)S(1)}, u32[]{:S(2)}, u32[]{:S(2)}) collective-permute-start(bf16[96,256]{1,0:T(8,128)(2,1)S(1)} %get-tuple-element.58), channel_id=1, source_target_pairs={{0,24},{4,28},{8,0},{12,4},{16,8},{20,12},{24,16},{28,20},{1,25},{... | collective-permute-start | bytes 147464 | tf_op jit(solution)/shard_map/ppermute | solution.py:299
  172.6 0.6 collective-permute-start.12
  173.2 2.6 %collective-permute-start.13 = (bf16[96,256]{1,0:T(8,128)(2,1)S(1)}, bf16[96,256]{1,0:T(8,128)(2,1)S(1)}, u32[]{:S(2)}, u32[]{:S(2)}) collective-permute-start(bf16[96,256]{1,0:T(8,128)(2,1)S(1)} %get-tuple-element.60), channel_id=1, source_target_pairs={{0,28},{4,0},{8,4},{12,8},{16,12},{20,16},{24,20},{28,24},{1,29},{... | collective-permute-start | bytes 147464 | tf_op jit(solution)/shard_map/ppermute | solution.py:299
  176.3 1.5 collective-permute-done.12.refs_7_
  177.9 0.8 shard_map.80
  (39 shorter events, 3.5 us)
Async XLA Ops:
  0.6 0.8 copy-start
  1.4 0.8 copy-start.1
  2.2 0.7 copy-start.2
  2.9 0.7 copy-start.3
  3.5 0.7 copy-start.4
  5.2 37.7 %all-to-all-start = ((bf16[16,112,256]{2,1,0:T(8,128)(2,1)}), bf16[16,112,256]{2,1,0:T(8,128)(2,1)S(1)}, u32[]{:S(2)}, u32[]{:S(2)}) async-start(bf16[16,112,256]{2,1,0:T(8,128)(2,1)} %get-tuple-element.32), calls=%async_computation | async-start | bytes 1835008 | tf_op jit(solution)/shard_map/all_to_all | solution.py:296
  12.6 14.7 %collective-permute-start = (bf16[208,256]{1,0:T(8,128)(2,1)S(1)}, bf16[208,256]{1,0:T(8,128)(2,1)S(1)}, u32[]{:S(2)}, u32[]{:S(2)}) collective-permute-start(bf16[208,256]{1,0:T(8,128)(2,1)S(1)} %get-tuple-element.33.refs_1_), channel_id=1, source_target_pairs={{0,4},{4,8},{8,12},{12,16},{16,20},{20,24},{24,28},{28,0},{1,5},{5... | collective-permute-start | bytes 319496 | tf_op jit(solution)/shard_map/ppermute | solution.py:299
  14.5 16.5 %collective-permute-start.1 = (bf16[208,256]{1,0:T(8,128)(2,1)S(1)}, bf16[208,256]{1,0:T(8,128)(2,1)S(1)}, u32[]{:S(2)}, u32[]{:S(2)}) collective-permute-start(bf16[208,256]{1,0:T(8,128)(2,1)S(1)} %get-tuple-element.33.refs_1_), channel_id=1, source_target_pairs={{0,8},{4,12},{8,16},{12,20},{16,24},{20,28},{24,0},{28,4},{1,9},{5... | collective-permute-start | bytes 319496 | tf_op jit(solution)/shard_map/ppermute | solution.py:299
  17.8 18.0 %collective-permute-start.2 = (bf16[208,256]{1,0:T(8,128)(2,1)S(1)}, bf16[208,256]{1,0:T(8,128)(2,1)S(1)}, u32[]{:S(2)}, u32[]{:S(2)}) collective-permute-start(bf16[208,256]{1,0:T(8,128)(2,1)S(1)} %get-tuple-element.33.refs_1_), channel_id=1, source_target_pairs={{0,12},{4,16},{8,20},{12,24},{16,28},{20,0},{24,4},{28,8},{1,13},{... | collective-permute-start | bytes 319496 | tf_op jit(solution)/shard_map/ppermute | solution.py:299
  21.8 13.9 %collective-permute-start.3 = (bf16[208,256]{1,0:T(8,128)(2,1)S(1)}, bf16[208,256]{1,0:T(8,128)(2,1)S(1)}, u32[]{:S(2)}, u32[]{:S(2)}) collective-permute-start(bf16[208,256]{1,0:T(8,128)(2,1)S(1)} %get-tuple-element.33.refs_1_), channel_id=1, source_target_pairs={{0,16},{4,20},{8,24},{12,28},{16,0},{20,4},{24,8},{28,12},{1,17},{... | collective-permute-start | bytes 319496 | tf_op jit(solution)/shard_map/ppermute | solution.py:299
  22.4 18.5 %collective-permute-start.4 = (bf16[208,256]{1,0:T(8,128)(2,1)S(1)}, bf16[208,256]{1,0:T(8,128)(2,1)S(1)}, u32[]{:S(2)}, u32[]{:S(2)}) collective-permute-start(bf16[208,256]{1,0:T(8,128)(2,1)S(1)} %get-tuple-element.33.refs_1_), channel_id=1, source_target_pairs={{0,20},{4,24},{8,28},{12,0},{16,4},{20,8},{24,12},{28,16},{1,21},{... | collective-permute-start | bytes 319496 | tf_op jit(solution)/shard_map/ppermute | solution.py:299
  27.3 14.0 %collective-permute-start.5 = (bf16[208,256]{1,0:T(8,128)(2,1)S(1)}, bf16[208,256]{1,0:T(8,128)(2,1)S(1)}, u32[]{:S(2)}, u32[]{:S(2)}) collective-permute-start(bf16[208,256]{1,0:T(8,128)(2,1)S(1)} %get-tuple-element.33.refs_1_), channel_id=1, source_target_pairs={{0,24},{4,28},{8,0},{12,4},{16,8},{20,12},{24,16},{28,20},{1,25},{... | collective-permute-start | bytes 319496 | tf_op jit(solution)/shard_map/ppermute | solution.py:299
  31.0 11.9 %collective-permute-start.6 = (bf16[208,256]{1,0:T(8,128)(2,1)S(1)}, bf16[208,256]{1,0:T(8,128)(2,1)S(1)}, u32[]{:S(2)}, u32[]{:S(2)}) collective-permute-start(bf16[208,256]{1,0:T(8,128)(2,1)S(1)} %get-tuple-element.33.refs_1_), channel_id=1, source_target_pairs={{0,28},{4,0},{8,4},{12,8},{16,12},{20,16},{24,20},{28,24},{1,29},{... | collective-permute-start | bytes 319496 | tf_op jit(solution)/shard_map/ppermute | solution.py:299
  46.7 27.8 %copy-start.10 = (bf16[1536,256]{1,0:T(8,128)(2,1)}, bf16[1536,256]{1,0:T(8,128)(2,1)S(1)}, u32[]{:S(2)}) copy-start(bf16[1536,256]{1,0:T(8,128)(2,1)S(1)} %get-tuple-element.35.xi_ref.refs_5_) | copy-start | bytes 2359300
  46.7 27.8 %copy-start.14 = (bf16[768,256]{1,0:T(8,128)(2,1)}, bf16[768,256]{1,0:T(8,128)(2,1)S(1)}, u32[]{:S(2)}) copy-start(bf16[768,256]{1,0:T(8,128)(2,1)S(1)} %get-tuple-element.36.gj_ref) | copy-start | bytes 1179652
  46.7 84.7 %copy-start.5 = (f32[1536,768]{1,0:T(8,128)}, f32[1536,768]{1,0:T(8,128)S(1)}, u32[]{:S(2)}) copy-start(f32[1536,768]{1,0:T(8,128)S(1)} %get-tuple-element.34.plan_ref.refs_3_) | copy-start | bytes 14155780
  120.0 16.2 %copy-start.11 = (bf16[1536,256]{1,0:T(8,128)(2,1)S(1)}, bf16[1536,256]{1,0:T(8,128)(2,1)}, u32[]{:S(2)}) copy-start(bf16[1536,256]{1,0:T(8,128)(2,1)} %copy-done.10) | copy-start | bytes 2359300
  120.0 16.2 %copy-start.15 = (bf16[768,256]{1,0:T(8,128)(2,1)S(1)}, bf16[768,256]{1,0:T(8,128)(2,1)}, u32[]{:S(2)}) copy-start(bf16[768,256]{1,0:T(8,128)(2,1)} %copy-done.14) | copy-start | bytes 1179652
  132.7 11.3 %all-to-all-start.8 = ((f32[8,8,128]{2,1,0:T(8,128)}), f32[8,8,128]{2,1,0:T(8,128)S(1)}, u32[]{:S(2)}, u32[]{:S(2)}) async-start(f32[8,8,128]{2,1,0:T(8,128)} %get-tuple-element.47), calls=%async_computation.8 | async-start | bytes 65536 | tf_op jit(solution)/shard_map/all_to_all | solution.py:296
  136.2 2.3 %copy-start.6 = (f32[1536,768]{1,0:T(8,128)S(1)}, f32[1536,768]{1,0:T(8,128)}, u32[]{:S(2)}) copy-start(f32[1536,768]{1,0:T(8,128)} %copy-done.5) | copy-start | bytes 14155780
  140.6 2.2 %copy-start.8 = (f32[1536,768]{1,0:T(8,128)}, f32[1536,768]{1,0:T(8,128)S(1)}, u32[]{:S(2)}) copy-start(f32[1536,768]{1,0:T(8,128)S(1)} %get-tuple-element.49.refs_4_) | copy-start | bytes 14155780
  144.0 2.3 %copy-start.7 = (f32[1536,768]{1,0:T(8,128)S(1)}, f32[1536,768]{1,0:T(8,128)}, u32[]{:S(2)}) copy-start(f32[1536,768]{1,0:T(8,128)} %copy-done.5) | copy-start | bytes 14155780
  146.3 2.3 %copy-start.9 = (f32[1536,768]{1,0:T(8,128)S(1)}, f32[1536,768]{1,0:T(8,128)}, u32[]{:S(2)}) copy-start(f32[1536,768]{1,0:T(8,128)} %copy-done.8) | copy-start | bytes 14155780
  148.6 1.1 copy-start.12
  149.8 2.3 %copy-start.13 = (bf16[1536,256]{1,0:T(8,128)(2,1)S(1)}, bf16[1536,256]{1,0:T(8,128)(2,1)}, u32[]{:S(2)}) copy-start(bf16[1536,256]{1,0:T(8,128)(2,1)} %copy-done.10) | copy-start | bytes 2359300
  153.9 24.0 %all-to-all-start.9 = ((bf16[16,96,256]{2,1,0:T(8,128)(2,1)}), bf16[16,96,256]{2,1,0:T(8,128)(2,1)S(1)}, u32[]{:S(2)}, u32[]{:S(2)}) async-start(bf16[16,96,256]{2,1,0:T(8,128)(2,1)} %shard_map.79), calls=%async_computation.9 | async-start | bytes 1572864 | tf_op jit(solution)/shard_map/all_to_all | solution.py:296
  158.9 13.6 %collective-permute-start.7 = (bf16[96,256]{1,0:T(8,128)(2,1)S(1)}, bf16[96,256]{1,0:T(8,128)(2,1)S(1)}, u32[]{:S(2)}, u32[]{:S(2)}) collective-permute-start(bf16[96,256]{1,0:T(8,128)(2,1)S(1)} %get-tuple-element.54), channel_id=1, source_target_pairs={{0,16},{4,20},{8,24},{12,28},{16,0},{20,4},{24,8},{28,12},{1,17},{... | collective-permute-start | bytes 147464 | tf_op jit(solution)/shard_map/ppermute | solution.py:299
  163.4 9.8 %collective-permute-start.8 = (bf16[96,256]{1,0:T(8,128)(2,1)S(1)}, bf16[96,256]{1,0:T(8,128)(2,1)S(1)}, u32[]{:S(2)}, u32[]{:S(2)}) collective-permute-start(bf16[96,256]{1,0:T(8,128)(2,1)S(1)} %get-tuple-element.55), channel_id=1, source_target_pairs={{0,12},{4,16},{8,20},{12,24},{16,28},{20,0},{24,4},{28,8},{1,13},{... | collective-permute-start | bytes 147464 | tf_op jit(solution)/shard_map/ppermute | solution.py:299
  164.0 12.3 %collective-permute-start.9 = (bf16[96,256]{1,0:T(8,128)(2,1)S(1)}, bf16[96,256]{1,0:T(8,128)(2,1)S(1)}, u32[]{:S(2)}, u32[]{:S(2)}) collective-permute-start(bf16[96,256]{1,0:T(8,128)(2,1)S(1)} %get-tuple-element.56), channel_id=1, source_target_pairs={{0,20},{4,24},{8,28},{12,0},{16,4},{20,8},{24,12},{28,16},{1,21},{... | collective-permute-start | bytes 147464 | tf_op jit(solution)/shard_map/ppermute | solution.py:299
  168.4 7.9 %collective-permute-start.10 = (bf16[96,256]{1,0:T(8,128)(2,1)S(1)}, bf16[96,256]{1,0:T(8,128)(2,1)S(1)}, u32[]{:S(2)}, u32[]{:S(2)}) collective-permute-start(bf16[96,256]{1,0:T(8,128)(2,1)S(1)} %get-tuple-element.57), channel_id=1, source_target_pairs={{0,8},{4,12},{8,16},{12,20},{16,24},{20,28},{24,0},{28,4},{1,9},{5... | collective-permute-start | bytes 147464 | tf_op jit(solution)/shard_map/ppermute | solution.py:299
  169.0 7.3 %collective-permute-start.11 = (bf16[96,256]{1,0:T(8,128)(2,1)S(1)}, bf16[96,256]{1,0:T(8,128)(2,1)S(1)}, u32[]{:S(2)}, u32[]{:S(2)}) collective-permute-start(bf16[96,256]{1,0:T(8,128)(2,1)S(1)} %get-tuple-element.58), channel_id=1, source_target_pairs={{0,24},{4,28},{8,0},{12,4},{16,8},{20,12},{24,16},{28,20},{1,25},{... | collective-permute-start | bytes 147464 | tf_op jit(solution)/shard_map/ppermute | solution.py:299
  172.6 5.3 %collective-permute-start.12 = (bf16[96,256]{1,0:T(8,128)(2,1)S(1)}, bf16[96,256]{1,0:T(8,128)(2,1)S(1)}, u32[]{:S(2)}, u32[]{:S(2)}) collective-permute-start(bf16[96,256]{1,0:T(8,128)(2,1)S(1)} %get-tuple-element.59), channel_id=1, source_target_pairs={{0,4},{4,8},{8,12},{12,16},{16,20},{20,24},{24,28},{28,0},{1,5},{5... | collective-permute-start | bytes 147464 | tf_op jit(solution)/shard_map/ppermute | solution.py:299
  173.2 4.7 %collective-permute-start.13 = (bf16[96,256]{1,0:T(8,128)(2,1)S(1)}, bf16[96,256]{1,0:T(8,128)(2,1)S(1)}, u32[]{:S(2)}, u32[]{:S(2)}) collective-permute-start(bf16[96,256]{1,0:T(8,128)(2,1)S(1)} %get-tuple-element.60), channel_id=1, source_target_pairs={{0,28},{4,0},{8,4},{12,8},{16,12},{20,16},{24,20},{28,24},{1,29},{... | collective-permute-start | bytes 147464 | tf_op jit(solution)/shard_map/ppermute | solution.py:299

commit v3 on v2

v3 whole, which is shorter than its diff:
```python
import functools

import jax
import jax.numpy as jnp
from jax import lax
from jax.experimental import pallas as pl
from jax.experimental.pallas import tpu as pltpu
from jax.sharding import Mesh
from jax.sharding import PartitionSpec as P

ITERS = 4


EPS = 0.09

LANES = 128
AUX = 16
F32 = jnp.float32
BF16 = jnp.bfloat16


def params():
    return pltpu.CompilerParams(vmem_limit_bytes=12 << 20)


def whole(n):
    return [pl.BlockSpec(memory_space=pltpu.VMEM)] * n


def eye(own):
    rows = lax.broadcasted_iota(jnp.int32, (own, LANES), 0)
    lanes = lax.broadcasted_iota(jnp.int32, (own, LANES), 1)
    return rows == lanes


def to_row(col, own):
    return jnp.sum(jnp.where(eye(own), col, 0.0), axis=0, keepdims=True)


def to_col(row, own):
    return jnp.sum(jnp.where(eye(own), row, 0.0), axis=1, keepdims=True)


def lanes_of(col):
    out = []
    for k in range(col.shape[0] // LANES):
        out.append(to_row(col[k * LANES : (k + 1) * LANES], LANES))
    return jnp.concatenate(out, axis=1)


def slots_of(value, own, count):
    return jnp.concatenate([to_row(value[k * own : (k + 1) * own], own) for k in range(count)], axis=0)


def column_of(value, own, count):
    return jnp.concatenate([to_col(value[k : k + 1], own) for k in range(count)], axis=0)


def fold(block):
    return jnp.sum(block.reshape(block.shape[0] // 8, 8, block.shape[1]), axis=0)


def put_lanes(ref, slots, base, row):
    for k in range(row.shape[1] // LANES):
        piece = row[:, k * LANES : (k + 1) * LANES]
        for s in range(slots):
            ref[s, base + k : base + k + 1, :] = piece


def pack(own, width, jsrc, x_ref, gy_ref, f_ref, g_ref, w_ref, ipack_ref, jpack_ref, block_ref, line_ref, vec_ref, in_sem, out_sem):
    copies = [
        pltpu.make_async_copy(f_ref, vec_ref.at[0], in_sem.at[2]),
        pltpu.make_async_copy(w_ref, vec_ref.at[1], in_sem.at[3]),
        pltpu.make_async_copy(g_ref, vec_ref.at[2], in_sem.at[4]),
        pltpu.make_async_copy(x_ref, block_ref.at[pl.ds(0, own)], in_sem.at[0]),
        pltpu.make_async_copy(gy_ref, block_ref.at[pl.ds(own, own)], in_sem.at[1]),
    ]
    for copy in copies:
        copy.start()
    line_ref[...] = jnp.zeros_like(line_ref)
    for copy in copies:
        copy.wait()
    line_ref[0, 0:1, 0:own] = vec_ref[0].astype(F32)
    line_ref[0, 1:2, 0:own] = vec_ref[1].astype(F32)
    line_ref[1, 0:1, 0:own] = vec_ref[2].astype(F32)
    block_ref[2 * own : 2 * own + AUX, :] = line_ref[1].astype(BF16)
    outs = [pltpu.make_async_copy(block_ref, jpack_ref.at[s], out_sem.at[s]) for s in range(jsrc)]
    for copy in outs:
        copy.start()
    ipack_ref[0:own, :] = block_ref[0:own, :]
    ipack_ref[own : own + AUX, :] = line_ref[0].astype(BF16)
    for copy in outs:
        copy.wait()


def stack(own, count, *refs):
    out_ref = refs[count]
    size = own + AUX
    for k in range(count):
        place = behind("row", k, count)
        out_ref[pl.ds(pl.multiple_of(place * size, size), size), :] = refs[k][...]


GROUP = 4
NT = (((1,), (1,)), ((), ()))
TN = (((0,), (0,)), ((), ()))


def behind(axis, k, count):
    return lax.rem(lax.axis_index(axis) + (count - k), count)


def build(own, width, isrc, jsrc, *refs):
    steps = isrc // GROUP
    pi_refs, pj_ref = refs[:steps], refs[steps]
    plan_ref, inner_ref, xi_ref, xj_ref, gj_ref, w_ref, mass_ref, col_ref = refs[steps + 1 :]
    cols = jsrc * own
    size = own + AUX
    scale = 1.0 / (2.0 * width * EPS)
    bias = []
    for k in range(jsrc):
        part = pj_ref[k, 0:own, :]
        xj_ref[k * own : (k + 1) * own, :] = part
        gj_ref[k * own : (k + 1) * own, :] = pj_ref[k, own : 2 * own, :]
        pf = part.astype(F32)
        sq = jnp.sum(pf * pf, axis=1, keepdims=True)
        pot = to_col(pj_ref[k, 2 * own : 2 * own + AUX, :].astype(F32)[0:1, 0:LANES], own)
        bias.append(pot / EPS - sq * scale)
    jbias = lanes_of(jnp.concatenate(bias, axis=0))
    xj = xj_ref[...]
    gj = gj_ref[...]
    span = GROUP * own
    cmass = cph = None
    for m in range(steps):
        src = pi_refs[m]
        t = behind("y", m, steps)
        base = pl.multiple_of(t * span, span)
        first = pl.multiple_of(t * GROUP, GROUP)
        ibias = []
        for k in range(GROUP):
            part = src[k * size : k * size + own, :]
            xi_ref[pl.ds(pl.multiple_of(base + k * own, own), own), :] = part
            aux = src[k * size + own : (k + 1) * size, :].astype(F32)
            w_ref[pl.ds(first + k, 1), :] = aux[1:2, 0:LANES]
            pf = part.astype(F32)
            sq = jnp.sum(pf * pf, axis=1, keepdims=True)
            ibias.append(to_col(aux[0:1, 0:LANES], own) / EPS - sq * scale)
        ibias = jnp.concatenate(ibias, axis=0)
        part = xi_ref[pl.ds(base, span), :]
        cross = lax.dot_general(part, xj, NT, preferred_element_type=F32)
        plan = jnp.exp(cross * (2.0 * scale) + jbias + ibias)
        plan_ref[pl.ds(base, span), :] = plan
        inner = lax.dot_general(part, gj, NT, preferred_element_type=F32)
        inner_ref[pl.ds(base, span), :] = inner
        weighted = plan * inner
        mass = slots_of(jnp.sum(plan, axis=1, keepdims=True), own, GROUP)
        ph = slots_of(jnp.sum(weighted, axis=1, keepdims=True), own, GROUP)
        for k in range(GROUP):
            mass_ref[0, pl.ds(first + k, 1), :] = mass[k : k + 1]
            mass_ref[0, pl.ds(isrc + first + k, 1), :] = ph[k : k + 1]
        plan, weighted = fold(plan), fold(weighted)
        cmass = plan if cmass is None else cmass + plan
        cph = weighted if cph is None else cph + weighted
    for s in range(1, isrc):
        mass_ref[s] = mass_ref[0]
    col_ref[...] = jnp.zeros_like(col_ref)
    cmass = jnp.sum(cmass, axis=0, keepdims=True)
    cph = jnp.sum(cph, axis=0, keepdims=True)
    for k in range(cols // LANES):
        col_ref[k : k + 1, :] = cmass[:, k * LANES : (k + 1) * LANES]
        col_ref[8 + k : 9 + k, :] = cph[:, k * LANES : (k + 1) * LANES]


def apply_cols(own, isrc, phi, plan_ref):
    span = GROUP * own
    acc = None
    for t in range(isrc // GROUP):
        col = column_of(phi[t * GROUP : (t + 1) * GROUP], own, GROUP)
        part = fold(plan_ref[t * span : (t + 1) * span, :] * col)
        acc = part if acc is None else acc + part
    return jnp.sum(acc, axis=0, keepdims=True)


def valid(own, value):
    lanes = lax.broadcasted_iota(jnp.int32, value.shape, 1)
    return jnp.where(lanes < own, value, 0.0)


def phi_first(own, isrc, jsrc, got_ref, col_ref, plan_ref, mass_ref, send_ref):
    total = jnp.sum(got_ref[...], axis=0)
    mass_ref[...] = total
    phi = valid(own, -total[isrc:] / total[:isrc])
    applied = apply_cols(own, isrc, phi, plan_ref)
    for s in range(jsrc):
        send_ref[s, 0:16, :] = col_ref[...]
        send_ref[s, 16:24, :] = jnp.zeros((8, LANES), F32)
    put_lanes(send_ref, jsrc, 16, applied)


def phi_next(own, isrc, jsrc, got_ref, mass_ref, w_ref, plan_ref, phi_ref, send_ref):
    total = jnp.sum(got_ref[...], axis=0)
    mass = mass_ref[...]
    phi = valid(own, -(mass[isrc:] + total) / mass[:isrc])
    phi_ref[...] = phi
    applied = apply_cols(own, isrc, phi, plan_ref)
    wts = valid(own, w_ref[...])
    wsum = jnp.sum(wts, axis=0, keepdims=True)
    wphi = jnp.sum(wts * phi, axis=0, keepdims=True)
    for s in range(jsrc):
        send_ref[s, 6:7, :] = wsum
        send_ref[s, 7:8, :] = wphi
    put_lanes(send_ref, jsrc, 0, applied)


def row_of(value, count):
    return jnp.concatenate([value[k : k + 1, :] for k in range(count)], axis=1)


def apply_rows(own, isrc, psi, plan_ref, send_ref):
    span = GROUP * own
    for t in range(isrc // GROUP):
        col = jnp.sum(plan_ref[t * span : (t + 1) * span, :] * psi, axis=1, keepdims=True)
        part = slots_of(col, own, GROUP)
        for s in range(isrc):
            send_ref[s, t * GROUP : (t + 1) * GROUP, :] = part


def psi_first(own, isrc, got_ref, plan_ref, col_ref, send_ref):
    total = jnp.sum(got_ref[...], axis=0)
    col_ref[...] = total[:16]
    count = plan_ref.shape[1] // LANES
    psi = row_of(-(total[8:16] + total[16:24]) / total[0:8], count)
    apply_rows(own, isrc, psi, plan_ref, send_ref)


def psi_next(own, isrc, got_ref, col_ref, plan_ref, send_ref):
    total = jnp.sum(got_ref[...], axis=0)
    count = plan_ref.shape[1] // LANES
    psi = row_of(-(col_ref[8:16] + total) / col_ref[0:8], count)
    apply_rows(own, isrc, psi, plan_ref, send_ref)


def bit_of(axis, bit):
    return lax.rem(lax.shift_right_logical(lax.axis_index(axis), bit), 2)


def finish_cols(own, width, isrc, jsrc, every, got_ref, col_ref, phi_ref, plan_ref, inner_ref, xi_ref, mixed_ref, q_ref, gw_ref, send_ref, keep_ref, acc_ref):
    total = jnp.sum(got_ref[...], axis=0)
    count = plan_ref.shape[1] // LANES
    psi = row_of(-(col_ref[8:16] + total) / col_ref[0:8], count)
    wsum = jnp.sum(total[6:7], axis=1, keepdims=True)
    wphi = jnp.sum(total[7:8], axis=1, keepdims=True)
    gw_ref[...] = -(every / wsum) * (phi_ref[...] - wphi / wsum)
    span = GROUP * own
    for t in range(isrc // GROUP):
        at = slice(t * span, (t + 1) * span)
        col = column_of(phi_ref[t * GROUP : (t + 1) * GROUP, :], own, GROUP)
        mixed = plan_ref[at, :] * (inner_ref[at, :] + (col + psi))
        q_ref[at, :] = jnp.sum(mixed, axis=1, keepdims=True)
        mixed = mixed.astype(BF16)
        mixed_ref[at, :] = mixed
        term = lax.dot_general(mixed, xi_ref[at, :], TN, preferred_element_type=F32)
        if t:
            term = acc_ref[...] + term
        acc_ref[...] = term
    scale = 1.0 / (width * EPS)
    mine = bit_of("z", 0)
    for m in range(jsrc // 2):
        keep = pl.ds(pl.multiple_of((2 * m + mine) * own, own), own)
        give = pl.ds(pl.multiple_of((2 * m + 1 - mine) * own, own), own)
        at = slice(m * own, (m + 1) * own)
        keep_ref[at, :] = acc_ref[keep, :] * scale
        send_ref[at, :] = (acc_ref[give, :] * scale).astype(BF16)


def halve(own, bit, keep_ref, got_ref, next_ref, send_ref):
    mine = bit_of("z", bit)
    for m in range(next_ref.shape[0] // own):
        keep = pl.ds(pl.multiple_of((2 * m + mine) * own, own), own)
        give = pl.ds(pl.multiple_of((2 * m + 1 - mine) * own, own), own)
        at = slice(m * own, (m + 1) * own)
        next_ref[at, :] = keep_ref[keep, :] + got_ref[keep, :].astype(F32)
        send_ref[at, :] = (keep_ref[give, :] + got_ref[give, :].astype(F32)).astype(BF16)


def finish_rows(own, width, isrc, plan_ref, mixed_ref, q_ref, xi_ref, xj_ref, gj_ref, row_ref):
    scale = 1.0 / (width * EPS)
    span = GROUP * own
    xj = xj_ref[...]
    gj = gj_ref[...]
    for t in range(isrc // GROUP):
        at = slice(t * span, (t + 1) * span)
        base = jnp.dot(plan_ref[at, :].astype(BF16), gj, preferred_element_type=F32)
        term = jnp.dot(mixed_ref[at, :], xj, preferred_element_type=F32)
        term = base + (term - q_ref[at, :] * xi_ref[at, :].astype(F32)) * scale
        term = term.astype(BF16)
        for k in range(GROUP):
            row_ref[t * GROUP + k] = term[k * own : (k + 1) * own]


def total_up(rows_ref, keep_ref, got_ref, out_ref):
    acc = jnp.sum(rows_ref[...].astype(F32), axis=0)
    out_ref[...] = (acc + (keep_ref[...] + got_ref[...].astype(F32))).astype(BF16)


def local(particles, cotangent, row_potential, col_potential, weights):
    own, width = particles.shape
    iaxes, jaxes = ("y", "row"), ("z",)
    ysrc, xsrc = lax.axis_size("y"), lax.axis_size("row")
    isrc, jsrc = ysrc * xsrc, lax.axis_size("z")
    rows, cols = isrc * own, jsrc * own

    def swap(value, axes):
        return lax.all_to_all(value, axes, 0, 0, tiled=True)

    def shift(value, axis, k):
        n = lax.axis_size(axis)
        return lax.ppermute(value, axis, [(i, (i + k) % n) for i in range(n)])

    def flip(value, bit):
        return lax.ppermute(value, "z", [(i, i ^ bit) for i in range(jsrc)])

    def call(body, micros, outs, *args, scratch=(), in_specs=None, out_specs=None):
        return pl.pallas_call(
            body,
            out_shape=[jax.ShapeDtypeStruct(s, d) for s, d in outs],
            in_specs=in_specs or whole(len(args)),
            out_specs=out_specs or whole(len(outs)),
            scratch_shapes=list(scratch),
            compiler_params=params(),
            cost_estimate=pl.CostEstimate(flops=int(micros * 1e9), bytes_accessed=1024, transcendentals=0),
        )(*args)

    anywhere = pl.BlockSpec(memory_space=pltpu.HBM)
    ipack, jpack = call(
        functools.partial(pack, own, width, jsrc),
        2,
        [((own + AUX, width), BF16), ((jsrc, 2 * own + AUX, width), BF16)],
        particles,
        cotangent,
        row_potential.reshape(1, own),
        col_potential.reshape(1, own),
        weights.reshape(1, own),
        scratch=[
            pltpu.VMEM((2 * own + AUX, width), BF16),
            pltpu.VMEM((2, AUX, width), F32),
            pltpu.VMEM((3, 1, own), BF16),
            pltpu.SemaphoreType.DMA((5,)),
            pltpu.SemaphoreType.DMA((jsrc,)),
        ],
        in_specs=[anywhere] * 5,
        out_specs=whole(1) + [anywhere],
    )
    jgot = swap(jpack, jaxes)
    near = [shift(ipack, "row", k) for k in range(1, xsrc)]
    (line,) = call(
        functools.partial(stack, own, xsrc), 1, [((xsrc * (own + AUX), width), BF16)], ipack, *near
    )
    igot = [line] + [shift(line, "y", k) for k in range(1, ysrc)]
    plan, inner, xi, xj, gj, wts, send, col_part = call(
        functools.partial(build, own, width, isrc, jsrc),
        5,
        [
            ((rows, cols), F32),
            ((rows, cols), F32),
            ((rows, width), BF16),
            ((cols, width), BF16),
            ((cols, width), BF16),
            ((isrc, LANES), F32),
            ((isrc, 2 * isrc, LANES), F32),
            ((16, LANES), F32),
        ],
        *igot,
        jgot,
    )
    got = swap(send, iaxes)
    mass, send = call(
        functools.partial(phi_first, own, isrc, jsrc),
        1,
        [((2 * isrc, LANES), F32), ((jsrc, 24, LANES), F32)],
        got,
        col_part,
        plan,
    )
    got = swap(send, jaxes)
    col, send = call(
        functools.partial(psi_first, own, isrc),
        1,
        [((16, LANES), F32), ((isrc, isrc, LANES), F32)],
        got,
        plan,
    )
    for step in range(1, ITERS):
        got = swap(send, iaxes)
        phi, send = call(
            functools.partial(phi_next, own, isrc, jsrc),
            1,
            [((isrc, LANES), F32), ((jsrc, 8, LANES), F32)],
            got,
            mass,
            wts,
            plan,
        )
        got = swap(send, jaxes)
        if step < ITERS - 1:
            (send,) = call(
                functools.partial(psi_next, own, isrc),
                1,
                [((isrc, isrc, LANES), F32)],
                got,
                col,
                plan,
            )
    half = cols // 2
    mixed, q, gw, give, keep = call(
        functools.partial(finish_cols, own, width, isrc, jsrc, float(isrc * jsrc * own)),
        3,
        [((rows, cols), BF16), ((rows, 1), F32), ((isrc, LANES), F32), ((half, width), BF16), ((half, width), F32)],
        got,
        col,
        phi,
        plan,
        inner,
        xi,
        scratch=[pltpu.VMEM((cols, width), F32)],
    )
    taken = flip(give, 1)
    (row_send,) = call(
        functools.partial(finish_rows, own, width, isrc),
        3,
        [((isrc, own, width), BF16)],
        plan,
        mixed,
        q,
        xi,
        xj,
        gj,
    )
    row_send, taken = lax.optimization_barrier((row_send, taken))
    row_got = swap(row_send, iaxes)
    for bit in (1, 2):
        half //= 2
        keep, give = call(
            functools.partial(halve, own, bit), 1, [((half, width), F32), ((half, width), BF16)], keep, taken
        )
        taken = flip(give, 1 << bit)
    (grad,) = call(total_up, 1, [((own, width), BF16)], row_got, keep, taken)
    mine = lax.axis_index("y") * xsrc + lax.axis_index("row")
    grad_weights = lax.dynamic_slice(gw, (mine, 0), (1, own)).reshape(own)
    return (grad, grad_weights)


def solution(mesh):
    filt, row, col = mesh.devices.shape
    split = Mesh(mesh.devices.reshape(filt, row, 8, col // 8), ("filt", "row", "z", "y"))
    spec = ("filt", "row", "z", "y")
    return jax.shard_map(
        local,
        mesh=split,
        in_specs=(P(spec, None), P(spec, None), P(spec), P(spec), P(spec)),
        out_specs=(P(spec, None), P(spec)),
        check_vma=False,
    )
```

time: 180 us -> 166 us (0.922)
  starting transfers between devices: 52.2 us -> 25.2 us
  waiting for transfers between devices: 13.8 us -> 31.1 us
  local copies, waits for them, and re-layouts: 14.4 us -> 4.07 us
  blocking collectives: 81.4 us -> 90.4 us
  Pallas kernels: 16.1 us -> 14.2 us
    ppermute x14 -> x9, starting transfers between devices: 36.2 us -> 12.3 us  [the longest x6 10.7 us: shift(): return lax.ppermute(value, axis, [(i, (i + k) % n) for i in range(n)])]
    ppermute x14 -> x9, waiting for transfers between devices: 12.5 us -> 28.2 us  [the longest x3 17.3 us: flip(): return lax.ppermute(value, 'z', [(i, i ^ bit) for i in range(jsrc)])]
    unnamed x32 -> x10, local copies, waits for them, and re-layouts: 13.9 us -> 3.55 us
    all_to_all x7 -> x8, blocking collectives: 81.4 us -> 90.4 us  [swap(): return lax.all_to_all(value, axes, 0, 0, tiled=True)]
    all_to_all x3 -> x2, starting transfers between devices: 16 us -> 12.9 us  [swap(): return lax.all_to_all(value, axes, 0, 0, tiled=True)]
    pallas_call x13 -> x15, Pallas kernels: 16.1 us -> 14.2 us  [call(): pl.pallas_call(body, out_shape=[jax.ShapeDtypeStruct(s, d) for s, d in ou...]
  transfers between devices with their start and end apart: 17 -> 11, of which waited for: 7 -> 10; matrix products, arithmetic and copies ran while one was open for 0% -> 0% of each run, Pallas kernels for 1% -> 1%
where the time goes in v3:
time: 166 us
  blocking collectives  90.4 us (54%)
  waiting for transfers between devices  31.1 us (19%)
  starting transfers between devices  25.2 us (15%)
  Pallas kernels  14.2 us (9%)
  local copies, waits for them, and re-layouts  4.07 us (2%)
    all_to_all x8, blocking collectives, swap(): return lax.all_to_all(value, axes, 0, 0, tiled=True)  90.4 us
    ppermute x3, waiting for transfers between devices, flip(): return lax.ppermute(value, 'z', [(i, i ^ bit) for i in range(jsrc)])  17.3 us
    pallas_call x15, Pallas kernels, call(): pl.pallas_call(body, out_shape=[jax.ShapeDtypeStruct(s, d) for s, d in ou...  14.2 us
    all_to_all x2, starting transfers between devices, swap(): return lax.all_to_all(value, axes, 0, 0, tiled=True)  12.9 us
    ppermute x6, waiting for transfers between devices, shift(): return lax.ppermute(value, axis, [(i, (i + k) % n) for i in range(n)])  10.9 us
    ppermute x6, starting transfers between devices, shift(): return lax.ppermute(value, axis, [(i, (i + k) % n) for i in range(n)])  10.7 us
    unnamed x10, local copies, waits for them, and re-layouts  3.55 us
  transfers between devices with their start and end apart: 11, of which 10 were waited for; matrix products, arithmetic and copies ran while one was open for 0% of the time, Pallas kernels for 1%

profile of v3, /device:TPU:8, one launch (start us, length us, event | category | flops | bytes accessed | tf_op | source)
XLA Modules:
  0.0 165.7 jit_solution(5043090886750233241)
XLA Ops:
  0.6 0.8 copy-done
  1.4 0.8 copy-done.1
  2.2 0.7 copy-done.2
  2.9 0.7 copy-done.3
  3.5 0.7 copy-done.4
  4.2 1.2 shard_map.68
  5.4 8.5 %all-to-all-start = ((bf16[8,208,256]{2,1,0:T(8,128)(2,1)}), bf16[8,208,256]{2,1,0:T(8,128)(2,1)S(1)}, u32[]{:S(2)}, u32[]{:S(2)}) async-start(bf16[8,208,256]{2,1,0:T(8,128)(2,1)} %get-tuple-element.32), calls=%async_computation | async-start | bytes 1703936 | tf_op jit(solution)/shard_map/all_to_all | solution.py:314
  13.9 1.5 collective-permute-start
  15.3 2.7 %collective-permute-start.1 = (bf16[112,256]{1,0:T(8,128)(2,1)S(1)}, bf16[112,256]{1,0:T(8,128)(2,1)S(1)}, u32[]{:S(2)}, u32[]{:S(2)}) collective-permute-start(bf16[112,256]{1,0:T(8,128)(2,1)S(1)} %get-tuple-element.31.refs_0_), channel_id=1, source_target_pairs={{0,64},{32,96},{64,0},{96,32},{1,65},{33,97},{65,1},{97,33},{2,66}... | collective-permute-start | bytes 172040 | tf_op jit(solution)/shard_map/ppermute | solution.py:318
  18.1 1.4 collective-permute-start.2
  19.5 0.3 collective-permute-done.refs_1_
  19.9 1.2 collective-permute-done.1.refs_2_
  21.0 1.2 collective-permute-done.2.refs_3_
  22.3 1.7 collective-permute-start.3
  23.9 0.9 collective-permute-start.4
  24.9 2.4 %collective-permute-start.5 = (bf16[448,256]{1,0:T(8,128)(2,1)S(1)}, bf16[448,256]{1,0:T(8,128)(2,1)S(1)}, u32[]{:S(2)}, u32[]{:S(2)}) collective-permute-start(bf16[448,256]{1,0:T(8,128)(2,1)S(1)} %shard_map.69.refs_0_), channel_id=1, source_target_pairs={{0,3},{1,0},{2,1},{3,2},{4,7},{5,4},{6,5},{7,6},{8,11},{9,8},{10,9... | collective-permute-start | bytes 688136 | tf_op jit(solution)/shard_map/ppermute | solution.py:318
  27.3 3.5 %collective-permute-done.3.refs_1_ = bf16[448,256]{1,0:T(8,128)(2,1)S(1)} collective-permute-done((bf16[448,256]{1,0:T(8,128)(2,1)S(1)}, bf16[448,256]{1,0:T(8,128)(2,1)S(1)}, u32[]{:S(2)}, u32[]{:S(2)}) %collective-permute-start.3) | collective-permute-done | bytes 229408 | tf_op jit(solution)/shard_map/ppermute | solution.py:318
  30.7 3.0 %collective-permute-done.4.refs_2_ = bf16[448,256]{1,0:T(8,128)(2,1)S(1)} collective-permute-done((bf16[448,256]{1,0:T(8,128)(2,1)S(1)}, bf16[448,256]{1,0:T(8,128)(2,1)S(1)}, u32[]{:S(2)}, u32[]{:S(2)}) %collective-permute-start.4) | collective-permute-done | bytes 229408 | tf_op jit(solution)/shard_map/ppermute | solution.py:318
  33.8 1.7 %collective-permute-done.5.refs_3_ = bf16[448,256]{1,0:T(8,128)(2,1)S(1)} collective-permute-done((bf16[448,256]{1,0:T(8,128)(2,1)S(1)}, bf16[448,256]{1,0:T(8,128)(2,1)S(1)}, u32[]{:S(2)}, u32[]{:S(2)}) %collective-permute-start.5) | collective-permute-done | bytes 229408 | tf_op jit(solution)/shard_map/ppermute | solution.py:318
  35.5 2.9 %all-to-all-done.refs_4_ = bf16[8,208,256]{2,1,0:T(8,128)(2,1)S(1)} async-done(((bf16[8,208,256]{2,1,0:T(8,128)(2,1)}), bf16[8,208,256]{2,1,0:T(8,128)(2,1)S(1)}, u32[]{:S(2)}, u32[]{:S(2)}) %all-to-all-start) | async-done | bytes 852000 | tf_op jit(solution)/shard_map/all_to_all | solution.py:314
  38.4 3.1 %shard_map.70 = (f32[1536,768]{1,0:T(8,128)S(1)}, f32[1536,768]{1,0:T(8,128)S(1)}, bf16[1536,256]{1,0:T(8,128)(2,1)S(1)}, bf16[768,256]{1,0:T(8,128)(2,1)S(1)}, ...) custom-call(bf16[448,256]{1,0:T(8,128)(2,1)S(1)} %shard_map.69.refs_0_, ...), custom_call_target="tpu_custom_call" | custom-call | flops 5000000000 | bytes 1024 | tf_op jit(solution)/shard_map/pallas_call | solution.py:324
  41.5 14.2 %all_to_all.50.got_ref = f32[16,32,128]{2,1,0:T(8,128)S(1)} all-to-all(f32[16,32,128]{2,1,0:T(8,128)S(1)} %get-tuple-element.34), channel_id=1, replica_groups=mesh['filt'=2,'row'=4,'z'=8,'y'=4] {'y','row'}, dimensions={0} | all-to-all | bytes 524288 | tf_op jit(solution)/shard_map/all_to_all | solution.py:314
  55.7 0.7 shard_map.71
  56.4 11.6 %all_to_all.51.got_ref = f32[8,24,128]{2,1,0:T(8,128)S(1)} all-to-all(f32[8,24,128]{2,1,0:T(8,128)S(1)} %get-tuple-element.36), channel_id=1, replica_groups=mesh['filt'=2,'row'=4,'z'=8,'y'=4] {'z'}, dimensions={0} | all-to-all | bytes 196608 | tf_op jit(solution)/shard_map/all_to_all | solution.py:314
  67.9 0.4 shard_map.72
  68.4 11.4 %all_to_all.52.got_ref = f32[16,16,128]{2,1,0:T(8,128)S(1)} all-to-all(f32[16,16,128]{2,1,0:T(8,128)S(1)} %get-tuple-element.37), channel_id=1, replica_groups=mesh['filt'=2,'row'=4,'z'=8,'y'=4] {'y','row'}, dimensions={0} | all-to-all | bytes 262144 | tf_op jit(solution)/shard_map/all_to_all | solution.py:314
  79.7 0.7 shard_map.73
  80.4 10.4 %all_to_all.53.got_ref = f32[8,8,128]{2,1,0:T(8,128)S(1)} all-to-all(f32[8,8,128]{2,1,0:T(8,128)S(1)} %get-tuple-element.40), channel_id=1, replica_groups=mesh['filt'=2,'row'=4,'z'=8,'y'=4] {'z'}, dimensions={0} | all-to-all | bytes 65536 | tf_op jit(solution)/shard_map/all_to_all | solution.py:314
  90.8 0.4 shard_map.74
  91.2 11.1 %all_to_all.54.got_ref = f32[16,16,128]{2,1,0:T(8,128)S(1)} all-to-all(f32[16,16,128]{2,1,0:T(8,128)S(1)} %shard_map.74), channel_id=1, replica_groups=mesh['filt'=2,'row'=4,'z'=8,'y'=4] {'y','row'}, dimensions={0} | all-to-all | bytes 262144 | tf_op jit(solution)/shard_map/all_to_all | solution.py:314
  102.3 0.7 shard_map.75
  103.0 10.4 %all_to_all.55.got_ref = f32[8,8,128]{2,1,0:T(8,128)S(1)} all-to-all(f32[8,8,128]{2,1,0:T(8,128)S(1)} %get-tuple-element.42), channel_id=1, replica_groups=mesh['filt'=2,'row'=4,'z'=8,'y'=4] {'z'}, dimensions={0} | all-to-all | bytes 65536 | tf_op jit(solution)/shard_map/all_to_all | solution.py:314
  113.4 0.4 shard_map.76
  113.8 11.1 %all_to_all.56.got_ref = f32[16,16,128]{2,1,0:T(8,128)S(1)} all-to-all(f32[16,16,128]{2,1,0:T(8,128)S(1)} %shard_map.76), channel_id=1, replica_groups=mesh['filt'=2,'row'=4,'z'=8,'y'=4] {'y','row'}, dimensions={0} | all-to-all | bytes 262144 | tf_op jit(solution)/shard_map/all_to_all | solution.py:314
  124.9 0.7 shard_map.77
  125.6 10.4 %all_to_all.57.got_ref = f32[8,8,128]{2,1,0:T(8,128)S(1)} all-to-all(f32[8,8,128]{2,1,0:T(8,128)S(1)} %get-tuple-element.43), channel_id=1, replica_groups=mesh['filt'=2,'row'=4,'z'=8,'y'=4] {'z'}, dimensions={0} | all-to-all | bytes 65536 | tf_op jit(solution)/shard_map/all_to_all | solution.py:314
  136.0 2.7 %shard_map.78 = (bf16[1536,768]{1,0:T(8,128)(2,1)S(1)}, f32[1536,1]{1,0:T(8,128)S(1)}, f32[16,128]{1,0:T(8,128)S(1)}, bf16[384,256]{1,0:T(8,128)(2,1)S(1)}, f32[384,256]{1,0:T(8,128)S(1)}) custom-call(f32[8,8,128]{2,1,0:T(8,128)S(1)} %all_to_all.57.got_ref, f32[16,128]{1,0:T(8,128)S(1)} %get-tuple-element.41.col_ref, ...), custom_call_target="tpu_custom_call" | custom-call | flops 3000000000 | bytes 1024 | tf_op jit(solution)/shard_map/pallas_call | solution.py:324
  138.6 0.7 collective-permute-start.6
  139.3 2.4 %shard_map.79 = bf16[16,96,256]{2,1,0:T(8,128)(2,1)} custom-call(f32[1536,768]{1,0:T(8,128)S(1)} %get-tuple-element.33.plan_ref, bf16[1536,768]{1,0:T(8,128)(2,1)S(1)} %get-tuple-element.47.mixed_ref, f32[1536,1]{1,0:T(8,128)S(1)} %get-tuple-element.48.q_ref, bf16[1536,256]{1,0:T(8,128)(2,1)S(1)} %get-tuple-element.46.xi_ref, ...), custom_call_target="tpu_custom_call" | custom-call | flops 3000000000 | bytes 1024 | tf_op jit(solution)/shard_map/pallas_call | solution.py:324
  141.7 4.0 %collective-permute-done.6.got_ref = bf16[384,256]{1,0:T(8,128)(2,1)S(1)} collective-permute-done((bf16[384,256]{1,0:T(8,128)(2,1)S(1)}, bf16[384,256]{1,0:T(8,128)(2,1)S(1)}, u32[]{:S(2)}, u32[]{:S(2)}) %collective-permute-start.6) | collective-permute-done | bytes 196640 | tf_op jit(solution)/shard_map/ppermute | solution.py:321
  145.7 4.4 %all-to-all-start.9 = ((bf16[16,96,256]{2,1,0:T(8,128)(2,1)}), bf16[16,96,256]{2,1,0:T(8,128)(2,1)S(1)}, u32[]{:S(2)}, u32[]{:S(2)}) async-start(bf16[16,96,256]{2,1,0:T(8,128)(2,1)} %shard_map.79), calls=%async_computation.9 | async-start | bytes 1572864 | tf_op jit(solution)/shard_map/all_to_all | solution.py:314
  150.2 0.1 collective-permute-start.7
  150.3 6.5 %collective-permute-done.7.got_ref = bf16[192,256]{1,0:T(8,128)(2,1)S(1)} collective-permute-done((bf16[192,256]{1,0:T(8,128)(2,1)S(1)}, bf16[192,256]{1,0:T(8,128)(2,1)S(1)}, u32[]{:S(2)}, u32[]{:S(2)}) %collective-permute-start.7) | collective-permute-done | bytes 98336 | tf_op jit(solution)/shard_map/ppermute | solution.py:321
  156.9 0.8 collective-permute-start.8
  157.7 0.5 dynamic-slice_bitcast_fusion
  158.2 6.7 %collective-permute-done.8.got_ref = bf16[96,256]{1,0:T(8,128)(2,1)S(1)} collective-permute-done((bf16[96,256]{1,0:T(8,128)(2,1)S(1)}, bf16[96,256]{1,0:T(8,128)(2,1)S(1)}, u32[]{:S(2)}, u32[]{:S(2)}) %collective-permute-start.8) | collective-permute-done | bytes 49184 | tf_op jit(solution)/shard_map/ppermute | solution.py:321
  165.0 0.0 all-to-all-done.9.rows_ref
  165.0 0.7 shard_map.82
  (8 shorter events, 0.1 us)
Async XLA Ops:
  0.6 0.8 copy-start
  1.4 0.8 copy-start.1
  2.2 0.7 copy-start.2
  2.9 0.7 copy-start.3
  3.5 0.7 copy-start.4
  5.4 33.0 %all-to-all-start = ((bf16[8,208,256]{2,1,0:T(8,128)(2,1)}), bf16[8,208,256]{2,1,0:T(8,128)(2,1)S(1)}, u32[]{:S(2)}, u32[]{:S(2)}) async-start(bf16[8,208,256]{2,1,0:T(8,128)(2,1)} %get-tuple-element.32), calls=%async_computation | async-start | bytes 1703936 | tf_op jit(solution)/shard_map/all_to_all | solution.py:314
  13.9 6.0 %collective-permute-start = (bf16[112,256]{1,0:T(8,128)(2,1)S(1)}, bf16[112,256]{1,0:T(8,128)(2,1)S(1)}, u32[]{:S(2)}, u32[]{:S(2)}) collective-permute-start(bf16[112,256]{1,0:T(8,128)(2,1)S(1)} %get-tuple-element.31.refs_0_), channel_id=1, source_target_pairs={{0,32},{32,64},{64,96},{96,0},{1,33},{33,65},{65,97},{97,1},{2,34}... | collective-permute-start | bytes 172040 | tf_op jit(solution)/shard_map/ppermute | solution.py:318
  15.3 5.7 %collective-permute-start.1 = (bf16[112,256]{1,0:T(8,128)(2,1)S(1)}, bf16[112,256]{1,0:T(8,128)(2,1)S(1)}, u32[]{:S(2)}, u32[]{:S(2)}) collective-permute-start(bf16[112,256]{1,0:T(8,128)(2,1)S(1)} %get-tuple-element.31.refs_0_), channel_id=1, source_target_pairs={{0,64},{32,96},{64,0},{96,32},{1,65},{33,97},{65,1},{97,33},{2,66}... | collective-permute-start | bytes 172040 | tf_op jit(solution)/shard_map/ppermute | solution.py:318
  18.1 4.2 %collective-permute-start.2 = (bf16[112,256]{1,0:T(8,128)(2,1)S(1)}, bf16[112,256]{1,0:T(8,128)(2,1)S(1)}, u32[]{:S(2)}, u32[]{:S(2)}) collective-permute-start(bf16[112,256]{1,0:T(8,128)(2,1)S(1)} %get-tuple-element.31.refs_0_), channel_id=1, source_target_pairs={{0,96},{32,0},{64,32},{96,64},{1,97},{33,1},{65,33},{97,65},{2,98}... | collective-permute-start | bytes 172040 | tf_op jit(solution)/shard_map/ppermute | solution.py:318
  22.3 8.5 %collective-permute-start.3 = (bf16[448,256]{1,0:T(8,128)(2,1)S(1)}, bf16[448,256]{1,0:T(8,128)(2,1)S(1)}, u32[]{:S(2)}, u32[]{:S(2)}) collective-permute-start(bf16[448,256]{1,0:T(8,128)(2,1)S(1)} %shard_map.69.refs_0_), channel_id=1, source_target_pairs={{0,1},{1,2},{2,3},{3,0},{4,5},{5,6},{6,7},{7,4},{8,9},{9,10},{10,1... | collective-permute-start | bytes 688136 | tf_op jit(solution)/shard_map/ppermute | solution.py:318
  23.9 9.8 %collective-permute-start.4 = (bf16[448,256]{1,0:T(8,128)(2,1)S(1)}, bf16[448,256]{1,0:T(8,128)(2,1)S(1)}, u32[]{:S(2)}, u32[]{:S(2)}) collective-permute-start(bf16[448,256]{1,0:T(8,128)(2,1)S(1)} %shard_map.69.refs_0_), channel_id=1, source_target_pairs={{0,2},{1,3},{2,0},{3,1},{4,6},{5,7},{6,4},{7,5},{8,10},{9,11},{10,... | collective-permute-start | bytes 688136 | tf_op jit(solution)/shard_map/ppermute | solution.py:318
  24.9 10.6 %collective-permute-start.5 = (bf16[448,256]{1,0:T(8,128)(2,1)S(1)}, bf16[448,256]{1,0:T(8,128)(2,1)S(1)}, u32[]{:S(2)}, u32[]{:S(2)}) collective-permute-start(bf16[448,256]{1,0:T(8,128)(2,1)S(1)} %shard_map.69.refs_0_), channel_id=1, source_target_pairs={{0,3},{1,0},{2,1},{3,2},{4,7},{5,4},{6,5},{7,6},{8,11},{9,8},{10,9... | collective-permute-start | bytes 688136 | tf_op jit(solution)/shard_map/ppermute | solution.py:318
  138.6 7.1 %collective-permute-start.6 = (bf16[384,256]{1,0:T(8,128)(2,1)S(1)}, bf16[384,256]{1,0:T(8,128)(2,1)S(1)}, u32[]{:S(2)}, u32[]{:S(2)}) collective-permute-start(bf16[384,256]{1,0:T(8,128)(2,1)S(1)} %get-tuple-element.51), channel_id=1, source_target_pairs={{0,4},{4,0},{8,12},{12,8},{16,20},{20,16},{24,28},{28,24},{1,5},{5... | collective-permute-start | bytes 589832 | tf_op jit(solution)/shard_map/ppermute | solution.py:321
  145.7 19.2 %all-to-all-start.9 = ((bf16[16,96,256]{2,1,0:T(8,128)(2,1)}), bf16[16,96,256]{2,1,0:T(8,128)(2,1)S(1)}, u32[]{:S(2)}, u32[]{:S(2)}) async-start(bf16[16,96,256]{2,1,0:T(8,128)(2,1)} %shard_map.79), calls=%async_computation.9 | async-start | bytes 1572864 | tf_op jit(solution)/shard_map/all_to_all | solution.py:314
  150.2 6.7 %collective-permute-start.7 = (bf16[192,256]{1,0:T(8,128)(2,1)S(1)}, bf16[192,256]{1,0:T(8,128)(2,1)S(1)}, u32[]{:S(2)}, u32[]{:S(2)}) collective-permute-start(bf16[192,256]{1,0:T(8,128)(2,1)S(1)} %get-tuple-element.56), channel_id=1, source_target_pairs={{0,8},{4,12},{8,0},{12,4},{16,24},{20,28},{24,16},{28,20},{1,9},{5... | collective-permute-start | bytes 294920 | tf_op jit(solution)/shard_map/ppermute | solution.py:321
  156.9 8.1 %collective-permute-start.8 = (bf16[96,256]{1,0:T(8,128)(2,1)S(1)}, bf16[96,256]{1,0:T(8,128)(2,1)S(1)}, u32[]{:S(2)}, u32[]{:S(2)}) collective-permute-start(bf16[96,256]{1,0:T(8,128)(2,1)S(1)} %get-tuple-element.58), channel_id=1, source_target_pairs={{0,16},{4,20},{8,24},{12,28},{16,0},{20,4},{24,8},{28,12},{1,17},{... | collective-permute-start | bytes 147464 | tf_op jit(solution)/shard_map/ppermute | solution.py:321

commit v4 on v3

--- a/solution.py
+++ b/solution.py
@@ -14,13 +14,13 @@
 EPS = 0.09
 
 LANES = 128
-AUX = 16
+AUX = 8
 F32 = jnp.float32
 BF16 = jnp.bfloat16
 
 
-def params():
-    return pltpu.CompilerParams(vmem_limit_bytes=12 << 20)
+def params(mib):
+    return pltpu.CompilerParams(vmem_limit_bytes=mib << 20)
 
 
 def whole(n):
@@ -283,16 +283,22 @@
         send_ref[at, :] = (keep_ref[give, :] + got_ref[give, :].astype(F32)).astype(BF16)
 
 
-def finish_rows(own, width, isrc, plan_ref, mixed_ref, q_ref, xi_ref, xj_ref, gj_ref, row_ref):
-    scale = 1.0 / (width * EPS)
-    span = GROUP * own
-    xj = xj_ref[...]
+def spread(own, isrc, plan_ref, gj_ref, after_ref, base_ref):
+    span = GROUP * own
     gj = gj_ref[...]
     for t in range(isrc // GROUP):
         at = slice(t * span, (t + 1) * span)
-        base = jnp.dot(plan_ref[at, :].astype(BF16), gj, preferred_element_type=F32)
+        base_ref[at, :] = jnp.dot(plan_ref[at, :].astype(BF16), gj, preferred_element_type=F32)
+
+
+def finish_rows(own, width, isrc, base_ref, mixed_ref, q_ref, xi_ref, xj_ref, after_ref, row_ref):
+    scale = 1.0 / (width * EPS)
+    span = GROUP * own
+    xj = xj_ref[...]
+    for t in range(isrc // GROUP):
+        at = slice(t * span, (t + 1) * span)
         term = jnp.dot(mixed_ref[at, :], xj, preferred_element_type=F32)
-        term = base + (term - q_ref[at, :] * xi_ref[at, :].astype(F32)) * scale
+        term = base_ref[at, :] + (term - q_ref[at, :] * xi_ref[at, :].astype(F32)) * scale
         term = term.astype(BF16)
         for k in range(GROUP):
             row_ref[t * GROUP + k] = term[k * own : (k + 1) * own]
@@ -320,14 +326,14 @@
     def flip(value, bit):
         return lax.ppermute(value, "z", [(i, i ^ bit) for i in range(jsrc)])
 
-    def call(body, micros, outs, *args, scratch=(), in_specs=None, out_specs=None):
+    def call(body, micros, outs, *args, scratch=(), in_specs=None, out_specs=None, mib=12):
         return pl.pallas_call(
             body,
             out_shape=[jax.ShapeDtypeStruct(s, d) for s, d in outs],
             in_specs=in_specs or whole(len(args)),
             out_specs=out_specs or whole(len(outs)),
             scratch_shapes=list(scratch),
-            compiler_params=params(),
+            compiler_params=params(mib),
             cost_estimate=pl.CostEstimate(flops=int(micros * 1e9), bytes_accessed=1024, transcendentals=0),
         )(*args)
 
@@ -350,6 +356,7 @@
         ],
         in_specs=[anywhere] * 5,
         out_specs=whole(1) + [anywhere],
+        mib=60,
     )
     jgot = swap(jpack, jaxes)
     near = [shift(ipack, "row", k) for k in range(1, xsrc)]
@@ -425,25 +432,31 @@
         scratch=[pltpu.VMEM((cols, width), F32)],
     )
     taken = flip(give, 1)
+    (base,) = call(functools.partial(spread, own, isrc), 1, [((rows, width), F32)], plan, gj, gw)
+    base, taken = lax.optimization_barrier((base, taken))
+    half //= 2
+    keep, give = call(
+        functools.partial(halve, own, 1), 1, [((half, width), F32), ((half, width), BF16)], keep, taken
+    )
+    taken = flip(give, 2)
     (row_send,) = call(
         functools.partial(finish_rows, own, width, isrc),
-        3,
+        2,
         [((isrc, own, width), BF16)],
-        plan,
+        base,
         mixed,
         q,
         xi,
         xj,
-        gj,
+        keep,
     )
     row_send, taken = lax.optimization_barrier((row_send, taken))
+    half //= 2
+    keep, give = call(
+        functools.partial(halve, own, 2), 1, [((half, width), F32), ((half, width), BF16)], keep, taken
+    )
+    taken = flip(give, 4)
     row_got = swap(row_send, iaxes)
-    for bit in (1, 2):
-        half //= 2
-        keep, give = call(
-            functools.partial(halve, own, bit), 1, [((half, width), F32), ((half, width), BF16)], keep, taken
-        )
-        taken = flip(give, 1 << bit)
     (grad,) = call(total_up, 1, [((own, width), BF16)], row_got, keep, taken)
     mine = lax.axis_index("y") * xsrc + lax.axis_index("row")
     grad_weights = lax.dynamic_slice(gw, (mine, 0), (1, own)).reshape(own)

time: 166 us -> 166 us (level)
  local copies, waits for them, and re-layouts: 4.07 us -> 1.33 us
    unnamed x10 -> x2, local copies, waits for them, and re-layouts: 3.55 us -> 0.81 us
    pallas_call x15 -> x16, Pallas kernels: 14.2 us -> 15.1 us  [call(): pl.pallas_call(body, out_shape=[jax.ShapeDtypeStruct(s, d) for s, d in ou...]
  transfers between devices with their start and end apart: 11 -> 11, of which waited for: 10 -> 11; matrix products, arithmetic and copies ran while one was open for 0% -> 0% of each run, Pallas kernels for 1% -> 2%
where the time goes in v4:
time: 166 us; the launch traced here: 165 us
  blocking collectives  91.4 us (55%)
  waiting for transfers between devices  30 us (18%)
  starting transfers between devices  26.1 us (16%)
  Pallas kernels  15.1 us (9%)
    all_to_all x8, blocking collectives, swap(): return lax.all_to_all(value, axes, 0, 0, tiled=True)  91.4 us
    ppermute x3, waiting for transfers between devices, flip(): return lax.ppermute(value, 'z', [(i, i ^ bit) for i in range(jsrc)])  16.4 us
    pallas_call x16, Pallas kernels, call(): pl.pallas_call(body, out_shape=[jax.ShapeDtypeStruct(s, d) for s, d in ou...  15.1 us
    all_to_all x2, starting transfers between devices, swap(): return lax.all_to_all(value, axes, 0, 0, tiled=True)  14.2 us
    ppermute x6, starting transfers between devices, shift(): return lax.ppermute(value, axis, [(i, (i + k) % n) for i in range(n)])  10.7 us
    ppermute x6, waiting for transfers between devices, shift(): return lax.ppermute(value, axis, [(i, (i + k) % n) for i in range(n)])  10.4 us
  transfers between devices with their start and end apart: 11, of which 11 were waited for; matrix products, arithmetic and copies ran while one was open for 0% of the time, Pallas kernels for 2%

profile of v4, /device:TPU:8, one launch (start us, length us, event | category | flops | bytes accessed | tf_op | source)
XLA Modules:
  0.0 164.7 jit_solution(8286997777886528048)
XLA Ops:
  0.6 2.5 %shard_map.68 = (bf16[104,256]{1,0:T(8,128)(2,1)}, bf16[8,200,256]{2,1,0:T(8,128)(2,1)}) custom-call(bf16[96,256]{1,0:T(8,128)(2,1)} %x_ref.1, bf16[96,256]{1,0:T(8,128)(2,1)} %gy_ref.1, bf16[1,96]{1,0:T(2,128)(2,1)} %bitcast.5, bf16[1,96]{1,0:T(2,128)(2,1)} %bitcast.6, bf16[1,96]{1,0:T(2,128)(2,1)} %bitcast.7), custom_call_target="tpu_custom_call" | custom-call | flops 2000000000 | bytes 1024 | tf_op jit(solution)/shard_map/pallas_call | solution.py:330
  3.1 8.5 %all-to-all-start = ((bf16[8,200,256]{2,1,0:T(8,128)(2,1)}), bf16[8,200,256]{2,1,0:T(8,128)(2,1)S(1)}, u32[]{:S(2)}, u32[]{:S(2)}) async-start(bf16[8,200,256]{2,1,0:T(8,128)(2,1)} %get-tuple-element.34), calls=%async_computation | async-start | bytes 1638400 | tf_op jit(solution)/shard_map/all_to_all | solution.py:320
  11.6 1.5 collective-permute-start
  13.1 2.7 %collective-permute-start.1 = (bf16[104,256]{1,0:T(8,128)(2,1)}, bf16[104,256]{1,0:T(8,128)(2,1)S(1)}, u32[]{:S(2)}, u32[]{:S(2)}) collective-permute-start(bf16[104,256]{1,0:T(8,128)(2,1)} %get-tuple-element.33.refs_0_), channel_id=1, source_target_pairs={{0,64},{32,96},{64,0},{96,32},{1,65},{33,97},{65,1},{97,33},{2,66}... | collective-permute-start | bytes 159752 | tf_op jit(solution)/shard_map/ppermute | solution.py:324
  15.8 1.4 collective-permute-start.2
  17.3 0.5 collective-permute-done.refs_1_
  17.7 1.2 collective-permute-done.1.refs_2_
  19.0 1.2 collective-permute-done.2.refs_3_
  20.2 0.0 copy-start
  20.2 0.8 copy-done
  21.0 1.7 %collective-permute-start.3 = (bf16[416,256]{1,0:T(8,128)(2,1)S(1)}, bf16[416,256]{1,0:T(8,128)(2,1)S(1)}, u32[]{:S(2)}, u32[]{:S(2)}) collective-permute-start(bf16[416,256]{1,0:T(8,128)(2,1)S(1)} %shard_map.69.refs_0_), channel_id=1, source_target_pairs={{0,1},{1,2},{2,3},{3,0},{4,5},{5,6},{6,7},{7,4},{8,9},{9,10},{10,1... | collective-permute-start | bytes 638984 | tf_op jit(solution)/shard_map/ppermute | solution.py:324
  22.7 0.9 collective-permute-start.4
  23.6 2.4 %collective-permute-start.5 = (bf16[416,256]{1,0:T(8,128)(2,1)S(1)}, bf16[416,256]{1,0:T(8,128)(2,1)S(1)}, u32[]{:S(2)}, u32[]{:S(2)}) collective-permute-start(bf16[416,256]{1,0:T(8,128)(2,1)S(1)} %shard_map.69.refs_0_), channel_id=1, source_target_pairs={{0,3},{1,0},{2,1},{3,2},{4,7},{5,4},{6,5},{7,6},{8,11},{9,8},{10,9... | collective-permute-start | bytes 638984 | tf_op jit(solution)/shard_map/ppermute | solution.py:324
  26.0 3.0 %collective-permute-done.3.refs_1_ = bf16[416,256]{1,0:T(8,128)(2,1)S(1)} collective-permute-done((bf16[416,256]{1,0:T(8,128)(2,1)S(1)}, bf16[416,256]{1,0:T(8,128)(2,1)S(1)}, u32[]{:S(2)}, u32[]{:S(2)}) %collective-permute-start.3) | collective-permute-done | bytes 213024 | tf_op jit(solution)/shard_map/ppermute | solution.py:324
  29.0 2.9 %collective-permute-done.4.refs_2_ = bf16[416,256]{1,0:T(8,128)(2,1)S(1)} collective-permute-done((bf16[416,256]{1,0:T(8,128)(2,1)S(1)}, bf16[416,256]{1,0:T(8,128)(2,1)S(1)}, u32[]{:S(2)}, u32[]{:S(2)}) %collective-permute-start.4) | collective-permute-done | bytes 213024 | tf_op jit(solution)/shard_map/ppermute | solution.py:324
  32.0 1.5 collective-permute-done.5.refs_3_
  33.5 2.0 %all-to-all-done.refs_4_ = bf16[8,200,256]{2,1,0:T(8,128)(2,1)S(1)} async-done(((bf16[8,200,256]{2,1,0:T(8,128)(2,1)}), bf16[8,200,256]{2,1,0:T(8,128)(2,1)S(1)}, u32[]{:S(2)}, u32[]{:S(2)}) %all-to-all-start) | async-done | bytes 819232 | tf_op jit(solution)/shard_map/all_to_all | solution.py:320
  35.4 3.0 %shard_map.70 = (f32[1536,768]{1,0:T(8,128)S(1)}, f32[1536,768]{1,0:T(8,128)S(1)}, bf16[1536,256]{1,0:T(8,128)(2,1)S(1)}, bf16[768,256]{1,0:T(8,128)(2,1)S(1)}, ...) custom-call(bf16[416,256]{1,0:T(8,128)(2,1)S(1)} %shard_map.69.refs_0_, ...), custom_call_target="tpu_custom_call" | custom-call | flops 5000000000 | bytes 1024 | tf_op jit(solution)/shard_map/pallas_call | solution.py:330
  38.4 14.2 %all_to_all.50.got_ref = f32[16,32,128]{2,1,0:T(8,128)S(1)} all-to-all(f32[16,32,128]{2,1,0:T(8,128)S(1)} %get-tuple-element.37), channel_id=1, replica_groups=mesh['filt'=2,'row'=4,'z'=8,'y'=4] {'y','row'}, dimensions={0} | all-to-all | bytes 524288 | tf_op jit(solution)/shard_map/all_to_all | solution.py:320
  52.6 0.7 shard_map.71
  53.3 12.5 %all_to_all.51.got_ref = f32[8,24,128]{2,1,0:T(8,128)S(1)} all-to-all(f32[8,24,128]{2,1,0:T(8,128)S(1)} %get-tuple-element.39), channel_id=1, replica_groups=mesh['filt'=2,'row'=4,'z'=8,'y'=4] {'z'}, dimensions={0} | all-to-all | bytes 196608 | tf_op jit(solution)/shard_map/all_to_all | solution.py:320
  65.8 0.4 shard_map.72
  66.2 11.4 %all_to_all.52.got_ref = f32[16,16,128]{2,1,0:T(8,128)S(1)} all-to-all(f32[16,16,128]{2,1,0:T(8,128)S(1)} %get-tuple-element.40), channel_id=1, replica_groups=mesh['filt'=2,'row'=4,'z'=8,'y'=4] {'y','row'}, dimensions={0} | all-to-all | bytes 262144 | tf_op jit(solution)/shard_map/all_to_all | solution.py:320
  77.6 0.6 shard_map.73
  78.2 10.4 %all_to_all.53.got_ref = f32[8,8,128]{2,1,0:T(8,128)S(1)} all-to-all(f32[8,8,128]{2,1,0:T(8,128)S(1)} %get-tuple-element.43), channel_id=1, replica_groups=mesh['filt'=2,'row'=4,'z'=8,'y'=4] {'z'}, dimensions={0} | all-to-all | bytes 65536 | tf_op jit(solution)/shard_map/all_to_all | solution.py:320
  88.6 0.4 shard_map.74
  89.0 11.1 %all_to_all.54.got_ref = f32[16,16,128]{2,1,0:T(8,128)S(1)} all-to-all(f32[16,16,128]{2,1,0:T(8,128)S(1)} %shard_map.74), channel_id=1, replica_groups=mesh['filt'=2,'row'=4,'z'=8,'y'=4] {'y','row'}, dimensions={0} | all-to-all | bytes 262144 | tf_op jit(solution)/shard_map/all_to_all | solution.py:320
  100.1 0.6 shard_map.75
  100.8 10.4 %all_to_all.55.got_ref = f32[8,8,128]{2,1,0:T(8,128)S(1)} all-to-all(f32[8,8,128]{2,1,0:T(8,128)S(1)} %get-tuple-element.45), channel_id=1, replica_groups=mesh['filt'=2,'row'=4,'z'=8,'y'=4] {'z'}, dimensions={0} | all-to-all | bytes 65536 | tf_op jit(solution)/shard_map/all_to_all | solution.py:320
  111.2 0.4 shard_map.76
  111.6 11.1 %all_to_all.56.got_ref = f32[16,16,128]{2,1,0:T(8,128)S(1)} all-to-all(f32[16,16,128]{2,1,0:T(8,128)S(1)} %shard_map.76), channel_id=1, replica_groups=mesh['filt'=2,'row'=4,'z'=8,'y'=4] {'y','row'}, dimensions={0} | all-to-all | bytes 262144 | tf_op jit(solution)/shard_map/all_to_all | solution.py:320
  122.6 0.6 shard_map.77
  123.3 10.5 %all_to_all.57.got_ref = f32[8,8,128]{2,1,0:T(8,128)S(1)} all-to-all(f32[8,8,128]{2,1,0:T(8,128)S(1)} %get-tuple-element.46), channel_id=1, replica_groups=mesh['filt'=2,'row'=4,'z'=8,'y'=4] {'z'}, dimensions={0} | all-to-all | bytes 65536 | tf_op jit(solution)/shard_map/all_to_all | solution.py:320
  133.8 2.5 %shard_map.78 = (bf16[1536,768]{1,0:T(8,128)(2,1)S(1)}, f32[1536,1]{1,0:T(8,128)S(1)}, f32[16,128]{1,0:T(8,128)S(1)}, bf16[384,256]{1,0:T(8,128)(2,1)S(1)}, f32[384,256]{1,0:T(8,128)S(1)}) custom-call(f32[8,8,128]{2,1,0:T(8,128)S(1)} %all_to_all.57.got_ref, f32[16,128]{1,0:T(8,128)S(1)} %get-tuple-element.44.col_ref, ...), custom_call_target="tpu_custom_call" | custom-call | flops 3000000000 | bytes 1024 | tf_op jit(solution)/shard_map/pallas_call | solution.py:330
  136.3 0.8 collective-permute-start.6
  137.1 0.8 shard_map.79.base_ref
  137.8 4.3 %collective-permute-done.6.got_ref = bf16[384,256]{1,0:T(8,128)(2,1)S(1)} collective-permute-done((bf16[384,256]{1,0:T(8,128)(2,1)S(1)}, bf16[384,256]{1,0:T(8,128)(2,1)S(1)}, u32[]{:S(2)}, u32[]{:S(2)}) %collective-permute-start.6) | collective-permute-done | bytes 196640 | tf_op jit(solution)/shard_map/ppermute | solution.py:327
  142.2 0.3 collective-permute-start.7
  142.6 1.7 %shard_map.81 = bf16[16,96,256]{2,1,0:T(8,128)(2,1)} custom-call(f32[1536,256]{1,0:T(8,128)S(1)} %shard_map.79.base_ref, bf16[1536,768]{1,0:T(8,128)(2,1)S(1)} %get-tuple-element.53.mixed_ref, f32[1536,1]{1,0:T(8,128)S(1)} %get-tuple-element.54.q_ref, bf16[1536,256]{1,0:T(8,128)(2,1)S(1)} %get-tuple-element.49.xi_ref, ...), custom_call_target="tpu_custom_call" | custom-call | flops 2000000000 | bytes 1024 | tf_op jit(solution)/shard_map/pallas_call | solution.py:330
  144.2 4.6 %collective-permute-done.7.got_ref = bf16[192,256]{1,0:T(8,128)(2,1)S(1)} collective-permute-done((bf16[192,256]{1,0:T(8,128)(2,1)S(1)}, bf16[192,256]{1,0:T(8,128)(2,1)S(1)}, u32[]{:S(2)}, u32[]{:S(2)}) %collective-permute-start.7) | collective-permute-done | bytes 98336 | tf_op jit(solution)/shard_map/ppermute | solution.py:327
  148.9 5.7 %all-to-all-start.9 = ((bf16[16,96,256]{2,1,0:T(8,128)(2,1)}), bf16[16,96,256]{2,1,0:T(8,128)(2,1)S(1)}, u32[]{:S(2)}, u32[]{:S(2)}) async-start(bf16[16,96,256]{2,1,0:T(8,128)(2,1)} %shard_map.81), calls=%async_computation.9 | async-start | bytes 1572864 | tf_op jit(solution)/shard_map/all_to_all | solution.py:320
  154.6 0.1 collective-permute-start.8
  154.7 0.5 dynamic-slice_bitcast_fusion
  155.2 7.5 %collective-permute-done.8.got_ref = bf16[96,256]{1,0:T(8,128)(2,1)S(1)} collective-permute-done((bf16[96,256]{1,0:T(8,128)(2,1)S(1)}, bf16[96,256]{1,0:T(8,128)(2,1)S(1)}, u32[]{:S(2)}, u32[]{:S(2)}) %collective-permute-start.8) | collective-permute-done | bytes 49184 | tf_op jit(solution)/shard_map/ppermute | solution.py:327
  162.7 1.3 all-to-all-done.9.rows_ref
  164.0 0.7 shard_map.83
  (3 shorter events, 0.1 us)
Async XLA Ops:
  3.1 32.3 %all-to-all-start = ((bf16[8,200,256]{2,1,0:T(8,128)(2,1)}), bf16[8,200,256]{2,1,0:T(8,128)(2,1)S(1)}, u32[]{:S(2)}, u32[]{:S(2)}) async-start(bf16[8,200,256]{2,1,0:T(8,128)(2,1)} %get-tuple-element.34), calls=%async_computation | async-start | bytes 1638400 | tf_op jit(solution)/shard_map/all_to_all | solution.py:320
  11.6 6.1 %collective-permute-start = (bf16[104,256]{1,0:T(8,128)(2,1)}, bf16[104,256]{1,0:T(8,128)(2,1)S(1)}, u32[]{:S(2)}, u32[]{:S(2)}) collective-permute-start(bf16[104,256]{1,0:T(8,128)(2,1)} %get-tuple-element.33.refs_0_), channel_id=1, source_target_pairs={{0,32},{32,64},{64,96},{96,0},{1,33},{33,65},{65,97},{97,1},{2,34}... | collective-permute-start | bytes 159752 | tf_op jit(solution)/shard_map/ppermute | solution.py:324
  13.1 5.8 %collective-permute-start.1 = (bf16[104,256]{1,0:T(8,128)(2,1)}, bf16[104,256]{1,0:T(8,128)(2,1)S(1)}, u32[]{:S(2)}, u32[]{:S(2)}) collective-permute-start(bf16[104,256]{1,0:T(8,128)(2,1)} %get-tuple-element.33.refs_0_), channel_id=1, source_target_pairs={{0,64},{32,96},{64,0},{96,32},{1,65},{33,97},{65,1},{97,33},{2,66}... | collective-permute-start | bytes 159752 | tf_op jit(solution)/shard_map/ppermute | solution.py:324
  15.8 4.3 %collective-permute-start.2 = (bf16[104,256]{1,0:T(8,128)(2,1)}, bf16[104,256]{1,0:T(8,128)(2,1)S(1)}, u32[]{:S(2)}, u32[]{:S(2)}) collective-permute-start(bf16[104,256]{1,0:T(8,128)(2,1)} %get-tuple-element.33.refs_0_), channel_id=1, source_target_pairs={{0,96},{32,0},{64,32},{96,64},{1,97},{33,1},{65,33},{97,65},{2,98}... | collective-permute-start | bytes 159752 | tf_op jit(solution)/shard_map/ppermute | solution.py:324
  20.2 0.8 copy-start
  21.0 8.0 %collective-permute-start.3 = (bf16[416,256]{1,0:T(8,128)(2,1)S(1)}, bf16[416,256]{1,0:T(8,128)(2,1)S(1)}, u32[]{:S(2)}, u32[]{:S(2)}) collective-permute-start(bf16[416,256]{1,0:T(8,128)(2,1)S(1)} %shard_map.69.refs_0_), channel_id=1, source_target_pairs={{0,1},{1,2},{2,3},{3,0},{4,5},{5,6},{6,7},{7,4},{8,9},{9,10},{10,1... | collective-permute-start | bytes 638984 | tf_op jit(solution)/shard_map/ppermute | solution.py:324
  22.7 9.3 %collective-permute-start.4 = (bf16[416,256]{1,0:T(8,128)(2,1)S(1)}, bf16[416,256]{1,0:T(8,128)(2,1)S(1)}, u32[]{:S(2)}, u32[]{:S(2)}) collective-permute-start(bf16[416,256]{1,0:T(8,128)(2,1)S(1)} %shard_map.69.refs_0_), channel_id=1, source_target_pairs={{0,2},{1,3},{2,0},{3,1},{4,6},{5,7},{6,4},{7,5},{8,10},{9,11},{10,... | collective-permute-start | bytes 638984 | tf_op jit(solution)/shard_map/ppermute | solution.py:324
  23.6 9.9 %collective-permute-start.5 = (bf16[416,256]{1,0:T(8,128)(2,1)S(1)}, bf16[416,256]{1,0:T(8,128)(2,1)S(1)}, u32[]{:S(2)}, u32[]{:S(2)}) collective-permute-start(bf16[416,256]{1,0:T(8,128)(2,1)S(1)} %shard_map.69.refs_0_), channel_id=1, source_target_pairs={{0,3},{1,0},{2,1},{3,2},{4,7},{5,4},{6,5},{7,6},{8,11},{9,8},{10,9... | collective-permute-start | bytes 638984 | tf_op jit(solution)/shard_map/ppermute | solution.py:324
  136.3 5.9 %collective-permute-start.6 = (bf16[384,256]{1,0:T(8,128)(2,1)S(1)}, bf16[384,256]{1,0:T(8,128)(2,1)S(1)}, u32[]{:S(2)}, u32[]{:S(2)}) collective-permute-start(bf16[384,256]{1,0:T(8,128)(2,1)S(1)} %get-tuple-element.51), channel_id=1, source_target_pairs={{0,4},{4,0},{8,12},{12,8},{16,20},{20,16},{24,28},{28,24},{1,5},{5... | collective-permute-start | bytes 589832 | tf_op jit(solution)/shard_map/ppermute | solution.py:327
  142.2 6.6 %collective-permute-start.7 = (bf16[192,256]{1,0:T(8,128)(2,1)S(1)}, bf16[192,256]{1,0:T(8,128)(2,1)S(1)}, u32[]{:S(2)}, u32[]{:S(2)}) collective-permute-start(bf16[192,256]{1,0:T(8,128)(2,1)S(1)} %get-tuple-element.59), channel_id=1, source_target_pairs={{0,8},{4,12},{8,0},{12,4},{16,24},{20,28},{24,16},{28,20},{1,9},{5... | collective-permute-start | bytes 294920 | tf_op jit(solution)/shard_map/ppermute | solution.py:327
  148.9 15.1 %all-to-all-start.9 = ((bf16[16,96,256]{2,1,0:T(8,128)(2,1)}), bf16[16,96,256]{2,1,0:T(8,128)(2,1)S(1)}, u32[]{:S(2)}, u32[]{:S(2)}) async-start(bf16[16,96,256]{2,1,0:T(8,128)(2,1)} %shard_map.81), calls=%async_computation.9 | async-start | bytes 1572864 | tf_op jit(solution)/shard_map/all_to_all | solution.py:320
  154.6 8.1 %collective-permute-start.8 = (bf16[96,256]{1,0:T(8,128)(2,1)S(1)}, bf16[96,256]{1,0:T(8,128)(2,1)S(1)}, u32[]{:S(2)}, u32[]{:S(2)}) collective-permute-start(bf16[96,256]{1,0:T(8,128)(2,1)S(1)} %get-tuple-element.63), channel_id=1, source_target_pairs={{0,16},{4,20},{8,24},{12,28},{16,0},{20,4},{24,8},{28,12},{1,17},{... | collective-permute-start | bytes 147464 | tf_op jit(solution)/shard_map/ppermute | solution.py:327

commit v5 on v4

--- a/solution.py
+++ b/solution.py
@@ -113,7 +113,7 @@
 def build(own, width, isrc, jsrc, *refs):
     steps = isrc // GROUP
     pi_refs, pj_ref = refs[:steps], refs[steps]
-    plan_ref, inner_ref, xi_ref, xj_ref, gj_ref, w_ref, mass_ref, col_ref = refs[steps + 1 :]
+    plan_ref, inner_ref, xi_ref, xj_hbm, gj_hbm, w_ref, mass_ref, col_ref, xj_ref, gj_ref, sem = refs[steps + 1 :]
     cols = jsrc * own
     size = own + AUX
     scale = 1.0 / (2.0 * width * EPS)
@@ -127,6 +127,9 @@
         pot = to_col(pj_ref[k, 2 * own : 2 * own + AUX, :].astype(F32)[0:1, 0:LANES], own)
         bias.append(pot / EPS - sq * scale)
     jbias = lanes_of(jnp.concatenate(bias, axis=0))
+    copies = [pltpu.make_async_copy(xj_ref, xj_hbm, sem.at[0]), pltpu.make_async_copy(gj_ref, gj_hbm, sem.at[1])]
+    for copy in copies:
+        copy.start()
     xj = xj_ref[...]
     gj = gj_ref[...]
     span = GROUP * own
@@ -163,6 +166,8 @@
         cph = weighted if cph is None else cph + weighted
     for s in range(1, isrc):
         mass_ref[s] = mass_ref[0]
+    for copy in copies:
+        copy.wait()
     col_ref[...] = jnp.zeros_like(col_ref)
     cmass = jnp.sum(cmass, axis=0, keepdims=True)
     cph = jnp.sum(cph, axis=0, keepdims=True)
@@ -233,80 +238,109 @@
     apply_rows(own, isrc, psi, plan_ref, send_ref)
 
 
-def psi_next(own, isrc, got_ref, col_ref, plan_ref, send_ref):
+def psi_next(own, isrc, got_ref, col_ref, plan_ref, psi_ref, send_ref):
     total = jnp.sum(got_ref[...], axis=0)
     count = plan_ref.shape[1] // LANES
-    psi = row_of(-(col_ref[8:16] + total) / col_ref[0:8], count)
-    apply_rows(own, isrc, psi, plan_ref, send_ref)
+    psi = -(col_ref[8:16] + total) / col_ref[0:8]
+    psi_ref[...] = psi
+    apply_rows(own, isrc, row_of(psi, count), plan_ref, send_ref)
 
 
 def bit_of(axis, bit):
     return lax.rem(lax.shift_right_logical(lax.axis_index(axis), bit), 2)
 
 
-def finish_cols(own, width, isrc, jsrc, every, got_ref, col_ref, phi_ref, plan_ref, inner_ref, xi_ref, mixed_ref, q_ref, gw_ref, send_ref, keep_ref, acc_ref):
-    total = jnp.sum(got_ref[...], axis=0)
-    count = plan_ref.shape[1] // LANES
-    psi = row_of(-(col_ref[8:16] + total) / col_ref[0:8], count)
-    wsum = jnp.sum(total[6:7], axis=1, keepdims=True)
-    wphi = jnp.sum(total[7:8], axis=1, keepdims=True)
-    gw_ref[...] = -(every / wsum) * (phi_ref[...] - wphi / wsum)
+def early_cols(own, width, isrc, jsrc, phi_ref, psi_ref, plan_ref, inner_ref, xi_ref, keep_ref, send_ref, acc_ref):
+    cols = plan_ref.shape[1]
+    psi = row_of(psi_ref[...], cols // LANES)
     span = GROUP * own
     for t in range(isrc // GROUP):
         at = slice(t * span, (t + 1) * span)
         col = column_of(phi_ref[t * GROUP : (t + 1) * GROUP, :], own, GROUP)
-        mixed = plan_ref[at, :] * (inner_ref[at, :] + (col + psi))
-        q_ref[at, :] = jnp.sum(mixed, axis=1, keepdims=True)
-        mixed = mixed.astype(BF16)
-        mixed_ref[at, :] = mixed
-        term = lax.dot_general(mixed, xi_ref[at, :], TN, preferred_element_type=F32)
-        if t:
-            term = acc_ref[...] + term
-        acc_ref[...] = term
+        plan = plan_ref[at, :]
+        mixed = (plan * (inner_ref[at, :] + (col + psi))).astype(BF16)
+        part = xi_ref[at, :]
+        for q, value in enumerate((mixed, plan.astype(BF16))):
+            term = lax.dot_general(value, part, TN, preferred_element_type=F32)
+            place = slice(q * cols, (q + 1) * cols)
+            if t:
+                term = acc_ref[place, :] + term
+            acc_ref[place, :] = term
     scale = 1.0 / (width * EPS)
     mine = bit_of("z", 0)
-    for m in range(jsrc // 2):
-        keep = pl.ds(pl.multiple_of((2 * m + mine) * own, own), own)
-        give = pl.ds(pl.multiple_of((2 * m + 1 - mine) * own, own), own)
-        at = slice(m * own, (m + 1) * own)
-        keep_ref[at, :] = acc_ref[keep, :] * scale
-        send_ref[at, :] = (acc_ref[give, :] * scale).astype(BF16)
+    for q in range(2):
+        for m in range(jsrc // 2):
+            keep = pl.ds(pl.multiple_of(q * cols + (2 * m + mine) * own, own), own)
+            give = pl.ds(pl.multiple_of(q * cols + (2 * m + 1 - mine) * own, own), own)
+            first = q * (cols // 2) + m * own
+            at = slice(first, first + own)
+            keep_ref[at, :] = acc_ref[keep, :] * scale
+            send_ref[at, :] = (acc_ref[give, :] * scale).astype(BF16)
 
 
 def halve(own, bit, keep_ref, got_ref, next_ref, send_ref):
     mine = bit_of("z", bit)
-    for m in range(next_ref.shape[0] // own):
-        keep = pl.ds(pl.multiple_of((2 * m + mine) * own, own), own)
-        give = pl.ds(pl.multiple_of((2 * m + 1 - mine) * own, own), own)
-        at = slice(m * own, (m + 1) * own)
-        next_ref[at, :] = keep_ref[keep, :] + got_ref[keep, :].astype(F32)
-        send_ref[at, :] = (keep_ref[give, :] + got_ref[give, :].astype(F32)).astype(BF16)
-
-
-def spread(own, isrc, plan_ref, gj_ref, after_ref, base_ref):
+    size, out = keep_ref.shape[0] // 2, next_ref.shape[0] // 2
+    for q in range(2):
+        for m in range(out // own):
+            keep = pl.ds(pl.multiple_of(q * size + (2 * m + mine) * own, own), own)
+            give = pl.ds(pl.multiple_of(q * size + (2 * m + 1 - mine) * own, own), own)
+            first = q * out + m * own
+            at = slice(first, first + own)
+            next_ref[at, :] = keep_ref[keep, :] + got_ref[keep, :].astype(F32)
+            send_ref[at, :] = (keep_ref[give, :] + got_ref[give, :].astype(F32)).astype(BF16)
+
+
+def finish_rows(own, width, isrc, every, *refs):
+    got_ref, col_ref, phi_ref, psi_ref, plan_hbm, inner_hbm, xi_hbm, xj_hbm, gj_hbm, after_ref = refs[:10]
+    row_ref, gw_ref, delta_ref, plan_ref, inner_ref, xi_ref, xj_ref, gj_ref, sem = refs[10:]
     span = GROUP * own
+    steps = isrc // GROUP
+    head = [pltpu.make_async_copy(xj_hbm, xj_ref, sem.at[3 * steps]), pltpu.make_async_copy(gj_hbm, gj_ref, sem.at[3 * steps + 1])]
+    parts = []
+    for t in range(steps):
+        at = pl.ds(t * span, span)
+        pairs = ((plan_hbm, plan_ref), (inner_hbm, inner_ref), (xi_hbm, xi_ref))
+        parts.append([pltpu.make_async_copy(a.at[at], b.at[at], sem.at[3 * t + n]) for n, (a, b) in enumerate(pairs)])
+    for copy in head + sum(parts, []):
+        copy.start()
+    total = jnp.sum(got_ref[...], axis=0)
+    cols = plan_ref.shape[1]
+    psi = -(col_ref[8:16] + total) / col_ref[0:8]
+    delta = row_of(psi - psi_ref[...], cols // LANES)
+    psi = row_of(psi, cols // LANES)
+    rows = lax.broadcasted_iota(jnp.int32, (own, cols), 0)
+    lanes = lax.broadcasted_iota(jnp.int32, (own, cols), 1)
+    first = lax.axis_index("z") * own
+    delta_ref[...] = jnp.sum(jnp.where(lanes == rows + first, delta, 0.0), axis=1, keepdims=True)
+    wsum = jnp.sum(total[6:7], axis=1, keepdims=True)
+    wphi = jnp.sum(total[7:8], axis=1, keepdims=True)
+    gw_ref[...] = -(every / wsum) * (phi_ref[...] - wphi / wsum)
+    scale = 1.0 / (width * EPS)
+    for copy in head:
+        copy.wait()
+    xj = xj_ref[...]
     gj = gj_ref[...]
-    for t in range(isrc // GROUP):
+    for t in range(steps):
         at = slice(t * span, (t + 1) * span)
-        base_ref[at, :] = jnp.dot(plan_ref[at, :].astype(BF16), gj, preferred_element_type=F32)
-
-
-def finish_rows(own, width, isrc, base_ref, mixed_ref, q_ref, xi_ref, xj_ref, after_ref, row_ref):
-    scale = 1.0 / (width * EPS)
-    span = GROUP * own
-    xj = xj_ref[...]
-    for t in range(isrc // GROUP):
-        at = slice(t * span, (t + 1) * span)
-        term = jnp.dot(mixed_ref[at, :], xj, preferred_element_type=F32)
-        term = base_ref[at, :] + (term - q_ref[at, :] * xi_ref[at, :].astype(F32)) * scale
+        col = column_of(phi_ref[t * GROUP : (t + 1) * GROUP, :], own, GROUP)
+        for copy in parts[t]:
+            copy.wait()
+        plan = plan_ref[at, :]
+        mixed = plan * (inner_ref[at, :] + (col + psi))
+        qrow = jnp.sum(mixed, axis=1, keepdims=True)
+        base = jnp.dot(plan.astype(BF16), gj, preferred_element_type=F32)
+        term = jnp.dot(mixed.astype(BF16), xj, preferred_element_type=F32)
+        term = base + (term - qrow * xi_ref[at, :].astype(F32)) * scale
         term = term.astype(BF16)
         for k in range(GROUP):
             row_ref[t * GROUP + k] = term[k * own : (k + 1) * own]
 
 
-def total_up(rows_ref, keep_ref, got_ref, out_ref):
+def total_up(own, rows_ref, keep_ref, got_ref, delta_ref, out_ref):
     acc = jnp.sum(rows_ref[...].astype(F32), axis=0)
-    out_ref[...] = (acc + (keep_ref[...] + got_ref[...].astype(F32))).astype(BF16)
+    sums = keep_ref[...] + got_ref[...].astype(F32)
+    out_ref[...] = (acc + (sums[:own] + delta_ref[...] * sums[own:])).astype(BF16)
 
 
 def local(particles, cotangent, row_potential, col_potential, weights):
@@ -326,10 +360,10 @@
     def flip(value, bit):
         return lax.ppermute(value, "z", [(i, i ^ bit) for i in range(jsrc)])
 
-    def call(body, micros, outs, *args, scratch=(), in_specs=None, out_specs=None, mib=12):
+    def call(body, micros, outs, *args, scratch=(), in_specs=None, out_specs=None, mib=12, hbm=()):
         return pl.pallas_call(
             body,
-            out_shape=[jax.ShapeDtypeStruct(s, d) for s, d in outs],
+            out_shape=[(pltpu.HBM if n in hbm else jax.ShapeDtypeStruct)(s, d) for n, (s, d) in enumerate(outs)],
             in_specs=in_specs or whole(len(args)),
             out_specs=out_specs or whole(len(outs)),
             scratch_shapes=list(scratch),
@@ -342,11 +376,16 @@
         functools.partial(pack, own, width, jsrc),
         2,
         [((own + AUX, width), BF16), ((jsrc, 2 * own + AUX, width), BF16)],
-        particles,
-        cotangent,
-        row_potential.reshape(1, own),
-        col_potential.reshape(1, own),
-        weights.reshape(1, own),
+        *[
+            pltpu.with_memory_space_constraint(v, pltpu.HBM)
+            for v in (
+                particles,
+                cotangent,
+                row_potential.reshape(1, own),
+                col_potential.reshape(1, own),
+                weights.reshape(1, own),
+            )
+        ],
         scratch=[
             pltpu.VMEM((2 * own + AUX, width), BF16),
             pltpu.VMEM((2, AUX, width), F32),
@@ -356,7 +395,7 @@
         ],
         in_specs=[anywhere] * 5,
         out_specs=whole(1) + [anywhere],
-        mib=60,
+        hbm=(1,),
     )
     jgot = swap(jpack, jaxes)
     near = [shift(ipack, "row", k) for k in range(1, xsrc)]
@@ -379,6 +418,9 @@
         ],
         *igot,
         jgot,
+        scratch=[pltpu.VMEM((cols, width), BF16), pltpu.VMEM((cols, width), BF16), pltpu.SemaphoreType.DMA((2,))],
+        out_specs=whole(3) + [anywhere] * 2 + whole(3),
+        hbm=(3, 4),
     )
     got = swap(send, iaxes)
     mass, send = call(
@@ -408,47 +450,56 @@
             wts,
             plan,
         )
-        got = swap(send, jaxes)
         if step < ITERS - 1:
-            (send,) = call(
+            got = swap(send, jaxes)
+            psi, send = call(
                 functools.partial(psi_next, own, isrc),
                 1,
-                [((isrc, isrc, LANES), F32)],
+                [((8, LANES), F32), ((isrc, isrc, LANES), F32)],
                 got,
                 col,
                 plan,
             )
-    half = cols // 2
-    mixed, q, gw, give, keep = call(
-        functools.partial(finish_cols, own, width, isrc, jsrc, float(isrc * jsrc * own)),
+    half = cols
+    keep, give = call(
+        functools.partial(early_cols, own, width, isrc, jsrc),
         3,
-        [((rows, cols), BF16), ((rows, 1), F32), ((isrc, LANES), F32), ((half, width), BF16), ((half, width), F32)],
+        [((half, width), F32), ((half, width), BF16)],
+        phi,
+        psi,
+        plan,
+        inner,
+        xi,
+        scratch=[pltpu.VMEM((2 * cols, width), F32)],
+    )
+    send, give = lax.optimization_barrier((send, give))
+    taken = flip(give, 1)
+    got = swap(send, jaxes)
+    half //= 2
+    keep, give = call(
+        functools.partial(halve, own, 1), 1, [((half, width), F32), ((half, width), BF16)], keep, taken
+    )
+    taken = flip(give, 2)
+    row_send, gw, delta = call(
+        functools.partial(finish_rows, own, width, isrc, float(isrc * jsrc * own)),
+        4,
+        [((isrc, own, width), BF16), ((isrc, LANES), F32), ((own, 1), F32)],
         got,
         col,
         phi,
-        plan,
-        inner,
-        xi,
-        scratch=[pltpu.VMEM((cols, width), F32)],
-    )
-    taken = flip(give, 1)
-    (base,) = call(functools.partial(spread, own, isrc), 1, [((rows, width), F32)], plan, gj, gw)
-    base, taken = lax.optimization_barrier((base, taken))
-    half //= 2
-    keep, give = call(
-        functools.partial(halve, own, 1), 1, [((half, width), F32), ((half, width), BF16)], keep, taken
-    )
-    taken = flip(give, 2)
-    (row_send,) = call(
-        functools.partial(finish_rows, own, width, isrc),
-        2,
-        [((isrc, own, width), BF16)],
-        base,
-        mixed,
-        q,
-        xi,
-        xj,
+        psi,
+        *[pltpu.with_memory_space_constraint(v, pltpu.HBM) for v in (plan, inner, xi, xj, gj)],
         keep,
+        scratch=[
+            pltpu.VMEM((rows, cols), F32),
+            pltpu.VMEM((rows, cols), F32),
+            pltpu.VMEM((rows, width), BF16),
+            pltpu.VMEM((cols, width), BF16),
+            pltpu.VMEM((cols, width), BF16),
+            pltpu.SemaphoreType.DMA((3 * (isrc // GROUP) + 2,)),
+        ],
+        in_specs=whole(4) + [anywhere] * 5 + whole(1),
+        mib=24,
     )
     row_send, taken = lax.optimization_barrier((row_send, taken))
     half //= 2
@@ -457,7 +508,9 @@
     )
     taken = flip(give, 4)
     row_got = swap(row_send, iaxes)
-    (grad,) = call(total_up, 1, [((own, width), BF16)], row_got, keep, taken)
+    (grad,) = call(
+        functools.partial(total_up, own), 1, [((own, width), BF16)], row_got, keep, taken, delta
+    )
     mine = lax.axis_index("y") * xsrc + lax.axis_index("row")
     grad_weights = lax.dynamic_slice(gw, (mine, 0), (1, own)).reshape(own)
     return (grad, grad_weights)

time: 166 us -> 162 us (0.976)
  blocking collectives: 91.4 us -> 79.9 us
  Pallas kernels: 15.1 us -> 20.2 us
  starting transfers between devices: 26.1 us -> 31.2 us
  waiting for transfers between devices: 30 us -> 28 us
    all_to_all x8 -> x7, blocking collectives: 91.4 us -> 79.9 us  [swap(): return lax.all_to_all(value, axes, 0, 0, tiled=True)]
    pallas_call x16 -> x15, Pallas kernels: 15.1 us -> 20.2 us  [call(): pl.pallas_call(body, out_shape=[(pltpu.HBM if n in hbm else jax.ShapeDtyp...]
    ppermute x3, waiting for transfers between devices: 16.4 us -> 12.6 us  [flip(): return lax.ppermute(value, 'z', [(i, i ^ bit) for i in range(jsrc)])]
    all_to_all x2 -> x3, starting transfers between devices: 14.2 us -> 17 us  [swap(): return lax.all_to_all(value, axes, 0, 0, tiled=True)]
    ppermute x3, starting transfers between devices: 1.19 us -> 3.61 us  [flip(): return lax.ppermute(value, 'z', [(i, i ^ bit) for i in range(jsrc)])]
    all_to_all x2 -> x3, waiting for transfers between devices: 3.23 us -> 5.21 us  [swap(): return lax.all_to_all(value, axes, 0, 0, tiled=True)]
  transfers between devices with their start and end apart: 11 -> 12, of which waited for: 11 -> 11; matrix products, arithmetic and copies ran while one was open for 0% -> 0% of each run, Pallas kernels for 2% -> 4%
where the time goes in v5:
time: 162 us; the launch traced here: 161 us
  blocking collectives  79.9 us (49%)
  starting transfers between devices  31.2 us (19%)
  waiting for transfers between devices  28 us (17%)
  Pallas kernels  20.2 us (12%)
    all_to_all x7, blocking collectives, swap(): return lax.all_to_all(value, axes, 0, 0, tiled=True)  79.9 us
    pallas_call x15, Pallas kernels, call(): pl.pallas_call(body, out_shape=[(pltpu.HBM if n in hbm else jax.ShapeDtyp...  20.2 us
    all_to_all x3, starting transfers between devices, swap(): return lax.all_to_all(value, axes, 0, 0, tiled=True)  17 us
    ppermute x3, waiting for transfers between devices, flip(): return lax.ppermute(value, 'z', [(i, i ^ bit) for i in range(jsrc)])  12.6 us
    ppermute x6, starting transfers between devices, shift(): return lax.ppermute(value, axis, [(i, (i + k) % n) for i in range(n)])  10.7 us
    ppermute x6, waiting for transfers between devices, shift(): return lax.ppermute(value, axis, [(i, (i + k) % n) for i in range(n)])  10.1 us
    all_to_all x3, waiting for transfers between devices, swap(): return lax.all_to_all(value, axes, 0, 0, tiled=True)  5.21 us
    ppermute x3, starting transfers between devices, flip(): return lax.ppermute(value, 'z', [(i, i ^ bit) for i in range(jsrc)])  3.61 us
  transfers between devices with their start and end apart: 12, of which 11 were waited for; matrix products, arithmetic and copies ran while one was open for 0% of the time, Pallas kernels for 4%

profile of v5, /device:TPU:8, one launch (start us, length us, event | category | flops | bytes accessed | tf_op | source)
XLA Modules:
  0.0 160.7 jit_solution(10344718775066227832)
XLA Ops:
  0.6 1.9 %shard_map.68 = (bf16[104,256]{1,0:T(8,128)(2,1)S(1)}, bf16[8,200,256]{2,1,0:T(8,128)(2,1)}) custom-call(bf16[96,256]{1,0:T(8,128)(2,1)} %x_ref.1, bf16[96,256]{1,0:T(8,128)(2,1)} %gy_ref.1, bf16[1,96]{1,0:T(2,128)(2,1)} %bitcast.5, bf16[1,96]{1,0:T(2,128)(2,1)} %bitcast.6, bf16[1,96]{1,0:T(2,128)(2,1)} %bitcast.7), custom_call_target="tpu_custom_call" | custom-call | flops 2000000000 | bytes 1024 | tf_op jit(solution)/shard_map/pallas_call | solution.py:364
  2.5 8.5 %all-to-all-start = ((bf16[8,200,256]{2,1,0:T(8,128)(2,1)}), bf16[8,200,256]{2,1,0:T(8,128)(2,1)S(1)}, u32[]{:S(2)}, u32[]{:S(2)}) async-start(bf16[8,200,256]{2,1,0:T(8,128)(2,1)} %get-tuple-element.37), calls=%async_computation | async-start | bytes 1638400 | tf_op jit(solution)/shard_map/all_to_all | solution.py:354
  11.0 1.5 collective-permute-start
  12.5 2.7 %collective-permute-start.1 = (bf16[104,256]{1,0:T(8,128)(2,1)S(1)}, bf16[104,256]{1,0:T(8,128)(2,1)S(1)}, u32[]{:S(2)}, u32[]{:S(2)}) collective-permute-start(bf16[104,256]{1,0:T(8,128)(2,1)S(1)} %get-tuple-element.36.refs_0_), channel_id=1, source_target_pairs={{0,64},{32,96},{64,0},{96,32},{1,65},{33,97},{65,1},{97,33},{2,66}... | collective-permute-start | bytes 159752 | tf_op jit(solution)/shard_map/ppermute | solution.py:358
  15.2 1.4 collective-permute-start.2
  16.7 0.3 collective-permute-done.refs_1_
  16.9 1.2 collective-permute-done.1.refs_2_
  18.1 1.2 collective-permute-done.2.refs_3_
  19.4 1.7 %collective-permute-start.3 = (bf16[416,256]{1,0:T(8,128)(2,1)S(1)}, bf16[416,256]{1,0:T(8,128)(2,1)S(1)}, u32[]{:S(2)}, u32[]{:S(2)}) collective-permute-start(bf16[416,256]{1,0:T(8,128)(2,1)S(1)} %shard_map.69.refs_0_), channel_id=1, source_target_pairs={{0,1},{1,2},{2,3},{3,0},{4,5},{5,6},{6,7},{7,4},{8,9},{9,10},{10,1... | collective-permute-start | bytes 638984 | tf_op jit(solution)/shard_map/ppermute | solution.py:358
  21.1 0.9 collective-permute-start.4
  22.0 2.4 %collective-permute-start.5 = (bf16[416,256]{1,0:T(8,128)(2,1)S(1)}, bf16[416,256]{1,0:T(8,128)(2,1)S(1)}, u32[]{:S(2)}, u32[]{:S(2)}) collective-permute-start(bf16[416,256]{1,0:T(8,128)(2,1)S(1)} %shard_map.69.refs_0_), channel_id=1, source_target_pairs={{0,3},{1,0},{2,1},{3,2},{4,7},{5,4},{6,5},{7,6},{8,11},{9,8},{10,9... | collective-permute-start | bytes 638984 | tf_op jit(solution)/shard_map/ppermute | solution.py:358
  24.4 3.0 %collective-permute-done.3.refs_1_ = bf16[416,256]{1,0:T(8,128)(2,1)S(1)} collective-permute-done((bf16[416,256]{1,0:T(8,128)(2,1)S(1)}, bf16[416,256]{1,0:T(8,128)(2,1)S(1)}, u32[]{:S(2)}, u32[]{:S(2)}) %collective-permute-start.3) | collective-permute-done | bytes 213024 | tf_op jit(solution)/shard_map/ppermute | solution.py:358
  27.4 2.9 %collective-permute-done.4.refs_2_ = bf16[416,256]{1,0:T(8,128)(2,1)S(1)} collective-permute-done((bf16[416,256]{1,0:T(8,128)(2,1)S(1)}, bf16[416,256]{1,0:T(8,128)(2,1)S(1)}, u32[]{:S(2)}, u32[]{:S(2)}) %collective-permute-start.4) | collective-permute-done | bytes 213024 | tf_op jit(solution)/shard_map/ppermute | solution.py:358
  30.4 1.5 collective-permute-done.5.refs_3_
  31.9 3.0 %all-to-all-done.refs_4_ = bf16[8,200,256]{2,1,0:T(8,128)(2,1)S(1)} async-done(((bf16[8,200,256]{2,1,0:T(8,128)(2,1)}), bf16[8,200,256]{2,1,0:T(8,128)(2,1)S(1)}, u32[]{:S(2)}, u32[]{:S(2)}) %all-to-all-start) | async-done | bytes 819232 | tf_op jit(solution)/shard_map/all_to_all | solution.py:354
  34.8 3.4 %shard_map.70 = (f32[1536,768]{1,0:T(8,128)S(1)}, f32[1536,768]{1,0:T(8,128)S(1)}, bf16[1536,256]{1,0:T(8,128)(2,1)S(1)}, bf16[768,256]{1,0:T(8,128)(2,1)}, bf16...) custom-call(bf16[416,256]{1,0:T(8,128)(2,1)S(1)} %shard_map.69.refs_0_, ...), custom_call_target="tpu_custom_call" | custom-call | flops 5000000000 | bytes 1024 | tf_op jit(solution)/shard_map/pallas_call | solution.py:364
  38.3 0.0 copy-start
  38.3 0.0 copy-start.1
  38.3 14.2 %all_to_all.50.got_ref = f32[16,32,128]{2,1,0:T(8,128)S(1)} all-to-all(f32[16,32,128]{2,1,0:T(8,128)S(1)} %get-tuple-element.38), channel_id=1, replica_groups=mesh['filt'=2,'row'=4,'z'=8,'y'=4] {'y','row'}, dimensions={0} | all-to-all | bytes 524288 | tf_op jit(solution)/shard_map/all_to_all | solution.py:354
  52.5 0.7 shard_map.71
  53.1 11.5 %all_to_all.51.got_ref = f32[8,24,128]{2,1,0:T(8,128)S(1)} all-to-all(f32[8,24,128]{2,1,0:T(8,128)S(1)} %get-tuple-element.41), channel_id=1, replica_groups=mesh['filt'=2,'row'=4,'z'=8,'y'=4] {'z'}, dimensions={0} | all-to-all | bytes 196608 | tf_op jit(solution)/shard_map/all_to_all | solution.py:354
  64.6 0.4 shard_map.72
  65.0 11.4 %all_to_all.52.got_ref = f32[16,16,128]{2,1,0:T(8,128)S(1)} all-to-all(f32[16,16,128]{2,1,0:T(8,128)S(1)} %get-tuple-element.42), channel_id=1, replica_groups=mesh['filt'=2,'row'=4,'z'=8,'y'=4] {'y','row'}, dimensions={0} | all-to-all | bytes 262144 | tf_op jit(solution)/shard_map/all_to_all | solution.py:354
  76.4 0.6 shard_map.73
  77.1 10.4 %all_to_all.53.got_ref = f32[8,8,128]{2,1,0:T(8,128)S(1)} all-to-all(f32[8,8,128]{2,1,0:T(8,128)S(1)} %get-tuple-element.45), channel_id=1, replica_groups=mesh['filt'=2,'row'=4,'z'=8,'y'=4] {'z'}, dimensions={0} | all-to-all | bytes 65536 | tf_op jit(solution)/shard_map/all_to_all | solution.py:354
  87.5 0.9 shard_map.74
  88.4 11.1 %all_to_all.54.got_ref = f32[16,16,128]{2,1,0:T(8,128)S(1)} all-to-all(f32[16,16,128]{2,1,0:T(8,128)S(1)} %get-tuple-element.47), channel_id=1, replica_groups=mesh['filt'=2,'row'=4,'z'=8,'y'=4] {'y','row'}, dimensions={0} | all-to-all | bytes 262144 | tf_op jit(solution)/shard_map/all_to_all | solution.py:354
  99.4 0.6 shard_map.75
  100.1 10.4 %all_to_all.55.got_ref = f32[8,8,128]{2,1,0:T(8,128)S(1)} all-to-all(f32[8,8,128]{2,1,0:T(8,128)S(1)} %get-tuple-element.48), channel_id=1, replica_groups=mesh['filt'=2,'row'=4,'z'=8,'y'=4] {'z'}, dimensions={0} | all-to-all | bytes 65536 | tf_op jit(solution)/shard_map/all_to_all | solution.py:354
  110.5 0.4 shard_map.76
  110.9 11.1 %all_to_all.56.got_ref = f32[16,16,128]{2,1,0:T(8,128)S(1)} all-to-all(f32[16,16,128]{2,1,0:T(8,128)S(1)} %get-tuple-element.49), channel_id=1, replica_groups=mesh['filt'=2,'row'=4,'z'=8,'y'=4] {'y','row'}, dimensions={0} | all-to-all | bytes 262144 | tf_op jit(solution)/shard_map/all_to_all | solution.py:354
  122.0 1.3 shard_map.77
  123.2 0.0 copy-done.1
  123.2 3.3 %shard_map.78 = (f32[768,256]{1,0:T(8,128)S(1)}, bf16[768,256]{1,0:T(8,128)(2,1)S(1)}) custom-call(f32[16,128]{1,0:T(8,128)S(1)} %get-tuple-element.51.phi_ref.refs_2_, f32[8,128]{1,0:T(8,128)S(1)} %get-tuple-element.52.psi_ref.refs_3_, f32[1536,768]{1,0:T(8,128)S(1)} %get-tuple-element.40.plan_ref.refs_4_, ...), custom_call_target="tpu_custom_call" | custom-call | flops 3000000000 | bytes 1024 | tf_op jit(solution)/shard_map/pallas_call | solution.py:364
  126.5 0.7 collective-permute-start.6
  127.2 3.3 %all-to-all-start.8 = ((f32[8,8,128]{2,1,0:T(8,128)}), f32[8,8,128]{2,1,0:T(8,128)S(1)}, u32[]{:S(2)}, u32[]{:S(2)}) async-start(f32[8,8,128]{2,1,0:T(8,128)} %get-tuple-element.56), calls=%async_computation.8 | async-start | bytes 65536 | tf_op jit(solution)/shard_map/all_to_all | solution.py:354
  130.5 5.5 %collective-permute-done.6.got_ref = bf16[768,256]{1,0:T(8,128)(2,1)S(1)} collective-permute-done((bf16[768,256]{1,0:T(8,128)(2,1)S(1)}, bf16[768,256]{1,0:T(8,128)(2,1)S(1)}, u32[]{:S(2)}, u32[]{:S(2)}) %collective-permute-start.6) | collective-permute-done | bytes 393248 | tf_op jit(solution)/shard_map/ppermute | solution.py:361
  136.1 0.1 shard_map.79
  136.1 0.1 collective-permute-start.7
  136.2 2.2 %all-to-all-done.8.refs_0_ = f32[8,8,128]{2,1,0:T(8,128)S(1)} async-done(((f32[8,8,128]{2,1,0:T(8,128)}), f32[8,8,128]{2,1,0:T(8,128)S(1)}, u32[]{:S(2)}, u32[]{:S(2)}) %all-to-all-start.8) | async-done | bytes 32800 | tf_op jit(solution)/shard_map/all_to_all | solution.py:354
  138.5 5.8 %shard_map.80 = (bf16[16,96,256]{2,1,0:T(8,128)(2,1)}, f32[16,128]{1,0:T(8,128)S(1)}, f32[96,1]{1,0:T(8,128)S(1)}) custom-call(f32[8,8,128]{2,1,0:T(8,128)S(1)} %all-to-all-done.8.refs_0_, f32[16,128]{1,0:T(8,128)S(1)} %get-tuple-element.46.col_ref.refs_1_, f32[16,128]{1,0:T(8,128)S(1)} %get-tuple-element.51.phi_ref.refs_2_, ...), custom_call_target="tpu_custom_call" | custom-call | flops 4000000000 | bytes 1024 | tf_op jit(solution)/shard_map/pallas_call | solution.py:364
  144.2 0.8 collective-permute-done.7.got_ref
  145.0 5.2 %all-to-all-start.9 = ((bf16[16,96,256]{2,1,0:T(8,128)(2,1)}), bf16[16,96,256]{2,1,0:T(8,128)(2,1)S(1)}, u32[]{:S(2)}, u32[]{:S(2)}) async-start(bf16[16,96,256]{2,1,0:T(8,128)(2,1)} %get-tuple-element.64), calls=%async_computation.9 | async-start | bytes 1572864 | tf_op jit(solution)/shard_map/all_to_all | solution.py:354
  150.2 2.9 %collective-permute-start.8 = (bf16[192,256]{1,0:T(8,128)(2,1)S(1)}, bf16[192,256]{1,0:T(8,128)(2,1)S(1)}, u32[]{:S(2)}, u32[]{:S(2)}) collective-permute-start(bf16[192,256]{1,0:T(8,128)(2,1)S(1)} %get-tuple-element.67), channel_id=1, source_target_pairs={{0,16},{4,20},{8,24},{12,28},{16,0},{20,4},{24,8},{28,12},{1,17},{... | collective-permute-start | bytes 294920 | tf_op jit(solution)/shard_map/ppermute | solution.py:361
  153.1 0.5 dynamic-slice_bitcast_fusion
  153.6 6.3 %collective-permute-done.8.got_ref = bf16[192,256]{1,0:T(8,128)(2,1)S(1)} collective-permute-done((bf16[192,256]{1,0:T(8,128)(2,1)S(1)}, bf16[192,256]{1,0:T(8,128)(2,1)S(1)}, u32[]{:S(2)}, u32[]{:S(2)}) %collective-permute-start.8) | collective-permute-done | bytes 98336 | tf_op jit(solution)/shard_map/ppermute | solution.py:361
  159.9 0.0 all-to-all-done.9.rows_ref
  159.9 0.8 shard_map.82
  (5 shorter events, 0.1 us)
Async XLA Ops:
  2.5 32.3 %all-to-all-start = ((bf16[8,200,256]{2,1,0:T(8,128)(2,1)}), bf16[8,200,256]{2,1,0:T(8,128)(2,1)S(1)}, u32[]{:S(2)}, u32[]{:S(2)}) async-start(bf16[8,200,256]{2,1,0:T(8,128)(2,1)} %get-tuple-element.37), calls=%async_computation | async-start | bytes 1638400 | tf_op jit(solution)/shard_map/all_to_all | solution.py:354
  11.0 5.9 %collective-permute-start = (bf16[104,256]{1,0:T(8,128)(2,1)S(1)}, bf16[104,256]{1,0:T(8,128)(2,1)S(1)}, u32[]{:S(2)}, u32[]{:S(2)}) collective-permute-start(bf16[104,256]{1,0:T(8,128)(2,1)S(1)} %get-tuple-element.36.refs_0_), channel_id=1, source_target_pairs={{0,32},{32,64},{64,96},{96,0},{1,33},{33,65},{65,97},{97,1},{2,34}... | collective-permute-start | bytes 159752 | tf_op jit(solution)/shard_map/ppermute | solution.py:358
  12.5 5.6 %collective-permute-start.1 = (bf16[104,256]{1,0:T(8,128)(2,1)S(1)}, bf16[104,256]{1,0:T(8,128)(2,1)S(1)}, u32[]{:S(2)}, u32[]{:S(2)}) collective-permute-start(bf16[104,256]{1,0:T(8,128)(2,1)S(1)} %get-tuple-element.36.refs_0_), channel_id=1, source_target_pairs={{0,64},{32,96},{64,0},{96,32},{1,65},{33,97},{65,1},{97,33},{2,66}... | collective-permute-start | bytes 159752 | tf_op jit(solution)/shard_map/ppermute | solution.py:358
  15.2 4.1 %collective-permute-start.2 = (bf16[104,256]{1,0:T(8,128)(2,1)S(1)}, bf16[104,256]{1,0:T(8,128)(2,1)S(1)}, u32[]{:S(2)}, u32[]{:S(2)}) collective-permute-start(bf16[104,256]{1,0:T(8,128)(2,1)S(1)} %get-tuple-element.36.refs_0_), channel_id=1, source_target_pairs={{0,96},{32,0},{64,32},{96,64},{1,97},{33,1},{65,33},{97,65},{2,98}... | collective-permute-start | bytes 159752 | tf_op jit(solution)/shard_map/ppermute | solution.py:358
  19.4 8.0 %collective-permute-start.3 = (bf16[416,256]{1,0:T(8,128)(2,1)S(1)}, bf16[416,256]{1,0:T(8,128)(2,1)S(1)}, u32[]{:S(2)}, u32[]{:S(2)}) collective-permute-start(bf16[416,256]{1,0:T(8,128)(2,1)S(1)} %shard_map.69.refs_0_), channel_id=1, source_target_pairs={{0,1},{1,2},{2,3},{3,0},{4,5},{5,6},{6,7},{7,4},{8,9},{9,10},{10,1... | collective-permute-start | bytes 638984 | tf_op jit(solution)/shard_map/ppermute | solution.py:358
  21.1 9.3 %collective-permute-start.4 = (bf16[416,256]{1,0:T(8,128)(2,1)S(1)}, bf16[416,256]{1,0:T(8,128)(2,1)S(1)}, u32[]{:S(2)}, u32[]{:S(2)}) collective-permute-start(bf16[416,256]{1,0:T(8,128)(2,1)S(1)} %shard_map.69.refs_0_), channel_id=1, source_target_pairs={{0,2},{1,3},{2,0},{3,1},{4,6},{5,7},{6,4},{7,5},{8,10},{9,11},{10,... | collective-permute-start | bytes 638984 | tf_op jit(solution)/shard_map/ppermute | solution.py:358
  22.0 9.9 %collective-permute-start.5 = (bf16[416,256]{1,0:T(8,128)(2,1)S(1)}, bf16[416,256]{1,0:T(8,128)(2,1)S(1)}, u32[]{:S(2)}, u32[]{:S(2)}) collective-permute-start(bf16[416,256]{1,0:T(8,128)(2,1)S(1)} %shard_map.69.refs_0_), channel_id=1, source_target_pairs={{0,3},{1,0},{2,1},{3,2},{4,7},{5,4},{6,5},{7,6},{8,11},{9,8},{10,9... | collective-permute-start | bytes 638984 | tf_op jit(solution)/shard_map/ppermute | solution.py:358
  38.3 85.0 %copy-start = (f32[1536,768]{1,0:T(8,128)}, f32[1536,768]{1,0:T(8,128)S(1)}, u32[]{:S(2)}) copy-start(f32[1536,768]{1,0:T(8,128)S(1)} %get-tuple-element.40.plan_ref.refs_4_) | copy-start | bytes 14155780
  38.3 85.0 %copy-start.1 = (f32[1536,768]{1,0:T(8,128)}, f32[1536,768]{1,0:T(8,128)S(1)}, u32[]{:S(2)}) copy-start(f32[1536,768]{1,0:T(8,128)S(1)} %get-tuple-element.53.inner_ref.refs_5_) | copy-start | bytes 14155780
  38.3 85.0 %copy-start.2 = (bf16[1536,256]{1,0:T(8,128)(2,1)}, bf16[1536,256]{1,0:T(8,128)(2,1)S(1)}, u32[]{:S(2)}) copy-start(bf16[1536,256]{1,0:T(8,128)(2,1)S(1)} %get-tuple-element.54.xi_ref.refs_6_) | copy-start | bytes 2359300
  126.5 9.5 %collective-permute-start.6 = (bf16[768,256]{1,0:T(8,128)(2,1)S(1)}, bf16[768,256]{1,0:T(8,128)(2,1)S(1)}, u32[]{:S(2)}, u32[]{:S(2)}) collective-permute-start(bf16[768,256]{1,0:T(8,128)(2,1)S(1)} %get-tuple-element.60), channel_id=1, source_target_pairs={{0,4},{4,0},{8,12},{12,8},{16,20},{20,16},{24,28},{28,24},{1,5},{5... | collective-permute-start | bytes 1179656 | tf_op jit(solution)/shard_map/ppermute | solution.py:361
  127.2 11.3 %all-to-all-start.8 = ((f32[8,8,128]{2,1,0:T(8,128)}), f32[8,8,128]{2,1,0:T(8,128)S(1)}, u32[]{:S(2)}, u32[]{:S(2)}) async-start(f32[8,8,128]{2,1,0:T(8,128)} %get-tuple-element.56), calls=%async_computation.8 | async-start | bytes 65536 | tf_op jit(solution)/shard_map/all_to_all | solution.py:354
  136.1 8.9 %collective-permute-start.7 = (bf16[384,256]{1,0:T(8,128)(2,1)S(1)}, bf16[384,256]{1,0:T(8,128)(2,1)S(1)}, u32[]{:S(2)}, u32[]{:S(2)}) collective-permute-start(bf16[384,256]{1,0:T(8,128)(2,1)S(1)} %get-tuple-element.63), channel_id=1, source_target_pairs={{0,8},{4,12},{8,0},{12,4},{16,24},{20,28},{24,16},{28,20},{1,9},{5... | collective-permute-start | bytes 589832 | tf_op jit(solution)/shard_map/ppermute | solution.py:361
  145.0 14.9 %all-to-all-start.9 = ((bf16[16,96,256]{2,1,0:T(8,128)(2,1)}), bf16[16,96,256]{2,1,0:T(8,128)(2,1)S(1)}, u32[]{:S(2)}, u32[]{:S(2)}) async-start(bf16[16,96,256]{2,1,0:T(8,128)(2,1)} %get-tuple-element.64), calls=%async_computation.9 | async-start | bytes 1572864 | tf_op jit(solution)/shard_map/all_to_all | solution.py:354
  150.2 9.7 %collective-permute-start.8 = (bf16[192,256]{1,0:T(8,128)(2,1)S(1)}, bf16[192,256]{1,0:T(8,128)(2,1)S(1)}, u32[]{:S(2)}, u32[]{:S(2)}) collective-permute-start(bf16[192,256]{1,0:T(8,128)(2,1)S(1)} %get-tuple-element.67), channel_id=1, source_target_pairs={{0,16},{4,20},{8,24},{12,28},{16,0},{20,4},{24,8},{28,12},{1,17},{... | collective-permute-start | bytes 294920 | tf_op jit(solution)/shard_map/ppermute | solution.py:361

commit v6 on v5

--- a/solution.py
+++ b/solution.py
@@ -113,7 +113,7 @@
 def build(own, width, isrc, jsrc, *refs):
     steps = isrc // GROUP
     pi_refs, pj_ref = refs[:steps], refs[steps]
-    plan_ref, inner_ref, xi_ref, xj_hbm, gj_hbm, w_ref, mass_ref, col_ref, xj_ref, gj_ref, sem = refs[steps + 1 :]
+    plan_ref, inner_ref, xi_ref, w_ref, mass_ref, col_ref, xj_ref, gj_ref = refs[steps + 1 :]
     cols = jsrc * own
     size = own + AUX
     scale = 1.0 / (2.0 * width * EPS)
@@ -127,9 +127,6 @@
         pot = to_col(pj_ref[k, 2 * own : 2 * own + AUX, :].astype(F32)[0:1, 0:LANES], own)
         bias.append(pot / EPS - sq * scale)
     jbias = lanes_of(jnp.concatenate(bias, axis=0))
-    copies = [pltpu.make_async_copy(xj_ref, xj_hbm, sem.at[0]), pltpu.make_async_copy(gj_ref, gj_hbm, sem.at[1])]
-    for copy in copies:
-        copy.start()
     xj = xj_ref[...]
     gj = gj_ref[...]
     span = GROUP * own
@@ -166,8 +163,6 @@
         cph = weighted if cph is None else cph + weighted
     for s in range(1, isrc):
         mass_ref[s] = mass_ref[0]
-    for copy in copies:
-        copy.wait()
     col_ref[...] = jnp.zeros_like(col_ref)
     cmass = jnp.sum(cmass, axis=0, keepdims=True)
     cph = jnp.sum(cph, axis=0, keepdims=True)
@@ -238,11 +233,12 @@
     apply_rows(own, isrc, psi, plan_ref, send_ref)
 
 
-def psi_next(own, isrc, got_ref, col_ref, plan_ref, psi_ref, send_ref):
+def psi_next(own, isrc, got_ref, col_ref, plan_ref, send_ref, *psi_refs):
     total = jnp.sum(got_ref[...], axis=0)
     count = plan_ref.shape[1] // LANES
     psi = -(col_ref[8:16] + total) / col_ref[0:8]
-    psi_ref[...] = psi
+    for ref in psi_refs:
+        ref[...] = psi
     apply_rows(own, isrc, row_of(psi, count), plan_ref, send_ref)
 
 
@@ -292,16 +288,22 @@
 
 
 def finish_rows(own, width, isrc, every, *refs):
-    got_ref, col_ref, phi_ref, psi_ref, plan_hbm, inner_hbm, xi_hbm, xj_hbm, gj_hbm, after_ref = refs[:10]
-    row_ref, gw_ref, delta_ref, plan_ref, inner_ref, xi_ref, xj_ref, gj_ref, sem = refs[10:]
+    got_ref, col_ref, phi_ref, psi_ref, plan_hbm, xi_hbm, pj_hbm, after_ref = refs[:8]
+    row_ref, gw_ref, delta_ref, plan_ref, xi_ref, xj_ref, gj_ref, sem = refs[8:]
     span = GROUP * own
     steps = isrc // GROUP
-    head = [pltpu.make_async_copy(xj_hbm, xj_ref, sem.at[3 * steps]), pltpu.make_async_copy(gj_hbm, gj_ref, sem.at[3 * steps + 1])]
+    jsrc = pj_hbm.shape[0]
+    head = []
+    for k in range(jsrc):
+        place = pl.ds(k * own, own)
+        for n, ref in enumerate((gj_ref, xj_ref)):
+            first = own if n == 0 else 0
+            head.append(pltpu.make_async_copy(pj_hbm.at[k, pl.ds(first, own)], ref.at[place], sem.at[2 * steps + 2 * k + n]))
     parts = []
     for t in range(steps):
         at = pl.ds(t * span, span)
-        pairs = ((plan_hbm, plan_ref), (inner_hbm, inner_ref), (xi_hbm, xi_ref))
-        parts.append([pltpu.make_async_copy(a.at[at], b.at[at], sem.at[3 * t + n]) for n, (a, b) in enumerate(pairs)])
+        pairs = ((xi_hbm, xi_ref), (plan_hbm, plan_ref))
+        parts.append([pltpu.make_async_copy(a.at[at], b.at[at], sem.at[2 * t + n]) for n, (a, b) in enumerate(pairs)])
     for copy in head + sum(parts, []):
         copy.start()
     total = jnp.sum(got_ref[...], axis=0)
@@ -327,7 +329,8 @@
         for copy in parts[t]:
             copy.wait()
         plan = plan_ref[at, :]
-        mixed = plan * (inner_ref[at, :] + (col + psi))
+        inner = lax.dot_general(xi_ref[at, :], gj, NT, preferred_element_type=F32)
+        mixed = plan * (inner + (col + psi))
         qrow = jnp.sum(mixed, axis=1, keepdims=True)
         base = jnp.dot(plan.astype(BF16), gj, preferred_element_type=F32)
         term = jnp.dot(mixed.astype(BF16), xj, preferred_element_type=F32)
@@ -403,24 +406,20 @@
         functools.partial(stack, own, xsrc), 1, [((xsrc * (own + AUX), width), BF16)], ipack, *near
     )
     igot = [line] + [shift(line, "y", k) for k in range(1, ysrc)]
-    plan, inner, xi, xj, gj, wts, send, col_part = call(
+    plan, inner, xi, wts, send, col_part = call(
         functools.partial(build, own, width, isrc, jsrc),
         5,
         [
             ((rows, cols), F32),
             ((rows, cols), F32),
             ((rows, width), BF16),
-            ((cols, width), BF16),
-            ((cols, width), BF16),
             ((isrc, LANES), F32),
             ((isrc, 2 * isrc, LANES), F32),
             ((16, LANES), F32),
         ],
         *igot,
         jgot,
-        scratch=[pltpu.VMEM((cols, width), BF16), pltpu.VMEM((cols, width), BF16), pltpu.SemaphoreType.DMA((2,))],
-        out_specs=whole(3) + [anywhere] * 2 + whole(3),
-        hbm=(3, 4),
+        scratch=[pltpu.VMEM((cols, width), BF16), pltpu.VMEM((cols, width), BF16)],
     )
     got = swap(send, iaxes)
     mass, send = call(
@@ -452,10 +451,10 @@
         )
         if step < ITERS - 1:
             got = swap(send, jaxes)
-            psi, send = call(
+            send, *kept = call(
                 functools.partial(psi_next, own, isrc),
                 1,
-                [((8, LANES), F32), ((isrc, isrc, LANES), F32)],
+                [((isrc, isrc, LANES), F32)] + [((8, LANES), F32)] * (step == ITERS - 2),
                 got,
                 col,
                 plan,
@@ -466,7 +465,7 @@
         3,
         [((half, width), F32), ((half, width), BF16)],
         phi,
-        psi,
+        *kept,
         plan,
         inner,
         xi,
@@ -487,18 +486,17 @@
         got,
         col,
         phi,
-        psi,
-        *[pltpu.with_memory_space_constraint(v, pltpu.HBM) for v in (plan, inner, xi, xj, gj)],
+        *kept,
+        *[pltpu.with_memory_space_constraint(v, pltpu.HBM) for v in (plan, xi, jgot)],
         keep,
         scratch=[
-            pltpu.VMEM((rows, cols), F32),
             pltpu.VMEM((rows, cols), F32),
             pltpu.VMEM((rows, width), BF16),
             pltpu.VMEM((cols, width), BF16),
             pltpu.VMEM((cols, width), BF16),
-            pltpu.SemaphoreType.DMA((3 * (isrc // GROUP) + 2,)),
+            pltpu.SemaphoreType.DMA((2 * (isrc // GROUP) + 2 * jsrc,)),
         ],
-        in_specs=whole(4) + [anywhere] * 5 + whole(1),
+        in_specs=whole(4) + [anywhere] * 3 + whole(1),
         mib=24,
     )
     row_send, taken = lax.optimization_barrier((row_send, taken))

time: 162 us -> 161 us (level)
  no operation moved by 1% of the time
where the time goes in v6:
time: 161 us; the launch traced here: 160 us
  blocking collectives  79.9 us (50%)
  starting transfers between devices  31.2 us (19%)
  waiting for transfers between devices  28 us (17%)
  Pallas kernels  19.4 us (12%)
    all_to_all x7, blocking collectives, swap(): return lax.all_to_all(value, axes, 0, 0, tiled=True)  79.9 us
    pallas_call x15, Pallas kernels, call(): pl.pallas_call(body, out_shape=[(pltpu.HBM if n in hbm else jax.ShapeDtyp...  19.4 us
    all_to_all x3, starting transfers between devices, swap(): return lax.all_to_all(value, axes, 0, 0, tiled=True)  17 us
    ppermute x3, waiting for transfers between devices, flip(): return lax.ppermute(value, 'z', [(i, i ^ bit) for i in range(jsrc)])  12.7 us
    ppermute x6, starting transfers between devices, shift(): return lax.ppermute(value, axis, [(i, (i + k) % n) for i in range(n)])  10.7 us
    ppermute x6, waiting for transfers between devices, shift(): return lax.ppermute(value, axis, [(i, (i + k) % n) for i in range(n)])  10.1 us
    all_to_all x3, waiting for transfers between devices, swap(): return lax.all_to_all(value, axes, 0, 0, tiled=True)  5.15 us
    ppermute x3, starting transfers between devices, flip(): return lax.ppermute(value, 'z', [(i, i ^ bit) for i in range(jsrc)])  3.61 us
  transfers between devices with their start and end apart: 12, of which 11 were waited for; matrix products, arithmetic and copies ran while one was open for 0% of the time, Pallas kernels for 4%

profile of v6, /device:TPU:8, one launch (start us, length us, event | category | flops | bytes accessed | tf_op | source)
XLA Modules:
  0.0 159.9 jit_solution(7634770005220800033)
XLA Ops:
  0.6 1.9 %shard_map.68 = (bf16[104,256]{1,0:T(8,128)(2,1)S(1)}, bf16[8,200,256]{2,1,0:T(8,128)(2,1)}) custom-call(bf16[96,256]{1,0:T(8,128)(2,1)} %x_ref.1, bf16[96,256]{1,0:T(8,128)(2,1)} %gy_ref.1, bf16[1,96]{1,0:T(2,128)(2,1)} %bitcast.5, bf16[1,96]{1,0:T(2,128)(2,1)} %bitcast.6, bf16[1,96]{1,0:T(2,128)(2,1)} %bitcast.7), custom_call_target="tpu_custom_call" | custom-call | flops 2000000000 | bytes 1024 | tf_op jit(solution)/shard_map/pallas_call | solution.py:367
  2.5 8.5 %all-to-all-start = ((bf16[8,200,256]{2,1,0:T(8,128)(2,1)}), bf16[8,200,256]{2,1,0:T(8,128)(2,1)S(1)}, u32[]{:S(2)}, u32[]{:S(2)}) async-start(bf16[8,200,256]{2,1,0:T(8,128)(2,1)} %get-tuple-element.34), calls=%async_computation | async-start | bytes 1638400 | tf_op jit(solution)/shard_map/all_to_all | solution.py:357
  11.0 1.5 collective-permute-start
  12.5 2.7 %collective-permute-start.1 = (bf16[104,256]{1,0:T(8,128)(2,1)S(1)}, bf16[104,256]{1,0:T(8,128)(2,1)S(1)}, u32[]{:S(2)}, u32[]{:S(2)}) collective-permute-start(bf16[104,256]{1,0:T(8,128)(2,1)S(1)} %get-tuple-element.33.refs_0_), channel_id=1, source_target_pairs={{0,64},{32,96},{64,0},{96,32},{1,65},{33,97},{65,1},{97,33},{2,66}... | collective-permute-start | bytes 159752 | tf_op jit(solution)/shard_map/ppermute | solution.py:361
  15.2 1.4 collective-permute-start.2
  16.7 0.3 collective-permute-done.refs_1_
  16.9 1.2 collective-permute-done.1.refs_2_
  18.2 1.2 collective-permute-done.2.refs_3_
  19.4 1.7 %collective-permute-start.3 = (bf16[416,256]{1,0:T(8,128)(2,1)S(1)}, bf16[416,256]{1,0:T(8,128)(2,1)S(1)}, u32[]{:S(2)}, u32[]{:S(2)}) collective-permute-start(bf16[416,256]{1,0:T(8,128)(2,1)S(1)} %shard_map.69.refs_0_), channel_id=1, source_target_pairs={{0,1},{1,2},{2,3},{3,0},{4,5},{5,6},{6,7},{7,4},{8,9},{9,10},{10,1... | collective-permute-start | bytes 638984 | tf_op jit(solution)/shard_map/ppermute | solution.py:361
  21.1 0.9 collective-permute-start.4
  22.0 2.4 %collective-permute-start.5 = (bf16[416,256]{1,0:T(8,128)(2,1)S(1)}, bf16[416,256]{1,0:T(8,128)(2,1)S(1)}, u32[]{:S(2)}, u32[]{:S(2)}) collective-permute-start(bf16[416,256]{1,0:T(8,128)(2,1)S(1)} %shard_map.69.refs_0_), channel_id=1, source_target_pairs={{0,3},{1,0},{2,1},{3,2},{4,7},{5,4},{6,5},{7,6},{8,11},{9,8},{10,9... | collective-permute-start | bytes 638984 | tf_op jit(solution)/shard_map/ppermute | solution.py:361
  24.4 3.0 %collective-permute-done.3.refs_1_ = bf16[416,256]{1,0:T(8,128)(2,1)S(1)} collective-permute-done((bf16[416,256]{1,0:T(8,128)(2,1)S(1)}, bf16[416,256]{1,0:T(8,128)(2,1)S(1)}, u32[]{:S(2)}, u32[]{:S(2)}) %collective-permute-start.3) | collective-permute-done | bytes 213024 | tf_op jit(solution)/shard_map/ppermute | solution.py:361
  27.4 2.9 %collective-permute-done.4.refs_2_ = bf16[416,256]{1,0:T(8,128)(2,1)S(1)} collective-permute-done((bf16[416,256]{1,0:T(8,128)(2,1)S(1)}, bf16[416,256]{1,0:T(8,128)(2,1)S(1)}, u32[]{:S(2)}, u32[]{:S(2)}) %collective-permute-start.4) | collective-permute-done | bytes 213024 | tf_op jit(solution)/shard_map/ppermute | solution.py:361
  30.4 1.5 collective-permute-done.5.refs_3_
  31.9 3.0 %all-to-all-done.refs_4_.refs_6_ = bf16[8,200,256]{2,1,0:T(8,128)(2,1)S(1)} async-done(((bf16[8,200,256]{2,1,0:T(8,128)(2,1)}), bf16[8,200,256]{2,1,0:T(8,128)(2,1)S(1)}, u32[]{:S(2)}, u32[]{:S(2)}) %all-to-all-start) | async-done | bytes 819232 | tf_op jit(solution)/shard_map/all_to_all | solution.py:357
  34.8 3.1 %shard_map.70 = (f32[1536,768]{1,0:T(8,128)S(1)}, f32[1536,768]{1,0:T(8,128)S(1)}, bf16[1536,256]{1,0:T(8,128)(2,1)S(1)}, f32[16,128]{1,0:T(8,128)S(1)}, f32[16,...) custom-call(bf16[416,256]{1,0:T(8,128)(2,1)S(1)} %shard_map.69.refs_0_, bf16[416,256]{1,0:T(8,128)(2,1)S(1)} %collective-permute-done.3.refs_1_, ...), custom_call_target="tpu_custom_call" | custom-call | flops 5000000000 | bytes 1024 | tf_op jit(solution)/shard_map/pallas_call | solution.py:367
  37.9 0.0 copy-done.1
  37.9 0.0 copy-start
  37.9 0.0 copy-start.2
  37.9 14.2 %all_to_all.50.got_ref = f32[16,32,128]{2,1,0:T(8,128)S(1)} all-to-all(f32[16,32,128]{2,1,0:T(8,128)S(1)} %get-tuple-element.35), channel_id=1, replica_groups=mesh['filt'=2,'row'=4,'z'=8,'y'=4] {'y','row'}, dimensions={0} | all-to-all | bytes 524288 | tf_op jit(solution)/shard_map/all_to_all | solution.py:357
  52.1 0.7 shard_map.71
  52.8 11.5 %all_to_all.51.got_ref = f32[8,24,128]{2,1,0:T(8,128)S(1)} all-to-all(f32[8,24,128]{2,1,0:T(8,128)S(1)} %get-tuple-element.38), channel_id=1, replica_groups=mesh['filt'=2,'row'=4,'z'=8,'y'=4] {'z'}, dimensions={0} | all-to-all | bytes 196608 | tf_op jit(solution)/shard_map/all_to_all | solution.py:357
  64.2 0.4 shard_map.72
  64.7 11.4 %all_to_all.52.got_ref = f32[16,16,128]{2,1,0:T(8,128)S(1)} all-to-all(f32[16,16,128]{2,1,0:T(8,128)S(1)} %get-tuple-element.39), channel_id=1, replica_groups=mesh['filt'=2,'row'=4,'z'=8,'y'=4] {'y','row'}, dimensions={0} | all-to-all | bytes 262144 | tf_op jit(solution)/shard_map/all_to_all | solution.py:357
  76.0 0.6 shard_map.73
  76.7 10.4 %all_to_all.53.got_ref = f32[8,8,128]{2,1,0:T(8,128)S(1)} all-to-all(f32[8,8,128]{2,1,0:T(8,128)S(1)} %get-tuple-element.42), channel_id=1, replica_groups=mesh['filt'=2,'row'=4,'z'=8,'y'=4] {'z'}, dimensions={0} | all-to-all | bytes 65536 | tf_op jit(solution)/shard_map/all_to_all | solution.py:357
  87.1 0.4 shard_map.74
  87.5 11.1 %all_to_all.54.got_ref = f32[16,16,128]{2,1,0:T(8,128)S(1)} all-to-all(f32[16,16,128]{2,1,0:T(8,128)S(1)} %shard_map.74), channel_id=1, replica_groups=mesh['filt'=2,'row'=4,'z'=8,'y'=4] {'y','row'}, dimensions={0} | all-to-all | bytes 262144 | tf_op jit(solution)/shard_map/all_to_all | solution.py:357
  98.6 0.6 shard_map.75
  99.2 10.4 %all_to_all.55.got_ref = f32[8,8,128]{2,1,0:T(8,128)S(1)} all-to-all(f32[8,8,128]{2,1,0:T(8,128)S(1)} %get-tuple-element.44), channel_id=1, replica_groups=mesh['filt'=2,'row'=4,'z'=8,'y'=4] {'z'}, dimensions={0} | all-to-all | bytes 65536 | tf_op jit(solution)/shard_map/all_to_all | solution.py:357
  109.6 0.4 shard_map.76
  110.1 11.1 %all_to_all.56.got_ref = f32[16,16,128]{2,1,0:T(8,128)S(1)} all-to-all(f32[16,16,128]{2,1,0:T(8,128)S(1)} %get-tuple-element.45), channel_id=1, replica_groups=mesh['filt'=2,'row'=4,'z'=8,'y'=4] {'y','row'}, dimensions={0} | all-to-all | bytes 262144 | tf_op jit(solution)/shard_map/all_to_all | solution.py:357
  121.1 1.3 shard_map.77
  122.4 3.3 %shard_map.78 = (f32[768,256]{1,0:T(8,128)S(1)}, bf16[768,256]{1,0:T(8,128)(2,1)S(1)}) custom-call(f32[16,128]{1,0:T(8,128)S(1)} %get-tuple-element.47.phi_ref.refs_2_, f32[8,128]{1,0:T(8,128)S(1)} %get-tuple-element.48.psi_ref.refs_3_, f32[1536,768]{1,0:T(8,128)S(1)} %get-tuple-element.37.plan_ref.refs_4_, f32[1536,768]{1,0:T(8,128)S(1)} %get-tuple-element.49.inner_ref, ...), custom_call_target="tpu_custom_call" | custom-call | flops 3000000000 | bytes 1024 | tf_op jit(solution)/shard_map/pallas_call | solution.py:367
  125.6 0.7 collective-permute-start.6
  126.3 3.3 %all-to-all-start.8 = ((f32[8,8,128]{2,1,0:T(8,128)}), f32[8,8,128]{2,1,0:T(8,128)S(1)}, u32[]{:S(2)}, u32[]{:S(2)}) async-start(f32[8,8,128]{2,1,0:T(8,128)} %get-tuple-element.52), calls=%async_computation.8 | async-start | bytes 65536 | tf_op jit(solution)/shard_map/all_to_all | solution.py:357
  129.7 5.6 %collective-permute-done.6.got_ref = bf16[768,256]{1,0:T(8,128)(2,1)S(1)} collective-permute-done((bf16[768,256]{1,0:T(8,128)(2,1)S(1)}, bf16[768,256]{1,0:T(8,128)(2,1)S(1)}, u32[]{:S(2)}, u32[]{:S(2)}) %collective-permute-start.6) | collective-permute-done | bytes 393248 | tf_op jit(solution)/shard_map/ppermute | solution.py:364
  135.2 0.1 shard_map.79
  135.3 0.1 collective-permute-start.7
  135.4 2.2 %all-to-all-done.8.refs_0_ = f32[8,8,128]{2,1,0:T(8,128)S(1)} async-done(((f32[8,8,128]{2,1,0:T(8,128)}), f32[8,8,128]{2,1,0:T(8,128)S(1)}, u32[]{:S(2)}, u32[]{:S(2)}) %all-to-all-start.8) | async-done | bytes 32800 | tf_op jit(solution)/shard_map/all_to_all | solution.py:357
  137.6 5.8 %shard_map.80 = (bf16[16,96,256]{2,1,0:T(8,128)(2,1)}, f32[16,128]{1,0:T(8,128)S(1)}, f32[96,1]{1,0:T(8,128)S(1)}) custom-call(f32[8,8,128]{2,1,0:T(8,128)S(1)} %all-to-all-done.8.refs_0_, f32[16,128]{1,0:T(8,128)S(1)} %get-tuple-element.43.col_ref.refs_1_, f32[16,128]{1,0:T(8,128)S(1)} %get-tuple-element.47.phi_ref.refs_2_, ...), custom_call_target="tpu_custom_call" | custom-call | flops 4000000000 | bytes 1024 | tf_op jit(solution)/shard_map/pallas_call | solution.py:367
  143.4 0.8 collective-permute-done.7.got_ref
  144.2 5.2 %all-to-all-start.9 = ((bf16[16,96,256]{2,1,0:T(8,128)(2,1)}), bf16[16,96,256]{2,1,0:T(8,128)(2,1)S(1)}, u32[]{:S(2)}, u32[]{:S(2)}) async-start(bf16[16,96,256]{2,1,0:T(8,128)(2,1)} %get-tuple-element.58), calls=%async_computation.9 | async-start | bytes 1572864 | tf_op jit(solution)/shard_map/all_to_all | solution.py:357
  149.4 2.9 %collective-permute-start.8 = (bf16[192,256]{1,0:T(8,128)(2,1)S(1)}, bf16[192,256]{1,0:T(8,128)(2,1)S(1)}, u32[]{:S(2)}, u32[]{:S(2)}) collective-permute-start(bf16[192,256]{1,0:T(8,128)(2,1)S(1)} %get-tuple-element.61), channel_id=1, source_target_pairs={{0,16},{4,20},{8,24},{12,28},{16,0},{20,4},{24,8},{28,12},{1,17},{... | collective-permute-start | bytes 294920 | tf_op jit(solution)/shard_map/ppermute | solution.py:364
  152.3 0.5 dynamic-slice_bitcast_fusion
  152.8 6.3 %collective-permute-done.8.got_ref = bf16[192,256]{1,0:T(8,128)(2,1)S(1)} collective-permute-done((bf16[192,256]{1,0:T(8,128)(2,1)S(1)}, bf16[192,256]{1,0:T(8,128)(2,1)S(1)}, u32[]{:S(2)}, u32[]{:S(2)}) %collective-permute-start.8) | collective-permute-done | bytes 98336 | tf_op jit(solution)/shard_map/ppermute | solution.py:364
  159.1 0.0 all-to-all-done.9.rows_ref
  159.1 0.8 shard_map.82
  (5 shorter events, 0.1 us)
Async XLA Ops:
  2.5 32.3 %all-to-all-start = ((bf16[8,200,256]{2,1,0:T(8,128)(2,1)}), bf16[8,200,256]{2,1,0:T(8,128)(2,1)S(1)}, u32[]{:S(2)}, u32[]{:S(2)}) async-start(bf16[8,200,256]{2,1,0:T(8,128)(2,1)} %get-tuple-element.34), calls=%async_computation | async-start | bytes 1638400 | tf_op jit(solution)/shard_map/all_to_all | solution.py:357
  11.0 5.9 %collective-permute-start = (bf16[104,256]{1,0:T(8,128)(2,1)S(1)}, bf16[104,256]{1,0:T(8,128)(2,1)S(1)}, u32[]{:S(2)}, u32[]{:S(2)}) collective-permute-start(bf16[104,256]{1,0:T(8,128)(2,1)S(1)} %get-tuple-element.33.refs_0_), channel_id=1, source_target_pairs={{0,32},{32,64},{64,96},{96,0},{1,33},{33,65},{65,97},{97,1},{2,34}... | collective-permute-start | bytes 159752 | tf_op jit(solution)/shard_map/ppermute | solution.py:361
  12.5 5.6 %collective-permute-start.1 = (bf16[104,256]{1,0:T(8,128)(2,1)S(1)}, bf16[104,256]{1,0:T(8,128)(2,1)S(1)}, u32[]{:S(2)}, u32[]{:S(2)}) collective-permute-start(bf16[104,256]{1,0:T(8,128)(2,1)S(1)} %get-tuple-element.33.refs_0_), channel_id=1, source_target_pairs={{0,64},{32,96},{64,0},{96,32},{1,65},{33,97},{65,1},{97,33},{2,66}... | collective-permute-start | bytes 159752 | tf_op jit(solution)/shard_map/ppermute | solution.py:361
  15.2 4.1 %collective-permute-start.2 = (bf16[104,256]{1,0:T(8,128)(2,1)S(1)}, bf16[104,256]{1,0:T(8,128)(2,1)S(1)}, u32[]{:S(2)}, u32[]{:S(2)}) collective-permute-start(bf16[104,256]{1,0:T(8,128)(2,1)S(1)} %get-tuple-element.33.refs_0_), channel_id=1, source_target_pairs={{0,96},{32,0},{64,32},{96,64},{1,97},{33,1},{65,33},{97,65},{2,98}... | collective-permute-start | bytes 159752 | tf_op jit(solution)/shard_map/ppermute | solution.py:361
  19.4 8.0 %collective-permute-start.3 = (bf16[416,256]{1,0:T(8,128)(2,1)S(1)}, bf16[416,256]{1,0:T(8,128)(2,1)S(1)}, u32[]{:S(2)}, u32[]{:S(2)}) collective-permute-start(bf16[416,256]{1,0:T(8,128)(2,1)S(1)} %shard_map.69.refs_0_), channel_id=1, source_target_pairs={{0,1},{1,2},{2,3},{3,0},{4,5},{5,6},{6,7},{7,4},{8,9},{9,10},{10,1... | collective-permute-start | bytes 638984 | tf_op jit(solution)/shard_map/ppermute | solution.py:361
  21.1 9.3 %collective-permute-start.4 = (bf16[416,256]{1,0:T(8,128)(2,1)S(1)}, bf16[416,256]{1,0:T(8,128)(2,1)S(1)}, u32[]{:S(2)}, u32[]{:S(2)}) collective-permute-start(bf16[416,256]{1,0:T(8,128)(2,1)S(1)} %shard_map.69.refs_0_), channel_id=1, source_target_pairs={{0,2},{1,3},{2,0},{3,1},{4,6},{5,7},{6,4},{7,5},{8,10},{9,11},{10,... | collective-permute-start | bytes 638984 | tf_op jit(solution)/shard_map/ppermute | solution.py:361
  22.0 9.9 %collective-permute-start.5 = (bf16[416,256]{1,0:T(8,128)(2,1)S(1)}, bf16[416,256]{1,0:T(8,128)(2,1)S(1)}, u32[]{:S(2)}, u32[]{:S(2)}) collective-permute-start(bf16[416,256]{1,0:T(8,128)(2,1)S(1)} %shard_map.69.refs_0_), channel_id=1, source_target_pairs={{0,3},{1,0},{2,1},{3,2},{4,7},{5,4},{6,5},{7,6},{8,11},{9,8},{10,9... | collective-permute-start | bytes 638984 | tf_op jit(solution)/shard_map/ppermute | solution.py:361
  34.8 3.1 %copy-start.1 = (bf16[8,200,256]{2,1,0:T(8,128)(2,1)}, bf16[8,200,256]{2,1,0:T(8,128)(2,1)S(1)}, u32[]{:S(2)}) copy-start(bf16[8,200,256]{2,1,0:T(8,128)(2,1)S(1)} %all-to-all-done.refs_4_.refs_6_) | copy-start | bytes 2457604
  37.9 84.5 %copy-start = (f32[1536,768]{1,0:T(8,128)}, f32[1536,768]{1,0:T(8,128)S(1)}, u32[]{:S(2)}) copy-start(f32[1536,768]{1,0:T(8,128)S(1)} %get-tuple-element.37.plan_ref.refs_4_) | copy-start | bytes 14155780
  37.9 84.5 %copy-start.2 = (bf16[1536,256]{1,0:T(8,128)(2,1)}, bf16[1536,256]{1,0:T(8,128)(2,1)S(1)}, u32[]{:S(2)}) copy-start(bf16[1536,256]{1,0:T(8,128)(2,1)S(1)} %get-tuple-element.50.xi_ref.refs_5_) | copy-start | bytes 2359300
  125.6 9.6 %collective-permute-start.6 = (bf16[768,256]{1,0:T(8,128)(2,1)S(1)}, bf16[768,256]{1,0:T(8,128)(2,1)S(1)}, u32[]{:S(2)}, u32[]{:S(2)}) collective-permute-start(bf16[768,256]{1,0:T(8,128)(2,1)S(1)} %get-tuple-element.54), channel_id=1, source_target_pairs={{0,4},{4,0},{8,12},{12,8},{16,20},{20,16},{24,28},{28,24},{1,5},{5... | collective-permute-start | bytes 1179656 | tf_op jit(solution)/shard_map/ppermute | solution.py:364
  126.3 11.3 %all-to-all-start.8 = ((f32[8,8,128]{2,1,0:T(8,128)}), f32[8,8,128]{2,1,0:T(8,128)S(1)}, u32[]{:S(2)}, u32[]{:S(2)}) async-start(f32[8,8,128]{2,1,0:T(8,128)} %get-tuple-element.52), calls=%async_computation.8 | async-start | bytes 65536 | tf_op jit(solution)/shard_map/all_to_all | solution.py:357
  135.3 8.9 %collective-permute-start.7 = (bf16[384,256]{1,0:T(8,128)(2,1)S(1)}, bf16[384,256]{1,0:T(8,128)(2,1)S(1)}, u32[]{:S(2)}, u32[]{:S(2)}) collective-permute-start(bf16[384,256]{1,0:T(8,128)(2,1)S(1)} %get-tuple-element.57), channel_id=1, source_target_pairs={{0,8},{4,12},{8,0},{12,4},{16,24},{20,28},{24,16},{28,20},{1,9},{5... | collective-permute-start | bytes 589832 | tf_op jit(solution)/shard_map/ppermute | solution.py:364
  144.2 14.9 %all-to-all-start.9 = ((bf16[16,96,256]{2,1,0:T(8,128)(2,1)}), bf16[16,96,256]{2,1,0:T(8,128)(2,1)S(1)}, u32[]{:S(2)}, u32[]{:S(2)}) async-start(bf16[16,96,256]{2,1,0:T(8,128)(2,1)} %get-tuple-element.58), calls=%async_computation.9 | async-start | bytes 1572864 | tf_op jit(solution)/shard_map/all_to_all | solution.py:357
  149.4 9.7 %collective-permute-start.8 = (bf16[192,256]{1,0:T(8,128)(2,1)S(1)}, bf16[192,256]{1,0:T(8,128)(2,1)S(1)}, u32[]{:S(2)}, u32[]{:S(2)}) collective-permute-start(bf16[192,256]{1,0:T(8,128)(2,1)S(1)} %get-tuple-element.61), channel_id=1, source_target_pairs={{0,16},{4,20},{8,24},{12,28},{16,0},{20,4},{24,8},{28,12},{1,17},{... | collective-permute-start | bytes 294920 | tf_op jit(solution)/shard_map/ppermute | solution.py:364

commit v7 on v6

--- a/solution.py
+++ b/solution.py
@@ -246,7 +246,12 @@
     return lax.rem(lax.shift_right_logical(lax.axis_index(axis), bit), 2)
 
 
-def early_cols(own, width, isrc, jsrc, phi_ref, psi_ref, plan_ref, inner_ref, xi_ref, keep_ref, send_ref, acc_ref):
+def phi_last(own, width, isrc, jsrc, *refs):
+    got_ref, mass_ref, w_ref, psi_ref, plan_ref, inner_ref, xi_ref = refs[:7]
+    phi_ref, send_hbm, keep_ref, give_ref, send_ref, mixed_ref, acc_ref, sem = refs[7:]
+    phi_next(own, isrc, jsrc, got_ref, mass_ref, w_ref, plan_ref, phi_ref, send_ref)
+    sent = pltpu.make_async_copy(send_ref, send_hbm, sem)
+    sent.start()
     cols = plan_ref.shape[1]
     psi = row_of(psi_ref[...], cols // LANES)
     span = GROUP * own
@@ -254,14 +259,12 @@
         at = slice(t * span, (t + 1) * span)
         col = column_of(phi_ref[t * GROUP : (t + 1) * GROUP, :], own, GROUP)
         plan = plan_ref[at, :]
-        mixed = (plan * (inner_ref[at, :] + (col + psi))).astype(BF16)
-        part = xi_ref[at, :]
-        for q, value in enumerate((mixed, plan.astype(BF16))):
-            term = lax.dot_general(value, part, TN, preferred_element_type=F32)
-            place = slice(q * cols, (q + 1) * cols)
-            if t:
-                term = acc_ref[place, :] + term
-            acc_ref[place, :] = term
+        mixed_ref[0, at, :] = (plan * (inner_ref[at, :] + (col + psi))).astype(BF16)
+        mixed_ref[1, at, :] = plan.astype(BF16)
+    part = xi_ref[...]
+    for q in range(2):
+        term = lax.dot_general(mixed_ref[q], part, TN, preferred_element_type=F32)
+        acc_ref[q * cols : (q + 1) * cols, :] = term
     scale = 1.0 / (width * EPS)
     mine = bit_of("z", 0)
     for q in range(2):
@@ -271,7 +274,8 @@
             first = q * (cols // 2) + m * own
             at = slice(first, first + own)
             keep_ref[at, :] = acc_ref[keep, :] * scale
-            send_ref[at, :] = (acc_ref[give, :] * scale).astype(BF16)
+            give_ref[at, :] = (acc_ref[give, :] * scale).astype(BF16)
+    sent.wait()
 
 
 def halve(own, bit, keep_ref, got_ref, next_ref, send_ref):
@@ -289,7 +293,7 @@
 
 def finish_rows(own, width, isrc, every, *refs):
     got_ref, col_ref, phi_ref, psi_ref, plan_hbm, xi_hbm, pj_hbm, after_ref = refs[:8]
-    row_ref, gw_ref, delta_ref, plan_ref, xi_ref, xj_ref, gj_ref, sem = refs[8:]
+    row_hbm, gw_ref, delta_ref, row_ref, plan_ref, xi_ref, xj_ref, gj_ref, sem, out_sem = refs[8:]
     span = GROUP * own
     steps = isrc // GROUP
     jsrc = pj_hbm.shape[0]
@@ -304,7 +308,7 @@
         at = pl.ds(t * span, span)
         pairs = ((xi_hbm, xi_ref), (plan_hbm, plan_ref))
         parts.append([pltpu.make_async_copy(a.at[at], b.at[at], sem.at[2 * t + n]) for n, (a, b) in enumerate(pairs)])
-    for copy in head + sum(parts, []):
+    for copy in head + parts[0] + parts[1]:
         copy.start()
     total = jnp.sum(got_ref[...], axis=0)
     cols = plan_ref.shape[1]
@@ -319,6 +323,7 @@
     wphi = jnp.sum(total[7:8], axis=1, keepdims=True)
     gw_ref[...] = -(every / wsum) * (phi_ref[...] - wphi / wsum)
     scale = 1.0 / (width * EPS)
+    outs = []
     for copy in head:
         copy.wait()
     xj = xj_ref[...]
@@ -328,6 +333,9 @@
         col = column_of(phi_ref[t * GROUP : (t + 1) * GROUP, :], own, GROUP)
         for copy in parts[t]:
             copy.wait()
+        if t + 2 < steps:
+            for copy in parts[t + 2]:
+                copy.start()
         plan = plan_ref[at, :]
         inner = lax.dot_general(xi_ref[at, :], gj, NT, preferred_element_type=F32)
         mixed = plan * (inner + (col + psi))
@@ -338,6 +346,11 @@
         term = term.astype(BF16)
         for k in range(GROUP):
             row_ref[t * GROUP + k] = term[k * own : (k + 1) * own]
+        group = pl.ds(t * GROUP, GROUP)
+        outs.append(pltpu.make_async_copy(row_ref.at[group], row_hbm.at[group], out_sem.at[t]))
+        outs[t].start()
+    for copy in outs:
+        copy.wait()
 
 
 def total_up(own, rows_ref, keep_ref, got_ref, delta_ref, out_ref):
@@ -440,16 +453,16 @@
     )
     for step in range(1, ITERS):
         got = swap(send, iaxes)
-        phi, send = call(
-            functools.partial(phi_next, own, isrc, jsrc),
-            1,
-            [((isrc, LANES), F32), ((jsrc, 8, LANES), F32)],
-            got,
-            mass,
-            wts,
-            plan,
-        )
         if step < ITERS - 1:
+            phi, send = call(
+                functools.partial(phi_next, own, isrc, jsrc),
+                1,
+                [((isrc, LANES), F32), ((jsrc, 8, LANES), F32)],
+                got,
+                mass,
+                wts,
+                plan,
+            )
             got = swap(send, jaxes)
             send, *kept = call(
                 functools.partial(psi_next, own, isrc),
@@ -460,16 +473,26 @@
                 plan,
             )
     half = cols
-    keep, give = call(
-        functools.partial(early_cols, own, width, isrc, jsrc),
-        3,
-        [((half, width), F32), ((half, width), BF16)],
-        phi,
+    phi, send, keep, give = call(
+        functools.partial(phi_last, own, width, isrc, jsrc),
+        4,
+        [((isrc, LANES), F32), ((jsrc, 8, LANES), F32), ((half, width), F32), ((half, width), BF16)],
+        got,
+        mass,
+        wts,
         *kept,
         plan,
         inner,
         xi,
-        scratch=[pltpu.VMEM((2 * cols, width), F32)],
+        scratch=[
+            pltpu.VMEM((jsrc, 8, LANES), F32),
+            pltpu.VMEM((2, rows, cols), BF16),
+            pltpu.VMEM((2 * cols, width), F32),
+            pltpu.SemaphoreType.DMA,
+        ],
+        out_specs=whole(1) + [anywhere] + whole(2),
+        hbm=(1,),
+        mib=20,
     )
     send, give = lax.optimization_barrier((send, give))
     taken = flip(give, 1)
@@ -490,13 +513,17 @@
         *[pltpu.with_memory_space_constraint(v, pltpu.HBM) for v in (plan, xi, jgot)],
         keep,
         scratch=[
+            pltpu.VMEM((isrc, own, width), BF16),
             pltpu.VMEM((rows, cols), F32),
             pltpu.VMEM((rows, width), BF16),
             pltpu.VMEM((cols, width), BF16),
             pltpu.VMEM((cols, width), BF16),
             pltpu.SemaphoreType.DMA((2 * (isrc // GROUP) + 2 * jsrc,)),
+            pltpu.SemaphoreType.DMA((isrc // GROUP,)),
         ],
         in_specs=whole(4) + [anywhere] * 3 + whole(1),
+        out_specs=[anywhere] + whole(2),
+        hbm=(0,),
         mib=24,
     )
     row_send, taken = lax.optimization_barrier((row_send, taken))

time: 161 us -> 161 us (level)
    pallas_call x15 -> x14, Pallas kernels: 19.4 us -> 18.1 us  [call(): pl.pallas_call(body, out_shape=[(pltpu.HBM if n in hbm else jax.ShapeDtyp...]
  transfers between devices with their start and end apart: 12 -> 12, of which waited for: 11 -> 12; matrix products, arithmetic and copies ran while one was open for 0% -> 0% of each run, Pallas kernels for 4% -> 4%
where the time goes in v7:
time: 161 us; the launch traced here: 159 us
  blocking collectives  79.9 us (50%)
  starting transfers between devices  31.2 us (19%)
  waiting for transfers between devices  28.8 us (18%)
  Pallas kernels  18.1 us (11%)
    all_to_all x7, blocking collectives, swap(): return lax.all_to_all(value, axes, 0, 0, tiled=True)  79.9 us
    pallas_call x14, Pallas kernels, call(): pl.pallas_call(body, out_shape=[(pltpu.HBM if n in hbm else jax.ShapeDtyp...  18.1 us
    all_to_all x3, starting transfers between devices, swap(): return lax.all_to_all(value, axes, 0, 0, tiled=True)  17.9 us
    ppermute x3, waiting for transfers between devices, flip(): return lax.ppermute(value, 'z', [(i, i ^ bit) for i in range(jsrc)])  12.7 us
    ppermute x6, starting transfers between devices, shift(): return lax.ppermute(value, axis, [(i, (i + k) % n) for i in range(n)])  10.7 us
    ppermute x6, waiting for transfers between devices, shift(): return lax.ppermute(value, axis, [(i, (i + k) % n) for i in range(n)])  10.1 us
    all_to_all x3, waiting for transfers between devices, swap(): return lax.all_to_all(value, axes, 0, 0, tiled=True)  5.94 us
  transfers between devices with their start and end apart: 12, of which 12 were waited for; matrix products, arithmetic and copies ran while one was open for 0% of the time, Pallas kernels for 4%

profile of v7, /device:TPU:8, one launch (start us, length us, event | category | flops | bytes accessed | tf_op | source)
XLA Modules:
  0.0 159.3 jit_solution(3539658578662277565)
XLA Ops:
  0.6 1.9 %shard_map.68 = (bf16[104,256]{1,0:T(8,128)(2,1)S(1)}, bf16[8,200,256]{2,1,0:T(8,128)(2,1)}) custom-call(bf16[96,256]{1,0:T(8,128)(2,1)} %x_ref.1, bf16[96,256]{1,0:T(8,128)(2,1)} %gy_ref.1, bf16[1,96]{1,0:T(2,128)(2,1)} %bitcast.5, bf16[1,96]{1,0:T(2,128)(2,1)} %bitcast.6, bf16[1,96]{1,0:T(2,128)(2,1)} %bitcast.7), custom_call_target="tpu_custom_call" | custom-call | flops 2000000000 | bytes 1024 | tf_op jit(solution)/shard_map/pallas_call | solution.py:380
  2.5 8.5 %all-to-all-start = ((bf16[8,200,256]{2,1,0:T(8,128)(2,1)}), bf16[8,200,256]{2,1,0:T(8,128)(2,1)S(1)}, u32[]{:S(2)}, u32[]{:S(2)}) async-start(bf16[8,200,256]{2,1,0:T(8,128)(2,1)} %get-tuple-element.34), calls=%async_computation | async-start | bytes 1638400 | tf_op jit(solution)/shard_map/all_to_all | solution.py:370
  11.0 1.5 collective-permute-start
  12.5 2.7 %collective-permute-start.1 = (bf16[104,256]{1,0:T(8,128)(2,1)S(1)}, bf16[104,256]{1,0:T(8,128)(2,1)S(1)}, u32[]{:S(2)}, u32[]{:S(2)}) collective-permute-start(bf16[104,256]{1,0:T(8,128)(2,1)S(1)} %get-tuple-element.33.refs_0_), channel_id=1, source_target_pairs={{0,64},{32,96},{64,0},{96,32},{1,65},{33,97},{65,1},{97,33},{2,66}... | collective-permute-start | bytes 159752 | tf_op jit(solution)/shard_map/ppermute | solution.py:374
  15.2 1.4 collective-permute-start.2
  16.7 0.3 collective-permute-done.refs_1_
  16.9 1.2 collective-permute-done.1.refs_2_
  18.2 1.2 collective-permute-done.2.refs_3_
  19.4 1.7 %collective-permute-start.3 = (bf16[416,256]{1,0:T(8,128)(2,1)S(1)}, bf16[416,256]{1,0:T(8,128)(2,1)S(1)}, u32[]{:S(2)}, u32[]{:S(2)}) collective-permute-start(bf16[416,256]{1,0:T(8,128)(2,1)S(1)} %shard_map.69.refs_0_), channel_id=1, source_target_pairs={{0,1},{1,2},{2,3},{3,0},{4,5},{5,6},{6,7},{7,4},{8,9},{9,10},{10,1... | collective-permute-start | bytes 638984 | tf_op jit(solution)/shard_map/ppermute | solution.py:374
  21.1 0.9 collective-permute-start.4
  22.0 2.4 %collective-permute-start.5 = (bf16[416,256]{1,0:T(8,128)(2,1)S(1)}, bf16[416,256]{1,0:T(8,128)(2,1)S(1)}, u32[]{:S(2)}, u32[]{:S(2)}) collective-permute-start(bf16[416,256]{1,0:T(8,128)(2,1)S(1)} %shard_map.69.refs_0_), channel_id=1, source_target_pairs={{0,3},{1,0},{2,1},{3,2},{4,7},{5,4},{6,5},{7,6},{8,11},{9,8},{10,9... | collective-permute-start | bytes 638984 | tf_op jit(solution)/shard_map/ppermute | solution.py:374
  24.4 3.0 %collective-permute-done.3.refs_1_ = bf16[416,256]{1,0:T(8,128)(2,1)S(1)} collective-permute-done((bf16[416,256]{1,0:T(8,128)(2,1)S(1)}, bf16[416,256]{1,0:T(8,128)(2,1)S(1)}, u32[]{:S(2)}, u32[]{:S(2)}) %collective-permute-start.3) | collective-permute-done | bytes 213024 | tf_op jit(solution)/shard_map/ppermute | solution.py:374
  27.4 2.9 %collective-permute-done.4.refs_2_ = bf16[416,256]{1,0:T(8,128)(2,1)S(1)} collective-permute-done((bf16[416,256]{1,0:T(8,128)(2,1)S(1)}, bf16[416,256]{1,0:T(8,128)(2,1)S(1)}, u32[]{:S(2)}, u32[]{:S(2)}) %collective-permute-start.4) | collective-permute-done | bytes 213024 | tf_op jit(solution)/shard_map/ppermute | solution.py:374
  30.4 1.5 collective-permute-done.5.refs_3_
  31.9 3.0 %all-to-all-done.refs_4_.refs_6_ = bf16[8,200,256]{2,1,0:T(8,128)(2,1)S(1)} async-done(((bf16[8,200,256]{2,1,0:T(8,128)(2,1)}), bf16[8,200,256]{2,1,0:T(8,128)(2,1)S(1)}, u32[]{:S(2)}, u32[]{:S(2)}) %all-to-all-start) | async-done | bytes 819232 | tf_op jit(solution)/shard_map/all_to_all | solution.py:370
  34.8 3.1 %shard_map.70 = (f32[1536,768]{1,0:T(8,128)S(1)}, f32[1536,768]{1,0:T(8,128)S(1)}, bf16[1536,256]{1,0:T(8,128)(2,1)S(1)}, f32[16,128]{1,0:T(8,128)S(1)}, f32[16,...) custom-call(bf16[416,256]{1,0:T(8,128)(2,1)S(1)} %shard_map.69.refs_0_, bf16[416,256]{1,0:T(8,128)(2,1)S(1)} %collective-permute-done.3.refs_1_, ...), custom_call_target="tpu_custom_call" | custom-call | flops 5000000000 | bytes 1024 | tf_op jit(solution)/shard_map/pallas_call | solution.py:380
  37.9 0.0 copy-done.1
  37.9 0.0 copy-start
  37.9 0.0 copy-start.2
  37.9 14.2 %all_to_all.50.got_ref = f32[16,32,128]{2,1,0:T(8,128)S(1)} all-to-all(f32[16,32,128]{2,1,0:T(8,128)S(1)} %get-tuple-element.35), channel_id=1, replica_groups=mesh['filt'=2,'row'=4,'z'=8,'y'=4] {'y','row'}, dimensions={0} | all-to-all | bytes 524288 | tf_op jit(solution)/shard_map/all_to_all | solution.py:370
  52.1 0.7 shard_map.71
  52.8 11.5 %all_to_all.51.got_ref = f32[8,24,128]{2,1,0:T(8,128)S(1)} all-to-all(f32[8,24,128]{2,1,0:T(8,128)S(1)} %get-tuple-element.38), channel_id=1, replica_groups=mesh['filt'=2,'row'=4,'z'=8,'y'=4] {'z'}, dimensions={0} | all-to-all | bytes 196608 | tf_op jit(solution)/shard_map/all_to_all | solution.py:370
  64.2 0.4 shard_map.72
  64.7 11.4 %all_to_all.52.got_ref = f32[16,16,128]{2,1,0:T(8,128)S(1)} all-to-all(f32[16,16,128]{2,1,0:T(8,128)S(1)} %get-tuple-element.39), channel_id=1, replica_groups=mesh['filt'=2,'row'=4,'z'=8,'y'=4] {'y','row'}, dimensions={0} | all-to-all | bytes 262144 | tf_op jit(solution)/shard_map/all_to_all | solution.py:370
  76.0 0.7 shard_map.73
  76.7 10.4 %all_to_all.53.got_ref = f32[8,8,128]{2,1,0:T(8,128)S(1)} all-to-all(f32[8,8,128]{2,1,0:T(8,128)S(1)} %get-tuple-element.42), channel_id=1, replica_groups=mesh['filt'=2,'row'=4,'z'=8,'y'=4] {'z'}, dimensions={0} | all-to-all | bytes 65536 | tf_op jit(solution)/shard_map/all_to_all | solution.py:370
  87.1 0.4 shard_map.74
  87.5 11.1 %all_to_all.54.got_ref = f32[16,16,128]{2,1,0:T(8,128)S(1)} all-to-all(f32[16,16,128]{2,1,0:T(8,128)S(1)} %shard_map.74), channel_id=1, replica_groups=mesh['filt'=2,'row'=4,'z'=8,'y'=4] {'y','row'}, dimensions={0} | all-to-all | bytes 262144 | tf_op jit(solution)/shard_map/all_to_all | solution.py:370
  98.6 0.7 shard_map.75
  99.2 10.4 %all_to_all.55.got_ref = f32[8,8,128]{2,1,0:T(8,128)S(1)} all-to-all(f32[8,8,128]{2,1,0:T(8,128)S(1)} %get-tuple-element.44), channel_id=1, replica_groups=mesh['filt'=2,'row'=4,'z'=8,'y'=4] {'z'}, dimensions={0} | all-to-all | bytes 65536 | tf_op jit(solution)/shard_map/all_to_all | solution.py:370
  109.6 0.4 shard_map.76
  110.1 11.1 %all_to_all.56.refs_0_ = f32[16,16,128]{2,1,0:T(8,128)S(1)} all-to-all(f32[16,16,128]{2,1,0:T(8,128)S(1)} %get-tuple-element.45), channel_id=1, replica_groups=mesh['filt'=2,'row'=4,'z'=8,'y'=4] {'y','row'}, dimensions={0} | all-to-all | bytes 262144 | tf_op jit(solution)/shard_map/all_to_all | solution.py:370
  121.1 0.0 copy-done
  121.1 3.4 %shard_map.77 = (f32[16,128]{1,0:T(8,128)S(1)}, f32[8,8,128]{2,1,0:T(8,128)}, f32[768,256]{1,0:T(8,128)S(1)}, bf16[768,256]{1,0:T(8,128)(2,1)S(1)}) custom-call(f32[16,16,128]{2,1,0:T(8,128)S(1)} %all_to_all.56.refs_0_, f32[32,128]{1,0:T(8,128)S(1)} %get-tuple-element.40.mass_ref.refs_1_, f32[16,128]{1,0:T(8,128)S(1)} %get-tuple-element.41.w_ref.refs_2_, ...), custom_call_target="tpu_custom_call" | custom-call | flops 4000000000 | bytes 1024 | tf_op jit(solution)/shard_map/pallas_call | solution.py:380
  124.5 0.7 collective-permute-start.6
  125.2 3.3 %all-to-all-start.8 = ((f32[8,8,128]{2,1,0:T(8,128)}), f32[8,8,128]{2,1,0:T(8,128)S(1)}, u32[]{:S(2)}, u32[]{:S(2)}) async-start(f32[8,8,128]{2,1,0:T(8,128)} %get-tuple-element.51), calls=%async_computation.8 | async-start | bytes 65536 | tf_op jit(solution)/shard_map/all_to_all | solution.py:370
  128.5 5.6 %collective-permute-done.6.got_ref = bf16[768,256]{1,0:T(8,128)(2,1)S(1)} collective-permute-done((bf16[768,256]{1,0:T(8,128)(2,1)S(1)}, bf16[768,256]{1,0:T(8,128)(2,1)S(1)}, u32[]{:S(2)}, u32[]{:S(2)}) %collective-permute-start.6) | collective-permute-done | bytes 393248 | tf_op jit(solution)/shard_map/ppermute | solution.py:377
  134.1 0.1 shard_map.78
  134.2 0.1 collective-permute-start.7
  134.3 2.2 %all-to-all-done.8.refs_0_ = f32[8,8,128]{2,1,0:T(8,128)S(1)} async-done(((f32[8,8,128]{2,1,0:T(8,128)}), f32[8,8,128]{2,1,0:T(8,128)S(1)}, u32[]{:S(2)}, u32[]{:S(2)}) %all-to-all-start.8) | async-done | bytes 32800 | tf_op jit(solution)/shard_map/all_to_all | solution.py:370
  136.4 5.6 %shard_map.79 = (bf16[16,96,256]{2,1,0:T(8,128)(2,1)}, f32[16,128]{1,0:T(8,128)S(1)}, f32[96,1]{1,0:T(8,128)S(1)}) custom-call(f32[8,8,128]{2,1,0:T(8,128)S(1)} %all-to-all-done.8.refs_0_, f32[16,128]{1,0:T(8,128)S(1)} %get-tuple-element.43.col_ref.refs_1_, f32[16,128]{1,0:T(8,128)S(1)} %get-tuple-element.52.refs_2_, ...), custom_call_target="tpu_custom_call" | custom-call | flops 4000000000 | bytes 1024 | tf_op jit(solution)/shard_map/pallas_call | solution.py:380
  142.1 1.0 collective-permute-done.7.got_ref
  143.1 6.1 %all-to-all-start.9 = ((bf16[16,96,256]{2,1,0:T(8,128)(2,1)}), bf16[16,96,256]{2,1,0:T(8,128)(2,1)S(1)}, u32[]{:S(2)}, u32[]{:S(2)}) async-start(bf16[16,96,256]{2,1,0:T(8,128)(2,1)} %get-tuple-element.58), calls=%async_computation.9 | async-start | bytes 1572864 | tf_op jit(solution)/shard_map/all_to_all | solution.py:370
  149.2 1.9 %collective-permute-start.8 = (bf16[192,256]{1,0:T(8,128)(2,1)S(1)}, bf16[192,256]{1,0:T(8,128)(2,1)S(1)}, u32[]{:S(2)}, u32[]{:S(2)}) collective-permute-start(bf16[192,256]{1,0:T(8,128)(2,1)S(1)} %get-tuple-element.61), channel_id=1, source_target_pairs={{0,16},{4,20},{8,24},{12,28},{16,0},{20,4},{24,8},{28,12},{1,17},{... | collective-permute-start | bytes 294920 | tf_op jit(solution)/shard_map/ppermute | solution.py:377
  151.1 0.5 dynamic-slice_bitcast_fusion
  151.6 6.2 %collective-permute-done.8.got_ref = bf16[192,256]{1,0:T(8,128)(2,1)S(1)} collective-permute-done((bf16[192,256]{1,0:T(8,128)(2,1)S(1)}, bf16[192,256]{1,0:T(8,128)(2,1)S(1)}, u32[]{:S(2)}, u32[]{:S(2)}) %collective-permute-start.8) | collective-permute-done | bytes 98336 | tf_op jit(solution)/shard_map/ppermute | solution.py:377
  157.8 0.8 all-to-all-done.9.rows_ref
  158.6 0.8 shard_map.81
  (4 shorter events, 0.1 us)
Async XLA Ops:
  2.5 32.3 %all-to-all-start = ((bf16[8,200,256]{2,1,0:T(8,128)(2,1)}), bf16[8,200,256]{2,1,0:T(8,128)(2,1)S(1)}, u32[]{:S(2)}, u32[]{:S(2)}) async-start(bf16[8,200,256]{2,1,0:T(8,128)(2,1)} %get-tuple-element.34), calls=%async_computation | async-start | bytes 1638400 | tf_op jit(solution)/shard_map/all_to_all | solution.py:370
  11.0 5.9 %collective-permute-start = (bf16[104,256]{1,0:T(8,128)(2,1)S(1)}, bf16[104,256]{1,0:T(8,128)(2,1)S(1)}, u32[]{:S(2)}, u32[]{:S(2)}) collective-permute-start(bf16[104,256]{1,0:T(8,128)(2,1)S(1)} %get-tuple-element.33.refs_0_), channel_id=1, source_target_pairs={{0,32},{32,64},{64,96},{96,0},{1,33},{33,65},{65,97},{97,1},{2,34}... | collective-permute-start | bytes 159752 | tf_op jit(solution)/shard_map/ppermute | solution.py:374
  12.5 5.6 %collective-permute-start.1 = (bf16[104,256]{1,0:T(8,128)(2,1)S(1)}, bf16[104,256]{1,0:T(8,128)(2,1)S(1)}, u32[]{:S(2)}, u32[]{:S(2)}) collective-permute-start(bf16[104,256]{1,0:T(8,128)(2,1)S(1)} %get-tuple-element.33.refs_0_), channel_id=1, source_target_pairs={{0,64},{32,96},{64,0},{96,32},{1,65},{33,97},{65,1},{97,33},{2,66}... | collective-permute-start | bytes 159752 | tf_op jit(solution)/shard_map/ppermute | solution.py:374
  15.2 4.1 %collective-permute-start.2 = (bf16[104,256]{1,0:T(8,128)(2,1)S(1)}, bf16[104,256]{1,0:T(8,128)(2,1)S(1)}, u32[]{:S(2)}, u32[]{:S(2)}) collective-permute-start(bf16[104,256]{1,0:T(8,128)(2,1)S(1)} %get-tuple-element.33.refs_0_), channel_id=1, source_target_pairs={{0,96},{32,0},{64,32},{96,64},{1,97},{33,1},{65,33},{97,65},{2,98}... | collective-permute-start | bytes 159752 | tf_op jit(solution)/shard_map/ppermute | solution.py:374
  19.4 8.0 %collective-permute-start.3 = (bf16[416,256]{1,0:T(8,128)(2,1)S(1)}, bf16[416,256]{1,0:T(8,128)(2,1)S(1)}, u32[]{:S(2)}, u32[]{:S(2)}) collective-permute-start(bf16[416,256]{1,0:T(8,128)(2,1)S(1)} %shard_map.69.refs_0_), channel_id=1, source_target_pairs={{0,1},{1,2},{2,3},{3,0},{4,5},{5,6},{6,7},{7,4},{8,9},{9,10},{10,1... | collective-permute-start | bytes 638984 | tf_op jit(solution)/shard_map/ppermute | solution.py:374
  21.1 9.3 %collective-permute-start.4 = (bf16[416,256]{1,0:T(8,128)(2,1)S(1)}, bf16[416,256]{1,0:T(8,128)(2,1)S(1)}, u32[]{:S(2)}, u32[]{:S(2)}) collective-permute-start(bf16[416,256]{1,0:T(8,128)(2,1)S(1)} %shard_map.69.refs_0_), channel_id=1, source_target_pairs={{0,2},{1,3},{2,0},{3,1},{4,6},{5,7},{6,4},{7,5},{8,10},{9,11},{10,... | collective-permute-start | bytes 638984 | tf_op jit(solution)/shard_map/ppermute | solution.py:374
  22.0 9.9 %collective-permute-start.5 = (bf16[416,256]{1,0:T(8,128)(2,1)S(1)}, bf16[416,256]{1,0:T(8,128)(2,1)S(1)}, u32[]{:S(2)}, u32[]{:S(2)}) collective-permute-start(bf16[416,256]{1,0:T(8,128)(2,1)S(1)} %shard_map.69.refs_0_), channel_id=1, source_target_pairs={{0,3},{1,0},{2,1},{3,2},{4,7},{5,4},{6,5},{7,6},{8,11},{9,8},{10,9... | collective-permute-start | bytes 638984 | tf_op jit(solution)/shard_map/ppermute | solution.py:374
  34.8 3.1 %copy-start.1 = (bf16[8,200,256]{2,1,0:T(8,128)(2,1)}, bf16[8,200,256]{2,1,0:T(8,128)(2,1)S(1)}, u32[]{:S(2)}) copy-start(bf16[8,200,256]{2,1,0:T(8,128)(2,1)S(1)} %all-to-all-done.refs_4_.refs_6_) | copy-start | bytes 2457604
  37.9 83.2 %copy-start = (f32[1536,768]{1,0:T(8,128)}, f32[1536,768]{1,0:T(8,128)S(1)}, u32[]{:S(2)}) copy-start(f32[1536,768]{1,0:T(8,128)S(1)} %get-tuple-element.37.plan_ref.refs_4_) | copy-start | bytes 14155780
  37.9 83.2 %copy-start.2 = (bf16[1536,256]{1,0:T(8,128)(2,1)}, bf16[1536,256]{1,0:T(8,128)(2,1)S(1)}, u32[]{:S(2)}) copy-start(bf16[1536,256]{1,0:T(8,128)(2,1)S(1)} %get-tuple-element.48.refs_6_.refs_5_) | copy-start | bytes 2359300
  124.5 9.6 %collective-permute-start.6 = (bf16[768,256]{1,0:T(8,128)(2,1)S(1)}, bf16[768,256]{1,0:T(8,128)(2,1)S(1)}, u32[]{:S(2)}, u32[]{:S(2)}) collective-permute-start(bf16[768,256]{1,0:T(8,128)(2,1)S(1)} %get-tuple-element.54), channel_id=1, source_target_pairs={{0,4},{4,0},{8,12},{12,8},{16,20},{20,16},{24,28},{28,24},{1,5},{5... | collective-permute-start | bytes 1179656 | tf_op jit(solution)/shard_map/ppermute | solution.py:377
  125.2 11.3 %all-to-all-start.8 = ((f32[8,8,128]{2,1,0:T(8,128)}), f32[8,8,128]{2,1,0:T(8,128)S(1)}, u32[]{:S(2)}, u32[]{:S(2)}) async-start(f32[8,8,128]{2,1,0:T(8,128)} %get-tuple-element.51), calls=%async_computation.8 | async-start | bytes 65536 | tf_op jit(solution)/shard_map/all_to_all | solution.py:370
  134.2 8.9 %collective-permute-start.7 = (bf16[384,256]{1,0:T(8,128)(2,1)S(1)}, bf16[384,256]{1,0:T(8,128)(2,1)S(1)}, u32[]{:S(2)}, u32[]{:S(2)}) collective-permute-start(bf16[384,256]{1,0:T(8,128)(2,1)S(1)} %get-tuple-element.57), channel_id=1, source_target_pairs={{0,8},{4,12},{8,0},{12,4},{16,24},{20,28},{24,16},{28,20},{1,9},{5... | collective-permute-start | bytes 589832 | tf_op jit(solution)/shard_map/ppermute | solution.py:377
  143.1 15.5 %all-to-all-start.9 = ((bf16[16,96,256]{2,1,0:T(8,128)(2,1)}), bf16[16,96,256]{2,1,0:T(8,128)(2,1)S(1)}, u32[]{:S(2)}, u32[]{:S(2)}) async-start(bf16[16,96,256]{2,1,0:T(8,128)(2,1)} %get-tuple-element.58), calls=%async_computation.9 | async-start | bytes 1572864 | tf_op jit(solution)/shard_map/all_to_all | solution.py:370
  149.2 8.6 %collective-permute-start.8 = (bf16[192,256]{1,0:T(8,128)(2,1)S(1)}, bf16[192,256]{1,0:T(8,128)(2,1)S(1)}, u32[]{:S(2)}, u32[]{:S(2)}) collective-permute-start(bf16[192,256]{1,0:T(8,128)(2,1)S(1)} %get-tuple-element.61), channel_id=1, source_target_pairs={{0,16},{4,20},{8,24},{12,28},{16,0},{20,4},{24,8},{28,12},{1,17},{... | collective-permute-start | bytes 294920 | tf_op jit(solution)/shard_map/ppermute | solution.py:377

commit v8 on v7

--- a/solution.py
+++ b/solution.py
@@ -113,7 +113,7 @@
 def build(own, width, isrc, jsrc, *refs):
     steps = isrc // GROUP
     pi_refs, pj_ref = refs[:steps], refs[steps]
-    plan_ref, inner_ref, xi_ref, w_ref, mass_ref, col_ref, xj_ref, gj_ref = refs[steps + 1 :]
+    plan_ref, inner_ref, xi_ref, w_ref, mass_ref, col_ref, bias_ref, xj_ref, gj_ref = refs[steps + 1 :]
     cols = jsrc * own
     size = own + AUX
     scale = 1.0 / (2.0 * width * EPS)
@@ -127,6 +127,9 @@
         pot = to_col(pj_ref[k, 2 * own : 2 * own + AUX, :].astype(F32)[0:1, 0:LANES], own)
         bias.append(pot / EPS - sq * scale)
     jbias = lanes_of(jnp.concatenate(bias, axis=0))
+    bias_ref[isrc : isrc + 8, :] = jnp.zeros((8, LANES), F32)
+    for k in range(cols // LANES):
+        bias_ref[isrc + k : isrc + k + 1, :] = jbias[:, k * LANES : (k + 1) * LANES]
     xj = xj_ref[...]
     gj = gj_ref[...]
     span = GROUP * own
@@ -146,6 +149,9 @@
             sq = jnp.sum(pf * pf, axis=1, keepdims=True)
             ibias.append(to_col(aux[0:1, 0:LANES], own) / EPS - sq * scale)
         ibias = jnp.concatenate(ibias, axis=0)
+        lines = slots_of(ibias, own, GROUP)
+        for k in range(GROUP):
+            bias_ref[pl.ds(first + k, 1), :] = lines[k : k + 1]
         part = xi_ref[pl.ds(base, span), :]
         cross = lax.dot_general(part, xj, NT, preferred_element_type=F32)
         plan = jnp.exp(cross * (2.0 * scale) + jbias + ibias)
@@ -292,29 +298,24 @@
 
 
 def finish_rows(own, width, isrc, every, *refs):
-    got_ref, col_ref, phi_ref, psi_ref, plan_hbm, xi_hbm, pj_hbm, after_ref = refs[:8]
-    row_hbm, gw_ref, delta_ref, row_ref, plan_ref, xi_ref, xj_ref, gj_ref, sem, out_sem = refs[8:]
+    got_ref, col_ref, phi_ref, psi_ref, bias_ref, xi_hbm, pj_ref, after_ref = refs[:8]
+    row_hbm, gw_ref, delta_ref, row_ref, xi_ref, xj_ref, gj_ref, sem, out_sem = refs[8:]
+    jsrc = pj_ref.shape[0]
     span = GROUP * own
-    steps = isrc // GROUP
-    jsrc = pj_hbm.shape[0]
-    head = []
+    parts = []
+    for t in range(isrc // GROUP):
+        at = pl.ds(t * span, span)
+        parts.append(pltpu.make_async_copy(xi_hbm.at[at], xi_ref.at[at], sem.at[t]))
+        parts[t].start()
     for k in range(jsrc):
-        place = pl.ds(k * own, own)
-        for n, ref in enumerate((gj_ref, xj_ref)):
-            first = own if n == 0 else 0
-            head.append(pltpu.make_async_copy(pj_hbm.at[k, pl.ds(first, own)], ref.at[place], sem.at[2 * steps + 2 * k + n]))
-    parts = []
-    for t in range(steps):
-        at = pl.ds(t * span, span)
-        pairs = ((xi_hbm, xi_ref), (plan_hbm, plan_ref))
-        parts.append([pltpu.make_async_copy(a.at[at], b.at[at], sem.at[2 * t + n]) for n, (a, b) in enumerate(pairs)])
-    for copy in head + parts[0] + parts[1]:
-        copy.start()
+        xj_ref[k * own : (k + 1) * own, :] = pj_ref[k, 0:own, :]
+        gj_ref[k * own : (k + 1) * own, :] = pj_ref[k, own : 2 * own, :]
     total = jnp.sum(got_ref[...], axis=0)
-    cols = plan_ref.shape[1]
+    cols = jsrc * own
     psi = -(col_ref[8:16] + total) / col_ref[0:8]
     delta = row_of(psi - psi_ref[...], cols // LANES)
     psi = row_of(psi, cols // LANES)
+    jbias = row_of(bias_ref[isrc:], cols // LANES)
     rows = lax.broadcasted_iota(jnp.int32, (own, cols), 0)
     lanes = lax.broadcasted_iota(jnp.int32, (own, cols), 1)
     first = lax.axis_index("z") * own
@@ -323,26 +324,23 @@
     wphi = jnp.sum(total[7:8], axis=1, keepdims=True)
     gw_ref[...] = -(every / wsum) * (phi_ref[...] - wphi / wsum)
     scale = 1.0 / (width * EPS)
-    outs = []
-    for copy in head:
-        copy.wait()
     xj = xj_ref[...]
     gj = gj_ref[...]
-    for t in range(steps):
-        at = slice(t * span, (t + 1) * span)
-        col = column_of(phi_ref[t * GROUP : (t + 1) * GROUP, :], own, GROUP)
-        for copy in parts[t]:
-            copy.wait()
-        if t + 2 < steps:
-            for copy in parts[t + 2]:
-                copy.start()
-        plan = plan_ref[at, :]
-        inner = lax.dot_general(xi_ref[at, :], gj, NT, preferred_element_type=F32)
+    outs = []
+    for t in range(isrc // GROUP):
+        group = slice(t * GROUP, (t + 1) * GROUP)
+        col = column_of(phi_ref[group, :], own, GROUP)
+        ibias = column_of(bias_ref[group, :], own, GROUP)
+        parts[t].wait()
+        part = xi_ref[t * span : (t + 1) * span, :]
+        cross = lax.dot_general(part, xj, NT, preferred_element_type=F32)
+        plan = jnp.exp(cross * scale + jbias + ibias)
+        inner = lax.dot_general(part, gj, NT, preferred_element_type=F32)
         mixed = plan * (inner + (col + psi))
         qrow = jnp.sum(mixed, axis=1, keepdims=True)
         base = jnp.dot(plan.astype(BF16), gj, preferred_element_type=F32)
         term = jnp.dot(mixed.astype(BF16), xj, preferred_element_type=F32)
-        term = base + (term - qrow * xi_ref[at, :].astype(F32)) * scale
+        term = base + (term - qrow * part.astype(F32)) * scale
         term = term.astype(BF16)
         for k in range(GROUP):
             row_ref[t * GROUP + k] = term[k * own : (k + 1) * own]
@@ -419,7 +417,7 @@
         functools.partial(stack, own, xsrc), 1, [((xsrc * (own + AUX), width), BF16)], ipack, *near
     )
     igot = [line] + [shift(line, "y", k) for k in range(1, ysrc)]
-    plan, inner, xi, wts, send, col_part = call(
+    plan, inner, xi, wts, send, col_part, bias = call(
         functools.partial(build, own, width, isrc, jsrc),
         5,
         [
@@ -429,6 +427,7 @@
             ((isrc, LANES), F32),
             ((isrc, 2 * isrc, LANES), F32),
             ((16, LANES), F32),
+            ((isrc + 8, LANES), F32),
         ],
         *igot,
         jgot,
@@ -510,18 +509,19 @@
         col,
         phi,
         *kept,
-        *[pltpu.with_memory_space_constraint(v, pltpu.HBM) for v in (plan, xi, jgot)],
+        bias,
+        pltpu.with_memory_space_constraint(xi, pltpu.HBM),
+        jgot,
         keep,
         scratch=[
             pltpu.VMEM((isrc, own, width), BF16),
-            pltpu.VMEM((rows, cols), F32),
             pltpu.VMEM((rows, width), BF16),
             pltpu.VMEM((cols, width), BF16),
             pltpu.VMEM((cols, width), BF16),
-            pltpu.SemaphoreType.DMA((2 * (isrc // GROUP) + 2 * jsrc,)),
+            pltpu.SemaphoreType.DMA((isrc // GROUP,)),
             pltpu.SemaphoreType.DMA((isrc // GROUP,)),
         ],
-        in_specs=whole(4) + [anywhere] * 3 + whole(1),
+        in_specs=whole(5) + [anywhere] + whole(2),
         out_specs=[anywhere] + whole(2),
         hbm=(0,),
         mib=24,

time: 161 us -> 161 us (level)
  transfers between devices with their start and end apart: 12 -> 12, of which waited for: 12 -> 12; matrix products, arithmetic and copies ran while one was open for 0% -> 0% of each run, Pallas kernels for 4% -> 3%
where the time goes in v8:
time: 161 us; the launch traced here: 159 us
  blocking collectives  79.9 us (50%)
  starting transfers between devices  31.2 us (19%)
  waiting for transfers between devices  29 us (18%)
  Pallas kernels  18.1 us (11%)
    all_to_all x7, blocking collectives, swap(): return lax.all_to_all(value, axes, 0, 0, tiled=True)  79.9 us
    pallas_call x14, Pallas kernels, call(): pl.pallas_call(body, out_shape=[(pltpu.HBM if n in hbm else jax.ShapeDtyp...  18.1 us
    all_to_all x3, starting transfers between devices, swap(): return lax.all_to_all(value, axes, 0, 0, tiled=True)  17.9 us
    ppermute x3, waiting for transfers between devices, flip(): return lax.ppermute(value, 'z', [(i, i ^ bit) for i in range(jsrc)])  12.9 us
    ppermute x6, starting transfers between devices, shift(): return lax.ppermute(value, axis, [(i, (i + k) % n) for i in range(n)])  10.7 us
    ppermute x6, waiting for transfers between devices, shift(): return lax.ppermute(value, axis, [(i, (i + k) % n) for i in range(n)])  10.1 us
    all_to_all x3, waiting for transfers between devices, swap(): return lax.all_to_all(value, axes, 0, 0, tiled=True)  5.97 us
  transfers between devices with their start and end apart: 12, of which 12 were waited for; matrix products, arithmetic and copies ran while one was open for 0% of the time, Pallas kernels for 3%

profile of v8, /device:TPU:8, one launch (start us, length us, event | category | flops | bytes accessed | tf_op | source)
XLA Modules:
  0.0 159.5 jit_solution(2127097087699690994)
XLA Ops:
  0.6 1.9 %shard_map.68 = (bf16[104,256]{1,0:T(8,128)(2,1)S(1)}, bf16[8,200,256]{2,1,0:T(8,128)(2,1)}) custom-call(bf16[96,256]{1,0:T(8,128)(2,1)} %x_ref.1, bf16[96,256]{1,0:T(8,128)(2,1)} %gy_ref.1, bf16[1,96]{1,0:T(2,128)(2,1)} %bitcast.5, bf16[1,96]{1,0:T(2,128)(2,1)} %bitcast.6, bf16[1,96]{1,0:T(2,128)(2,1)} %bitcast.7), custom_call_target="tpu_custom_call" | custom-call | flops 2000000000 | bytes 1024 | tf_op jit(solution)/shard_map/pallas_call | solution.py:378
  2.5 8.5 %all-to-all-start = ((bf16[8,200,256]{2,1,0:T(8,128)(2,1)}), bf16[8,200,256]{2,1,0:T(8,128)(2,1)S(1)}, u32[]{:S(2)}, u32[]{:S(2)}) async-start(bf16[8,200,256]{2,1,0:T(8,128)(2,1)} %get-tuple-element.35), calls=%async_computation | async-start | bytes 1638400 | tf_op jit(solution)/shard_map/all_to_all | solution.py:368
  11.0 1.5 collective-permute-start
  12.5 2.7 %collective-permute-start.1 = (bf16[104,256]{1,0:T(8,128)(2,1)S(1)}, bf16[104,256]{1,0:T(8,128)(2,1)S(1)}, u32[]{:S(2)}, u32[]{:S(2)}) collective-permute-start(bf16[104,256]{1,0:T(8,128)(2,1)S(1)} %get-tuple-element.34.refs_0_), channel_id=1, source_target_pairs={{0,64},{32,96},{64,0},{96,32},{1,65},{33,97},{65,1},{97,33},{2,66}... | collective-permute-start | bytes 159752 | tf_op jit(solution)/shard_map/ppermute | solution.py:372
  15.2 1.4 collective-permute-start.2
  16.7 0.3 collective-permute-done.refs_1_
  16.9 1.2 collective-permute-done.1.refs_2_
  18.1 1.2 collective-permute-done.2.refs_3_
  19.4 1.7 %collective-permute-start.3 = (bf16[416,256]{1,0:T(8,128)(2,1)S(1)}, bf16[416,256]{1,0:T(8,128)(2,1)S(1)}, u32[]{:S(2)}, u32[]{:S(2)}) collective-permute-start(bf16[416,256]{1,0:T(8,128)(2,1)S(1)} %shard_map.69.refs_0_), channel_id=1, source_target_pairs={{0,1},{1,2},{2,3},{3,0},{4,5},{5,6},{6,7},{7,4},{8,9},{9,10},{10,1... | collective-permute-start | bytes 638984 | tf_op jit(solution)/shard_map/ppermute | solution.py:372
  21.1 0.9 collective-permute-start.4
  22.0 2.4 %collective-permute-start.5 = (bf16[416,256]{1,0:T(8,128)(2,1)S(1)}, bf16[416,256]{1,0:T(8,128)(2,1)S(1)}, u32[]{:S(2)}, u32[]{:S(2)}) collective-permute-start(bf16[416,256]{1,0:T(8,128)(2,1)S(1)} %shard_map.69.refs_0_), channel_id=1, source_target_pairs={{0,3},{1,0},{2,1},{3,2},{4,7},{5,4},{6,5},{7,6},{8,11},{9,8},{10,9... | collective-permute-start | bytes 638984 | tf_op jit(solution)/shard_map/ppermute | solution.py:372
  24.4 3.0 %collective-permute-done.3.refs_1_ = bf16[416,256]{1,0:T(8,128)(2,1)S(1)} collective-permute-done((bf16[416,256]{1,0:T(8,128)(2,1)S(1)}, bf16[416,256]{1,0:T(8,128)(2,1)S(1)}, u32[]{:S(2)}, u32[]{:S(2)}) %collective-permute-start.3) | collective-permute-done | bytes 213024 | tf_op jit(solution)/shard_map/ppermute | solution.py:372
  27.4 2.9 %collective-permute-done.4.refs_2_ = bf16[416,256]{1,0:T(8,128)(2,1)S(1)} collective-permute-done((bf16[416,256]{1,0:T(8,128)(2,1)S(1)}, bf16[416,256]{1,0:T(8,128)(2,1)S(1)}, u32[]{:S(2)}, u32[]{:S(2)}) %collective-permute-start.4) | collective-permute-done | bytes 213024 | tf_op jit(solution)/shard_map/ppermute | solution.py:372
  30.4 1.5 collective-permute-done.5.refs_3_
  31.9 3.0 %all-to-all-done.refs_4_.refs_6_ = bf16[8,200,256]{2,1,0:T(8,128)(2,1)S(1)} async-done(((bf16[8,200,256]{2,1,0:T(8,128)(2,1)}), bf16[8,200,256]{2,1,0:T(8,128)(2,1)S(1)}, u32[]{:S(2)}, u32[]{:S(2)}) %all-to-all-start) | async-done | bytes 819232 | tf_op jit(solution)/shard_map/all_to_all | solution.py:368
  34.8 3.2 %shard_map.70 = (f32[1536,768]{1,0:T(8,128)S(1)}, f32[1536,768]{1,0:T(8,128)S(1)}, bf16[1536,256]{1,0:T(8,128)(2,1)S(1)}, f32[16,128]{1,0:T(8,128)S(1)}, f32[16,...) custom-call(bf16[416,256]{1,0:T(8,128)(2,1)S(1)} %shard_map.69.refs_0_, ...), custom_call_target="tpu_custom_call" | custom-call | flops 5000000000 | bytes 1024 | tf_op jit(solution)/shard_map/pallas_call | solution.py:378
  38.1 0.0 copy-start
  38.1 14.2 %all_to_all.50.got_ref = f32[16,32,128]{2,1,0:T(8,128)S(1)} all-to-all(f32[16,32,128]{2,1,0:T(8,128)S(1)} %get-tuple-element.36), channel_id=1, replica_groups=mesh['filt'=2,'row'=4,'z'=8,'y'=4] {'y','row'}, dimensions={0} | all-to-all | bytes 524288 | tf_op jit(solution)/shard_map/all_to_all | solution.py:368
  52.3 0.7 shard_map.71
  52.9 11.5 %all_to_all.51.got_ref = f32[8,24,128]{2,1,0:T(8,128)S(1)} all-to-all(f32[8,24,128]{2,1,0:T(8,128)S(1)} %get-tuple-element.39), channel_id=1, replica_groups=mesh['filt'=2,'row'=4,'z'=8,'y'=4] {'z'}, dimensions={0} | all-to-all | bytes 196608 | tf_op jit(solution)/shard_map/all_to_all | solution.py:368
  64.4 0.4 shard_map.72
  64.8 11.4 %all_to_all.52.got_ref = f32[16,16,128]{2,1,0:T(8,128)S(1)} all-to-all(f32[16,16,128]{2,1,0:T(8,128)S(1)} %get-tuple-element.40), channel_id=1, replica_groups=mesh['filt'=2,'row'=4,'z'=8,'y'=4] {'y','row'}, dimensions={0} | all-to-all | bytes 262144 | tf_op jit(solution)/shard_map/all_to_all | solution.py:368
  76.2 0.7 shard_map.73
  76.9 10.4 %all_to_all.53.got_ref = f32[8,8,128]{2,1,0:T(8,128)S(1)} all-to-all(f32[8,8,128]{2,1,0:T(8,128)S(1)} %get-tuple-element.43), channel_id=1, replica_groups=mesh['filt'=2,'row'=4,'z'=8,'y'=4] {'z'}, dimensions={0} | all-to-all | bytes 65536 | tf_op jit(solution)/shard_map/all_to_all | solution.py:368
  87.2 0.4 shard_map.74
  87.7 11.1 %all_to_all.54.got_ref = f32[16,16,128]{2,1,0:T(8,128)S(1)} all-to-all(f32[16,16,128]{2,1,0:T(8,128)S(1)} %shard_map.74), channel_id=1, replica_groups=mesh['filt'=2,'row'=4,'z'=8,'y'=4] {'y','row'}, dimensions={0} | all-to-all | bytes 262144 | tf_op jit(solution)/shard_map/all_to_all | solution.py:368
  98.7 0.7 shard_map.75
  99.4 10.4 %all_to_all.55.got_ref = f32[8,8,128]{2,1,0:T(8,128)S(1)} all-to-all(f32[8,8,128]{2,1,0:T(8,128)S(1)} %get-tuple-element.45), channel_id=1, replica_groups=mesh['filt'=2,'row'=4,'z'=8,'y'=4] {'z'}, dimensions={0} | all-to-all | bytes 65536 | tf_op jit(solution)/shard_map/all_to_all | solution.py:368
  109.8 0.4 shard_map.76
  110.2 11.1 %all_to_all.56.refs_0_ = f32[16,16,128]{2,1,0:T(8,128)S(1)} all-to-all(f32[16,16,128]{2,1,0:T(8,128)S(1)} %get-tuple-element.46), channel_id=1, replica_groups=mesh['filt'=2,'row'=4,'z'=8,'y'=4] {'y','row'}, dimensions={0} | all-to-all | bytes 262144 | tf_op jit(solution)/shard_map/all_to_all | solution.py:368
  121.3 0.0 copy-done
  121.3 3.4 %shard_map.77 = (f32[16,128]{1,0:T(8,128)S(1)}, f32[8,8,128]{2,1,0:T(8,128)}, f32[768,256]{1,0:T(8,128)S(1)}, bf16[768,256]{1,0:T(8,128)(2,1)S(1)}) custom-call(f32[16,16,128]{2,1,0:T(8,128)S(1)} %all_to_all.56.refs_0_, f32[32,128]{1,0:T(8,128)S(1)} %get-tuple-element.41.mass_ref.refs_1_, f32[16,128]{1,0:T(8,128)S(1)} %get-tuple-element.42.w_ref.refs_2_, ...), custom_call_target="tpu_custom_call" | custom-call | flops 4000000000 | bytes 1024 | tf_op jit(solution)/shard_map/pallas_call | solution.py:378
  124.6 0.7 collective-permute-start.6
  125.3 3.3 %all-to-all-start.8 = ((f32[8,8,128]{2,1,0:T(8,128)}), f32[8,8,128]{2,1,0:T(8,128)S(1)}, u32[]{:S(2)}, u32[]{:S(2)}) async-start(f32[8,8,128]{2,1,0:T(8,128)} %get-tuple-element.52), calls=%async_computation.8 | async-start | bytes 65536 | tf_op jit(solution)/shard_map/all_to_all | solution.py:368
  128.7 5.6 %collective-permute-done.6.got_ref = bf16[768,256]{1,0:T(8,128)(2,1)S(1)} collective-permute-done((bf16[768,256]{1,0:T(8,128)(2,1)S(1)}, bf16[768,256]{1,0:T(8,128)(2,1)S(1)}, u32[]{:S(2)}, u32[]{:S(2)}) %collective-permute-start.6) | collective-permute-done | bytes 393248 | tf_op jit(solution)/shard_map/ppermute | solution.py:375
  134.2 0.1 shard_map.78
  134.3 0.1 collective-permute-start.7
  134.4 2.2 %all-to-all-done.8.refs_0_ = f32[8,8,128]{2,1,0:T(8,128)S(1)} async-done(((f32[8,8,128]{2,1,0:T(8,128)}), f32[8,8,128]{2,1,0:T(8,128)S(1)}, u32[]{:S(2)}, u32[]{:S(2)}) %all-to-all-start.8) | async-done | bytes 32800 | tf_op jit(solution)/shard_map/all_to_all | solution.py:368
  136.6 5.5 %shard_map.79 = (bf16[16,96,256]{2,1,0:T(8,128)(2,1)}, f32[16,128]{1,0:T(8,128)S(1)}, f32[96,1]{1,0:T(8,128)S(1)}) custom-call(f32[8,8,128]{2,1,0:T(8,128)S(1)} %all-to-all-done.8.refs_0_, f32[16,128]{1,0:T(8,128)S(1)} %get-tuple-element.44.col_ref.refs_1_, f32[16,128]{1,0:T(8,128)S(1)} %get-tuple-element.53.refs_2_, ...), custom_call_target="tpu_custom_call" | custom-call | flops 4000000000 | bytes 1024 | tf_op jit(solution)/shard_map/pallas_call | solution.py:378
  142.1 1.1 collective-permute-done.7.got_ref
  143.2 6.1 %all-to-all-start.9 = ((bf16[16,96,256]{2,1,0:T(8,128)(2,1)}), bf16[16,96,256]{2,1,0:T(8,128)(2,1)S(1)}, u32[]{:S(2)}, u32[]{:S(2)}) async-start(bf16[16,96,256]{2,1,0:T(8,128)(2,1)} %get-tuple-element.60), calls=%async_computation.9 | async-start | bytes 1572864 | tf_op jit(solution)/shard_map/all_to_all | solution.py:368
  149.3 1.9 %collective-permute-start.8 = (bf16[192,256]{1,0:T(8,128)(2,1)S(1)}, bf16[192,256]{1,0:T(8,128)(2,1)S(1)}, u32[]{:S(2)}, u32[]{:S(2)}) collective-permute-start(bf16[192,256]{1,0:T(8,128)(2,1)S(1)} %get-tuple-element.63), channel_id=1, source_target_pairs={{0,16},{4,20},{8,24},{12,28},{16,0},{20,4},{24,8},{28,12},{1,17},{... | collective-permute-start | bytes 294920 | tf_op jit(solution)/shard_map/ppermute | solution.py:375
  151.2 0.5 dynamic-slice_bitcast_fusion
  151.8 6.2 %collective-permute-done.8.got_ref = bf16[192,256]{1,0:T(8,128)(2,1)S(1)} collective-permute-done((bf16[192,256]{1,0:T(8,128)(2,1)S(1)}, bf16[192,256]{1,0:T(8,128)(2,1)S(1)}, u32[]{:S(2)}, u32[]{:S(2)}) %collective-permute-start.8) | collective-permute-done | bytes 98336 | tf_op jit(solution)/shard_map/ppermute | solution.py:375
  157.9 0.8 all-to-all-done.9.rows_ref
  158.7 0.8 shard_map.81
  (2 shorter events, 0.1 us)
Async XLA Ops:
  2.5 32.3 %all-to-all-start = ((bf16[8,200,256]{2,1,0:T(8,128)(2,1)}), bf16[8,200,256]{2,1,0:T(8,128)(2,1)S(1)}, u32[]{:S(2)}, u32[]{:S(2)}) async-start(bf16[8,200,256]{2,1,0:T(8,128)(2,1)} %get-tuple-element.35), calls=%async_computation | async-start | bytes 1638400 | tf_op jit(solution)/shard_map/all_to_all | solution.py:368
  11.0 5.9 %collective-permute-start = (bf16[104,256]{1,0:T(8,128)(2,1)S(1)}, bf16[104,256]{1,0:T(8,128)(2,1)S(1)}, u32[]{:S(2)}, u32[]{:S(2)}) collective-permute-start(bf16[104,256]{1,0:T(8,128)(2,1)S(1)} %get-tuple-element.34.refs_0_), channel_id=1, source_target_pairs={{0,32},{32,64},{64,96},{96,0},{1,33},{33,65},{65,97},{97,1},{2,34}... | collective-permute-start | bytes 159752 | tf_op jit(solution)/shard_map/ppermute | solution.py:372
  12.5 5.6 %collective-permute-start.1 = (bf16[104,256]{1,0:T(8,128)(2,1)S(1)}, bf16[104,256]{1,0:T(8,128)(2,1)S(1)}, u32[]{:S(2)}, u32[]{:S(2)}) collective-permute-start(bf16[104,256]{1,0:T(8,128)(2,1)S(1)} %get-tuple-element.34.refs_0_), channel_id=1, source_target_pairs={{0,64},{32,96},{64,0},{96,32},{1,65},{33,97},{65,1},{97,33},{2,66}... | collective-permute-start | bytes 159752 | tf_op jit(solution)/shard_map/ppermute | solution.py:372
  15.2 4.1 %collective-permute-start.2 = (bf16[104,256]{1,0:T(8,128)(2,1)S(1)}, bf16[104,256]{1,0:T(8,128)(2,1)S(1)}, u32[]{:S(2)}, u32[]{:S(2)}) collective-permute-start(bf16[104,256]{1,0:T(8,128)(2,1)S(1)} %get-tuple-element.34.refs_0_), channel_id=1, source_target_pairs={{0,96},{32,0},{64,32},{96,64},{1,97},{33,1},{65,33},{97,65},{2,98}... | collective-permute-start | bytes 159752 | tf_op jit(solution)/shard_map/ppermute | solution.py:372
  19.4 8.0 %collective-permute-start.3 = (bf16[416,256]{1,0:T(8,128)(2,1)S(1)}, bf16[416,256]{1,0:T(8,128)(2,1)S(1)}, u32[]{:S(2)}, u32[]{:S(2)}) collective-permute-start(bf16[416,256]{1,0:T(8,128)(2,1)S(1)} %shard_map.69.refs_0_), channel_id=1, source_target_pairs={{0,1},{1,2},{2,3},{3,0},{4,5},{5,6},{6,7},{7,4},{8,9},{9,10},{10,1... | collective-permute-start | bytes 638984 | tf_op jit(solution)/shard_map/ppermute | solution.py:372
  21.1 9.3 %collective-permute-start.4 = (bf16[416,256]{1,0:T(8,128)(2,1)S(1)}, bf16[416,256]{1,0:T(8,128)(2,1)S(1)}, u32[]{:S(2)}, u32[]{:S(2)}) collective-permute-start(bf16[416,256]{1,0:T(8,128)(2,1)S(1)} %shard_map.69.refs_0_), channel_id=1, source_target_pairs={{0,2},{1,3},{2,0},{3,1},{4,6},{5,7},{6,4},{7,5},{8,10},{9,11},{10,... | collective-permute-start | bytes 638984 | tf_op jit(solution)/shard_map/ppermute | solution.py:372
  22.0 9.9 %collective-permute-start.5 = (bf16[416,256]{1,0:T(8,128)(2,1)S(1)}, bf16[416,256]{1,0:T(8,128)(2,1)S(1)}, u32[]{:S(2)}, u32[]{:S(2)}) collective-permute-start(bf16[416,256]{1,0:T(8,128)(2,1)S(1)} %shard_map.69.refs_0_), channel_id=1, source_target_pairs={{0,3},{1,0},{2,1},{3,2},{4,7},{5,4},{6,5},{7,6},{8,11},{9,8},{10,9... | collective-permute-start | bytes 638984 | tf_op jit(solution)/shard_map/ppermute | solution.py:372
  38.1 83.2 %copy-start = (bf16[1536,256]{1,0:T(8,128)(2,1)}, bf16[1536,256]{1,0:T(8,128)(2,1)S(1)}, u32[]{:S(2)}) copy-start(bf16[1536,256]{1,0:T(8,128)(2,1)S(1)} %get-tuple-element.49.refs_6_.refs_5_) | copy-start | bytes 2359300
  124.6 9.6 %collective-permute-start.6 = (bf16[768,256]{1,0:T(8,128)(2,1)S(1)}, bf16[768,256]{1,0:T(8,128)(2,1)S(1)}, u32[]{:S(2)}, u32[]{:S(2)}) collective-permute-start(bf16[768,256]{1,0:T(8,128)(2,1)S(1)} %get-tuple-element.56), channel_id=1, source_target_pairs={{0,4},{4,0},{8,12},{12,8},{16,20},{20,16},{24,28},{28,24},{1,5},{5... | collective-permute-start | bytes 1179656 | tf_op jit(solution)/shard_map/ppermute | solution.py:375
  125.3 11.3 %all-to-all-start.8 = ((f32[8,8,128]{2,1,0:T(8,128)}), f32[8,8,128]{2,1,0:T(8,128)S(1)}, u32[]{:S(2)}, u32[]{:S(2)}) async-start(f32[8,8,128]{2,1,0:T(8,128)} %get-tuple-element.52), calls=%async_computation.8 | async-start | bytes 65536 | tf_op jit(solution)/shard_map/all_to_all | solution.py:368
  134.3 8.9 %collective-permute-start.7 = (bf16[384,256]{1,0:T(8,128)(2,1)S(1)}, bf16[384,256]{1,0:T(8,128)(2,1)S(1)}, u32[]{:S(2)}, u32[]{:S(2)}) collective-permute-start(bf16[384,256]{1,0:T(8,128)(2,1)S(1)} %get-tuple-element.59), channel_id=1, source_target_pairs={{0,8},{4,12},{8,0},{12,4},{16,24},{20,28},{24,16},{28,20},{1,9},{5... | collective-permute-start | bytes 589832 | tf_op jit(solution)/shard_map/ppermute | solution.py:375
  143.2 15.5 %all-to-all-start.9 = ((bf16[16,96,256]{2,1,0:T(8,128)(2,1)}), bf16[16,96,256]{2,1,0:T(8,128)(2,1)S(1)}, u32[]{:S(2)}, u32[]{:S(2)}) async-start(bf16[16,96,256]{2,1,0:T(8,128)(2,1)} %get-tuple-element.60), calls=%async_computation.9 | async-start | bytes 1572864 | tf_op jit(solution)/shard_map/all_to_all | solution.py:368
  149.3 8.6 %collective-permute-start.8 = (bf16[192,256]{1,0:T(8,128)(2,1)S(1)}, bf16[192,256]{1,0:T(8,128)(2,1)S(1)}, u32[]{:S(2)}, u32[]{:S(2)}) collective-permute-start(bf16[192,256]{1,0:T(8,128)(2,1)S(1)} %get-tuple-element.63), channel_id=1, source_target_pairs={{0,16},{4,20},{8,24},{12,28},{16,0},{20,4},{24,8},{28,12},{1,17},{... | collective-permute-start | bytes 294920 | tf_op jit(solution)/shard_map/ppermute | solution.py:375

commit v9 on v8

--- a/solution.py
+++ b/solution.py
@@ -279,7 +279,7 @@
             give = pl.ds(pl.multiple_of(q * cols + (2 * m + 1 - mine) * own, own), own)
             first = q * (cols // 2) + m * own
             at = slice(first, first + own)
-            keep_ref[at, :] = acc_ref[keep, :] * scale
+            keep_ref[at, :] = (acc_ref[keep, :] * scale).astype(BF16)
             give_ref[at, :] = (acc_ref[give, :] * scale).astype(BF16)
     sent.wait()
 
@@ -293,20 +293,15 @@
             give = pl.ds(pl.multiple_of(q * size + (2 * m + 1 - mine) * own, own), own)
             first = q * out + m * own
             at = slice(first, first + own)
-            next_ref[at, :] = keep_ref[keep, :] + got_ref[keep, :].astype(F32)
-            send_ref[at, :] = (keep_ref[give, :] + got_ref[give, :].astype(F32)).astype(BF16)
+            next_ref[at, :] = keep_ref[keep, :].astype(F32) + got_ref[keep, :].astype(F32)
+            send_ref[at, :] = (keep_ref[give, :].astype(F32) + got_ref[give, :].astype(F32)).astype(BF16)
 
 
 def finish_rows(own, width, isrc, every, *refs):
-    got_ref, col_ref, phi_ref, psi_ref, bias_ref, xi_hbm, pj_ref, after_ref = refs[:8]
-    row_hbm, gw_ref, delta_ref, row_ref, xi_ref, xj_ref, gj_ref, sem, out_sem = refs[8:]
+    got_ref, col_ref, phi_ref, psi_ref, bias_ref, xi_ref, pj_ref, after_ref = refs[:8]
+    row_ref, gw_ref, delta_ref, xj_ref, gj_ref = refs[8:]
     jsrc = pj_ref.shape[0]
     span = GROUP * own
-    parts = []
-    for t in range(isrc // GROUP):
-        at = pl.ds(t * span, span)
-        parts.append(pltpu.make_async_copy(xi_hbm.at[at], xi_ref.at[at], sem.at[t]))
-        parts[t].start()
     for k in range(jsrc):
         xj_ref[k * own : (k + 1) * own, :] = pj_ref[k, 0:own, :]
         gj_ref[k * own : (k + 1) * own, :] = pj_ref[k, own : 2 * own, :]
@@ -326,12 +321,10 @@
     scale = 1.0 / (width * EPS)
     xj = xj_ref[...]
     gj = gj_ref[...]
-    outs = []
     for t in range(isrc // GROUP):
         group = slice(t * GROUP, (t + 1) * GROUP)
         col = column_of(phi_ref[group, :], own, GROUP)
         ibias = column_of(bias_ref[group, :], own, GROUP)
-        parts[t].wait()
         part = xi_ref[t * span : (t + 1) * span, :]
         cross = lax.dot_general(part, xj, NT, preferred_element_type=F32)
         plan = jnp.exp(cross * scale + jbias + ibias)
@@ -344,11 +337,6 @@
         term = term.astype(BF16)
         for k in range(GROUP):
             row_ref[t * GROUP + k] = term[k * own : (k + 1) * own]
-        group = pl.ds(t * GROUP, GROUP)
-        outs.append(pltpu.make_async_copy(row_ref.at[group], row_hbm.at[group], out_sem.at[t]))
-        outs[t].start()
-    for copy in outs:
-        copy.wait()
 
 
 def total_up(own, rows_ref, keep_ref, got_ref, delta_ref, out_ref):
@@ -475,7 +463,7 @@
     phi, send, keep, give = call(
         functools.partial(phi_last, own, width, isrc, jsrc),
         4,
-        [((isrc, LANES), F32), ((jsrc, 8, LANES), F32), ((half, width), F32), ((half, width), BF16)],
+        [((isrc, LANES), F32), ((jsrc, 8, LANES), F32), ((half, width), BF16), ((half, width), BF16)],
         got,
         mass,
         wts,
@@ -510,20 +498,13 @@
         phi,
         *kept,
         bias,
-        pltpu.with_memory_space_constraint(xi, pltpu.HBM),
+        xi,
         jgot,
         keep,
         scratch=[
-            pltpu.VMEM((isrc, own, width), BF16),
-            pltpu.VMEM((rows, width), BF16),
             pltpu.VMEM((cols, width), BF16),
             pltpu.VMEM((cols, width), BF16),
-            pltpu.SemaphoreType.DMA((isrc // GROUP,)),
-            pltpu.SemaphoreType.DMA((isrc // GROUP,)),
         ],
-        in_specs=whole(5) + [anywhere] + whole(2),
-        out_specs=[anywhere] + whole(2),
-        hbm=(0,),
         mib=24,
     )
     row_send, taken = lax.optimization_barrier((row_send, taken))

time: 161 us -> 161 us (level)
  waiting for transfers between devices: 29 us -> 31.2 us
    ppermute x3, waiting for transfers between devices: 12.9 us -> 15.1 us  [flip(): return lax.ppermute(value, 'z', [(i, i ^ bit) for i in range(jsrc)])]
where the time goes in v9:
time: 161 us; the launch traced here: 159 us
  blocking collectives  79.9 us (50%)
  waiting for transfers between devices  31.2 us (19%)
  starting transfers between devices  30.3 us (19%)
  Pallas kernels  16.5 us (10%)
    all_to_all x7, blocking collectives, swap(): return lax.all_to_all(value, axes, 0, 0, tiled=True)  79.9 us
    all_to_all x3, starting transfers between devices, swap(): return lax.all_to_all(value, axes, 0, 0, tiled=True)  17 us
    pallas_call x14, Pallas kernels, call(): pl.pallas_call(body, out_shape=[(pltpu.HBM if n in hbm else jax.ShapeDtyp...  16.5 us
    ppermute x3, waiting for transfers between devices, flip(): return lax.ppermute(value, 'z', [(i, i ^ bit) for i in range(jsrc)])  15.1 us
    ppermute x6, starting transfers between devices, shift(): return lax.ppermute(value, axis, [(i, (i + k) % n) for i in range(n)])  10.7 us
    ppermute x6, waiting for transfers between devices, shift(): return lax.ppermute(value, axis, [(i, (i + k) % n) for i in range(n)])  10.1 us
    all_to_all x3, waiting for transfers between devices, swap(): return lax.all_to_all(value, axes, 0, 0, tiled=True)  5.95 us
  transfers between devices with their start and end apart: 12, of which 12 were waited for; matrix products, arithmetic and copies ran while one was open for 0% of the time, Pallas kernels for 3%

profile of v9, /device:TPU:8, one launch (start us, length us, event | category | flops | bytes accessed | tf_op | source)
XLA Modules:
  0.0 159.2 jit_solution(11572776137149608258)
XLA Ops:
  0.6 1.9 %shard_map.68 = (bf16[104,256]{1,0:T(8,128)(2,1)S(1)}, bf16[8,200,256]{2,1,0:T(8,128)(2,1)}) custom-call(bf16[96,256]{1,0:T(8,128)(2,1)} %x_ref.1, bf16[96,256]{1,0:T(8,128)(2,1)} %gy_ref.1, bf16[1,96]{1,0:T(2,128)(2,1)} %bitcast.5, bf16[1,96]{1,0:T(2,128)(2,1)} %bitcast.6, bf16[1,96]{1,0:T(2,128)(2,1)} %bitcast.7), custom_call_target="tpu_custom_call" | custom-call | flops 2000000000 | bytes 1024 | tf_op jit(solution)/shard_map/pallas_call | solution.py:366
  2.5 8.5 %all-to-all-start = ((bf16[8,200,256]{2,1,0:T(8,128)(2,1)}), bf16[8,200,256]{2,1,0:T(8,128)(2,1)S(1)}, u32[]{:S(2)}, u32[]{:S(2)}) async-start(bf16[8,200,256]{2,1,0:T(8,128)(2,1)} %get-tuple-element.35), calls=%async_computation | async-start | bytes 1638400 | tf_op jit(solution)/shard_map/all_to_all | solution.py:356
  11.0 1.5 collective-permute-start
  12.5 2.7 %collective-permute-start.1 = (bf16[104,256]{1,0:T(8,128)(2,1)S(1)}, bf16[104,256]{1,0:T(8,128)(2,1)S(1)}, u32[]{:S(2)}, u32[]{:S(2)}) collective-permute-start(bf16[104,256]{1,0:T(8,128)(2,1)S(1)} %get-tuple-element.34.refs_0_), channel_id=1, source_target_pairs={{0,64},{32,96},{64,0},{96,32},{1,65},{33,97},{65,1},{97,33},{2,66}... | collective-permute-start | bytes 159752 | tf_op jit(solution)/shard_map/ppermute | solution.py:360
  15.2 1.4 collective-permute-start.2
  16.7 0.3 collective-permute-done.refs_1_
  16.9 1.2 collective-permute-done.1.refs_2_
  18.1 1.2 collective-permute-done.2.refs_3_
  19.4 1.7 %collective-permute-start.3 = (bf16[416,256]{1,0:T(8,128)(2,1)S(1)}, bf16[416,256]{1,0:T(8,128)(2,1)S(1)}, u32[]{:S(2)}, u32[]{:S(2)}) collective-permute-start(bf16[416,256]{1,0:T(8,128)(2,1)S(1)} %shard_map.69.refs_0_), channel_id=1, source_target_pairs={{0,1},{1,2},{2,3},{3,0},{4,5},{5,6},{6,7},{7,4},{8,9},{9,10},{10,1... | collective-permute-start | bytes 638984 | tf_op jit(solution)/shard_map/ppermute | solution.py:360
  21.1 0.9 collective-permute-start.4
  22.0 2.4 %collective-permute-start.5 = (bf16[416,256]{1,0:T(8,128)(2,1)S(1)}, bf16[416,256]{1,0:T(8,128)(2,1)S(1)}, u32[]{:S(2)}, u32[]{:S(2)}) collective-permute-start(bf16[416,256]{1,0:T(8,128)(2,1)S(1)} %shard_map.69.refs_0_), channel_id=1, source_target_pairs={{0,3},{1,0},{2,1},{3,2},{4,7},{5,4},{6,5},{7,6},{8,11},{9,8},{10,9... | collective-permute-start | bytes 638984 | tf_op jit(solution)/shard_map/ppermute | solution.py:360
  24.4 3.0 %collective-permute-done.3.refs_1_ = bf16[416,256]{1,0:T(8,128)(2,1)S(1)} collective-permute-done((bf16[416,256]{1,0:T(8,128)(2,1)S(1)}, bf16[416,256]{1,0:T(8,128)(2,1)S(1)}, u32[]{:S(2)}, u32[]{:S(2)}) %collective-permute-start.3) | collective-permute-done | bytes 213024 | tf_op jit(solution)/shard_map/ppermute | solution.py:360
  27.4 2.9 %collective-permute-done.4.refs_2_ = bf16[416,256]{1,0:T(8,128)(2,1)S(1)} collective-permute-done((bf16[416,256]{1,0:T(8,128)(2,1)S(1)}, bf16[416,256]{1,0:T(8,128)(2,1)S(1)}, u32[]{:S(2)}, u32[]{:S(2)}) %collective-permute-start.4) | collective-permute-done | bytes 213024 | tf_op jit(solution)/shard_map/ppermute | solution.py:360
  30.3 1.5 collective-permute-done.5.refs_3_
  31.8 3.0 %all-to-all-done.refs_4_.refs_6_ = bf16[8,200,256]{2,1,0:T(8,128)(2,1)S(1)} async-done(((bf16[8,200,256]{2,1,0:T(8,128)(2,1)}), bf16[8,200,256]{2,1,0:T(8,128)(2,1)S(1)}, u32[]{:S(2)}, u32[]{:S(2)}) %all-to-all-start) | async-done | bytes 819232 | tf_op jit(solution)/shard_map/all_to_all | solution.py:356
  34.8 3.2 %shard_map.70 = (f32[1536,768]{1,0:T(8,128)S(1)}, f32[1536,768]{1,0:T(8,128)S(1)}, bf16[1536,256]{1,0:T(8,128)(2,1)S(1)}, f32[16,128]{1,0:T(8,128)S(1)}, f32[16,...) custom-call(bf16[416,256]{1,0:T(8,128)(2,1)S(1)} %shard_map.69.refs_0_, ...), custom_call_target="tpu_custom_call" | custom-call | flops 5000000000 | bytes 1024 | tf_op jit(solution)/shard_map/pallas_call | solution.py:366
  38.1 14.2 %all_to_all.50.got_ref = f32[16,32,128]{2,1,0:T(8,128)S(1)} all-to-all(f32[16,32,128]{2,1,0:T(8,128)S(1)} %get-tuple-element.36), channel_id=1, replica_groups=mesh['filt'=2,'row'=4,'z'=8,'y'=4] {'y','row'}, dimensions={0} | all-to-all | bytes 524288 | tf_op jit(solution)/shard_map/all_to_all | solution.py:356
  52.2 0.7 shard_map.71
  52.9 11.5 %all_to_all.51.got_ref = f32[8,24,128]{2,1,0:T(8,128)S(1)} all-to-all(f32[8,24,128]{2,1,0:T(8,128)S(1)} %get-tuple-element.39), channel_id=1, replica_groups=mesh['filt'=2,'row'=4,'z'=8,'y'=4] {'z'}, dimensions={0} | all-to-all | bytes 196608 | tf_op jit(solution)/shard_map/all_to_all | solution.py:356
  64.4 0.4 shard_map.72
  64.8 11.4 %all_to_all.52.got_ref = f32[16,16,128]{2,1,0:T(8,128)S(1)} all-to-all(f32[16,16,128]{2,1,0:T(8,128)S(1)} %get-tuple-element.40), channel_id=1, replica_groups=mesh['filt'=2,'row'=4,'z'=8,'y'=4] {'y','row'}, dimensions={0} | all-to-all | bytes 262144 | tf_op jit(solution)/shard_map/all_to_all | solution.py:356
  76.2 0.7 shard_map.73
  76.8 10.4 %all_to_all.53.got_ref = f32[8,8,128]{2,1,0:T(8,128)S(1)} all-to-all(f32[8,8,128]{2,1,0:T(8,128)S(1)} %get-tuple-element.43), channel_id=1, replica_groups=mesh['filt'=2,'row'=4,'z'=8,'y'=4] {'z'}, dimensions={0} | all-to-all | bytes 65536 | tf_op jit(solution)/shard_map/all_to_all | solution.py:356
  87.2 0.4 shard_map.74
  87.7 11.1 %all_to_all.54.got_ref = f32[16,16,128]{2,1,0:T(8,128)S(1)} all-to-all(f32[16,16,128]{2,1,0:T(8,128)S(1)} %shard_map.74), channel_id=1, replica_groups=mesh['filt'=2,'row'=4,'z'=8,'y'=4] {'y','row'}, dimensions={0} | all-to-all | bytes 262144 | tf_op jit(solution)/shard_map/all_to_all | solution.py:356
  98.7 0.7 shard_map.75
  99.4 10.4 %all_to_all.55.got_ref = f32[8,8,128]{2,1,0:T(8,128)S(1)} all-to-all(f32[8,8,128]{2,1,0:T(8,128)S(1)} %get-tuple-element.45), channel_id=1, replica_groups=mesh['filt'=2,'row'=4,'z'=8,'y'=4] {'z'}, dimensions={0} | all-to-all | bytes 65536 | tf_op jit(solution)/shard_map/all_to_all | solution.py:356
  109.8 0.4 shard_map.76
  110.2 11.1 %all_to_all.56.refs_0_ = f32[16,16,128]{2,1,0:T(8,128)S(1)} all-to-all(f32[16,16,128]{2,1,0:T(8,128)S(1)} %get-tuple-element.46), channel_id=1, replica_groups=mesh['filt'=2,'row'=4,'z'=8,'y'=4] {'y','row'}, dimensions={0} | all-to-all | bytes 262144 | tf_op jit(solution)/shard_map/all_to_all | solution.py:356
  121.3 3.1 %shard_map.77 = (f32[16,128]{1,0:T(8,128)S(1)}, f32[8,8,128]{2,1,0:T(8,128)}, bf16[768,256]{1,0:T(8,128)(2,1)S(1)}, bf16[768,256]{1,0:T(8,128)(2,1)S(1)}) custom-call(f32[16,16,128]{2,1,0:T(8,128)S(1)} %all_to_all.56.refs_0_, f32[32,128]{1,0:T(8,128)S(1)} %get-tuple-element.41.mass_ref.refs_1_, f32[16,128]{1,0:T(8,128)S(1)} %get-tuple-element.42.w_ref.refs_2_, ...), custom_call_target="tpu_custom_call" | custom-call | flops 4000000000 | bytes 1024 | tf_op jit(solution)/shard_map/pallas_call | solution.py:366
  124.3 0.7 collective-permute-start.6
  125.0 3.3 %all-to-all-start.8 = ((f32[8,8,128]{2,1,0:T(8,128)}), f32[8,8,128]{2,1,0:T(8,128)S(1)}, u32[]{:S(2)}, u32[]{:S(2)}) async-start(f32[8,8,128]{2,1,0:T(8,128)} %get-tuple-element.52), calls=%async_computation.8 | async-start | bytes 65536 | tf_op jit(solution)/shard_map/all_to_all | solution.py:356
  128.4 5.6 %collective-permute-done.6.got_ref = bf16[768,256]{1,0:T(8,128)(2,1)S(1)} collective-permute-done((bf16[768,256]{1,0:T(8,128)(2,1)S(1)}, bf16[768,256]{1,0:T(8,128)(2,1)S(1)}, u32[]{:S(2)}, u32[]{:S(2)}) %collective-permute-start.6) | collective-permute-done | bytes 393248 | tf_op jit(solution)/shard_map/ppermute | solution.py:363
  133.9 0.1 shard_map.78
  134.0 0.1 collective-permute-start.7
  134.1 2.2 %all-to-all-done.8.refs_0_ = f32[8,8,128]{2,1,0:T(8,128)S(1)} async-done(((f32[8,8,128]{2,1,0:T(8,128)}), f32[8,8,128]{2,1,0:T(8,128)S(1)}, u32[]{:S(2)}, u32[]{:S(2)}) %all-to-all-start.8) | async-done | bytes 32800 | tf_op jit(solution)/shard_map/all_to_all | solution.py:356
  136.3 4.2 %shard_map.79 = (bf16[16,96,256]{2,1,0:T(8,128)(2,1)}, f32[16,128]{1,0:T(8,128)S(1)}, f32[96,1]{1,0:T(8,128)S(1)}) custom-call(f32[8,8,128]{2,1,0:T(8,128)S(1)} %all-to-all-done.8.refs_0_, f32[16,128]{1,0:T(8,128)S(1)} %get-tuple-element.44.col_ref.refs_1_, f32[16,128]{1,0:T(8,128)S(1)} %get-tuple-element.53.refs_2_, ...), custom_call_target="tpu_custom_call" | custom-call | flops 4000000000 | bytes 1024 | tf_op jit(solution)/shard_map/pallas_call | solution.py:366
  140.5 3.4 %collective-permute-done.7.got_ref = bf16[384,256]{1,0:T(8,128)(2,1)S(1)} collective-permute-done((bf16[384,256]{1,0:T(8,128)(2,1)S(1)}, bf16[384,256]{1,0:T(8,128)(2,1)S(1)}, u32[]{:S(2)}, u32[]{:S(2)}) %collective-permute-start.7) | collective-permute-done | bytes 196640 | tf_op jit(solution)/shard_map/ppermute | solution.py:363
  143.9 5.1 %all-to-all-start.9 = ((bf16[16,96,256]{2,1,0:T(8,128)(2,1)}), bf16[16,96,256]{2,1,0:T(8,128)(2,1)S(1)}, u32[]{:S(2)}, u32[]{:S(2)}) async-start(bf16[16,96,256]{2,1,0:T(8,128)(2,1)} %get-tuple-element.60), calls=%async_computation.9 | async-start | bytes 1572864 | tf_op jit(solution)/shard_map/all_to_all | solution.py:356
  149.0 1.9 %collective-permute-start.8 = (bf16[192,256]{1,0:T(8,128)(2,1)S(1)}, bf16[192,256]{1,0:T(8,128)(2,1)S(1)}, u32[]{:S(2)}, u32[]{:S(2)}) collective-permute-start(bf16[192,256]{1,0:T(8,128)(2,1)S(1)} %get-tuple-element.63), channel_id=1, source_target_pairs={{0,16},{4,20},{8,24},{12,28},{16,0},{20,4},{24,8},{28,12},{1,17},{... | collective-permute-start | bytes 294920 | tf_op jit(solution)/shard_map/ppermute | solution.py:363
  151.0 0.5 dynamic-slice_bitcast_fusion
  151.5 6.2 %collective-permute-done.8.got_ref = bf16[192,256]{1,0:T(8,128)(2,1)S(1)} collective-permute-done((bf16[192,256]{1,0:T(8,128)(2,1)S(1)}, bf16[192,256]{1,0:T(8,128)(2,1)S(1)}, u32[]{:S(2)}, u32[]{:S(2)}) %collective-permute-start.8) | collective-permute-done | bytes 98336 | tf_op jit(solution)/shard_map/ppermute | solution.py:363
  157.7 0.8 all-to-all-done.9.rows_ref
  158.4 0.8 shard_map.81
  (2 shorter events, 0.1 us)
Async XLA Ops:
  2.5 32.3 %all-to-all-start = ((bf16[8,200,256]{2,1,0:T(8,128)(2,1)}), bf16[8,200,256]{2,1,0:T(8,128)(2,1)S(1)}, u32[]{:S(2)}, u32[]{:S(2)}) async-start(bf16[8,200,256]{2,1,0:T(8,128)(2,1)} %get-tuple-element.35), calls=%async_computation | async-start | bytes 1638400 | tf_op jit(solution)/shard_map/all_to_all | solution.py:356
  11.0 5.9 %collective-permute-start = (bf16[104,256]{1,0:T(8,128)(2,1)S(1)}, bf16[104,256]{1,0:T(8,128)(2,1)S(1)}, u32[]{:S(2)}, u32[]{:S(2)}) collective-permute-start(bf16[104,256]{1,0:T(8,128)(2,1)S(1)} %get-tuple-element.34.refs_0_), channel_id=1, source_target_pairs={{0,32},{32,64},{64,96},{96,0},{1,33},{33,65},{65,97},{97,1},{2,34}... | collective-permute-start | bytes 159752 | tf_op jit(solution)/shard_map/ppermute | solution.py:360
  12.5 5.6 %collective-permute-start.1 = (bf16[104,256]{1,0:T(8,128)(2,1)S(1)}, bf16[104,256]{1,0:T(8,128)(2,1)S(1)}, u32[]{:S(2)}, u32[]{:S(2)}) collective-permute-start(bf16[104,256]{1,0:T(8,128)(2,1)S(1)} %get-tuple-element.34.refs_0_), channel_id=1, source_target_pairs={{0,64},{32,96},{64,0},{96,32},{1,65},{33,97},{65,1},{97,33},{2,66}... | collective-permute-start | bytes 159752 | tf_op jit(solution)/shard_map/ppermute | solution.py:360
  15.2 4.1 %collective-permute-start.2 = (bf16[104,256]{1,0:T(8,128)(2,1)S(1)}, bf16[104,256]{1,0:T(8,128)(2,1)S(1)}, u32[]{:S(2)}, u32[]{:S(2)}) collective-permute-start(bf16[104,256]{1,0:T(8,128)(2,1)S(1)} %get-tuple-element.34.refs_0_), channel_id=1, source_target_pairs={{0,96},{32,0},{64,32},{96,64},{1,97},{33,1},{65,33},{97,65},{2,98}... | collective-permute-start | bytes 159752 | tf_op jit(solution)/shard_map/ppermute | solution.py:360
  19.4 8.0 %collective-permute-start.3 = (bf16[416,256]{1,0:T(8,128)(2,1)S(1)}, bf16[416,256]{1,0:T(8,128)(2,1)S(1)}, u32[]{:S(2)}, u32[]{:S(2)}) collective-permute-start(bf16[416,256]{1,0:T(8,128)(2,1)S(1)} %shard_map.69.refs_0_), channel_id=1, source_target_pairs={{0,1},{1,2},{2,3},{3,0},{4,5},{5,6},{6,7},{7,4},{8,9},{9,10},{10,1... | collective-permute-start | bytes 638984 | tf_op jit(solution)/shard_map/ppermute | solution.py:360
  21.1 9.3 %collective-permute-start.4 = (bf16[416,256]{1,0:T(8,128)(2,1)S(1)}, bf16[416,256]{1,0:T(8,128)(2,1)S(1)}, u32[]{:S(2)}, u32[]{:S(2)}) collective-permute-start(bf16[416,256]{1,0:T(8,128)(2,1)S(1)} %shard_map.69.refs_0_), channel_id=1, source_target_pairs={{0,2},{1,3},{2,0},{3,1},{4,6},{5,7},{6,4},{7,5},{8,10},{9,11},{10,... | collective-permute-start | bytes 638984 | tf_op jit(solution)/shard_map/ppermute | solution.py:360
  22.0 9.9 %collective-permute-start.5 = (bf16[416,256]{1,0:T(8,128)(2,1)S(1)}, bf16[416,256]{1,0:T(8,128)(2,1)S(1)}, u32[]{:S(2)}, u32[]{:S(2)}) collective-permute-start(bf16[416,256]{1,0:T(8,128)(2,1)S(1)} %shard_map.69.refs_0_), channel_id=1, source_target_pairs={{0,3},{1,0},{2,1},{3,2},{4,7},{5,4},{6,5},{7,6},{8,11},{9,8},{10,9... | collective-permute-start | bytes 638984 | tf_op jit(solution)/shard_map/ppermute | solution.py:360
  124.3 9.6 %collective-permute-start.6 = (bf16[768,256]{1,0:T(8,128)(2,1)S(1)}, bf16[768,256]{1,0:T(8,128)(2,1)S(1)}, u32[]{:S(2)}, u32[]{:S(2)}) collective-permute-start(bf16[768,256]{1,0:T(8,128)(2,1)S(1)} %get-tuple-element.56), channel_id=1, source_target_pairs={{0,4},{4,0},{8,12},{12,8},{16,20},{20,16},{24,28},{28,24},{1,5},{5... | collective-permute-start | bytes 1179656 | tf_op jit(solution)/shard_map/ppermute | solution.py:363
  125.0 11.3 %all-to-all-start.8 = ((f32[8,8,128]{2,1,0:T(8,128)}), f32[8,8,128]{2,1,0:T(8,128)S(1)}, u32[]{:S(2)}, u32[]{:S(2)}) async-start(f32[8,8,128]{2,1,0:T(8,128)} %get-tuple-element.52), calls=%async_computation.8 | async-start | bytes 65536 | tf_op jit(solution)/shard_map/all_to_all | solution.py:356
  134.0 9.8 %collective-permute-start.7 = (bf16[384,256]{1,0:T(8,128)(2,1)S(1)}, bf16[384,256]{1,0:T(8,128)(2,1)S(1)}, u32[]{:S(2)}, u32[]{:S(2)}) collective-permute-start(bf16[384,256]{1,0:T(8,128)(2,1)S(1)} %get-tuple-element.59), channel_id=1, source_target_pairs={{0,8},{4,12},{8,0},{12,4},{16,24},{20,28},{24,16},{28,20},{1,9},{5... | collective-permute-start | bytes 589832 | tf_op jit(solution)/shard_map/ppermute | solution.py:363
  143.9 14.6 %all-to-all-start.9 = ((bf16[16,96,256]{2,1,0:T(8,128)(2,1)}), bf16[16,96,256]{2,1,0:T(8,128)(2,1)S(1)}, u32[]{:S(2)}, u32[]{:S(2)}) async-start(bf16[16,96,256]{2,1,0:T(8,128)(2,1)} %get-tuple-element.60), calls=%async_computation.9 | async-start | bytes 1572864 | tf_op jit(solution)/shard_map/all_to_all | solution.py:356
  149.0 8.6 %collective-permute-start.8 = (bf16[192,256]{1,0:T(8,128)(2,1)S(1)}, bf16[192,256]{1,0:T(8,128)(2,1)S(1)}, u32[]{:S(2)}, u32[]{:S(2)}) collective-permute-start(bf16[192,256]{1,0:T(8,128)(2,1)S(1)} %get-tuple-element.63), channel_id=1, source_target_pairs={{0,16},{4,20},{8,24},{12,28},{16,0},{20,4},{24,8},{28,12},{1,17},{... | collective-permute-start | bytes 294920 | tf_op jit(solution)/shard_map/ppermute | solution.py:363

commit v10 on v9

--- a/solution.py
+++ b/solution.py
@@ -284,17 +284,31 @@
     sent.wait()
 
 
-def halve(own, bit, keep_ref, got_ref, next_ref, send_ref):
-    mine = bit_of("z", bit)
-    size, out = keep_ref.shape[0] // 2, next_ref.shape[0] // 2
-    for q in range(2):
-        for m in range(out // own):
-            keep = pl.ds(pl.multiple_of(q * size + (2 * m + mine) * own, own), own)
-            give = pl.ds(pl.multiple_of(q * size + (2 * m + 1 - mine) * own, own), own)
-            first = q * out + m * own
-            at = slice(first, first + own)
-            next_ref[at, :] = keep_ref[keep, :].astype(F32) + got_ref[keep, :].astype(F32)
-            send_ref[at, :] = (keep_ref[give, :].astype(F32) + got_ref[give, :].astype(F32)).astype(BF16)
+def halve_apart(own, keep_ref, got_ref, next_ref, right_ref, left_ref):
+    count = keep_ref.shape[0] // (2 * own)
+    mine = lax.shift_right_logical(lax.axis_index("z"), 1)
+
+    def block(q, i):
+        place = q * count + lax.rem(mine + i, count)
+        at = pl.ds(pl.multiple_of(place * own, own), own)
+        return keep_ref[at, :].astype(F32) + got_ref[at, :].astype(F32)
+
+    for m in range(count // 2):
+        at = slice(m * own, (m + 1) * own)
+        for q in range(2):
+            first = (q * (count // 2) + m) * own
+            next_ref[first : first + own, :] = block(q, 2 * m)
+        right_ref[at, :] = block(0, 2 * m + 1).astype(BF16)
+        left_ref[at, :] = block(1, (2 * m + count - 1) % count).astype(BF16)
+
+
+def halve_across(own, keep_ref, right_ref, left_ref, next_ref, send_ref):
+    for q, got_ref in enumerate((right_ref, left_ref)):
+        at = slice(q * own, (q + 1) * own)
+        for m, ref in enumerate((next_ref, send_ref)):
+            first = (2 * q + m) * own
+            value = keep_ref[first : first + own, :] + got_ref[m * own : (m + 1) * own, :].astype(F32)
+            ref[at, :] = value.astype(ref.dtype)
 
 
 def finish_rows(own, width, isrc, every, *refs):
@@ -484,11 +498,14 @@
     send, give = lax.optimization_barrier((send, give))
     taken = flip(give, 1)
     got = swap(send, jaxes)
-    half //= 2
-    keep, give = call(
-        functools.partial(halve, own, 1), 1, [((half, width), F32), ((half, width), BF16)], keep, taken
-    )
-    taken = flip(give, 2)
+    keep, right, left = call(
+        functools.partial(halve_apart, own),
+        1,
+        [((half // 2, width), F32), ((half // 4, width), BF16), ((half // 4, width), BF16)],
+        keep,
+        taken,
+    )
+    right, left = shift(right, "z", 2), shift(left, "z", jsrc - 2)
     row_send, gw, delta = call(
         functools.partial(finish_rows, own, width, isrc, float(isrc * jsrc * own)),
         4,
@@ -507,10 +524,14 @@
         ],
         mib=24,
     )
-    row_send, taken = lax.optimization_barrier((row_send, taken))
-    half //= 2
+    row_send, right, left = lax.optimization_barrier((row_send, right, left))
     keep, give = call(
-        functools.partial(halve, own, 2), 1, [((half, width), F32), ((half, width), BF16)], keep, taken
+        functools.partial(halve_across, own),
+        1,
+        [((half // 4, width), F32), ((half // 4, width), BF16)],
+        keep,
+        right,
+        left,
     )
     taken = flip(give, 4)
     row_got = swap(row_send, iaxes)

time: 161 us -> 159 us (0.988)
  waiting for transfers between devices: 31.2 us -> 23.9 us
  starting transfers between devices: 30.3 us -> 35.8 us
    ppermute x3 -> x2, waiting for transfers between devices: 15.1 us -> 9.52 us  [flip(): return lax.ppermute(value, 'z', [(i, i ^ bit) for i in range(jsrc)])]
    ppermute x6 -> x8, starting transfers between devices: 10.7 us -> 14.9 us  [shift(): return lax.ppermute(value, axis, [(i, (i + k) % n) for i in range(n)])]
    all_to_all x3, waiting for transfers between devices: 5.95 us -> 3.7 us  [swap(): return lax.all_to_all(value, axes, 0, 0, tiled=True)]
    ppermute x3 -> x2, starting transfers between devices: 2.66 us -> 3.89 us  [flip(): return lax.ppermute(value, 'z', [(i, i ^ bit) for i in range(jsrc)])]
    ppermute x6 -> x8, waiting for transfers between devices: 10.1 us -> 10.7 us  [shift(): return lax.ppermute(value, axis, [(i, (i + k) % n) for i in range(n)])]
  transfers between devices with their start and end apart: 12 -> 13, of which waited for: 12 -> 11; matrix products, arithmetic and copies ran while one was open for 0% -> 0% of each run, Pallas kernels for 3% -> 3%
where the time goes in v10:
time: 159 us; the launch traced here: 157 us
  blocking collectives  79.9 us (50%)
  starting transfers between devices  35.8 us (23%)
  waiting for transfers between devices  23.9 us (15%)
  Pallas kernels  16.6 us (10%)
    all_to_all x7, blocking collectives, swap(): return lax.all_to_all(value, axes, 0, 0, tiled=True)  79.9 us
    all_to_all x3, starting transfers between devices, swap(): return lax.all_to_all(value, axes, 0, 0, tiled=True)  17.1 us
    pallas_call x14, Pallas kernels, call(): pl.pallas_call(body, out_shape=[(pltpu.HBM if n in hbm else jax.ShapeDtyp...  16.6 us
    ppermute x8, starting transfers between devices, shift(): return lax.ppermute(value, axis, [(i, (i + k) % n) for i in range(n)])  14.9 us
    ppermute x8, waiting for transfers between devices, shift(): return lax.ppermute(value, axis, [(i, (i + k) % n) for i in range(n)])  10.7 us
    ppermute x2, waiting for transfers between devices, flip(): return lax.ppermute(value, 'z', [(i, i ^ bit) for i in range(jsrc)])  9.52 us
    ppermute x2, starting transfers between devices, flip(): return lax.ppermute(value, 'z', [(i, i ^ bit) for i in range(jsrc)])  3.89 us
    all_to_all x3, waiting for transfers between devices, swap(): return lax.all_to_all(value, axes, 0, 0, tiled=True)  3.7 us
  transfers between devices with their start and end apart: 13, of which 11 were waited for; matrix products, arithmetic and copies ran while one was open for 0% of the time, Pallas kernels for 3%

profile of v10, /device:TPU:8, one launch (start us, length us, event | category | flops | bytes accessed | tf_op | source)
XLA Modules:
  0.0 157.4 jit_solution(7063034415867703897)
XLA Ops:
  0.6 1.9 %shard_map.68 = (bf16[104,256]{1,0:T(8,128)(2,1)S(1)}, bf16[8,200,256]{2,1,0:T(8,128)(2,1)}) custom-call(bf16[96,256]{1,0:T(8,128)(2,1)} %x_ref.1, bf16[96,256]{1,0:T(8,128)(2,1)} %gy_ref.1, bf16[1,96]{1,0:T(2,128)(2,1)} %bitcast.5, bf16[1,96]{1,0:T(2,128)(2,1)} %bitcast.6, bf16[1,96]{1,0:T(2,128)(2,1)} %bitcast.7), custom_call_target="tpu_custom_call" | custom-call | flops 2000000000 | bytes 1024 | tf_op jit(solution)/shard_map/pallas_call | solution.py:380
  2.5 8.5 %all-to-all-start = ((bf16[8,200,256]{2,1,0:T(8,128)(2,1)}), bf16[8,200,256]{2,1,0:T(8,128)(2,1)S(1)}, u32[]{:S(2)}, u32[]{:S(2)}) async-start(bf16[8,200,256]{2,1,0:T(8,128)(2,1)} %get-tuple-element.37), calls=%async_computation | async-start | bytes 1638400 | tf_op jit(solution)/shard_map/all_to_all | solution.py:370
  11.0 1.5 collective-permute-start
  12.5 2.7 %collective-permute-start.1 = (bf16[104,256]{1,0:T(8,128)(2,1)S(1)}, bf16[104,256]{1,0:T(8,128)(2,1)S(1)}, u32[]{:S(2)}, u32[]{:S(2)}) collective-permute-start(bf16[104,256]{1,0:T(8,128)(2,1)S(1)} %get-tuple-element.36.refs_0_), channel_id=1, source_target_pairs={{0,64},{32,96},{64,0},{96,32},{1,65},{33,97},{65,1},{97,33},{2,66}... | collective-permute-start | bytes 159752 | tf_op jit(solution)/shard_map/ppermute | solution.py:374
  15.2 1.4 collective-permute-start.2
  16.7 0.3 collective-permute-done.refs_1_
  16.9 1.2 collective-permute-done.1.refs_2_
  18.1 1.2 collective-permute-done.2.refs_3_
  19.4 1.7 %collective-permute-start.3 = (bf16[416,256]{1,0:T(8,128)(2,1)S(1)}, bf16[416,256]{1,0:T(8,128)(2,1)S(1)}, u32[]{:S(2)}, u32[]{:S(2)}) collective-permute-start(bf16[416,256]{1,0:T(8,128)(2,1)S(1)} %shard_map.69.refs_0_), channel_id=1, source_target_pairs={{0,1},{1,2},{2,3},{3,0},{4,5},{5,6},{6,7},{7,4},{8,9},{9,10},{10,1... | collective-permute-start | bytes 638984 | tf_op jit(solution)/shard_map/ppermute | solution.py:374
  21.1 0.9 collective-permute-start.4
  22.0 2.4 %collective-permute-start.5 = (bf16[416,256]{1,0:T(8,128)(2,1)S(1)}, bf16[416,256]{1,0:T(8,128)(2,1)S(1)}, u32[]{:S(2)}, u32[]{:S(2)}) collective-permute-start(bf16[416,256]{1,0:T(8,128)(2,1)S(1)} %shard_map.69.refs_0_), channel_id=1, source_target_pairs={{0,3},{1,0},{2,1},{3,2},{4,7},{5,4},{6,5},{7,6},{8,11},{9,8},{10,9... | collective-permute-start | bytes 638984 | tf_op jit(solution)/shard_map/ppermute | solution.py:374
  24.4 3.0 %collective-permute-done.3.refs_1_ = bf16[416,256]{1,0:T(8,128)(2,1)S(1)} collective-permute-done((bf16[416,256]{1,0:T(8,128)(2,1)S(1)}, bf16[416,256]{1,0:T(8,128)(2,1)S(1)}, u32[]{:S(2)}, u32[]{:S(2)}) %collective-permute-start.3) | collective-permute-done | bytes 213024 | tf_op jit(solution)/shard_map/ppermute | solution.py:374
  27.4 2.9 %collective-permute-done.4.refs_2_ = bf16[416,256]{1,0:T(8,128)(2,1)S(1)} collective-permute-done((bf16[416,256]{1,0:T(8,128)(2,1)S(1)}, bf16[416,256]{1,0:T(8,128)(2,1)S(1)}, u32[]{:S(2)}, u32[]{:S(2)}) %collective-permute-start.4) | collective-permute-done | bytes 213024 | tf_op jit(solution)/shard_map/ppermute | solution.py:374
  30.4 1.5 collective-permute-done.5.refs_3_
  31.9 3.0 %all-to-all-done.refs_4_.refs_6_ = bf16[8,200,256]{2,1,0:T(8,128)(2,1)S(1)} async-done(((bf16[8,200,256]{2,1,0:T(8,128)(2,1)}), bf16[8,200,256]{2,1,0:T(8,128)(2,1)S(1)}, u32[]{:S(2)}, u32[]{:S(2)}) %all-to-all-start) | async-done | bytes 819232 | tf_op jit(solution)/shard_map/all_to_all | solution.py:370
  34.8 3.2 %shard_map.70 = (f32[1536,768]{1,0:T(8,128)S(1)}, f32[1536,768]{1,0:T(8,128)S(1)}, bf16[1536,256]{1,0:T(8,128)(2,1)S(1)}, f32[16,128]{1,0:T(8,128)S(1)}, f32[16,...) custom-call(bf16[416,256]{1,0:T(8,128)(2,1)S(1)} %shard_map.69.refs_0_, ...), custom_call_target="tpu_custom_call" | custom-call | flops 5000000000 | bytes 1024 | tf_op jit(solution)/shard_map/pallas_call | solution.py:380
  38.1 14.2 %all_to_all.50.got_ref = f32[16,32,128]{2,1,0:T(8,128)S(1)} all-to-all(f32[16,32,128]{2,1,0:T(8,128)S(1)} %get-tuple-element.38), channel_id=1, replica_groups=mesh['filt'=2,'row'=4,'z'=8,'y'=4] {'y','row'}, dimensions={0} | all-to-all | bytes 524288 | tf_op jit(solution)/shard_map/all_to_all | solution.py:370
  52.2 0.7 shard_map.71
  52.9 11.5 %all_to_all.51.got_ref = f32[8,24,128]{2,1,0:T(8,128)S(1)} all-to-all(f32[8,24,128]{2,1,0:T(8,128)S(1)} %get-tuple-element.41), channel_id=1, replica_groups=mesh['filt'=2,'row'=4,'z'=8,'y'=4] {'z'}, dimensions={0} | all-to-all | bytes 196608 | tf_op jit(solution)/shard_map/all_to_all | solution.py:370
  64.4 0.4 shard_map.72
  64.8 11.4 %all_to_all.52.got_ref = f32[16,16,128]{2,1,0:T(8,128)S(1)} all-to-all(f32[16,16,128]{2,1,0:T(8,128)S(1)} %get-tuple-element.42), channel_id=1, replica_groups=mesh['filt'=2,'row'=4,'z'=8,'y'=4] {'y','row'}, dimensions={0} | all-to-all | bytes 262144 | tf_op jit(solution)/shard_map/all_to_all | solution.py:370
  76.2 0.6 shard_map.73
  76.8 10.4 %all_to_all.53.got_ref = f32[8,8,128]{2,1,0:T(8,128)S(1)} all-to-all(f32[8,8,128]{2,1,0:T(8,128)S(1)} %get-tuple-element.45), channel_id=1, replica_groups=mesh['filt'=2,'row'=4,'z'=8,'y'=4] {'z'}, dimensions={0} | all-to-all | bytes 65536 | tf_op jit(solution)/shard_map/all_to_all | solution.py:370
  87.2 0.4 shard_map.74
  87.7 11.1 %all_to_all.54.got_ref = f32[16,16,128]{2,1,0:T(8,128)S(1)} all-to-all(f32[16,16,128]{2,1,0:T(8,128)S(1)} %shard_map.74), channel_id=1, replica_groups=mesh['filt'=2,'row'=4,'z'=8,'y'=4] {'y','row'}, dimensions={0} | all-to-all | bytes 262144 | tf_op jit(solution)/shard_map/all_to_all | solution.py:370
  98.7 0.6 shard_map.75
  99.4 10.4 %all_to_all.55.got_ref = f32[8,8,128]{2,1,0:T(8,128)S(1)} all-to-all(f32[8,8,128]{2,1,0:T(8,128)S(1)} %get-tuple-element.47), channel_id=1, replica_groups=mesh['filt'=2,'row'=4,'z'=8,'y'=4] {'z'}, dimensions={0} | all-to-all | bytes 65536 | tf_op jit(solution)/shard_map/all_to_all | solution.py:370
  109.8 0.4 shard_map.76
  110.2 11.1 %all_to_all.56.refs_0_ = f32[16,16,128]{2,1,0:T(8,128)S(1)} all-to-all(f32[16,16,128]{2,1,0:T(8,128)S(1)} %get-tuple-element.48), channel_id=1, replica_groups=mesh['filt'=2,'row'=4,'z'=8,'y'=4] {'y','row'}, dimensions={0} | all-to-all | bytes 262144 | tf_op jit(solution)/shard_map/all_to_all | solution.py:370
  121.3 3.1 %shard_map.77 = (f32[16,128]{1,0:T(8,128)S(1)}, f32[8,8,128]{2,1,0:T(8,128)}, bf16[768,256]{1,0:T(8,128)(2,1)S(1)}, bf16[768,256]{1,0:T(8,128)(2,1)S(1)}) custom-call(f32[16,16,128]{2,1,0:T(8,128)S(1)} %all_to_all.56.refs_0_, f32[32,128]{1,0:T(8,128)S(1)} %get-tuple-element.43.mass_ref.refs_1_, f32[16,128]{1,0:T(8,128)S(1)} %get-tuple-element.44.w_ref.refs_2_, ...), custom_call_target="tpu_custom_call" | custom-call | flops 4000000000 | bytes 1024 | tf_op jit(solution)/shard_map/pallas_call | solution.py:380
  124.4 0.7 collective-permute-start.6
  125.0 3.3 %all-to-all-start.8 = ((f32[8,8,128]{2,1,0:T(8,128)}), f32[8,8,128]{2,1,0:T(8,128)S(1)}, u32[]{:S(2)}, u32[]{:S(2)}) async-start(f32[8,8,128]{2,1,0:T(8,128)} %get-tuple-element.54), calls=%async_computation.8 | async-start | bytes 65536 | tf_op jit(solution)/shard_map/all_to_all | solution.py:370
  128.4 4.6 %collective-permute-done.6.got_ref = bf16[768,256]{1,0:T(8,128)(2,1)S(1)} collective-permute-done((bf16[768,256]{1,0:T(8,128)(2,1)S(1)}, bf16[768,256]{1,0:T(8,128)(2,1)S(1)}, u32[]{:S(2)}, u32[]{:S(2)}) %collective-permute-start.6) | collective-permute-done | bytes 393248 | tf_op jit(solution)/shard_map/ppermute | solution.py:377
  133.0 0.1 shard_map.78
  133.0 0.8 collective-permute-start.7
  133.9 3.4 %collective-permute-start.8 = (bf16[192,256]{1,0:T(8,128)(2,1)S(1)}, bf16[192,256]{1,0:T(8,128)(2,1)S(1)}, u32[]{:S(2)}, u32[]{:S(2)}) collective-permute-start(bf16[192,256]{1,0:T(8,128)(2,1)S(1)} %get-tuple-element.62), channel_id=1, source_target_pairs={{0,24},{4,28},{8,0},{12,4},{16,8},{20,12},{24,16},{28,20},{1,25},{... | collective-permute-start | bytes 294920 | tf_op jit(solution)/shard_map/ppermute | solution.py:374
  137.3 0.0 all-to-all-done.8.refs_0_
  137.3 4.2 %shard_map.79 = (bf16[16,96,256]{2,1,0:T(8,128)(2,1)}, f32[16,128]{1,0:T(8,128)S(1)}, f32[96,1]{1,0:T(8,128)S(1)}) custom-call(f32[8,8,128]{2,1,0:T(8,128)S(1)} %all-to-all-done.8.refs_0_, f32[16,128]{1,0:T(8,128)S(1)} %get-tuple-element.46.col_ref.refs_1_, f32[16,128]{1,0:T(8,128)S(1)} %get-tuple-element.55.refs_2_, ...), custom_call_target="tpu_custom_call" | custom-call | flops 4000000000 | bytes 1024 | tf_op jit(solution)/shard_map/pallas_call | solution.py:380
  141.5 0.0 collective-permute-done.7.right_ref
  141.5 0.5 collective-permute-done.8.left_ref
  142.0 5.3 %all-to-all-start.9 = ((bf16[16,96,256]{2,1,0:T(8,128)(2,1)}), bf16[16,96,256]{2,1,0:T(8,128)(2,1)S(1)}, u32[]{:S(2)}, u32[]{:S(2)}) async-start(bf16[16,96,256]{2,1,0:T(8,128)(2,1)} %get-tuple-element.63), calls=%async_computation.9 | async-start | bytes 1572864 | tf_op jit(solution)/shard_map/all_to_all | solution.py:370
  147.3 3.2 %collective-permute-start.9 = (bf16[192,256]{1,0:T(8,128)(2,1)S(1)}, bf16[192,256]{1,0:T(8,128)(2,1)S(1)}, u32[]{:S(2)}, u32[]{:S(2)}) collective-permute-start(bf16[192,256]{1,0:T(8,128)(2,1)S(1)} %get-tuple-element.67), channel_id=1, source_target_pairs={{0,16},{4,20},{8,24},{12,28},{16,0},{20,4},{24,8},{28,12},{1,17},{... | collective-permute-start | bytes 294920 | tf_op jit(solution)/shard_map/ppermute | solution.py:377
  150.5 0.5 dynamic-slice_bitcast_fusion
  151.0 4.9 %collective-permute-done.9.got_ref = bf16[192,256]{1,0:T(8,128)(2,1)S(1)} collective-permute-done((bf16[192,256]{1,0:T(8,128)(2,1)S(1)}, bf16[192,256]{1,0:T(8,128)(2,1)S(1)}, u32[]{:S(2)}, u32[]{:S(2)}) %collective-permute-start.9) | collective-permute-done | bytes 98336 | tf_op jit(solution)/shard_map/ppermute | solution.py:377
  156.0 0.7 all-to-all-done.9.rows_ref
  156.7 0.8 shard_map.81
  (2 shorter events, 0.1 us)
Async XLA Ops:
  2.5 32.3 %all-to-all-start = ((bf16[8,200,256]{2,1,0:T(8,128)(2,1)}), bf16[8,200,256]{2,1,0:T(8,128)(2,1)S(1)}, u32[]{:S(2)}, u32[]{:S(2)}) async-start(bf16[8,200,256]{2,1,0:T(8,128)(2,1)} %get-tuple-element.37), calls=%async_computation | async-start | bytes 1638400 | tf_op jit(solution)/shard_map/all_to_all | solution.py:370
  11.0 5.9 %collective-permute-start = (bf16[104,256]{1,0:T(8,128)(2,1)S(1)}, bf16[104,256]{1,0:T(8,128)(2,1)S(1)}, u32[]{:S(2)}, u32[]{:S(2)}) collective-permute-start(bf16[104,256]{1,0:T(8,128)(2,1)S(1)} %get-tuple-element.36.refs_0_), channel_id=1, source_target_pairs={{0,32},{32,64},{64,96},{96,0},{1,33},{33,65},{65,97},{97,1},{2,34}... | collective-permute-start | bytes 159752 | tf_op jit(solution)/shard_map/ppermute | solution.py:374
  12.5 5.6 %collective-permute-start.1 = (bf16[104,256]{1,0:T(8,128)(2,1)S(1)}, bf16[104,256]{1,0:T(8,128)(2,1)S(1)}, u32[]{:S(2)}, u32[]{:S(2)}) collective-permute-start(bf16[104,256]{1,0:T(8,128)(2,1)S(1)} %get-tuple-element.36.refs_0_), channel_id=1, source_target_pairs={{0,64},{32,96},{64,0},{96,32},{1,65},{33,97},{65,1},{97,33},{2,66}... | collective-permute-start | bytes 159752 | tf_op jit(solution)/shard_map/ppermute | solution.py:374
  15.2 4.1 %collective-permute-start.2 = (bf16[104,256]{1,0:T(8,128)(2,1)S(1)}, bf16[104,256]{1,0:T(8,128)(2,1)S(1)}, u32[]{:S(2)}, u32[]{:S(2)}) collective-permute-start(bf16[104,256]{1,0:T(8,128)(2,1)S(1)} %get-tuple-element.36.refs_0_), channel_id=1, source_target_pairs={{0,96},{32,0},{64,32},{96,64},{1,97},{33,1},{65,33},{97,65},{2,98}... | collective-permute-start | bytes 159752 | tf_op jit(solution)/shard_map/ppermute | solution.py:374
  19.4 8.0 %collective-permute-start.3 = (bf16[416,256]{1,0:T(8,128)(2,1)S(1)}, bf16[416,256]{1,0:T(8,128)(2,1)S(1)}, u32[]{:S(2)}, u32[]{:S(2)}) collective-permute-start(bf16[416,256]{1,0:T(8,128)(2,1)S(1)} %shard_map.69.refs_0_), channel_id=1, source_target_pairs={{0,1},{1,2},{2,3},{3,0},{4,5},{5,6},{6,7},{7,4},{8,9},{9,10},{10,1... | collective-permute-start | bytes 638984 | tf_op jit(solution)/shard_map/ppermute | solution.py:374
  21.1 9.3 %collective-permute-start.4 = (bf16[416,256]{1,0:T(8,128)(2,1)S(1)}, bf16[416,256]{1,0:T(8,128)(2,1)S(1)}, u32[]{:S(2)}, u32[]{:S(2)}) collective-permute-start(bf16[416,256]{1,0:T(8,128)(2,1)S(1)} %shard_map.69.refs_0_), channel_id=1, source_target_pairs={{0,2},{1,3},{2,0},{3,1},{4,6},{5,7},{6,4},{7,5},{8,10},{9,11},{10,... | collective-permute-start | bytes 638984 | tf_op jit(solution)/shard_map/ppermute | solution.py:374
  22.0 9.9 %collective-permute-start.5 = (bf16[416,256]{1,0:T(8,128)(2,1)S(1)}, bf16[416,256]{1,0:T(8,128)(2,1)S(1)}, u32[]{:S(2)}, u32[]{:S(2)}) collective-permute-start(bf16[416,256]{1,0:T(8,128)(2,1)S(1)} %shard_map.69.refs_0_), channel_id=1, source_target_pairs={{0,3},{1,0},{2,1},{3,2},{4,7},{5,4},{6,5},{7,6},{8,11},{9,8},{10,9... | collective-permute-start | bytes 638984 | tf_op jit(solution)/shard_map/ppermute | solution.py:374
  124.4 8.6 %collective-permute-start.6 = (bf16[768,256]{1,0:T(8,128)(2,1)S(1)}, bf16[768,256]{1,0:T(8,128)(2,1)S(1)}, u32[]{:S(2)}, u32[]{:S(2)}) collective-permute-start(bf16[768,256]{1,0:T(8,128)(2,1)S(1)} %get-tuple-element.58), channel_id=1, source_target_pairs={{0,4},{4,0},{8,12},{12,8},{16,20},{20,16},{24,28},{28,24},{1,5},{5... | collective-permute-start | bytes 1179656 | tf_op jit(solution)/shard_map/ppermute | solution.py:377
  125.0 12.3 %all-to-all-start.8 = ((f32[8,8,128]{2,1,0:T(8,128)}), f32[8,8,128]{2,1,0:T(8,128)S(1)}, u32[]{:S(2)}, u32[]{:S(2)}) async-start(f32[8,8,128]{2,1,0:T(8,128)} %get-tuple-element.54), calls=%async_computation.8 | async-start | bytes 65536 | tf_op jit(solution)/shard_map/all_to_all | solution.py:370
  133.0 8.4 %collective-permute-start.7 = (bf16[192,256]{1,0:T(8,128)(2,1)S(1)}, bf16[192,256]{1,0:T(8,128)(2,1)S(1)}, u32[]{:S(2)}, u32[]{:S(2)}) collective-permute-start(bf16[192,256]{1,0:T(8,128)(2,1)S(1)} %get-tuple-element.61), channel_id=1, source_target_pairs={{0,8},{4,12},{8,16},{12,20},{16,24},{20,28},{24,0},{28,4},{1,9},{5... | collective-permute-start | bytes 294920 | tf_op jit(solution)/shard_map/ppermute | solution.py:374
  133.9 8.1 %collective-permute-start.8 = (bf16[192,256]{1,0:T(8,128)(2,1)S(1)}, bf16[192,256]{1,0:T(8,128)(2,1)S(1)}, u32[]{:S(2)}, u32[]{:S(2)}) collective-permute-start(bf16[192,256]{1,0:T(8,128)(2,1)S(1)} %get-tuple-element.62), channel_id=1, source_target_pairs={{0,24},{4,28},{8,0},{12,4},{16,8},{20,12},{24,16},{28,20},{1,25},{... | collective-permute-start | bytes 294920 | tf_op jit(solution)/shard_map/ppermute | solution.py:374
  142.0 14.7 %all-to-all-start.9 = ((bf16[16,96,256]{2,1,0:T(8,128)(2,1)}), bf16[16,96,256]{2,1,0:T(8,128)(2,1)S(1)}, u32[]{:S(2)}, u32[]{:S(2)}) async-start(bf16[16,96,256]{2,1,0:T(8,128)(2,1)} %get-tuple-element.63), calls=%async_computation.9 | async-start | bytes 1572864 | tf_op jit(solution)/shard_map/all_to_all | solution.py:370
  147.3 8.7 %collective-permute-start.9 = (bf16[192,256]{1,0:T(8,128)(2,1)S(1)}, bf16[192,256]{1,0:T(8,128)(2,1)S(1)}, u32[]{:S(2)}, u32[]{:S(2)}) collective-permute-start(bf16[192,256]{1,0:T(8,128)(2,1)S(1)} %get-tuple-element.67), channel_id=1, source_target_pairs={{0,16},{4,20},{8,24},{12,28},{16,0},{20,4},{24,8},{28,12},{1,17},{... | collective-permute-start | bytes 294920 | tf_op jit(solution)/shard_map/ppermute | solution.py:377

commit v11 on v10

--- a/solution.py
+++ b/solution.py
@@ -302,13 +302,12 @@
         left_ref[at, :] = block(1, (2 * m + count - 1) % count).astype(BF16)
 
 
-def halve_across(own, keep_ref, right_ref, left_ref, next_ref, send_ref):
-    for q, got_ref in enumerate((right_ref, left_ref)):
-        at = slice(q * own, (q + 1) * own)
-        for m, ref in enumerate((next_ref, send_ref)):
-            first = (2 * q + m) * own
-            value = keep_ref[first : first + own, :] + got_ref[m * own : (m + 1) * own, :].astype(F32)
-            ref[at, :] = value.astype(ref.dtype)
+def halve_across(own, keep_ref, right_ref, left_ref, delta_ref, next_ref, send_ref):
+    for m, ref in enumerate((next_ref, send_ref)):
+        at = slice(m * own, (m + 1) * own)
+        sums = keep_ref[at, :] + right_ref[at, :].astype(F32)
+        fix = keep_ref[(2 + m) * own : (3 + m) * own, :] + left_ref[at, :].astype(F32)
+        ref[...] = (sums + delta_ref[at, :] * fix).astype(ref.dtype)
 
 
 def finish_rows(own, width, isrc, every, *refs):
@@ -327,8 +326,10 @@
     jbias = row_of(bias_ref[isrc:], cols // LANES)
     rows = lax.broadcasted_iota(jnp.int32, (own, cols), 0)
     lanes = lax.broadcasted_iota(jnp.int32, (own, cols), 1)
-    first = lax.axis_index("z") * own
-    delta_ref[...] = jnp.sum(jnp.where(lanes == rows + first, delta, 0.0), axis=1, keepdims=True)
+    for m in range(2):
+        first = lax.rem(lax.axis_index("z") + m * (jsrc // 2), jsrc) * own
+        column = jnp.sum(jnp.where(lanes == rows + first, delta, 0.0), axis=1, keepdims=True)
+        delta_ref[m * own : (m + 1) * own, :] = column
     wsum = jnp.sum(total[6:7], axis=1, keepdims=True)
     wphi = jnp.sum(total[7:8], axis=1, keepdims=True)
     gw_ref[...] = -(every / wsum) * (phi_ref[...] - wphi / wsum)
@@ -353,10 +354,9 @@
             row_ref[t * GROUP + k] = term[k * own : (k + 1) * own]
 
 
-def total_up(own, rows_ref, keep_ref, got_ref, delta_ref, out_ref):
+def total_up(rows_ref, keep_ref, got_ref, out_ref):
     acc = jnp.sum(rows_ref[...].astype(F32), axis=0)
-    sums = keep_ref[...] + got_ref[...].astype(F32)
-    out_ref[...] = (acc + (sums[:own] + delta_ref[...] * sums[own:])).astype(BF16)
+    out_ref[...] = (acc + (keep_ref[...] + got_ref[...].astype(F32))).astype(BF16)
 
 
 def local(particles, cotangent, row_potential, col_potential, weights):
@@ -509,7 +509,7 @@
     row_send, gw, delta = call(
         functools.partial(finish_rows, own, width, isrc, float(isrc * jsrc * own)),
         4,
-        [((isrc, own, width), BF16), ((isrc, LANES), F32), ((own, 1), F32)],
+        [((isrc, own, width), BF16), ((isrc, LANES), F32), ((2 * own, 1), F32)],
         got,
         col,
         phi,
@@ -528,16 +528,15 @@
     keep, give = call(
         functools.partial(halve_across, own),
         1,
-        [((half // 4, width), F32), ((half // 4, width), BF16)],
+        [((own, width), F32), ((own, width), BF16)],
         keep,
         right,
         left,
+        delta,
     )
     taken = flip(give, 4)
     row_got = swap(row_send, iaxes)
-    (grad,) = call(
-        functools.partial(total_up, own), 1, [((own, width), BF16)], row_got, keep, taken, delta
-    )
+    (grad,) = call(total_up, 1, [((own, width), BF16)], row_got, keep, taken)
     mine = lax.axis_index("y") * xsrc + lax.axis_index("row")
     grad_weights = lax.dynamic_slice(gw, (mine, 0), (1, own)).reshape(own)
     return (grad, grad_weights)

time: 159 us -> 158 us (level)
  transfers between devices with their start and end apart: 13 -> 13, of which waited for: 11 -> 10; matrix products, arithmetic and copies ran while one was open for 0% -> 0% of each run, Pallas kernels for 3% -> 3%
where the time goes in v11:
time: 158 us; the launch traced here: 157 us
  blocking collectives  79.9 us (51%)
  starting transfers between devices  35.3 us (22%)
  waiting for transfers between devices  23.8 us (15%)
  Pallas kernels  16.6 us (11%)
    all_to_all x7, blocking collectives, swap(): return lax.all_to_all(value, axes, 0, 0, tiled=True)  79.9 us
    all_to_all x3, starting transfers between devices, swap(): return lax.all_to_all(value, axes, 0, 0, tiled=True)  17 us
    pallas_call x14, Pallas kernels, call(): pl.pallas_call(body, out_shape=[(pltpu.HBM if n in hbm else jax.ShapeDtyp...  16.6 us
    ppermute x8, starting transfers between devices, shift(): return lax.ppermute(value, axis, [(i, (i + k) % n) for i in range(n)])  14.9 us
    ppermute x8, waiting for transfers between devices, shift(): return lax.ppermute(value, axis, [(i, (i + k) % n) for i in range(n)])  10.1 us
    ppermute x2, waiting for transfers between devices, flip(): return lax.ppermute(value, 'z', [(i, i ^ bit) for i in range(jsrc)])  9.45 us
    all_to_all x3, waiting for transfers between devices, swap(): return lax.all_to_all(value, axes, 0, 0, tiled=True)  4.18 us
    ppermute x2, starting transfers between devices, flip(): return lax.ppermute(value, 'z', [(i, i ^ bit) for i in range(jsrc)])  3.42 us
  transfers between devices with their start and end apart: 13, of which 10 were waited for; matrix products, arithmetic and copies ran while one was open for 0% of the time, Pallas kernels for 3%

profile of v11, /device:TPU:8, one launch (start us, length us, event | category | flops | bytes accessed | tf_op | source)
XLA Modules:
  0.0 156.8 jit_solution(12311930976222742034)
XLA Ops:
  0.6 1.9 %shard_map.68 = (bf16[104,256]{1,0:T(8,128)(2,1)S(1)}, bf16[8,200,256]{2,1,0:T(8,128)(2,1)}) custom-call(bf16[96,256]{1,0:T(8,128)(2,1)} %x_ref.1, bf16[96,256]{1,0:T(8,128)(2,1)} %gy_ref.1, bf16[1,96]{1,0:T(2,128)(2,1)} %bitcast.5, bf16[1,96]{1,0:T(2,128)(2,1)} %bitcast.6, bf16[1,96]{1,0:T(2,128)(2,1)} %bitcast.7), custom_call_target="tpu_custom_call" | custom-call | flops 2000000000 | bytes 1024 | tf_op jit(solution)/shard_map/pallas_call | solution.py:380
  2.5 8.5 %all-to-all-start = ((bf16[8,200,256]{2,1,0:T(8,128)(2,1)}), bf16[8,200,256]{2,1,0:T(8,128)(2,1)S(1)}, u32[]{:S(2)}, u32[]{:S(2)}) async-start(bf16[8,200,256]{2,1,0:T(8,128)(2,1)} %get-tuple-element.37), calls=%async_computation | async-start | bytes 1638400 | tf_op jit(solution)/shard_map/all_to_all | solution.py:370
  11.0 1.5 collective-permute-start
  12.5 2.7 %collective-permute-start.1 = (bf16[104,256]{1,0:T(8,128)(2,1)S(1)}, bf16[104,256]{1,0:T(8,128)(2,1)S(1)}, u32[]{:S(2)}, u32[]{:S(2)}) collective-permute-start(bf16[104,256]{1,0:T(8,128)(2,1)S(1)} %get-tuple-element.36.refs_0_), channel_id=1, source_target_pairs={{0,64},{32,96},{64,0},{96,32},{1,65},{33,97},{65,1},{97,33},{2,66}... | collective-permute-start | bytes 159752 | tf_op jit(solution)/shard_map/ppermute | solution.py:374
  15.2 1.4 collective-permute-start.2
  16.7 0.3 collective-permute-done.refs_1_
  16.9 1.2 collective-permute-done.1.refs_2_
  18.1 1.2 collective-permute-done.2.refs_3_
  19.4 1.7 %collective-permute-start.3 = (bf16[416,256]{1,0:T(8,128)(2,1)S(1)}, bf16[416,256]{1,0:T(8,128)(2,1)S(1)}, u32[]{:S(2)}, u32[]{:S(2)}) collective-permute-start(bf16[416,256]{1,0:T(8,128)(2,1)S(1)} %shard_map.69.refs_0_), channel_id=1, source_target_pairs={{0,1},{1,2},{2,3},{3,0},{4,5},{5,6},{6,7},{7,4},{8,9},{9,10},{10,1... | collective-permute-start | bytes 638984 | tf_op jit(solution)/shard_map/ppermute | solution.py:374
  21.1 0.9 collective-permute-start.4
  22.0 2.4 %collective-permute-start.5 = (bf16[416,256]{1,0:T(8,128)(2,1)S(1)}, bf16[416,256]{1,0:T(8,128)(2,1)S(1)}, u32[]{:S(2)}, u32[]{:S(2)}) collective-permute-start(bf16[416,256]{1,0:T(8,128)(2,1)S(1)} %shard_map.69.refs_0_), channel_id=1, source_target_pairs={{0,3},{1,0},{2,1},{3,2},{4,7},{5,4},{6,5},{7,6},{8,11},{9,8},{10,9... | collective-permute-start | bytes 638984 | tf_op jit(solution)/shard_map/ppermute | solution.py:374
  24.4 3.0 %collective-permute-done.3.refs_1_ = bf16[416,256]{1,0:T(8,128)(2,1)S(1)} collective-permute-done((bf16[416,256]{1,0:T(8,128)(2,1)S(1)}, bf16[416,256]{1,0:T(8,128)(2,1)S(1)}, u32[]{:S(2)}, u32[]{:S(2)}) %collective-permute-start.3) | collective-permute-done | bytes 213024 | tf_op jit(solution)/shard_map/ppermute | solution.py:374
  27.4 2.9 %collective-permute-done.4.refs_2_ = bf16[416,256]{1,0:T(8,128)(2,1)S(1)} collective-permute-done((bf16[416,256]{1,0:T(8,128)(2,1)S(1)}, bf16[416,256]{1,0:T(8,128)(2,1)S(1)}, u32[]{:S(2)}, u32[]{:S(2)}) %collective-permute-start.4) | collective-permute-done | bytes 213024 | tf_op jit(solution)/shard_map/ppermute | solution.py:374
  30.4 1.5 collective-permute-done.5.refs_3_
  31.9 3.0 %all-to-all-done.refs_4_.refs_6_ = bf16[8,200,256]{2,1,0:T(8,128)(2,1)S(1)} async-done(((bf16[8,200,256]{2,1,0:T(8,128)(2,1)}), bf16[8,200,256]{2,1,0:T(8,128)(2,1)S(1)}, u32[]{:S(2)}, u32[]{:S(2)}) %all-to-all-start) | async-done | bytes 819232 | tf_op jit(solution)/shard_map/all_to_all | solution.py:370
  34.8 3.2 %shard_map.70 = (f32[1536,768]{1,0:T(8,128)S(1)}, f32[1536,768]{1,0:T(8,128)S(1)}, bf16[1536,256]{1,0:T(8,128)(2,1)S(1)}, f32[16,128]{1,0:T(8,128)S(1)}, f32[16,...) custom-call(bf16[416,256]{1,0:T(8,128)(2,1)S(1)} %shard_map.69.refs_0_, ...), custom_call_target="tpu_custom_call" | custom-call | flops 5000000000 | bytes 1024 | tf_op jit(solution)/shard_map/pallas_call | solution.py:380
  38.1 14.2 %all_to_all.50.got_ref = f32[16,32,128]{2,1,0:T(8,128)S(1)} all-to-all(f32[16,32,128]{2,1,0:T(8,128)S(1)} %get-tuple-element.38), channel_id=1, replica_groups=mesh['filt'=2,'row'=4,'z'=8,'y'=4] {'y','row'}, dimensions={0} | all-to-all | bytes 524288 | tf_op jit(solution)/shard_map/all_to_all | solution.py:370
  52.2 0.7 shard_map.71
  52.9 11.5 %all_to_all.51.got_ref = f32[8,24,128]{2,1,0:T(8,128)S(1)} all-to-all(f32[8,24,128]{2,1,0:T(8,128)S(1)} %get-tuple-element.41), channel_id=1, replica_groups=mesh['filt'=2,'row'=4,'z'=8,'y'=4] {'z'}, dimensions={0} | all-to-all | bytes 196608 | tf_op jit(solution)/shard_map/all_to_all | solution.py:370
  64.4 0.4 shard_map.72
  64.8 11.4 %all_to_all.52.got_ref = f32[16,16,128]{2,1,0:T(8,128)S(1)} all-to-all(f32[16,16,128]{2,1,0:T(8,128)S(1)} %get-tuple-element.42), channel_id=1, replica_groups=mesh['filt'=2,'row'=4,'z'=8,'y'=4] {'y','row'}, dimensions={0} | all-to-all | bytes 262144 | tf_op jit(solution)/shard_map/all_to_all | solution.py:370
  76.2 0.6 shard_map.73
  76.8 10.4 %all_to_all.53.got_ref = f32[8,8,128]{2,1,0:T(8,128)S(1)} all-to-all(f32[8,8,128]{2,1,0:T(8,128)S(1)} %get-tuple-element.45), channel_id=1, replica_groups=mesh['filt'=2,'row'=4,'z'=8,'y'=4] {'z'}, dimensions={0} | all-to-all | bytes 65536 | tf_op jit(solution)/shard_map/all_to_all | solution.py:370
  87.2 0.4 shard_map.74
  87.7 11.1 %all_to_all.54.got_ref = f32[16,16,128]{2,1,0:T(8,128)S(1)} all-to-all(f32[16,16,128]{2,1,0:T(8,128)S(1)} %shard_map.74), channel_id=1, replica_groups=mesh['filt'=2,'row'=4,'z'=8,'y'=4] {'y','row'}, dimensions={0} | all-to-all | bytes 262144 | tf_op jit(solution)/shard_map/all_to_all | solution.py:370
  98.7 0.6 shard_map.75
  99.4 10.4 %all_to_all.55.got_ref = f32[8,8,128]{2,1,0:T(8,128)S(1)} all-to-all(f32[8,8,128]{2,1,0:T(8,128)S(1)} %get-tuple-element.47), channel_id=1, replica_groups=mesh['filt'=2,'row'=4,'z'=8,'y'=4] {'z'}, dimensions={0} | all-to-all | bytes 65536 | tf_op jit(solution)/shard_map/all_to_all | solution.py:370
  109.8 0.4 shard_map.76
  110.2 11.1 %all_to_all.56.refs_0_ = f32[16,16,128]{2,1,0:T(8,128)S(1)} all-to-all(f32[16,16,128]{2,1,0:T(8,128)S(1)} %get-tuple-element.48), channel_id=1, replica_groups=mesh['filt'=2,'row'=4,'z'=8,'y'=4] {'y','row'}, dimensions={0} | all-to-all | bytes 262144 | tf_op jit(solution)/shard_map/all_to_all | solution.py:370
  121.3 3.1 %shard_map.77 = (f32[16,128]{1,0:T(8,128)S(1)}, f32[8,8,128]{2,1,0:T(8,128)}, bf16[768,256]{1,0:T(8,128)(2,1)S(1)}, bf16[768,256]{1,0:T(8,128)(2,1)S(1)}) custom-call(f32[16,16,128]{2,1,0:T(8,128)S(1)} %all_to_all.56.refs_0_, f32[32,128]{1,0:T(8,128)S(1)} %get-tuple-element.43.mass_ref.refs_1_, f32[16,128]{1,0:T(8,128)S(1)} %get-tuple-element.44.w_ref.refs_2_, ...), custom_call_target="tpu_custom_call" | custom-call | flops 4000000000 | bytes 1024 | tf_op jit(solution)/shard_map/pallas_call | solution.py:380
  124.4 0.7 collective-permute-start.6
  125.0 3.3 %all-to-all-start.8 = ((f32[8,8,128]{2,1,0:T(8,128)}), f32[8,8,128]{2,1,0:T(8,128)S(1)}, u32[]{:S(2)}, u32[]{:S(2)}) async-start(f32[8,8,128]{2,1,0:T(8,128)} %get-tuple-element.54), calls=%async_computation.8 | async-start | bytes 65536 | tf_op jit(solution)/shard_map/all_to_all | solution.py:370
  128.4 4.6 %collective-permute-done.6.got_ref = bf16[768,256]{1,0:T(8,128)(2,1)S(1)} collective-permute-done((bf16[768,256]{1,0:T(8,128)(2,1)S(1)}, bf16[768,256]{1,0:T(8,128)(2,1)S(1)}, u32[]{:S(2)}, u32[]{:S(2)}) %collective-permute-start.6) | collective-permute-done | bytes 393248 | tf_op jit(solution)/shard_map/ppermute | solution.py:377
  133.0 0.1 shard_map.78
  133.0 0.8 collective-permute-start.7
  133.9 3.4 %collective-permute-start.8 = (bf16[192,256]{1,0:T(8,128)(2,1)S(1)}, bf16[192,256]{1,0:T(8,128)(2,1)S(1)}, u32[]{:S(2)}, u32[]{:S(2)}) collective-permute-start(bf16[192,256]{1,0:T(8,128)(2,1)S(1)} %get-tuple-element.62), channel_id=1, source_target_pairs={{0,24},{4,28},{8,0},{12,4},{16,8},{20,12},{24,16},{28,20},{1,25},{... | collective-permute-start | bytes 294920 | tf_op jit(solution)/shard_map/ppermute | solution.py:374
  137.3 0.0 all-to-all-done.8.refs_0_
  137.3 4.2 %shard_map.79 = (bf16[16,96,256]{2,1,0:T(8,128)(2,1)}, f32[16,128]{1,0:T(8,128)S(1)}, f32[192,1]{1,0:T(8,128)S(1)}) custom-call(f32[8,8,128]{2,1,0:T(8,128)S(1)} %all-to-all-done.8.refs_0_, f32[16,128]{1,0:T(8,128)S(1)} %get-tuple-element.46.col_ref.refs_1_, f32[16,128]{1,0:T(8,128)S(1)} %get-tuple-element.55.refs_2_, ...), custom_call_target="tpu_custom_call" | custom-call | flops 4000000000 | bytes 1024 | tf_op jit(solution)/shard_map/pallas_call | solution.py:380
  141.5 0.0 collective-permute-done.7.right_ref
  141.5 0.0 collective-permute-done.8.left_ref
  141.5 5.2 %all-to-all-start.9 = ((bf16[16,96,256]{2,1,0:T(8,128)(2,1)}), bf16[16,96,256]{2,1,0:T(8,128)(2,1)S(1)}, u32[]{:S(2)}, u32[]{:S(2)}) async-start(bf16[16,96,256]{2,1,0:T(8,128)(2,1)} %get-tuple-element.63), calls=%async_computation.9 | async-start | bytes 1572864 | tf_op jit(solution)/shard_map/all_to_all | solution.py:370
  146.7 0.1 shard_map.80
  146.8 2.8 %collective-permute-start.9 = (bf16[96,256]{1,0:T(8,128)(2,1)S(1)}, bf16[96,256]{1,0:T(8,128)(2,1)S(1)}, u32[]{:S(2)}, u32[]{:S(2)}) collective-permute-start(bf16[96,256]{1,0:T(8,128)(2,1)S(1)} %get-tuple-element.68), channel_id=1, source_target_pairs={{0,16},{4,20},{8,24},{12,28},{16,0},{20,4},{24,8},{28,12},{1,17},{... | collective-permute-start | bytes 147464 | tf_op jit(solution)/shard_map/ppermute | solution.py:377
  149.5 0.5 dynamic-slice_bitcast_fusion
  150.0 4.8 %collective-permute-done.9.got_ref = bf16[96,256]{1,0:T(8,128)(2,1)S(1)} collective-permute-done((bf16[96,256]{1,0:T(8,128)(2,1)S(1)}, bf16[96,256]{1,0:T(8,128)(2,1)S(1)}, u32[]{:S(2)}, u32[]{:S(2)}) %collective-permute-start.9) | collective-permute-done | bytes 49184 | tf_op jit(solution)/shard_map/ppermute | solution.py:377
  154.9 1.2 all-to-all-done.9.rows_ref
  156.1 0.7 shard_map.81
  (1 shorter events, 0.0 us)
Async XLA Ops:
  2.5 32.3 %all-to-all-start = ((bf16[8,200,256]{2,1,0:T(8,128)(2,1)}), bf16[8,200,256]{2,1,0:T(8,128)(2,1)S(1)}, u32[]{:S(2)}, u32[]{:S(2)}) async-start(bf16[8,200,256]{2,1,0:T(8,128)(2,1)} %get-tuple-element.37), calls=%async_computation | async-start | bytes 1638400 | tf_op jit(solution)/shard_map/all_to_all | solution.py:370
  11.0 5.9 %collective-permute-start = (bf16[104,256]{1,0:T(8,128)(2,1)S(1)}, bf16[104,256]{1,0:T(8,128)(2,1)S(1)}, u32[]{:S(2)}, u32[]{:S(2)}) collective-permute-start(bf16[104,256]{1,0:T(8,128)(2,1)S(1)} %get-tuple-element.36.refs_0_), channel_id=1, source_target_pairs={{0,32},{32,64},{64,96},{96,0},{1,33},{33,65},{65,97},{97,1},{2,34}... | collective-permute-start | bytes 159752 | tf_op jit(solution)/shard_map/ppermute | solution.py:374
  12.5 5.6 %collective-permute-start.1 = (bf16[104,256]{1,0:T(8,128)(2,1)S(1)}, bf16[104,256]{1,0:T(8,128)(2,1)S(1)}, u32[]{:S(2)}, u32[]{:S(2)}) collective-permute-start(bf16[104,256]{1,0:T(8,128)(2,1)S(1)} %get-tuple-element.36.refs_0_), channel_id=1, source_target_pairs={{0,64},{32,96},{64,0},{96,32},{1,65},{33,97},{65,1},{97,33},{2,66}... | collective-permute-start | bytes 159752 | tf_op jit(solution)/shard_map/ppermute | solution.py:374
  15.2 4.1 %collective-permute-start.2 = (bf16[104,256]{1,0:T(8,128)(2,1)S(1)}, bf16[104,256]{1,0:T(8,128)(2,1)S(1)}, u32[]{:S(2)}, u32[]{:S(2)}) collective-permute-start(bf16[104,256]{1,0:T(8,128)(2,1)S(1)} %get-tuple-element.36.refs_0_), channel_id=1, source_target_pairs={{0,96},{32,0},{64,32},{96,64},{1,97},{33,1},{65,33},{97,65},{2,98}... | collective-permute-start | bytes 159752 | tf_op jit(solution)/shard_map/ppermute | solution.py:374
  19.4 8.0 %collective-permute-start.3 = (bf16[416,256]{1,0:T(8,128)(2,1)S(1)}, bf16[416,256]{1,0:T(8,128)(2,1)S(1)}, u32[]{:S(2)}, u32[]{:S(2)}) collective-permute-start(bf16[416,256]{1,0:T(8,128)(2,1)S(1)} %shard_map.69.refs_0_), channel_id=1, source_target_pairs={{0,1},{1,2},{2,3},{3,0},{4,5},{5,6},{6,7},{7,4},{8,9},{9,10},{10,1... | collective-permute-start | bytes 638984 | tf_op jit(solution)/shard_map/ppermute | solution.py:374
  21.1 9.3 %collective-permute-start.4 = (bf16[416,256]{1,0:T(8,128)(2,1)S(1)}, bf16[416,256]{1,0:T(8,128)(2,1)S(1)}, u32[]{:S(2)}, u32[]{:S(2)}) collective-permute-start(bf16[416,256]{1,0:T(8,128)(2,1)S(1)} %shard_map.69.refs_0_), channel_id=1, source_target_pairs={{0,2},{1,3},{2,0},{3,1},{4,6},{5,7},{6,4},{7,5},{8,10},{9,11},{10,... | collective-permute-start | bytes 638984 | tf_op jit(solution)/shard_map/ppermute | solution.py:374
  22.0 9.9 %collective-permute-start.5 = (bf16[416,256]{1,0:T(8,128)(2,1)S(1)}, bf16[416,256]{1,0:T(8,128)(2,1)S(1)}, u32[]{:S(2)}, u32[]{:S(2)}) collective-permute-start(bf16[416,256]{1,0:T(8,128)(2,1)S(1)} %shard_map.69.refs_0_), channel_id=1, source_target_pairs={{0,3},{1,0},{2,1},{3,2},{4,7},{5,4},{6,5},{7,6},{8,11},{9,8},{10,9... | collective-permute-start | bytes 638984 | tf_op jit(solution)/shard_map/ppermute | solution.py:374
  124.4 8.6 %collective-permute-start.6 = (bf16[768,256]{1,0:T(8,128)(2,1)S(1)}, bf16[768,256]{1,0:T(8,128)(2,1)S(1)}, u32[]{:S(2)}, u32[]{:S(2)}) collective-permute-start(bf16[768,256]{1,0:T(8,128)(2,1)S(1)} %get-tuple-element.58), channel_id=1, source_target_pairs={{0,4},{4,0},{8,12},{12,8},{16,20},{20,16},{24,28},{28,24},{1,5},{5... | collective-permute-start | bytes 1179656 | tf_op jit(solution)/shard_map/ppermute | solution.py:377
  125.0 12.3 %all-to-all-start.8 = ((f32[8,8,128]{2,1,0:T(8,128)}), f32[8,8,128]{2,1,0:T(8,128)S(1)}, u32[]{:S(2)}, u32[]{:S(2)}) async-start(f32[8,8,128]{2,1,0:T(8,128)} %get-tuple-element.54), calls=%async_computation.8 | async-start | bytes 65536 | tf_op jit(solution)/shard_map/all_to_all | solution.py:370
  133.0 8.4 %collective-permute-start.7 = (bf16[192,256]{1,0:T(8,128)(2,1)S(1)}, bf16[192,256]{1,0:T(8,128)(2,1)S(1)}, u32[]{:S(2)}, u32[]{:S(2)}) collective-permute-start(bf16[192,256]{1,0:T(8,128)(2,1)S(1)} %get-tuple-element.61), channel_id=1, source_target_pairs={{0,8},{4,12},{8,16},{12,20},{16,24},{20,28},{24,0},{28,4},{1,9},{5... | collective-permute-start | bytes 294920 | tf_op jit(solution)/shard_map/ppermute | solution.py:374
  133.9 7.6 %collective-permute-start.8 = (bf16[192,256]{1,0:T(8,128)(2,1)S(1)}, bf16[192,256]{1,0:T(8,128)(2,1)S(1)}, u32[]{:S(2)}, u32[]{:S(2)}) collective-permute-start(bf16[192,256]{1,0:T(8,128)(2,1)S(1)} %get-tuple-element.62), channel_id=1, source_target_pairs={{0,24},{4,28},{8,0},{12,4},{16,8},{20,12},{24,16},{28,20},{1,25},{... | collective-permute-start | bytes 294920 | tf_op jit(solution)/shard_map/ppermute | solution.py:374
  141.5 14.6 %all-to-all-start.9 = ((bf16[16,96,256]{2,1,0:T(8,128)(2,1)}), bf16[16,96,256]{2,1,0:T(8,128)(2,1)S(1)}, u32[]{:S(2)}, u32[]{:S(2)}) async-start(bf16[16,96,256]{2,1,0:T(8,128)(2,1)} %get-tuple-element.63), calls=%async_computation.9 | async-start | bytes 1572864 | tf_op jit(solution)/shard_map/all_to_all | solution.py:370
  146.8 8.1 %collective-permute-start.9 = (bf16[96,256]{1,0:T(8,128)(2,1)S(1)}, bf16[96,256]{1,0:T(8,128)(2,1)S(1)}, u32[]{:S(2)}, u32[]{:S(2)}) collective-permute-start(bf16[96,256]{1,0:T(8,128)(2,1)S(1)} %get-tuple-element.68), channel_id=1, source_target_pairs={{0,16},{4,20},{8,24},{12,28},{16,0},{20,4},{24,8},{28,12},{1,17},{... | collective-permute-start | bytes 147464 | tf_op jit(solution)/shard_map/ppermute | solution.py:377

commit v12 on v11

--- a/solution.py
+++ b/solution.py
@@ -67,28 +67,29 @@
             ref[s, base + k : base + k + 1, :] = piece
 
 
-def pack(own, width, jsrc, x_ref, gy_ref, f_ref, g_ref, w_ref, ipack_ref, jpack_ref, block_ref, line_ref, vec_ref, in_sem, out_sem):
-    copies = [
-        pltpu.make_async_copy(f_ref, vec_ref.at[0], in_sem.at[2]),
-        pltpu.make_async_copy(w_ref, vec_ref.at[1], in_sem.at[3]),
-        pltpu.make_async_copy(g_ref, vec_ref.at[2], in_sem.at[4]),
-        pltpu.make_async_copy(x_ref, block_ref.at[pl.ds(0, own)], in_sem.at[0]),
-        pltpu.make_async_copy(gy_ref, block_ref.at[pl.ds(own, own)], in_sem.at[1]),
-    ]
-    for copy in copies:
+def pack(own, width, jsrc, x_ref, gy_ref, f_ref, g_ref, w_ref, ipack_ref, jpack_ref, line_ref, vec_ref, aux_ref, in_sem, out_sem):
+    vectors = [pltpu.make_async_copy(ref, vec_ref.at[n], in_sem.at[n]) for n, ref in enumerate((g_ref, f_ref, w_ref))]
+    mine = pltpu.make_async_copy(x_ref, ipack_ref.at[pl.ds(0, own)], in_sem.at[3])
+    for copy in vectors:
         copy.start()
+    outs = []
+    for s in range(jsrc):
+        for n, ref in enumerate((x_ref, gy_ref)):
+            outs.append(pltpu.make_async_copy(ref, jpack_ref.at[s, pl.ds(n * own, own)], out_sem.at[3 * s + n]))
+            outs[-1].start()
+    mine.start()
     line_ref[...] = jnp.zeros_like(line_ref)
-    for copy in copies:
+    for copy in vectors:
         copy.wait()
     line_ref[0, 0:1, 0:own] = vec_ref[0].astype(F32)
-    line_ref[0, 1:2, 0:own] = vec_ref[1].astype(F32)
-    line_ref[1, 0:1, 0:own] = vec_ref[2].astype(F32)
-    block_ref[2 * own : 2 * own + AUX, :] = line_ref[1].astype(BF16)
-    outs = [pltpu.make_async_copy(block_ref, jpack_ref.at[s], out_sem.at[s]) for s in range(jsrc)]
-    for copy in outs:
-        copy.start()
-    ipack_ref[0:own, :] = block_ref[0:own, :]
-    ipack_ref[own : own + AUX, :] = line_ref[0].astype(BF16)
+    aux_ref[...] = line_ref[0].astype(BF16)
+    for s in range(jsrc):
+        outs.append(pltpu.make_async_copy(aux_ref, jpack_ref.at[s, pl.ds(2 * own, AUX)], out_sem.at[3 * s + 2]))
+        outs[-1].start()
+    line_ref[1, 0:1, 0:own] = vec_ref[1].astype(F32)
+    line_ref[1, 1:2, 0:own] = vec_ref[2].astype(F32)
+    ipack_ref[own : own + AUX, :] = line_ref[1].astype(BF16)
+    mine.wait()
     for copy in outs:
         copy.wait()
 
@@ -403,11 +404,11 @@
             )
         ],
         scratch=[
-            pltpu.VMEM((2 * own + AUX, width), BF16),
             pltpu.VMEM((2, AUX, width), F32),
             pltpu.VMEM((3, 1, own), BF16),
-            pltpu.SemaphoreType.DMA((5,)),
-            pltpu.SemaphoreType.DMA((jsrc,)),
+            pltpu.VMEM((AUX, width), BF16),
+            pltpu.SemaphoreType.DMA((4,)),
+            pltpu.SemaphoreType.DMA((3 * jsrc,)),
         ],
         in_specs=[anywhere] * 5,
         out_specs=whole(1) + [anywhere],

time: 158 us -> 182 us (1.15)
  Pallas kernels: 16.6 us -> 39.9 us
    pallas_call x14, Pallas kernels: 16.6 us -> 39.9 us  [call(): pl.pallas_call(body, out_shape=[(pltpu.HBM if n in hbm else jax.ShapeDtyp...]
  transfers between devices with their start and end apart: 13 -> 13, of which waited for: 10 -> 10; matrix products, arithmetic and copies ran while one was open for 0% -> 0% of each run, Pallas kernels for 3% -> 2%
where the time goes in v12:
time: 182 us; the launch traced here: 180 us
  blocking collectives  79.9 us (44%)
  Pallas kernels  39.9 us (22%)
  starting transfers between devices  35.3 us (19%)
  waiting for transfers between devices  23.8 us (13%)
    all_to_all x7, blocking collectives, swap(): return lax.all_to_all(value, axes, 0, 0, tiled=True)  79.9 us
    pallas_call x14, Pallas kernels, call(): pl.pallas_call(body, out_shape=[(pltpu.HBM if n in hbm else jax.ShapeDtyp...  39.9 us
    all_to_all x3, starting transfers between devices, swap(): return lax.all_to_all(value, axes, 0, 0, tiled=True)  17 us
    ppermute x8, starting transfers between devices, shift(): return lax.ppermute(value, axis, [(i, (i + k) % n) for i in range(n)])  14.9 us
    ppermute x8, waiting for transfers between devices, shift(): return lax.ppermute(value, axis, [(i, (i + k) % n) for i in range(n)])  10.1 us
    ppermute x2, waiting for transfers between devices, flip(): return lax.ppermute(value, 'z', [(i, i ^ bit) for i in range(jsrc)])  9.42 us
    all_to_all x3, waiting for transfers between devices, swap(): return lax.all_to_all(value, axes, 0, 0, tiled=True)  4.18 us
  transfers between devices with their start and end apart: 13, of which 10 were waited for; matrix products, arithmetic and copies ran while one was open for 0% of the time, Pallas kernels for 2%

profile of v12, /device:TPU:8, one launch (start us, length us, event | category | flops | bytes accessed | tf_op | source)
XLA Modules:
  0.0 180.1 jit_solution(8029950812915208375)
XLA Ops:
  0.6 25.2 %shard_map.68 = (bf16[104,256]{1,0:T(8,128)(2,1)S(1)}, bf16[8,200,256]{2,1,0:T(8,128)(2,1)}) custom-call(bf16[96,256]{1,0:T(8,128)(2,1)} %x_ref.1, bf16[96,256]{1,0:T(8,128)(2,1)} %gy_ref.1, bf16[1,96]{1,0:T(2,128)(2,1)} %bitcast.5, bf16[1,96]{1,0:T(2,128)(2,1)} %bitcast.6, bf16[1,96]{1,0:T(2,128)(2,1)} %bitcast.7), custom_call_target="tpu_custom_call" | custom-call | flops 2000000000 | bytes 1024 | tf_op jit(solution)/shard_map/pallas_call | solution.py:381
  25.8 8.5 %all-to-all-start = ((bf16[8,200,256]{2,1,0:T(8,128)(2,1)}), bf16[8,200,256]{2,1,0:T(8,128)(2,1)S(1)}, u32[]{:S(2)}, u32[]{:S(2)}) async-start(bf16[8,200,256]{2,1,0:T(8,128)(2,1)} %get-tuple-element.37), calls=%async_computation | async-start | bytes 1638400 | tf_op jit(solution)/shard_map/all_to_all | solution.py:371
  34.3 1.5 collective-permute-start
  35.8 2.7 %collective-permute-start.1 = (bf16[104,256]{1,0:T(8,128)(2,1)S(1)}, bf16[104,256]{1,0:T(8,128)(2,1)S(1)}, u32[]{:S(2)}, u32[]{:S(2)}) collective-permute-start(bf16[104,256]{1,0:T(8,128)(2,1)S(1)} %get-tuple-element.36.refs_0_), channel_id=1, source_target_pairs={{0,64},{32,96},{64,0},{96,32},{1,65},{33,97},{65,1},{97,33},{2,66}... | collective-permute-start | bytes 159752 | tf_op jit(solution)/shard_map/ppermute | solution.py:375
  38.5 1.4 collective-permute-start.2
  40.0 0.3 collective-permute-done.refs_1_
  40.2 1.2 collective-permute-done.1.refs_2_
  41.4 1.2 collective-permute-done.2.refs_3_
  42.7 1.7 collective-permute-start.3
  44.4 0.9 collective-permute-start.4
  45.3 2.4 %collective-permute-start.5 = (bf16[416,256]{1,0:T(8,128)(2,1)S(1)}, bf16[416,256]{1,0:T(8,128)(2,1)S(1)}, u32[]{:S(2)}, u32[]{:S(2)}) collective-permute-start(bf16[416,256]{1,0:T(8,128)(2,1)S(1)} %shard_map.69.refs_0_), channel_id=1, source_target_pairs={{0,3},{1,0},{2,1},{3,2},{4,7},{5,4},{6,5},{7,6},{8,11},{9,8},{10,9... | collective-permute-start | bytes 638984 | tf_op jit(solution)/shard_map/ppermute | solution.py:375
  47.7 3.0 %collective-permute-done.3.refs_1_ = bf16[416,256]{1,0:T(8,128)(2,1)S(1)} collective-permute-done((bf16[416,256]{1,0:T(8,128)(2,1)S(1)}, bf16[416,256]{1,0:T(8,128)(2,1)S(1)}, u32[]{:S(2)}, u32[]{:S(2)}) %collective-permute-start.3) | collective-permute-done | bytes 213024 | tf_op jit(solution)/shard_map/ppermute | solution.py:375
  50.7 2.9 %collective-permute-done.4.refs_2_ = bf16[416,256]{1,0:T(8,128)(2,1)S(1)} collective-permute-done((bf16[416,256]{1,0:T(8,128)(2,1)S(1)}, bf16[416,256]{1,0:T(8,128)(2,1)S(1)}, u32[]{:S(2)}, u32[]{:S(2)}) %collective-permute-start.4) | collective-permute-done | bytes 213024 | tf_op jit(solution)/shard_map/ppermute | solution.py:375
  53.6 1.5 collective-permute-done.5.refs_3_
  55.1 3.0 %all-to-all-done.refs_4_.refs_6_ = bf16[8,200,256]{2,1,0:T(8,128)(2,1)S(1)} async-done(((bf16[8,200,256]{2,1,0:T(8,128)(2,1)}), bf16[8,200,256]{2,1,0:T(8,128)(2,1)S(1)}, u32[]{:S(2)}, u32[]{:S(2)}) %all-to-all-start) | async-done | bytes 819232 | tf_op jit(solution)/shard_map/all_to_all | solution.py:371
  58.1 3.2 %shard_map.70 = (f32[1536,768]{1,0:T(8,128)S(1)}, f32[1536,768]{1,0:T(8,128)S(1)}, bf16[1536,256]{1,0:T(8,128)(2,1)S(1)}, f32[16,128]{1,0:T(8,128)S(1)}, f32[16,...) custom-call(bf16[416,256]{1,0:T(8,128)(2,1)S(1)} %shard_map.69.refs_0_, ...), custom_call_target="tpu_custom_call" | custom-call | flops 5000000000 | bytes 1024 | tf_op jit(solution)/shard_map/pallas_call | solution.py:381
  61.4 14.2 %all_to_all.50.got_ref = f32[16,32,128]{2,1,0:T(8,128)S(1)} all-to-all(f32[16,32,128]{2,1,0:T(8,128)S(1)} %get-tuple-element.38), channel_id=1, replica_groups=mesh['filt'=2,'row'=4,'z'=8,'y'=4] {'y','row'}, dimensions={0} | all-to-all | bytes 524288 | tf_op jit(solution)/shard_map/all_to_all | solution.py:371
  75.5 0.7 shard_map.71
  76.2 11.5 %all_to_all.51.got_ref = f32[8,24,128]{2,1,0:T(8,128)S(1)} all-to-all(f32[8,24,128]{2,1,0:T(8,128)S(1)} %get-tuple-element.41), channel_id=1, replica_groups=mesh['filt'=2,'row'=4,'z'=8,'y'=4] {'z'}, dimensions={0} | all-to-all | bytes 196608 | tf_op jit(solution)/shard_map/all_to_all | solution.py:371
  87.7 0.4 shard_map.72
  88.1 11.4 %all_to_all.52.got_ref = f32[16,16,128]{2,1,0:T(8,128)S(1)} all-to-all(f32[16,16,128]{2,1,0:T(8,128)S(1)} %get-tuple-element.42), channel_id=1, replica_groups=mesh['filt'=2,'row'=4,'z'=8,'y'=4] {'y','row'}, dimensions={0} | all-to-all | bytes 262144 | tf_op jit(solution)/shard_map/all_to_all | solution.py:371
  99.5 0.6 shard_map.73
  100.1 10.4 %all_to_all.53.got_ref = f32[8,8,128]{2,1,0:T(8,128)S(1)} all-to-all(f32[8,8,128]{2,1,0:T(8,128)S(1)} %get-tuple-element.45), channel_id=1, replica_groups=mesh['filt'=2,'row'=4,'z'=8,'y'=4] {'z'}, dimensions={0} | all-to-all | bytes 65536 | tf_op jit(solution)/shard_map/all_to_all | solution.py:371
  110.5 0.4 shard_map.74
  111.0 11.1 %all_to_all.54.got_ref = f32[16,16,128]{2,1,0:T(8,128)S(1)} all-to-all(f32[16,16,128]{2,1,0:T(8,128)S(1)} %shard_map.74), channel_id=1, replica_groups=mesh['filt'=2,'row'=4,'z'=8,'y'=4] {'y','row'}, dimensions={0} | all-to-all | bytes 262144 | tf_op jit(solution)/shard_map/all_to_all | solution.py:371
  122.0 0.6 shard_map.75
  122.7 10.4 %all_to_all.55.got_ref = f32[8,8,128]{2,1,0:T(8,128)S(1)} all-to-all(f32[8,8,128]{2,1,0:T(8,128)S(1)} %get-tuple-element.47), channel_id=1, replica_groups=mesh['filt'=2,'row'=4,'z'=8,'y'=4] {'z'}, dimensions={0} | all-to-all | bytes 65536 | tf_op jit(solution)/shard_map/all_to_all | solution.py:371
  133.1 0.4 shard_map.76
  133.5 11.1 %all_to_all.56.refs_0_ = f32[16,16,128]{2,1,0:T(8,128)S(1)} all-to-all(f32[16,16,128]{2,1,0:T(8,128)S(1)} %get-tuple-element.48), channel_id=1, replica_groups=mesh['filt'=2,'row'=4,'z'=8,'y'=4] {'y','row'}, dimensions={0} | all-to-all | bytes 262144 | tf_op jit(solution)/shard_map/all_to_all | solution.py:371
  144.6 3.1 %shard_map.77 = (f32[16,128]{1,0:T(8,128)S(1)}, f32[8,8,128]{2,1,0:T(8,128)}, bf16[768,256]{1,0:T(8,128)(2,1)S(1)}, bf16[768,256]{1,0:T(8,128)(2,1)S(1)}) custom-call(f32[16,16,128]{2,1,0:T(8,128)S(1)} %all_to_all.56.refs_0_, f32[32,128]{1,0:T(8,128)S(1)} %get-tuple-element.43.mass_ref.refs_1_, f32[16,128]{1,0:T(8,128)S(1)} %get-tuple-element.44.w_ref.refs_2_, ...), custom_call_target="tpu_custom_call" | custom-call | flops 4000000000 | bytes 1024 | tf_op jit(solution)/shard_map/pallas_call | solution.py:381
  147.6 0.7 collective-permute-start.6
  148.3 3.3 %all-to-all-start.8 = ((f32[8,8,128]{2,1,0:T(8,128)}), f32[8,8,128]{2,1,0:T(8,128)S(1)}, u32[]{:S(2)}, u32[]{:S(2)}) async-start(f32[8,8,128]{2,1,0:T(8,128)} %get-tuple-element.54), calls=%async_computation.8 | async-start | bytes 65536 | tf_op jit(solution)/shard_map/all_to_all | solution.py:371
  151.7 4.6 %collective-permute-done.6.got_ref = bf16[768,256]{1,0:T(8,128)(2,1)S(1)} collective-permute-done((bf16[768,256]{1,0:T(8,128)(2,1)S(1)}, bf16[768,256]{1,0:T(8,128)(2,1)S(1)}, u32[]{:S(2)}, u32[]{:S(2)}) %collective-permute-start.6) | collective-permute-done | bytes 393248 | tf_op jit(solution)/shard_map/ppermute | solution.py:378
  156.2 0.1 shard_map.78
  156.3 0.8 collective-permute-start.7
  157.2 3.4 %collective-permute-start.8 = (bf16[192,256]{1,0:T(8,128)(2,1)S(1)}, bf16[192,256]{1,0:T(8,128)(2,1)S(1)}, u32[]{:S(2)}, u32[]{:S(2)}) collective-permute-start(bf16[192,256]{1,0:T(8,128)(2,1)S(1)} %get-tuple-element.62), channel_id=1, source_target_pairs={{0,24},{4,28},{8,0},{12,4},{16,8},{20,12},{24,16},{28,20},{1,25},{... | collective-permute-start | bytes 294920 | tf_op jit(solution)/shard_map/ppermute | solution.py:375
  160.5 0.0 all-to-all-done.8.refs_0_
  160.5 4.2 %shard_map.79 = (bf16[16,96,256]{2,1,0:T(8,128)(2,1)}, f32[16,128]{1,0:T(8,128)S(1)}, f32[192,1]{1,0:T(8,128)S(1)}) custom-call(f32[8,8,128]{2,1,0:T(8,128)S(1)} %all-to-all-done.8.refs_0_, f32[16,128]{1,0:T(8,128)S(1)} %get-tuple-element.46.col_ref.refs_1_, f32[16,128]{1,0:T(8,128)S(1)} %get-tuple-element.55.refs_2_, ...), custom_call_target="tpu_custom_call" | custom-call | flops 4000000000 | bytes 1024 | tf_op jit(solution)/shard_map/pallas_call | solution.py:381
  164.7 0.0 collective-permute-done.7.right_ref
  164.7 0.0 collective-permute-done.8.left_ref
  164.7 5.2 %all-to-all-start.9 = ((bf16[16,96,256]{2,1,0:T(8,128)(2,1)}), bf16[16,96,256]{2,1,0:T(8,128)(2,1)S(1)}, u32[]{:S(2)}, u32[]{:S(2)}) async-start(bf16[16,96,256]{2,1,0:T(8,128)(2,1)} %get-tuple-element.63), calls=%async_computation.9 | async-start | bytes 1572864 | tf_op jit(solution)/shard_map/all_to_all | solution.py:371
  169.9 0.1 shard_map.80
  170.0 2.8 %collective-permute-start.9 = (bf16[96,256]{1,0:T(8,128)(2,1)S(1)}, bf16[96,256]{1,0:T(8,128)(2,1)S(1)}, u32[]{:S(2)}, u32[]{:S(2)}) collective-permute-start(bf16[96,256]{1,0:T(8,128)(2,1)S(1)} %get-tuple-element.68), channel_id=1, source_target_pairs={{0,16},{4,20},{8,24},{12,28},{16,0},{20,4},{24,8},{28,12},{1,17},{... | collective-permute-start | bytes 147464 | tf_op jit(solution)/shard_map/ppermute | solution.py:378
  172.8 0.5 dynamic-slice_bitcast_fusion
  173.3 4.8 %collective-permute-done.9.got_ref = bf16[96,256]{1,0:T(8,128)(2,1)S(1)} collective-permute-done((bf16[96,256]{1,0:T(8,128)(2,1)S(1)}, bf16[96,256]{1,0:T(8,128)(2,1)S(1)}, u32[]{:S(2)}, u32[]{:S(2)}) %collective-permute-start.9) | collective-permute-done | bytes 49184 | tf_op jit(solution)/shard_map/ppermute | solution.py:378
  178.2 1.2 all-to-all-done.9.rows_ref
  179.4 0.7 shard_map.81
  (1 shorter events, 0.0 us)
Async XLA Ops:
  25.8 32.3 %all-to-all-start = ((bf16[8,200,256]{2,1,0:T(8,128)(2,1)}), bf16[8,200,256]{2,1,0:T(8,128)(2,1)S(1)}, u32[]{:S(2)}, u32[]{:S(2)}) async-start(bf16[8,200,256]{2,1,0:T(8,128)(2,1)} %get-tuple-element.37), calls=%async_computation | async-start | bytes 1638400 | tf_op jit(solution)/shard_map/all_to_all | solution.py:371
  34.3 5.9 %collective-permute-start = (bf16[104,256]{1,0:T(8,128)(2,1)S(1)}, bf16[104,256]{1,0:T(8,128)(2,1)S(1)}, u32[]{:S(2)}, u32[]{:S(2)}) collective-permute-start(bf16[104,256]{1,0:T(8,128)(2,1)S(1)} %get-tuple-element.36.refs_0_), channel_id=1, source_target_pairs={{0,32},{32,64},{64,96},{96,0},{1,33},{33,65},{65,97},{97,1},{2,34}... | collective-permute-start | bytes 159752 | tf_op jit(solution)/shard_map/ppermute | solution.py:375
  35.8 5.6 %collective-permute-start.1 = (bf16[104,256]{1,0:T(8,128)(2,1)S(1)}, bf16[104,256]{1,0:T(8,128)(2,1)S(1)}, u32[]{:S(2)}, u32[]{:S(2)}) collective-permute-start(bf16[104,256]{1,0:T(8,128)(2,1)S(1)} %get-tuple-element.36.refs_0_), channel_id=1, source_target_pairs={{0,64},{32,96},{64,0},{96,32},{1,65},{33,97},{65,1},{97,33},{2,66}... | collective-permute-start | bytes 159752 | tf_op jit(solution)/shard_map/ppermute | solution.py:375
  38.5 4.1 %collective-permute-start.2 = (bf16[104,256]{1,0:T(8,128)(2,1)S(1)}, bf16[104,256]{1,0:T(8,128)(2,1)S(1)}, u32[]{:S(2)}, u32[]{:S(2)}) collective-permute-start(bf16[104,256]{1,0:T(8,128)(2,1)S(1)} %get-tuple-element.36.refs_0_), channel_id=1, source_target_pairs={{0,96},{32,0},{64,32},{96,64},{1,97},{33,1},{65,33},{97,65},{2,98}... | collective-permute-start | bytes 159752 | tf_op jit(solution)/shard_map/ppermute | solution.py:375
  42.7 8.0 %collective-permute-start.3 = (bf16[416,256]{1,0:T(8,128)(2,1)S(1)}, bf16[416,256]{1,0:T(8,128)(2,1)S(1)}, u32[]{:S(2)}, u32[]{:S(2)}) collective-permute-start(bf16[416,256]{1,0:T(8,128)(2,1)S(1)} %shard_map.69.refs_0_), channel_id=1, source_target_pairs={{0,1},{1,2},{2,3},{3,0},{4,5},{5,6},{6,7},{7,4},{8,9},{9,10},{10,1... | collective-permute-start | bytes 638984 | tf_op jit(solution)/shard_map/ppermute | solution.py:375
  44.4 9.3 %collective-permute-start.4 = (bf16[416,256]{1,0:T(8,128)(2,1)S(1)}, bf16[416,256]{1,0:T(8,128)(2,1)S(1)}, u32[]{:S(2)}, u32[]{:S(2)}) collective-permute-start(bf16[416,256]{1,0:T(8,128)(2,1)S(1)} %shard_map.69.refs_0_), channel_id=1, source_target_pairs={{0,2},{1,3},{2,0},{3,1},{4,6},{5,7},{6,4},{7,5},{8,10},{9,11},{10,... | collective-permute-start | bytes 638984 | tf_op jit(solution)/shard_map/ppermute | solution.py:375
  45.3 9.9 %collective-permute-start.5 = (bf16[416,256]{1,0:T(8,128)(2,1)S(1)}, bf16[416,256]{1,0:T(8,128)(2,1)S(1)}, u32[]{:S(2)}, u32[]{:S(2)}) collective-permute-start(bf16[416,256]{1,0:T(8,128)(2,1)S(1)} %shard_map.69.refs_0_), channel_id=1, source_target_pairs={{0,3},{1,0},{2,1},{3,2},{4,7},{5,4},{6,5},{7,6},{8,11},{9,8},{10,9... | collective-permute-start | bytes 638984 | tf_op jit(solution)/shard_map/ppermute | solution.py:375
  147.6 8.6 %collective-permute-start.6 = (bf16[768,256]{1,0:T(8,128)(2,1)S(1)}, bf16[768,256]{1,0:T(8,128)(2,1)S(1)}, u32[]{:S(2)}, u32[]{:S(2)}) collective-permute-start(bf16[768,256]{1,0:T(8,128)(2,1)S(1)} %get-tuple-element.58), channel_id=1, source_target_pairs={{0,4},{4,0},{8,12},{12,8},{16,20},{20,16},{24,28},{28,24},{1,5},{5... | collective-permute-start | bytes 1179656 | tf_op jit(solution)/shard_map/ppermute | solution.py:378
  148.3 12.2 %all-to-all-start.8 = ((f32[8,8,128]{2,1,0:T(8,128)}), f32[8,8,128]{2,1,0:T(8,128)S(1)}, u32[]{:S(2)}, u32[]{:S(2)}) async-start(f32[8,8,128]{2,1,0:T(8,128)} %get-tuple-element.54), calls=%async_computation.8 | async-start | bytes 65536 | tf_op jit(solution)/shard_map/all_to_all | solution.py:371
  156.3 8.4 %collective-permute-start.7 = (bf16[192,256]{1,0:T(8,128)(2,1)S(1)}, bf16[192,256]{1,0:T(8,128)(2,1)S(1)}, u32[]{:S(2)}, u32[]{:S(2)}) collective-permute-start(bf16[192,256]{1,0:T(8,128)(2,1)S(1)} %get-tuple-element.61), channel_id=1, source_target_pairs={{0,8},{4,12},{8,16},{12,20},{16,24},{20,28},{24,0},{28,4},{1,9},{5... | collective-permute-start | bytes 294920 | tf_op jit(solution)/shard_map/ppermute | solution.py:375
  157.2 7.6 %collective-permute-start.8 = (bf16[192,256]{1,0:T(8,128)(2,1)S(1)}, bf16[192,256]{1,0:T(8,128)(2,1)S(1)}, u32[]{:S(2)}, u32[]{:S(2)}) collective-permute-start(bf16[192,256]{1,0:T(8,128)(2,1)S(1)} %get-tuple-element.62), channel_id=1, source_target_pairs={{0,24},{4,28},{8,0},{12,4},{16,8},{20,12},{24,16},{28,20},{1,25},{... | collective-permute-start | bytes 294920 | tf_op jit(solution)/shard_map/ppermute | solution.py:375
  164.7 14.6 %all-to-all-start.9 = ((bf16[16,96,256]{2,1,0:T(8,128)(2,1)}), bf16[16,96,256]{2,1,0:T(8,128)(2,1)S(1)}, u32[]{:S(2)}, u32[]{:S(2)}) async-start(bf16[16,96,256]{2,1,0:T(8,128)(2,1)} %get-tuple-element.63), calls=%async_computation.9 | async-start | bytes 1572864 | tf_op jit(solution)/shard_map/all_to_all | solution.py:371
  170.0 8.1 %collective-permute-start.9 = (bf16[96,256]{1,0:T(8,128)(2,1)S(1)}, bf16[96,256]{1,0:T(8,128)(2,1)S(1)}, u32[]{:S(2)}, u32[]{:S(2)}) collective-permute-start(bf16[96,256]{1,0:T(8,128)(2,1)S(1)} %get-tuple-element.68), channel_id=1, source_target_pairs={{0,16},{4,20},{8,24},{12,28},{16,0},{20,4},{24,8},{28,12},{1,17},{... | collective-permute-start | bytes 147464 | tf_op jit(solution)/shard_map/ppermute | solution.py:378

commit v13 on v11

--- a/solution.py
+++ b/solution.py
@@ -93,11 +93,15 @@
         copy.wait()
 
 
+def reach(count):
+    return [0] + sorted(range(1, count), key=lambda k: -min(k, count - k))
+
+
 def stack(own, count, *refs):
     out_ref = refs[count]
     size = own + AUX
     for k in range(count):
-        place = behind("row", k, count)
+        place = behind("row", reach(count)[k], count)
         out_ref[pl.ds(pl.multiple_of(place * size, size), size), :] = refs[k][...]
 
 
@@ -136,7 +140,7 @@
     cmass = cph = None
     for m in range(steps):
         src = pi_refs[m]
-        t = behind("y", m, steps)
+        t = behind("y", reach(steps)[m], steps)
         base = pl.multiple_of(t * span, span)
         first = pl.multiple_of(t * GROUP, GROUP)
         ibias = []
@@ -414,11 +418,11 @@
         hbm=(1,),
     )
     jgot = swap(jpack, jaxes)
-    near = [shift(ipack, "row", k) for k in range(1, xsrc)]
+    near = [shift(ipack, "row", k) for k in reach(xsrc)[1:]]
     (line,) = call(
         functools.partial(stack, own, xsrc), 1, [((xsrc * (own + AUX), width), BF16)], ipack, *near
     )
-    igot = [line] + [shift(line, "y", k) for k in range(1, ysrc)]
+    igot = [line] + [shift(line, "y", k) for k in reach(ysrc)[1:]]
     plan, inner, xi, wts, send, col_part, bias = call(
         functools.partial(build, own, width, isrc, jsrc),
         5,

time: 158 us -> 158 us (level)
  transfers between devices with their start and end apart: 13 -> 13, of which waited for: 10 -> 7; matrix products, arithmetic and copies ran while one was open for 0% -> 0% of each run, Pallas kernels for 3% -> 3%
where the time goes in v13:
time: 158 us; the launch traced here: 157 us
  blocking collectives  79.9 us (51%)
  starting transfers between devices  35.3 us (22%)
  waiting for transfers between devices  23.8 us (15%)
  Pallas kernels  16.6 us (11%)
    all_to_all x7, blocking collectives, swap(): return lax.all_to_all(value, axes, 0, 0, tiled=True)  79.9 us
    all_to_all x3, starting transfers between devices, swap(): return lax.all_to_all(value, axes, 0, 0, tiled=True)  17 us
    pallas_call x14, Pallas kernels, call(): pl.pallas_call(body, out_shape=[(pltpu.HBM if n in hbm else jax.ShapeDtyp...  16.6 us
    ppermute x8, starting transfers between devices, shift(): return lax.ppermute(value, axis, [(i, (i + k) % n) for i in range(n)])  14.9 us
    ppermute x2, waiting for transfers between devices, flip(): return lax.ppermute(value, 'z', [(i, i ^ bit) for i in range(jsrc)])  9.51 us
    ppermute x8, waiting for transfers between devices, shift(): return lax.ppermute(value, axis, [(i, (i + k) % n) for i in range(n)])  9.31 us
    all_to_all x3, waiting for transfers between devices, swap(): return lax.all_to_all(value, axes, 0, 0, tiled=True)  5.01 us
    ppermute x2, starting transfers between devices, flip(): return lax.ppermute(value, 'z', [(i, i ^ bit) for i in range(jsrc)])  3.43 us
  transfers between devices with their start and end apart: 13, of which 7 were waited for; matrix products, arithmetic and copies ran while one was open for 0% of the time, Pallas kernels for 3%

profile of v13, /device:TPU:8, one launch (start us, length us, event | category | flops | bytes accessed | tf_op | source)
XLA Modules:
  0.0 156.8 jit_solution(5093560645681758259)
XLA Ops:
  0.6 1.9 %shard_map.68 = (bf16[104,256]{1,0:T(8,128)(2,1)S(1)}, bf16[8,200,256]{2,1,0:T(8,128)(2,1)}) custom-call(bf16[96,256]{1,0:T(8,128)(2,1)} %x_ref.1, bf16[96,256]{1,0:T(8,128)(2,1)} %gy_ref.1, bf16[1,96]{1,0:T(2,128)(2,1)} %bitcast.5, bf16[1,96]{1,0:T(2,128)(2,1)} %bitcast.6, bf16[1,96]{1,0:T(2,128)(2,1)} %bitcast.7), custom_call_target="tpu_custom_call" | custom-call | flops 2000000000 | bytes 1024 | tf_op jit(solution)/shard_map/pallas_call | solution.py:384
  2.5 8.5 %all-to-all-start = ((bf16[8,200,256]{2,1,0:T(8,128)(2,1)}), bf16[8,200,256]{2,1,0:T(8,128)(2,1)S(1)}, u32[]{:S(2)}, u32[]{:S(2)}) async-start(bf16[8,200,256]{2,1,0:T(8,128)(2,1)} %get-tuple-element.37), calls=%async_computation | async-start | bytes 1638400 | tf_op jit(solution)/shard_map/all_to_all | solution.py:374
  11.0 3.0 %collective-permute-start = (bf16[104,256]{1,0:T(8,128)(2,1)S(1)}, bf16[104,256]{1,0:T(8,128)(2,1)S(1)}, u32[]{:S(2)}, u32[]{:S(2)}) collective-permute-start(bf16[104,256]{1,0:T(8,128)(2,1)S(1)} %get-tuple-element.36.refs_0_), channel_id=1, source_target_pairs={{0,64},{32,96},{64,0},{96,32},{1,65},{33,97},{65,1},{97,33},{2,66}... | collective-permute-start | bytes 159752 | tf_op jit(solution)/shard_map/ppermute | solution.py:378
  14.0 0.6 collective-permute-start.1
  14.6 2.6 %collective-permute-start.2 = (bf16[104,256]{1,0:T(8,128)(2,1)S(1)}, bf16[104,256]{1,0:T(8,128)(2,1)S(1)}, u32[]{:S(2)}, u32[]{:S(2)}) collective-permute-start(bf16[104,256]{1,0:T(8,128)(2,1)S(1)} %get-tuple-element.36.refs_0_), channel_id=1, source_target_pairs={{0,96},{32,0},{64,32},{96,64},{1,97},{33,1},{65,33},{97,65},{2,98}... | collective-permute-start | bytes 159752 | tf_op jit(solution)/shard_map/ppermute | solution.py:378
  17.3 0.0 collective-permute-done.refs_1_
  17.3 2.1 %collective-permute-done.1.refs_2_ = bf16[104,256]{1,0:T(8,128)(2,1)S(1)} collective-permute-done((bf16[104,256]{1,0:T(8,128)(2,1)S(1)}, bf16[104,256]{1,0:T(8,128)(2,1)S(1)}, u32[]{:S(2)}, u32[]{:S(2)}) %collective-permute-start.1) | collective-permute-done | bytes 53280 | tf_op jit(solution)/shard_map/ppermute | solution.py:378
  19.4 0.0 collective-permute-done.2.refs_3_
  19.4 2.4 %collective-permute-start.3 = (bf16[416,256]{1,0:T(8,128)(2,1)S(1)}, bf16[416,256]{1,0:T(8,128)(2,1)S(1)}, u32[]{:S(2)}, u32[]{:S(2)}) collective-permute-start(bf16[416,256]{1,0:T(8,128)(2,1)S(1)} %shard_map.69.refs_0_), channel_id=1, source_target_pairs={{0,2},{1,3},{2,0},{3,1},{4,6},{5,7},{6,4},{7,5},{8,10},{9,11},{10,... | collective-permute-start | bytes 638984 | tf_op jit(solution)/shard_map/ppermute | solution.py:378
  21.8 0.0 collective-permute-start.4
  21.8 2.0 %collective-permute-start.5 = (bf16[416,256]{1,0:T(8,128)(2,1)S(1)}, bf16[416,256]{1,0:T(8,128)(2,1)S(1)}, u32[]{:S(2)}, u32[]{:S(2)}) collective-permute-start(bf16[416,256]{1,0:T(8,128)(2,1)S(1)} %shard_map.69.refs_0_), channel_id=1, source_target_pairs={{0,3},{1,0},{2,1},{3,2},{4,7},{5,4},{6,5},{7,6},{8,11},{9,8},{10,9... | collective-permute-start | bytes 638984 | tf_op jit(solution)/shard_map/ppermute | solution.py:378
  23.8 4.9 %collective-permute-done.3.refs_1_ = bf16[416,256]{1,0:T(8,128)(2,1)S(1)} collective-permute-done((bf16[416,256]{1,0:T(8,128)(2,1)S(1)}, bf16[416,256]{1,0:T(8,128)(2,1)S(1)}, u32[]{:S(2)}, u32[]{:S(2)}) %collective-permute-start.3) | collective-permute-done | bytes 213024 | tf_op jit(solution)/shard_map/ppermute | solution.py:378
  28.7 2.3 %collective-permute-done.4.refs_2_ = bf16[416,256]{1,0:T(8,128)(2,1)S(1)} collective-permute-done((bf16[416,256]{1,0:T(8,128)(2,1)S(1)}, bf16[416,256]{1,0:T(8,128)(2,1)S(1)}, u32[]{:S(2)}, u32[]{:S(2)}) %collective-permute-start.4) | collective-permute-done | bytes 213024 | tf_op jit(solution)/shard_map/ppermute | solution.py:378
  31.0 0.0 collective-permute-done.5.refs_3_
  31.0 3.8 %all-to-all-done.refs_4_.refs_6_ = bf16[8,200,256]{2,1,0:T(8,128)(2,1)S(1)} async-done(((bf16[8,200,256]{2,1,0:T(8,128)(2,1)}), bf16[8,200,256]{2,1,0:T(8,128)(2,1)S(1)}, u32[]{:S(2)}, u32[]{:S(2)}) %all-to-all-start) | async-done | bytes 819232 | tf_op jit(solution)/shard_map/all_to_all | solution.py:374
  34.8 3.3 %shard_map.70 = (f32[1536,768]{1,0:T(8,128)S(1)}, f32[1536,768]{1,0:T(8,128)S(1)}, bf16[1536,256]{1,0:T(8,128)(2,1)S(1)}, f32[16,128]{1,0:T(8,128)S(1)}, f32[16,...) custom-call(bf16[416,256]{1,0:T(8,128)(2,1)S(1)} %shard_map.69.refs_0_, ...), custom_call_target="tpu_custom_call" | custom-call | flops 5000000000 | bytes 1024 | tf_op jit(solution)/shard_map/pallas_call | solution.py:384
  38.1 14.2 %all_to_all.50.got_ref = f32[16,32,128]{2,1,0:T(8,128)S(1)} all-to-all(f32[16,32,128]{2,1,0:T(8,128)S(1)} %get-tuple-element.38), channel_id=1, replica_groups=mesh['filt'=2,'row'=4,'z'=8,'y'=4] {'y','row'}, dimensions={0} | all-to-all | bytes 524288 | tf_op jit(solution)/shard_map/all_to_all | solution.py:374
  52.3 0.7 shard_map.71
  52.9 11.4 %all_to_all.51.got_ref = f32[8,24,128]{2,1,0:T(8,128)S(1)} all-to-all(f32[8,24,128]{2,1,0:T(8,128)S(1)} %get-tuple-element.41), channel_id=1, replica_groups=mesh['filt'=2,'row'=4,'z'=8,'y'=4] {'z'}, dimensions={0} | all-to-all | bytes 196608 | tf_op jit(solution)/shard_map/all_to_all | solution.py:374
  64.3 0.4 shard_map.72
  64.8 11.4 %all_to_all.52.got_ref = f32[16,16,128]{2,1,0:T(8,128)S(1)} all-to-all(f32[16,16,128]{2,1,0:T(8,128)S(1)} %get-tuple-element.42), channel_id=1, replica_groups=mesh['filt'=2,'row'=4,'z'=8,'y'=4] {'y','row'}, dimensions={0} | all-to-all | bytes 262144 | tf_op jit(solution)/shard_map/all_to_all | solution.py:374
  76.1 0.6 shard_map.73
  76.8 10.4 %all_to_all.53.got_ref = f32[8,8,128]{2,1,0:T(8,128)S(1)} all-to-all(f32[8,8,128]{2,1,0:T(8,128)S(1)} %get-tuple-element.45), channel_id=1, replica_groups=mesh['filt'=2,'row'=4,'z'=8,'y'=4] {'z'}, dimensions={0} | all-to-all | bytes 65536 | tf_op jit(solution)/shard_map/all_to_all | solution.py:374
  87.2 0.4 shard_map.74
  87.6 11.1 %all_to_all.54.got_ref = f32[16,16,128]{2,1,0:T(8,128)S(1)} all-to-all(f32[16,16,128]{2,1,0:T(8,128)S(1)} %shard_map.74), channel_id=1, replica_groups=mesh['filt'=2,'row'=4,'z'=8,'y'=4] {'y','row'}, dimensions={0} | all-to-all | bytes 262144 | tf_op jit(solution)/shard_map/all_to_all | solution.py:374
  98.7 0.6 shard_map.75
  99.3 10.4 %all_to_all.55.got_ref = f32[8,8,128]{2,1,0:T(8,128)S(1)} all-to-all(f32[8,8,128]{2,1,0:T(8,128)S(1)} %get-tuple-element.47), channel_id=1, replica_groups=mesh['filt'=2,'row'=4,'z'=8,'y'=4] {'z'}, dimensions={0} | all-to-all | bytes 65536 | tf_op jit(solution)/shard_map/all_to_all | solution.py:374
  109.7 0.4 shard_map.76
  110.2 11.1 %all_to_all.56.refs_0_ = f32[16,16,128]{2,1,0:T(8,128)S(1)} all-to-all(f32[16,16,128]{2,1,0:T(8,128)S(1)} %get-tuple-element.48), channel_id=1, replica_groups=mesh['filt'=2,'row'=4,'z'=8,'y'=4] {'y','row'}, dimensions={0} | all-to-all | bytes 262144 | tf_op jit(solution)/shard_map/all_to_all | solution.py:374
  121.2 3.1 %shard_map.77 = (f32[16,128]{1,0:T(8,128)S(1)}, f32[8,8,128]{2,1,0:T(8,128)}, bf16[768,256]{1,0:T(8,128)(2,1)S(1)}, bf16[768,256]{1,0:T(8,128)(2,1)S(1)}) custom-call(f32[16,16,128]{2,1,0:T(8,128)S(1)} %all_to_all.56.refs_0_, f32[32,128]{1,0:T(8,128)S(1)} %get-tuple-element.43.mass_ref.refs_1_, f32[16,128]{1,0:T(8,128)S(1)} %get-tuple-element.44.w_ref.refs_2_, ...), custom_call_target="tpu_custom_call" | custom-call | flops 4000000000 | bytes 1024 | tf_op jit(solution)/shard_map/pallas_call | solution.py:384
  124.3 0.7 collective-permute-start.6
  125.0 3.3 %all-to-all-start.8 = ((f32[8,8,128]{2,1,0:T(8,128)}), f32[8,8,128]{2,1,0:T(8,128)S(1)}, u32[]{:S(2)}, u32[]{:S(2)}) async-start(f32[8,8,128]{2,1,0:T(8,128)} %get-tuple-element.54), calls=%async_computation.8 | async-start | bytes 65536 | tf_op jit(solution)/shard_map/all_to_all | solution.py:374
  128.3 4.7 %collective-permute-done.6.got_ref = bf16[768,256]{1,0:T(8,128)(2,1)S(1)} collective-permute-done((bf16[768,256]{1,0:T(8,128)(2,1)S(1)}, bf16[768,256]{1,0:T(8,128)(2,1)S(1)}, u32[]{:S(2)}, u32[]{:S(2)}) %collective-permute-start.6) | collective-permute-done | bytes 393248 | tf_op jit(solution)/shard_map/ppermute | solution.py:381
  133.0 0.1 shard_map.78
  133.1 0.8 collective-permute-start.7
  133.8 3.5 %collective-permute-start.8 = (bf16[192,256]{1,0:T(8,128)(2,1)S(1)}, bf16[192,256]{1,0:T(8,128)(2,1)S(1)}, u32[]{:S(2)}, u32[]{:S(2)}) collective-permute-start(bf16[192,256]{1,0:T(8,128)(2,1)S(1)} %get-tuple-element.62), channel_id=1, source_target_pairs={{0,24},{4,28},{8,0},{12,4},{16,8},{20,12},{24,16},{28,20},{1,25},{... | collective-permute-start | bytes 294920 | tf_op jit(solution)/shard_map/ppermute | solution.py:378
  137.3 0.0 all-to-all-done.8.refs_0_
  137.3 4.2 %shard_map.79 = (bf16[16,96,256]{2,1,0:T(8,128)(2,1)}, f32[16,128]{1,0:T(8,128)S(1)}, f32[192,1]{1,0:T(8,128)S(1)}) custom-call(f32[8,8,128]{2,1,0:T(8,128)S(1)} %all-to-all-done.8.refs_0_, f32[16,128]{1,0:T(8,128)S(1)} %get-tuple-element.46.col_ref.refs_1_, f32[16,128]{1,0:T(8,128)S(1)} %get-tuple-element.55.refs_2_, ...), custom_call_target="tpu_custom_call" | custom-call | flops 4000000000 | bytes 1024 | tf_op jit(solution)/shard_map/pallas_call | solution.py:384
  141.5 0.0 collective-permute-done.7.right_ref
  141.5 0.0 collective-permute-done.8.left_ref
  141.5 5.2 %all-to-all-start.9 = ((bf16[16,96,256]{2,1,0:T(8,128)(2,1)}), bf16[16,96,256]{2,1,0:T(8,128)(2,1)S(1)}, u32[]{:S(2)}, u32[]{:S(2)}) async-start(bf16[16,96,256]{2,1,0:T(8,128)(2,1)} %get-tuple-element.63), calls=%async_computation.9 | async-start | bytes 1572864 | tf_op jit(solution)/shard_map/all_to_all | solution.py:374
  146.7 0.1 shard_map.80
  146.8 2.8 %collective-permute-start.9 = (bf16[96,256]{1,0:T(8,128)(2,1)S(1)}, bf16[96,256]{1,0:T(8,128)(2,1)S(1)}, u32[]{:S(2)}, u32[]{:S(2)}) collective-permute-start(bf16[96,256]{1,0:T(8,128)(2,1)S(1)} %get-tuple-element.68), channel_id=1, source_target_pairs={{0,16},{4,20},{8,24},{12,28},{16,0},{20,4},{24,8},{28,12},{1,17},{... | collective-permute-start | bytes 147464 | tf_op jit(solution)/shard_map/ppermute | solution.py:381
  149.5 0.5 dynamic-slice_bitcast_fusion
  150.1 4.8 %collective-permute-done.9.got_ref = bf16[96,256]{1,0:T(8,128)(2,1)S(1)} collective-permute-done((bf16[96,256]{1,0:T(8,128)(2,1)S(1)}, bf16[96,256]{1,0:T(8,128)(2,1)S(1)}, u32[]{:S(2)}, u32[]{:S(2)}) %collective-permute-start.9) | collective-permute-done | bytes 49184 | tf_op jit(solution)/shard_map/ppermute | solution.py:381
  154.9 1.2 all-to-all-done.9.rows_ref
  156.1 0.7 shard_map.81
  (1 shorter events, 0.0 us)
Async XLA Ops:
  2.5 32.3 %all-to-all-start = ((bf16[8,200,256]{2,1,0:T(8,128)(2,1)}), bf16[8,200,256]{2,1,0:T(8,128)(2,1)S(1)}, u32[]{:S(2)}, u32[]{:S(2)}) async-start(bf16[8,200,256]{2,1,0:T(8,128)(2,1)} %get-tuple-element.37), calls=%async_computation | async-start | bytes 1638400 | tf_op jit(solution)/shard_map/all_to_all | solution.py:374
  11.0 6.3 %collective-permute-start = (bf16[104,256]{1,0:T(8,128)(2,1)S(1)}, bf16[104,256]{1,0:T(8,128)(2,1)S(1)}, u32[]{:S(2)}, u32[]{:S(2)}) collective-permute-start(bf16[104,256]{1,0:T(8,128)(2,1)S(1)} %get-tuple-element.36.refs_0_), channel_id=1, source_target_pairs={{0,64},{32,96},{64,0},{96,32},{1,65},{33,97},{65,1},{97,33},{2,66}... | collective-permute-start | bytes 159752 | tf_op jit(solution)/shard_map/ppermute | solution.py:378
  14.0 5.3 %collective-permute-start.1 = (bf16[104,256]{1,0:T(8,128)(2,1)S(1)}, bf16[104,256]{1,0:T(8,128)(2,1)S(1)}, u32[]{:S(2)}, u32[]{:S(2)}) collective-permute-start(bf16[104,256]{1,0:T(8,128)(2,1)S(1)} %get-tuple-element.36.refs_0_), channel_id=1, source_target_pairs={{0,32},{32,64},{64,96},{96,0},{1,33},{33,65},{65,97},{97,1},{2,34}... | collective-permute-start | bytes 159752 | tf_op jit(solution)/shard_map/ppermute | solution.py:378
  14.6 4.8 %collective-permute-start.2 = (bf16[104,256]{1,0:T(8,128)(2,1)S(1)}, bf16[104,256]{1,0:T(8,128)(2,1)S(1)}, u32[]{:S(2)}, u32[]{:S(2)}) collective-permute-start(bf16[104,256]{1,0:T(8,128)(2,1)S(1)} %get-tuple-element.36.refs_0_), channel_id=1, source_target_pairs={{0,96},{32,0},{64,32},{96,64},{1,97},{33,1},{65,33},{97,65},{2,98}... | collective-permute-start | bytes 159752 | tf_op jit(solution)/shard_map/ppermute | solution.py:378
  19.4 9.3 %collective-permute-start.3 = (bf16[416,256]{1,0:T(8,128)(2,1)S(1)}, bf16[416,256]{1,0:T(8,128)(2,1)S(1)}, u32[]{:S(2)}, u32[]{:S(2)}) collective-permute-start(bf16[416,256]{1,0:T(8,128)(2,1)S(1)} %shard_map.69.refs_0_), channel_id=1, source_target_pairs={{0,2},{1,3},{2,0},{3,1},{4,6},{5,7},{6,4},{7,5},{8,10},{9,11},{10,... | collective-permute-start | bytes 638984 | tf_op jit(solution)/shard_map/ppermute | solution.py:378
  21.8 9.2 %collective-permute-start.4 = (bf16[416,256]{1,0:T(8,128)(2,1)S(1)}, bf16[416,256]{1,0:T(8,128)(2,1)S(1)}, u32[]{:S(2)}, u32[]{:S(2)}) collective-permute-start(bf16[416,256]{1,0:T(8,128)(2,1)S(1)} %shard_map.69.refs_0_), channel_id=1, source_target_pairs={{0,1},{1,2},{2,3},{3,0},{4,5},{5,6},{6,7},{7,4},{8,9},{9,10},{10,1... | collective-permute-start | bytes 638984 | tf_op jit(solution)/shard_map/ppermute | solution.py:378
  21.8 9.2 %collective-permute-start.5 = (bf16[416,256]{1,0:T(8,128)(2,1)S(1)}, bf16[416,256]{1,0:T(8,128)(2,1)S(1)}, u32[]{:S(2)}, u32[]{:S(2)}) collective-permute-start(bf16[416,256]{1,0:T(8,128)(2,1)S(1)} %shard_map.69.refs_0_), channel_id=1, source_target_pairs={{0,3},{1,0},{2,1},{3,2},{4,7},{5,4},{6,5},{7,6},{8,11},{9,8},{10,9... | collective-permute-start | bytes 638984 | tf_op jit(solution)/shard_map/ppermute | solution.py:378
  124.3 8.7 %collective-permute-start.6 = (bf16[768,256]{1,0:T(8,128)(2,1)S(1)}, bf16[768,256]{1,0:T(8,128)(2,1)S(1)}, u32[]{:S(2)}, u32[]{:S(2)}) collective-permute-start(bf16[768,256]{1,0:T(8,128)(2,1)S(1)} %get-tuple-element.58), channel_id=1, source_target_pairs={{0,4},{4,0},{8,12},{12,8},{16,20},{20,16},{24,28},{28,24},{1,5},{5... | collective-permute-start | bytes 1179656 | tf_op jit(solution)/shard_map/ppermute | solution.py:381
  125.0 12.3 %all-to-all-start.8 = ((f32[8,8,128]{2,1,0:T(8,128)}), f32[8,8,128]{2,1,0:T(8,128)S(1)}, u32[]{:S(2)}, u32[]{:S(2)}) async-start(f32[8,8,128]{2,1,0:T(8,128)} %get-tuple-element.54), calls=%async_computation.8 | async-start | bytes 65536 | tf_op jit(solution)/shard_map/all_to_all | solution.py:374
  133.1 8.4 %collective-permute-start.7 = (bf16[192,256]{1,0:T(8,128)(2,1)S(1)}, bf16[192,256]{1,0:T(8,128)(2,1)S(1)}, u32[]{:S(2)}, u32[]{:S(2)}) collective-permute-start(bf16[192,256]{1,0:T(8,128)(2,1)S(1)} %get-tuple-element.61), channel_id=1, source_target_pairs={{0,8},{4,12},{8,16},{12,20},{16,24},{20,28},{24,0},{28,4},{1,9},{5... | collective-permute-start | bytes 294920 | tf_op jit(solution)/shard_map/ppermute | solution.py:378
  133.8 7.7 %collective-permute-start.8 = (bf16[192,256]{1,0:T(8,128)(2,1)S(1)}, bf16[192,256]{1,0:T(8,128)(2,1)S(1)}, u32[]{:S(2)}, u32[]{:S(2)}) collective-permute-start(bf16[192,256]{1,0:T(8,128)(2,1)S(1)} %get-tuple-element.62), channel_id=1, source_target_pairs={{0,24},{4,28},{8,0},{12,4},{16,8},{20,12},{24,16},{28,20},{1,25},{... | collective-permute-start | bytes 294920 | tf_op jit(solution)/shard_map/ppermute | solution.py:378
  141.5 14.6 %all-to-all-start.9 = ((bf16[16,96,256]{2,1,0:T(8,128)(2,1)}), bf16[16,96,256]{2,1,0:T(8,128)(2,1)S(1)}, u32[]{:S(2)}, u32[]{:S(2)}) async-start(bf16[16,96,256]{2,1,0:T(8,128)(2,1)} %get-tuple-element.63), calls=%async_computation.9 | async-start | bytes 1572864 | tf_op jit(solution)/shard_map/all_to_all | solution.py:374
  146.8 8.1 %collective-permute-start.9 = (bf16[96,256]{1,0:T(8,128)(2,1)S(1)}, bf16[96,256]{1,0:T(8,128)(2,1)S(1)}, u32[]{:S(2)}, u32[]{:S(2)}) collective-permute-start(bf16[96,256]{1,0:T(8,128)(2,1)S(1)} %get-tuple-element.68), channel_id=1, source_target_pairs={{0,16},{4,20},{8,24},{12,28},{16,0},{20,4},{24,8},{28,12},{1,17},{... | collective-permute-start | bytes 147464 | tf_op jit(solution)/shard_map/ppermute | solution.py:381
